TPU v7x, 512 devices: a whole 4x8x8 slice. The times are simulated.
512 devices in a mesh: dp: 16 (over z, core), tensor: 8 (over y), pipe: 4 (over x).
Axes of the slice: x: 4, y: 8, z: 8, core: 2. Of those that a mesh axis runs over, the one named last changes fastest.
Arguments:
- query: bfloat16 [4, 4096, 8, 640], P('pipe', 'dp', 'tensor'), may hold values from -40 to 40
- keys_values: bfloat16 [4, 4096, 8, 256], P('pipe', 'dp', 'tensor'), may hold values from -4 to 4
- doc_lengths: int32 [4, 8], P('pipe'), may hold values from 1 to 3072, 4096 in all within a row
- incoming_output_grad: bfloat16 [4, 4096, 8, 640], P('pipe', ('dp', 'tensor')), may hold values from -6 to 6
Outputs:
- attn_out: bfloat16 [4, 4096, 8, 640], P('pipe', 'dp', 'tensor')
- grad_query: bfloat16 [4, 4096, 8, 640], P('pipe', 'dp', 'tensor')
- grad_keys_values: bfloat16 [4, 4096, 8, 256], P('pipe', 'dp', 'tensor')
Inputs may be any that keep to these rules, and one draw needn't show every extreme that they name: `doc_lengths`: each row sums to 4096; no document is longer than 3072 positions, and some document of each row is exactly that long.
All inputs are finite; a program needn't handle non-finite values.
Results may differ from a plain program's by a relative error of at most 0.04.
Values may be sent and summed in bfloat16 or wider, within the bound.
No kernel may reach another device: no remote copies, remote signals or barrier semaphores. Data moves between devices by JAX's collectives and lax.ppermute only.
A program may use at most 64 MiB of HBM per device.

v0:
```python
import math

import jax
import jax.numpy as jnp
from jax import lax
from jax.sharding import PartitionSpec as P

NEG_LARGE = -1e30


def from_behind(value, axis, steps):
    count = lax.axis_size(axis)
    pairs = [(source, (source + steps) % count) for source in range(count)]
    return lax.ppermute(value, axis, pairs)


def document_of(positions, doc_ends):
    return jnp.sum((positions[:, None] >= doc_ends[None, :]).astype(jnp.int32), axis=1)


def first_start(position, doc_ends, lengths):
    starts = doc_ends - lengths
    return jnp.max(jnp.where(starts <= position, starts, 0))


def tile_setup(queries, query_start, key_pairs, key_start, key_block, doc_ends, lengths):
    query_rows, kv_heads, columns = queries.shape
    head_dim = key_pairs.shape[2] // 2
    group_size = columns // head_dim
    grouped_heads = queries.reshape(query_rows, kv_heads, group_size, head_dim)
    query_pos = query_start + jnp.arange(query_rows, dtype=jnp.int32)
    query_doc = document_of(query_pos, doc_ends)
    earliest = first_start(query_start, doc_ends, lengths)
    blocks = key_pairs.reshape(key_pairs.shape[0] // key_block, key_block, kv_heads, 2 * head_dim)
    offsets = jnp.arange(blocks.shape[0], dtype=jnp.int32) * key_block + key_start
    return (grouped_heads, query_pos, query_doc, earliest, blocks, offsets)


def tile_scores(grouped_heads, key_tile, offset, query_pos, query_doc, key_block, doc_ends):
    head_dim = grouped_heads.shape[3]
    key_pos = offset + jnp.arange(key_block, dtype=jnp.int32)
    key_doc = document_of(key_pos, doc_ends)
    allowed = (
        (key_pos[None, :] <= query_pos[:, None])
        & (key_doc[None, :] == query_doc[:, None])
        & (key_pos[None, :] >= 0)
    )
    scores = jnp.einsum(
        "bkgd,ckd->kgbc",
        grouped_heads,
        key_tile[:, :, :head_dim],
        preferred_element_type=jnp.float32,
    )
    scores = scores * (1.0 / math.sqrt(head_dim))
    return (jnp.where(allowed, scores, NEG_LARGE), allowed)


def attend_forward(queries, query_start, key_pairs, key_start, key_block, doc_ends, lengths):
    grouped_heads, query_pos, query_doc, earliest, blocks, offsets = tile_setup(
        queries, query_start, key_pairs, key_start, key_block, doc_ends, lengths
    )
    query_rows, kv_heads, group_size, head_dim = grouped_heads.shape

    def visit(carried, inputs):
        key_tile, offset = inputs

        def compute(current):
            running, totals, accumulated = current
            scores, allowed = tile_scores(
                grouped_heads, key_tile, offset, query_pos, query_doc, key_block, doc_ends
            )
            updated = jnp.maximum(running, jnp.max(scores, axis=3))
            numerators = jnp.where(allowed, jnp.exp(scores - updated[..., None]), 0.0)
            factor = jnp.exp(running - updated)
            totals = totals * factor + jnp.sum(numerators, axis=3)
            weights = numerators.astype(jnp.bfloat16)
            accumulated = accumulated * factor[..., None] + jnp.einsum(
                "kgbc,ckd->kgbd",
                weights,
                key_tile[:, :, head_dim:],
                preferred_element_type=jnp.float32,
            )
            return (updated, totals, accumulated)

        skipped = (offset > query_start + query_rows - 1) | (offset + key_block - 1 < earliest)
        return (lax.cond(skipped, lambda current: current, compute, carried), None)

    initial = (
        jnp.full((kv_heads, group_size, query_rows), NEG_LARGE, jnp.float32),
        jnp.zeros((kv_heads, group_size, query_rows), jnp.float32),
        jnp.zeros((kv_heads, group_size, query_rows, head_dim), jnp.float32),
    )
    (running, totals, accumulated), unused = lax.scan(visit, initial, (blocks, offsets))
    result = (accumulated / totals[..., None]).transpose(2, 0, 1, 3)
    result = result.reshape(query_rows, kv_heads, group_size * head_dim).astype(jnp.bfloat16)
    return (result, running + jnp.log(totals))


def attend_backward(
    queries,
    query_start,
    log_totals,
    outputs,
    cotangent,
    key_pairs,
    key_start,
    key_block,
    doc_ends,
    lengths,
):
    grouped_heads, query_pos, query_doc, earliest, blocks, offsets = tile_setup(
        queries, query_start, key_pairs, key_start, key_block, doc_ends, lengths
    )
    query_rows, kv_heads, group_size, head_dim = grouped_heads.shape
    inv_root = 1.0 / math.sqrt(head_dim)
    grouped_grad = cotangent.reshape(query_rows, kv_heads, group_size, head_dim)
    grouped_out = outputs.reshape(query_rows, kv_heads, group_size, head_dim)
    delta = jnp.sum(
        grouped_grad.astype(jnp.float32) * grouped_out.astype(jnp.float32), axis=3
    ).transpose(1, 2, 0)

    def visit(carried, inputs):
        key_tile, offset = inputs

        def compute(query_grad):
            scores, allowed = tile_scores(
                grouped_heads, key_tile, offset, query_pos, query_doc, key_block, doc_ends
            )
            probs = jnp.where(allowed, jnp.exp(scores - log_totals[..., None]), 0.0)
            probs_low = probs.astype(jnp.bfloat16)
            value_grad = jnp.einsum(
                "kgbc,bkgd->ckd", probs_low, grouped_grad, preferred_element_type=jnp.float32
            )
            prob_grad = jnp.einsum(
                "bkgd,ckd->kgbc",
                grouped_grad,
                key_tile[:, :, head_dim:],
                preferred_element_type=jnp.float32,
            )
            score_grad = (probs * (prob_grad - delta[..., None])).astype(jnp.bfloat16)
            query_grad = query_grad + jnp.einsum(
                "kgbc,ckd->bkgd",
                score_grad,
                key_tile[:, :, :head_dim],
                preferred_element_type=jnp.float32,
            )
            key_grad = (
                jnp.einsum(
                    "kgbc,bkgd->ckd", score_grad, grouped_heads, preferred_element_type=jnp.float32
                )
                * inv_root
            )
            return (query_grad, jnp.concatenate([key_grad, value_grad], axis=2))

        def passed(query_grad):
            return (query_grad, jnp.zeros((key_block, kv_heads, 2 * head_dim), jnp.float32))

        skipped = (offset > query_start + query_rows - 1) | (offset + key_block - 1 < earliest)
        return lax.cond(skipped, passed, compute, carried)

    initial = jnp.zeros((query_rows, kv_heads, group_size, head_dim), jnp.float32)
    query_grad, tiles = lax.scan(visit, initial, (blocks, offsets))
    query_grad = (
        (query_grad * inv_root)
        .reshape(query_rows, kv_heads, group_size * head_dim)
        .astype(jnp.bfloat16)
    )
    return (query_grad, tiles.reshape(key_pairs.shape[0], kv_heads, 2 * head_dim))


def per_device(query, keys_values, doc_lengths, incoming_output_grad):
    arrived = from_behind(incoming_output_grad, "pipe", -1)
    cotangent = lax.all_to_all(arrived, "tensor", split_axis=2, concat_axis=1, tiled=True)[0]
    local_query = query[0]
    local_pairs = keys_values[0]
    lengths = doc_lengths[0]
    doc_ends = jnp.cumsum(lengths)
    shard_rows = local_query.shape[0]
    row_start = lax.axis_index("dp") * shard_rows
    every_pair = lax.all_gather(local_pairs, "dp", axis=0, tiled=True)
    outputs, log_totals = attend_forward(
        local_query, row_start, every_pair, 0, shard_rows, doc_ends, lengths
    )
    query_grad, key_partial = attend_backward(
        local_query,
        row_start,
        log_totals,
        outputs,
        cotangent,
        every_pair,
        0,
        shard_rows,
        doc_ends,
        lengths,
    )
    key_gradient_rows = lax.psum_scatter(
        key_partial.astype(jnp.bfloat16), "dp", scatter_dimension=0, tiled=True
    )
    return (outputs[None], query_grad[None], key_gradient_rows[None])


def solution(mesh):
    in_specs = (
        P("pipe", "dp", "tensor", None),
        P("pipe", "dp", "tensor", None),
        P("pipe", None),
        P("pipe", ("dp", "tensor"), None, None),
    )
    out_specs = (
        P("pipe", "dp", "tensor", None),
        P("pipe", "dp", "tensor", None),
        P("pipe", "dp", "tensor", None),
    )
    return jax.shard_map(
        per_device, mesh=mesh, in_specs=in_specs, out_specs=out_specs, check_vma=False
    )
```

profile of v0, /device:TPU:1, one launch (start us, length us, event | category | flops | bytes accessed | tf_op | source)
XLA Modules:
  0.0 320.0 jit_solution(670749666200704993)
XLA Ops:
  7.2 0.7 all-gather.3.cloned.1.call-update
  7.9 1.0 copy.63
  8.9 5.2 %collective-permute-start = (bf16[1,32,8,640]{3,1,0,2:T(8,128)(2,1)S(1)}, bf16[1,32,8,640]{3,1,0,2:T(8,128)(2,1)}, u32[]{:S(2)}, u32[]{:S(2)}) collective-permute-start(bf16[1,32,8,640]{3,1,0,2:T(8,128)(2,1)S(1)} %copy.63), channel_id=1, source_target_pairs={{0,3},{1,0},{2,1},{3,2},{4,7},{5,4},{6,5},{7,6},{8,11},{9,8},{10,9... | collective-permute-start | bytes 983048 | tf_op jit(solution)/shard_map/ppermute | solution.py:14
  14.2 4.0 %collective-permute-done = bf16[1,32,8,640]{3,1,0,2:T(8,128)(2,1)} collective-permute-done((bf16[1,32,8,640]{3,1,0,2:T(8,128)(2,1)S(1)}, bf16[1,32,8,640]{3,1,0,2:T(8,128)(2,1)}, u32[]{:S(2)}, u32[]{:S(2)}) %collective-permute-start) | collective-permute-done | bytes 327712 | tf_op jit(solution)/shard_map/ppermute | solution.py:14
  18.2 9.2 %all-to-all-start = ((bf16[1,32,8,640]{3,1,0,2:T(8,128)(2,1)}), bf16[1,32,8,640]{3,1,0,2:T(8,128)(2,1)S(1)}, u32[]{:S(2)}, u32[]{:S(2)}) async-start(bf16[1,32,8,640]{3,1,0,2:T(8,128)(2,1)} %collective-permute-done), calls=%async_computation | async-start | bytes 655360 | tf_op jit(solution)/shard_map/all_to_all | solution.py:173
  28.0 0.7 fusion.31
  28.8 9.6 %all-to-all-done = bf16[1,32,8,640]{3,1,0,2:T(8,128)(2,1)S(1)} async-done(((bf16[1,32,8,640]{3,1,0,2:T(8,128)(2,1)}), bf16[1,32,8,640]{3,1,0,2:T(8,128)(2,1)S(1)}, u32[]{:S(2)}, u32[]{:S(2)}) %all-to-all-start) | async-done | bytes 327712 | tf_op jit(solution)/shard_map/all_to_all | solution.py:173
  39.1 20.2 %all-gather.3.cloned.1.call-done = bf16[1,4096,1,256]{3,1,2,0:T(8,128)(2,1)} async-done(((bf16[1,256,1,256]{3,1,2,0:T(8,128)(2,1)}), bf16[1,4096,1,256]{3,1,2,0:T(8,128)(2,1)}) %all-gather.3.cloned.1.call-update) | async-done | bytes 2097168 | tf_op jit(solution)/shard_map/all_gather | solution.py:180
  59.3 48.2 %while.41 = (s32[]{:T(128)}, f32[1,5,256]{2,1,0:T(8,128)S(1)}, f32[1,5,256]{2,1,0:T(8,128)S(1)}, f32[1,5,256,128]{3,2,1,0:T(8,128)S(1)}, s32[16]{0:T(128)S(1)}, ...) while((s32[]{:T(128)}, f32[1,5,256]{2,1,0:T(8,128)S(1)}, ...), condition=%wide.region_9.10_spmd.clone, body=%wide.region_3.9_spmd.clone.sunk | while | flops 171321856 | bytes 6325111 | solution.py:93
  61.8 3.7 %conditional.6 = (f32[1,5,256]{2,1,0:T(8,128)S(1)}, f32[1,5,256]{2,1,0:T(8,128)S(1)}, f32[1,5,256,128]{3,2,1,0:T(8,128)S(1)}) conditional(s32[]{:T(128)} %convert_element_type.144, (s32[]{:T(128)}, s32[]{:T(128)}, s32[8]{0:T(128)S(1)}, s32[256]{0:T(256)S(1)}, bf16[16,256,1,256]{3,1,2,0:T(8,128)(2,1)}, /*index=5*/s32[]{:T(128)}, ...), branch_computations={%region_4.7_spmd, %region_8.8_spmd} | conditional | flops 171321856 | bytes 6313544 | solution.py:86
  63.4 0.9 dynamic-slice_bitcast_fusion
  68.1 3.7 %conditional.6 = (f32[1,5,256]{2,1,0:T(8,128)S(1)}, f32[1,5,256]{2,1,0:T(8,128)S(1)}, f32[1,5,256,128]{3,2,1,0:T(8,128)S(1)}) conditional(s32[]{:T(128)} %convert_element_type.144, (s32[]{:T(128)}, s32[]{:T(128)}, s32[8]{0:T(128)S(1)}, s32[256]{0:T(256)S(1)}, bf16[16,256,1,256]{3,1,2,0:T(8,128)(2,1)}, /*index=5*/s32[]{:T(128)}, ...), branch_computations={%region_4.7_spmd, %region_8.8_spmd} | conditional | flops 171321856 | bytes 6313544 | solution.py:86
  69.6 0.9 dynamic-slice_bitcast_fusion
  108.0 59.6 %while.42 = (s32[]{:T(128)}, f32[256,1,5,128]{0,3,2,1:T(8,128)S(1)}, bf16[16,256,1,256]{1,3,2,0:T(8,128)(2,1)}, s32[16]{0:T(128)S(1)}, s32[]{:T(128)}, /*index=5...) while((s32[]{:T(128)}, ...), condition=%wide.region_15.16_spmd.clone, body=%wide.region_11.15_spmd.clone.sunk | while | flops 422812416 | bytes 9792879 | solution.py:162
  110.5 4.3 %conditional.7 = (f32[256,1,5,128]{0,3,2,1:T(8,128)S(1)}, bf16[1,256,1,256]{1,3,2,0:T(8,128)(2,1)S(1)}) conditional(s32[]{:T(128)} %convert_element_type.145, (bf16[16,256,1,256]{3,1,2,0:T(8,128)(2,1)}, s32[]{:T(128)}, s32[]{:T(128)}, s32[]{:T(128)}, s32[8]{0:T(128)S(1)}, /*index=5*/s32[256]{0:T(256)S(1)}, bf16[256,1,5,128]{0,3,2,1:T(8,128)(2,1)S(1)}, ...), branch_computations={%region_12.13_spmd, %region_14.14_spmd} | conditional | flops 422812416 | bytes 9528896 | solution.py:159
  112.0 0.9 dynamic-slice_bitcast_fusion.1
  117.9 4.3 %conditional.7 = (f32[256,1,5,128]{0,3,2,1:T(8,128)S(1)}, bf16[1,256,1,256]{1,3,2,0:T(8,128)(2,1)S(1)}) conditional(s32[]{:T(128)} %convert_element_type.145, (bf16[16,256,1,256]{3,1,2,0:T(8,128)(2,1)}, s32[]{:T(128)}, s32[]{:T(128)}, s32[]{:T(128)}, s32[8]{0:T(128)S(1)}, /*index=5*/s32[256]{0:T(256)S(1)}, bf16[256,1,5,128]{0,3,2,1:T(8,128)(2,1)S(1)}, ...), branch_computations={%region_12.13_spmd, %region_14.14_spmd} | conditional | flops 422812416 | bytes 9528896 | solution.py:159
  119.5 0.9 dynamic-slice_bitcast_fusion.1
  151.0 0.7 constant_dynamic-update-slice_fusion.2
  166.9 0.7 constant_dynamic-update-slice_fusion.2
  167.6 3.9 %copy.66 = bf16[16,256,1,256]{3,1,0,2:T(8,128)(2,1)} copy(bf16[16,256,1,256]{1,3,2,0:T(8,128)(2,1)} %get-tuple-element.752) | data formatting | bytes 4194304 | tf_op jit(solution)/shard_map/convert_element_type | solution.py:197
  171.5 0.9 copy.67
  172.5 0.9 copy.68
  173.4 139.7 %reduce-scatter.2.cloned.1.call-done = bf16[256,1,256]{2,0,1:T(8,128)(2,1)} async-done(((bf16[4096,1,256]{2,0,1:T(8,128)(2,1)}), bf16[256,1,256]{2,0,1:T(8,128)(2,1)}) %reduce-scatter.2.cloned.1.call-update) | async-done | bytes 131088 | tf_op jit(solution)/shard_map/reduce_scatter | solution.py:196
  (212 shorter events, 44.0 us)
Async XLA Ops:
  7.2 20.2 %copy-start.1 = (s32[1,8]{1,0:T(1,128)S(1)}, s32[1,8]{1,0:T(1,128)}, u32[]{:S(2)}) copy-start(s32[1,8]{1,0:T(1,128)} %param.14) | copy-start | bytes 100
  7.2 20.4 %copy-start = (bf16[1,256,1,640]{3,1,2,0:T(8,128)(2,1)S(1)}, bf16[1,256,1,640]{3,1,2,0:T(8,128)(2,1)}, u32[]{:S(2)}) copy-start(bf16[1,256,1,640]{3,1,2,0:T(8,128)(2,1)} %param.12) | copy-start | bytes 983044
  7.2 52.1 %all-gather.3.cloned.1.call-start = ((), (), s32[]{:S(2)}) async-start(), calls=%async_computation.3 | async-start | bytes 2228224 | tf_op jit(solution)/shard_map/all_gather | solution.py:180
  8.9 9.2 %collective-permute-start = (bf16[1,32,8,640]{3,1,0,2:T(8,128)(2,1)S(1)}, bf16[1,32,8,640]{3,1,0,2:T(8,128)(2,1)}, u32[]{:S(2)}, u32[]{:S(2)}) collective-permute-start(bf16[1,32,8,640]{3,1,0,2:T(8,128)(2,1)S(1)} %copy.63), channel_id=1, source_target_pairs={{0,3},{1,0},{2,1},{3,2},{4,7},{5,4},{6,5},{7,6},{8,11},{9,8},{10,9... | collective-permute-start | bytes 983048 | tf_op jit(solution)/shard_map/ppermute | solution.py:14
  18.2 20.3 %all-to-all-start = ((bf16[1,32,8,640]{3,1,0,2:T(8,128)(2,1)}), bf16[1,32,8,640]{3,1,0,2:T(8,128)(2,1)S(1)}, u32[]{:S(2)}, u32[]{:S(2)}) async-start(bf16[1,32,8,640]{3,1,0,2:T(8,128)(2,1)} %collective-permute-done), calls=%async_computation | async-start | bytes 655360 | tf_op jit(solution)/shard_map/all_to_all | solution.py:173
  27.3 285.8 %reduce-scatter.2.cloned.1.call-start = ((), (), s32[]{:S(2)}) async-start(), calls=%async_computation.2 | async-start | bytes 2228224 | tf_op jit(solution)/shard_map/reduce_scatter | solution.py:196
Sparse Core Ops, SparseCore 0:
  10.1 49.1 all-gather.2
  171.6 141.4 reduce-scatter.1
where the time goes:
time: 324 us; the launch traced here: 320 us
  waiting for transfers between devices  174 us (54%)
  loops' own time  61.8 us (19%)
  local copies, waits for them, and re-layouts  42 us (13%)
  starting transfers between devices  14.5 us (4%)
  between operations  14.2 us (4%)
  other arithmetic  7.68 us (2%)
  matrix products  5.56 us (2%)
    reduce_scatter x1, waiting for transfers between devices, per_device(): lax.psum_scatter(key_partial.astype(jnp.bfloat16), 'dp', scatter_dimensio...  140 us
    another operation x1, loops' own time, attend_forward(): lax.scan(visit, initial, (blocks, offsets))  30.4 us
    another operation x1, loops' own time, attend_backward(): query_grad, tiles = lax.scan(visit, initial, (blocks, offsets))  30.3 us
    all_gather x1, waiting for transfers between devices, per_device(): every_pair = lax.all_gather(local_pairs, 'dp', axis=0, tiled=True)  20.2 us
    dynamic_slice x32, local copies, waits for them, and re-layouts, attend_forward(): lax.scan(visit, initial, (blocks, offsets))  19.3 us
    dynamic_update_slice x16, local copies, waits for them, and re-layouts, attend_backward(): query_grad, tiles = lax.scan(visit, initial, (blocks, offsets))  10.6 us
    all_to_all x1, waiting for transfers between devices, per_device(): lax.all_to_all(arrived, 'tensor', split_axis=2, concat_axis=1, tiled=True)  9.62 us
    all_to_all x1, starting transfers between devices, per_device(): lax.all_to_all(arrived, 'tensor', split_axis=2, concat_axis=1, tiled=True)  9.18 us
  transfers between devices with their start and end apart: 4, of which 4 were waited for; matrix products, arithmetic and copies ran while one was open for 2% of the time, Pallas kernels for 0%

commit v1 on v0

v1 whole, which is shorter than its diff:
```python
import functools
import math

import jax
import jax.numpy as jnp
from jax import lax
from jax.experimental import pallas as pl
from jax.experimental.pallas import tpu as pltpu
from jax.sharding import Mesh, PartitionSpec as P

NEG_LARGE = -1e30
LOG2E = math.log2(math.e)
HEAD = 128
LONGEST = 3072


def matmul(left, right):
    return jnp.dot(left, right, preferred_element_type=jnp.float32)


def block_mask(block, rows, bounds_ref, starts_ref):
    key_pos = block * rows + lax.broadcasted_iota(jnp.int32, (rows, rows), 0)
    query_pos = bounds_ref[0] * rows + lax.broadcasted_iota(jnp.int32, (rows, rows), 1)
    return (key_pos <= query_pos) & (key_pos >= starts_ref[...])


def over_blocks(visit, bounds_ref):
    own, first, clear = bounds_ref[0], bounds_ref[1], bounds_ref[2]

    def masked(step, unused):
        visit(jnp.where(step == 0, own, first + step - 1), True)
        return unused

    def plain(block, unused):
        visit(block, False)
        return unused

    lax.fori_loop(0, clear - first + 1, masked, 0)
    lax.fori_loop(clear, own, plain, 0)


def forward_kernel(
    bounds_ref, starts_ref, turned_ref, pairs_ref, turned_grad_ref,
    out_ref, log_ref, delta_ref, top_ref, total_ref, acc_ref,
):
    rows = starts_ref.shape[1]
    heads = turned_ref.shape[1] // rows
    scale = LOG2E / math.sqrt(HEAD)
    top_ref[...] = jnp.full_like(top_ref, NEG_LARGE)
    total_ref[...] = jnp.zeros_like(total_ref)
    acc_ref[...] = jnp.zeros_like(acc_ref)

    def visit(block, masked):
        at = pl.ds(pl.multiple_of(block * rows, rows), rows)
        keys = pairs_ref[at, :HEAD]
        turned_values = pairs_ref[at, HEAD:].T
        if masked:
            allowed = block_mask(block, rows, bounds_ref, starts_ref)
        for head in range(heads):
            span = slice(head * rows, (head + 1) * rows)
            scores = matmul(keys, turned_ref[:, span]) * scale
            if masked:
                scores = jnp.where(allowed, scores, NEG_LARGE)
            before = top_ref[:, span]
            top = jnp.maximum(before, jnp.max(scores, axis=0, keepdims=True))
            numerators = jnp.exp2(scores - top)
            factor = jnp.exp2(before - top)
            top_ref[:, span] = top
            total_ref[:, span] = total_ref[:, span] * factor + jnp.sum(
                numerators, axis=0, keepdims=True
            )
            acc_ref[:, span] = acc_ref[:, span] * factor + matmul(
                turned_values, numerators.astype(jnp.bfloat16)
            )

    over_blocks(visit, bounds_ref)
    totals = total_ref[...]
    log_ref[...] = top_ref[...] + jnp.log2(totals)
    for head in range(heads):
        span = slice(head * rows, (head + 1) * rows)
        result = (acc_ref[:, span] / total_ref[:, span]).astype(jnp.bfloat16)
        delta_ref[:, span] = jnp.sum(
            result.astype(jnp.float32) * turned_grad_ref[:, span].astype(jnp.float32),
            axis=0,
            keepdims=True,
        )
        out_ref[:, head * HEAD : (head + 1) * HEAD] = result.T


def backward_kernel(
    bounds_ref, starts_ref, query_ref, grad_ref, turned_ref, turned_grad_ref,
    pairs_ref, log_ref, delta_ref, query_grad_ref, pair_grad_ref, acc_ref,
):
    rows = starts_ref.shape[1]
    heads = turned_ref.shape[1] // rows
    root = 1.0 / math.sqrt(HEAD)
    scale = LOG2E * root
    acc_ref[...] = jnp.zeros_like(acc_ref)
    pair_grad_ref[...] = jnp.zeros_like(pair_grad_ref)
    half = pair_grad_ref.shape[0] // 2
    own = bounds_ref[0]

    def visit(block, masked):
        at = pl.ds(pl.multiple_of(block * rows, rows), rows)
        keys = pairs_ref[at, :HEAD]
        values = pairs_ref[at, HEAD:]
        turned_keys = keys.T
        if masked:
            allowed = block_mask(block, rows, bounds_ref, starts_ref)
        key_grad = jnp.zeros((rows, HEAD), jnp.float32)
        value_grad = jnp.zeros((rows, HEAD), jnp.float32)
        for head in range(heads):
            span = slice(head * rows, (head + 1) * rows)
            columns = slice(head * HEAD, (head + 1) * HEAD)
            scores = matmul(keys, turned_ref[:, span]) * scale
            if masked:
                scores = jnp.where(allowed, scores, NEG_LARGE)
            probs = jnp.exp2(scores - log_ref[:, span])
            prob_grad = matmul(values, turned_grad_ref[:, span])
            score_grad = (probs * (prob_grad - delta_ref[:, span])).astype(jnp.bfloat16)
            value_grad += matmul(probs.astype(jnp.bfloat16), grad_ref[:, columns])
            key_grad += matmul(score_grad, query_ref[:, columns])
            acc_ref[:, span] += matmul(turned_keys, score_grad)
        back = own // 2 - block // 2
        other = jnp.where(block % 2 == own % 2, 0, half)
        to = pl.ds(pl.multiple_of(other + back * rows, rows), rows)
        pair_grad_ref[to, :HEAD] = (key_grad * root).astype(jnp.bfloat16)
        pair_grad_ref[to, HEAD:] = value_grad.astype(jnp.bfloat16)

    over_blocks(visit, bounds_ref)
    for head in range(heads):
        span = slice(head * rows, (head + 1) * rows)
        turned = (acc_ref[:, span] * root).astype(jnp.bfloat16)
        query_grad_ref[:, head * HEAD : (head + 1) * HEAD] = turned.T


def smem():
    return pl.BlockSpec(memory_space=pltpu.SMEM)


def vmem():
    return pl.BlockSpec(memory_space=pltpu.VMEM)


def forward(bounds, starts, turned, pairs, turned_grad, rows):
    wide = turned.shape[1]
    columns = wide // rows * HEAD
    return pl.pallas_call(
        forward_kernel,
        out_shape=(
            jax.ShapeDtypeStruct((rows, columns), jnp.bfloat16),
            jax.ShapeDtypeStruct((1, wide), jnp.float32),
            jax.ShapeDtypeStruct((1, wide), jnp.float32),
        ),
        in_specs=[smem()] + [vmem()] * 4,
        out_specs=(vmem(),) * 3,
        scratch_shapes=[
            pltpu.VMEM((1, wide), jnp.float32),
            pltpu.VMEM((1, wide), jnp.float32),
            pltpu.VMEM((HEAD, wide), jnp.float32),
        ],
        compiler_params=pltpu.CompilerParams(vmem_limit_bytes=40 << 20),
        name="attend_forward",
    )(bounds, starts, turned, pairs, turned_grad)


def backward(bounds, starts, query, grad, turned, turned_grad, pairs, log_totals, delta, slots):
    rows = query.shape[0]
    wide = turned.shape[1]
    return pl.pallas_call(
        backward_kernel,
        out_shape=(
            jax.ShapeDtypeStruct(query.shape, jnp.bfloat16),
            jax.ShapeDtypeStruct((2 * slots * rows, 2 * HEAD), jnp.bfloat16),
        ),
        in_specs=[smem()] + [vmem()] * 8,
        out_specs=(vmem(),) * 2,
        scratch_shapes=[pltpu.VMEM((HEAD, wide), jnp.float32)],
        compiler_params=pltpu.CompilerParams(vmem_limit_bytes=40 << 20),
        name="attend_backward",
    )(bounds, starts, query, grad, turned, turned_grad, pairs, log_totals, delta)


def turn(array):
    rows, columns = array.shape
    heads = columns // HEAD
    return array.reshape(rows, heads, HEAD).transpose(2, 1, 0).reshape(HEAD, heads * rows)


def block_bounds(lengths, own, rows):
    ends = jnp.cumsum(lengths)
    begins = ends - lengths
    positions = own * rows + jnp.arange(rows, dtype=jnp.int32)
    starts = jnp.max(jnp.where(begins[:, None] <= positions[None, :], begins[:, None], 0), axis=0)
    first = starts[0] // rows
    clear = jnp.minimum((starts[-1] + rows - 1) // rows, own)
    return jnp.stack([own, first, clear]).astype(jnp.int32), starts[None, :]


def swap_cores(value):
    return lax.ppermute(value, "core", [(0, 1), (1, 0)])


def per_device(query, keys_values, doc_lengths, incoming_output_grad):
    chips = lax.axis_size("chip")
    query = query[0, :, 0, :]
    pairs = keys_values[0, :, 0, :]
    rows = query.shape[0]
    own = lax.axis_index("chip") * 2 + lax.axis_index("core")
    every_pair = lax.all_gather(pairs, ("chip", "core"), axis=0, tiled=True)
    sections = lax.axis_size("pipe")
    arrived = lax.ppermute(
        incoming_output_grad, "pipe", [(s, (s - 1) % sections) for s in range(sections)]
    )
    grad = lax.all_to_all(arrived, "tensor", split_axis=2, concat_axis=1, tiled=True)[0, :, 0, :]
    bounds, starts = block_bounds(doc_lengths[0], own, rows)
    turned, turned_grad = turn(query), turn(grad)
    outputs, log_totals, delta = forward(bounds, starts, turned, every_pair, turned_grad, rows)
    reach = min((LONGEST + 2 * rows - 1) // (2 * rows), chips - 1)
    slots = reach + 1
    query_grad, partial = backward(
        bounds, starts, query, grad, turned, turned_grad, every_pair, log_totals, delta, slots
    )
    half = slots * rows
    mine = partial[:half].astype(jnp.float32) + swap_cores(partial[half:]).astype(jnp.float32)
    mine = mine.reshape(slots, rows, 2 * HEAD)
    sums = mine[0]
    low = mine.astype(jnp.bfloat16)
    for back in range(1, slots):
        sums += lax.ppermute(
            low[back], "chip", [(c, c - back) for c in range(back, chips)]
        ).astype(jnp.float32)
    pair_grad = sums.astype(jnp.bfloat16)
    return (outputs[None, :, None, :], query_grad[None, :, None, :], pair_grad[None, :, None, :])


def solution(mesh):
    shape = mesh.devices.shape
    split = Mesh(
        mesh.devices.reshape((shape[0] // 2, 2) + shape[1:]), ("chip", "core", "tensor", "pipe")
    )
    dp = ("chip", "core")
    by_head = P("pipe", dp, "tensor", None)
    in_specs = (by_head, by_head, P("pipe", None), P("pipe", dp + ("tensor",), None, None))
    return jax.shard_map(
        per_device, mesh=split, in_specs=in_specs, out_specs=(by_head,) * 3, check_vma=False
    )
```

time: 324 us -> 131 us (0.40)
  the two profiles are of different devices: /device:TPU:1 before, /device:TPU:192 now
where the time goes in v1:
time: 131 us; the launch traced here: 130 us
  waiting for transfers between devices  56.2 us (43%)
  starting transfers between devices  25.2 us (19%)
  Pallas kernels  23.1 us (18%)
  between operations  17.5 us (13%)
  local copies, waits for them, and re-layouts  5.45 us (4%)
  other arithmetic  2.69 us (2%)
    ppermute x6, waiting for transfers between devices, per_device(): lax.ppermute(low[back], 'chip', [(c, c - back) for c in range(back, chips)])  27.4 us
    all_gather x1, waiting for transfers between devices, per_device(): every_pair = lax.all_gather(pairs, ('chip', 'core'), axis=0, tiled=True)  13.9 us
    pallas_call x1, Pallas kernels, forward(): pl.pallas_call(forward_kernel, out_shape=(jax.ShapeDtypeStruct((rows, col...  12.1 us
    pallas_call x1, Pallas kernels, backward(): pl.pallas_call(backward_kernel, out_shape=(jax.ShapeDtypeStruct(query.sha...  11.1 us
    ppermute x6, starting transfers between devices, per_device(): lax.ppermute(low[back], 'chip', [(c, c - back) for c in range(back, chips)])  8.38 us
    all_to_all x1, starting transfers between devices, per_device(): lax.all_to_all(arrived, 'tensor', split_axis=2, concat_axis=1, tiled=True)  7.1 us
    ppermute x1, waiting for transfers between devices, per_device(): lax.ppermute(incoming_output_grad, 'pipe', [(s, (s - 1) % sections) for s...  6.94 us
    all_to_all x1, waiting for transfers between devices, per_device(): lax.all_to_all(arrived, 'tensor', split_axis=2, concat_axis=1, tiled=True)  5.33 us
  transfers between devices with their start and end apart: 10, of which 7 were waited for; matrix products, arithmetic and copies ran while one was open for 4% of the time, Pallas kernels for 0%

profile of v1, /device:TPU:192, one launch (start us, length us, event | category | flops | bytes accessed | tf_op | source)
XLA Modules:
  0.0 130.2 jit_solution(4251573990594531131)
XLA Ops:
  7.2 0.7 all-gather.3.cloned.1.call-update
  7.9 1.0 copy.28
  8.9 4.7 %collective-permute-start = (bf16[1,32,8,640]{3,1,0,2:T(8,128)(2,1)S(1)}, bf16[1,32,8,640]{3,1,0,2:T(8,128)(2,1)}, u32[]{:S(2)}, u32[]{:S(2)}) collective-permute-start(bf16[1,32,8,640]{3,1,0,2:T(8,128)(2,1)S(1)} %copy.28), channel_id=1, source_target_pairs={{0,3},{1,0},{2,1},{3,2},{4,7},{5,4},{6,5},{7,6},{8,11},{9,8},{10,9... | collective-permute-start | bytes 983048 | tf_op jit(solution)/shard_map/ppermute | solution.py:212
  13.6 6.9 %collective-permute-done = bf16[1,32,8,640]{3,1,0,2:T(8,128)(2,1)} collective-permute-done((bf16[1,32,8,640]{3,1,0,2:T(8,128)(2,1)S(1)}, bf16[1,32,8,640]{3,1,0,2:T(8,128)(2,1)}, u32[]{:S(2)}, u32[]{:S(2)}) %collective-permute-start) | collective-permute-done | bytes 327712 | tf_op jit(solution)/shard_map/ppermute | solution.py:212
  20.5 7.1 %all-to-all-start = ((bf16[1,32,8,640]{3,1,0,2:T(8,128)(2,1)}), bf16[1,32,8,640]{3,1,0,2:T(8,128)(2,1)S(1)}, u32[]{:S(2)}, u32[]{:S(2)}) async-start(bf16[1,32,8,640]{3,1,0,2:T(8,128)(2,1)} %collective-permute-done), calls=%async_computation | async-start | bytes 655360 | tf_op jit(solution)/shard_map/all_to_all | solution.py:215
  27.6 0.8 reduce-window.8
  33.1 1.1 copy.26
  34.7 5.3 %all-to-all-done = bf16[1,32,8,640]{3,1,0,2:T(8,128)(2,1)S(1)} async-done(((bf16[1,32,8,640]{3,1,0,2:T(8,128)(2,1)}), bf16[1,32,8,640]{3,1,0,2:T(8,128)(2,1)S(1)}, u32[]{:S(2)}, u32[]{:S(2)}) %all-to-all-start) | async-done | bytes 327712 | tf_op jit(solution)/shard_map/all_to_all | solution.py:215
  40.7 13.9 %all-gather.3.cloned.1.call-done = bf16[1,4096,1,256]{3,1,2,0:T(8,128)(2,1)} async-done(((bf16[1,256,1,256]{3,1,2,0:T(8,128)(2,1)}), bf16[1,4096,1,256]{3,1,2,0:T(8,128)(2,1)}) %all-gather.3.cloned.1.call-update) | async-done | bytes 2097168 | tf_op jit(solution)/shard_map/all_gather | solution.py:210
  54.5 1.6 %copy-done = bf16[1,4096,1,256]{3,1,2,0:T(8,128)(2,1)S(1)} copy-done((bf16[1,4096,1,256]{3,1,2,0:T(8,128)(2,1)S(1)}, bf16[1,4096,1,256]{3,1,2,0:T(8,128)(2,1)}, u32[]{:S(2)}) %copy-start) | copy-done | bytes 2097176
  56.1 12.1 %attend_forward.1 = (bf16[256,640]{1,0:T(8,128)(2,1)}, f32[1,1280]{1,0:T(1,128)S(1)}, f32[1,1280]{1,0:T(1,128)S(1)}) custom-call(s32[3]{0:T(128)S(1)} %pad_add_fusion.bounds_ref, s32[1,256]{1,0:T(1,128)S(1)} %bitcast.37, bf16[128,1280]{1,0:T(8,128)(2,1)S(1)} %copy.30.turned_ref, bf16[4096,256]{1,0:T(8,128)(2,1)S(1)} %bitcast.32, ...), custom_call_target="tpu_custom_call" | custom-call | tf_op jit(solution)/shard_map/attend_forward/pallas_call | solution.py:148
  68.2 11.1 %attend_backward.1 = (bf16[256,640]{1,0:T(8,128)(2,1)}, bf16[3584,256]{1,0:T(8,128)(2,1)S(1)}) custom-call(s32[3]{0:T(128)S(1)} %pad_add_fusion.bounds_ref, s32[1,256]{1,0:T(1,128)S(1)} %bitcast.38, bf16[256,640]{1,0:T(8,128)(2,1)S(1)} %bitcast.36, bf16[256,640]{1,0:T(8,128)(2,1)S(1)} %bitcast.35, bf16[128,1280]{1,0:T(8,128)(2,1)S(1)} %copy.30.turned_ref, ...), custom_call_target="tpu_custom_call" | custom-call | tf_op jit(solution)/shard_map/attend_backward/pallas_call | solution.py:170
  79.3 5.0 %collective-permute-start.1 = (bf16[1792,256]{1,0:T(8,128)(2,1)S(1)}, bf16[1792,256]{1,0:T(8,128)(2,1)S(1)}, u32[]{:S(2)}, u32[]{:S(2)}) collective-permute-start(bf16[1792,256]{1,0:T(8,128)(2,1)S(1)} %slice.43), channel_id=1, source_target_pairs={{0,32},{32,0},{1,33},{33,1},{2,34},{34,2},{3,35},{35,3},{4,36},{36... | collective-permute-start | bytes 2752520 | tf_op jit(solution)/shard_map/ppermute | solution.py:201
  84.3 2.1 %collective-permute-done.1 = bf16[1792,256]{1,0:T(8,128)(2,1)S(1)} collective-permute-done((bf16[1792,256]{1,0:T(8,128)(2,1)S(1)}, bf16[1792,256]{1,0:T(8,128)(2,1)S(1)}, u32[]{:S(2)}, u32[]{:S(2)}) %collective-permute-start.1) | collective-permute-done | bytes 917536 | tf_op jit(solution)/shard_map/ppermute | solution.py:201
  86.7 1.9 %collective-permute-start.2 = (bf16[256,256]{1,0:T(8,128)(2,1)S(1)}, bf16[256,256]{1,0:T(8,128)(2,1)S(1)}, u32[]{:S(2)}, u32[]{:S(2)}) collective-permute-start(bf16[256,256]{1,0:T(8,128)(2,1)S(1)} %get-tuple-element.15), channel_id=1, source_target_pairs={{64,0},{128,64},{192,128},{256,192},{320,256},{384,320},{448,384},... | collective-permute-start | bytes 393224 | tf_op jit(solution)/shard_map/ppermute | solution.py:230
  88.6 0.7 collective-permute-start.7
  89.3 0.7 collective-permute-start.6
  90.0 1.3 collective-permute-start.5
  91.3 1.9 %collective-permute-start.4 = (bf16[256,256]{1,0:T(8,128)(2,1)S(1)}, bf16[256,256]{1,0:T(8,128)(2,1)S(1)}, u32[]{:S(2)}, u32[]{:S(2)}) collective-permute-start(bf16[256,256]{1,0:T(8,128)(2,1)S(1)} %get-tuple-element.19), channel_id=1, source_target_pairs={{192,0},{256,64},{320,128},{384,192},{448,256},{193,1},{257,65},{3... | collective-permute-start | bytes 393224 | tf_op jit(solution)/shard_map/ppermute | solution.py:230
  93.2 8.7 %collective-permute-done.2 = bf16[256,256]{1,0:T(8,128)(2,1)S(1)} collective-permute-done((bf16[256,256]{1,0:T(8,128)(2,1)S(1)}, bf16[256,256]{1,0:T(8,128)(2,1)S(1)}, u32[]{:S(2)}, u32[]{:S(2)}) %collective-permute-start.2) | collective-permute-done | bytes 131104 | tf_op jit(solution)/shard_map/ppermute | solution.py:230
  102.0 1.9 %collective-permute-start.3 = (bf16[256,256]{1,0:T(8,128)(2,1)S(1)}, bf16[256,256]{1,0:T(8,128)(2,1)S(1)}, u32[]{:S(2)}, u32[]{:S(2)}) collective-permute-start(bf16[256,256]{1,0:T(8,128)(2,1)S(1)} %get-tuple-element.20), channel_id=1, source_target_pairs={{128,0},{192,64},{256,128},{320,192},{384,256},{448,320},{129,1},{... | collective-permute-start | bytes 393224 | tf_op jit(solution)/shard_map/ppermute | solution.py:230
  103.9 8.5 %collective-permute-done.4 = bf16[256,256]{1,0:T(8,128)(2,1)S(1)} collective-permute-done((bf16[256,256]{1,0:T(8,128)(2,1)S(1)}, bf16[256,256]{1,0:T(8,128)(2,1)S(1)}, u32[]{:S(2)}, u32[]{:S(2)}) %collective-permute-start.4) | collective-permute-done | bytes 131104 | tf_op jit(solution)/shard_map/ppermute | solution.py:230
  112.4 10.1 %collective-permute-done.3 = bf16[256,256]{1,0:T(8,128)(2,1)S(1)} collective-permute-done((bf16[256,256]{1,0:T(8,128)(2,1)S(1)}, bf16[256,256]{1,0:T(8,128)(2,1)S(1)}, u32[]{:S(2)}, u32[]{:S(2)}) %collective-permute-start.3) | collective-permute-done | bytes 131104 | tf_op jit(solution)/shard_map/ppermute | solution.py:230
  122.5 0.8 fusion.6
  (20 shorter events, 2.8 us)
Async XLA Ops:
  7.2 47.4 %all-gather.3.cloned.1.call-start = ((), (), s32[]{:S(2)}) async-start(), calls=%async_computation.1 | async-start | bytes 2228224 | tf_op jit(solution)/shard_map/all_gather | solution.py:210
  8.9 11.6 %collective-permute-start = (bf16[1,32,8,640]{3,1,0,2:T(8,128)(2,1)S(1)}, bf16[1,32,8,640]{3,1,0,2:T(8,128)(2,1)}, u32[]{:S(2)}, u32[]{:S(2)}) collective-permute-start(bf16[1,32,8,640]{3,1,0,2:T(8,128)(2,1)S(1)} %copy.28), channel_id=1, source_target_pairs={{0,3},{1,0},{2,1},{3,2},{4,7},{5,4},{6,5},{7,6},{8,11},{9,8},{10,9... | collective-permute-start | bytes 983048 | tf_op jit(solution)/shard_map/ppermute | solution.py:212
  20.5 19.5 %all-to-all-start = ((bf16[1,32,8,640]{3,1,0,2:T(8,128)(2,1)}), bf16[1,32,8,640]{3,1,0,2:T(8,128)(2,1)S(1)}, u32[]{:S(2)}, u32[]{:S(2)}) async-start(bf16[1,32,8,640]{3,1,0,2:T(8,128)(2,1)} %collective-permute-done), calls=%async_computation | async-start | bytes 655360 | tf_op jit(solution)/shard_map/all_to_all | solution.py:215
  40.5 27.7 %copy-start.1 = (bf16[1,256,1,640]{3,1,2,0:T(8,128)(2,1)S(1)}, bf16[1,256,1,640]{3,1,2,0:T(8,128)(2,1)}, u32[]{:S(2)}) copy-start(bf16[1,256,1,640]{3,1,2,0:T(8,128)(2,1)} %param.4) | copy-start | bytes 983044
  54.5 1.6 %copy-start = (bf16[1,4096,1,256]{3,1,2,0:T(8,128)(2,1)S(1)}, bf16[1,4096,1,256]{3,1,2,0:T(8,128)(2,1)}, u32[]{:S(2)}) copy-start(bf16[1,4096,1,256]{3,1,2,0:T(8,128)(2,1)} %all-gather.3.cloned.1.call-done) | copy-start | bytes 6291460
  79.3 7.1 %collective-permute-start.1 = (bf16[1792,256]{1,0:T(8,128)(2,1)S(1)}, bf16[1792,256]{1,0:T(8,128)(2,1)S(1)}, u32[]{:S(2)}, u32[]{:S(2)}) collective-permute-start(bf16[1792,256]{1,0:T(8,128)(2,1)S(1)} %slice.43), channel_id=1, source_target_pairs={{0,32},{32,0},{1,33},{33,1},{2,34},{34,2},{3,35},{35,3},{4,36},{36... | collective-permute-start | bytes 2752520 | tf_op jit(solution)/shard_map/ppermute | solution.py:201
  86.7 15.2 %collective-permute-start.2 = (bf16[256,256]{1,0:T(8,128)(2,1)S(1)}, bf16[256,256]{1,0:T(8,128)(2,1)S(1)}, u32[]{:S(2)}, u32[]{:S(2)}) collective-permute-start(bf16[256,256]{1,0:T(8,128)(2,1)S(1)} %get-tuple-element.15), channel_id=1, source_target_pairs={{64,0},{128,64},{192,128},{256,192},{320,256},{384,320},{448,384},... | collective-permute-start | bytes 393224 | tf_op jit(solution)/shard_map/ppermute | solution.py:230
  88.6 15.2 %collective-permute-start.7 = (bf16[256,256]{1,0:T(8,128)(2,1)S(1)}, bf16[256,256]{1,0:T(8,128)(2,1)S(1)}, u32[]{:S(2)}, u32[]{:S(2)}) collective-permute-start(bf16[256,256]{1,0:T(8,128)(2,1)S(1)} %get-tuple-element.16), channel_id=1, source_target_pairs={{384,0},{448,64},{385,1},{449,65},{386,2},{450,66},{387,3},{451,67... | collective-permute-start | bytes 393224 | tf_op jit(solution)/shard_map/ppermute | solution.py:230
  89.3 14.6 %collective-permute-start.6 = (bf16[256,256]{1,0:T(8,128)(2,1)S(1)}, bf16[256,256]{1,0:T(8,128)(2,1)S(1)}, u32[]{:S(2)}, u32[]{:S(2)}) collective-permute-start(bf16[256,256]{1,0:T(8,128)(2,1)S(1)} %get-tuple-element.17), channel_id=1, source_target_pairs={{320,0},{384,64},{448,128},{321,1},{385,65},{449,129},{322,2},{386... | collective-permute-start | bytes 393224 | tf_op jit(solution)/shard_map/ppermute | solution.py:230
  90.0 13.9 %collective-permute-start.5 = (bf16[256,256]{1,0:T(8,128)(2,1)S(1)}, bf16[256,256]{1,0:T(8,128)(2,1)S(1)}, u32[]{:S(2)}, u32[]{:S(2)}) collective-permute-start(bf16[256,256]{1,0:T(8,128)(2,1)S(1)} %get-tuple-element.18), channel_id=1, source_target_pairs={{256,0},{320,64},{384,128},{448,192},{257,1},{321,65},{385,129},{4... | collective-permute-start | bytes 393224 | tf_op jit(solution)/shard_map/ppermute | solution.py:230
  91.3 21.1 %collective-permute-start.4 = (bf16[256,256]{1,0:T(8,128)(2,1)S(1)}, bf16[256,256]{1,0:T(8,128)(2,1)S(1)}, u32[]{:S(2)}, u32[]{:S(2)}) collective-permute-start(bf16[256,256]{1,0:T(8,128)(2,1)S(1)} %get-tuple-element.19), channel_id=1, source_target_pairs={{192,0},{256,64},{320,128},{384,192},{448,256},{193,1},{257,65},{3... | collective-permute-start | bytes 393224 | tf_op jit(solution)/shard_map/ppermute | solution.py:230
  102.0 20.6 %collective-permute-start.3 = (bf16[256,256]{1,0:T(8,128)(2,1)S(1)}, bf16[256,256]{1,0:T(8,128)(2,1)S(1)}, u32[]{:S(2)}, u32[]{:S(2)}) collective-permute-start(bf16[256,256]{1,0:T(8,128)(2,1)S(1)} %get-tuple-element.20), channel_id=1, source_target_pairs={{128,0},{192,64},{256,128},{320,192},{384,256},{448,320},{129,1},{... | collective-permute-start | bytes 393224 | tf_op jit(solution)/shard_map/ppermute | solution.py:230
Sparse Core Ops, SparseCore 0:
  10.1 44.3 all-gather.2

commit v2 on v1

v2 whole, which is shorter than its diff:
```python
import functools
import math

import jax
import jax.numpy as jnp
from jax import lax
from jax.experimental import pallas as pl
from jax.experimental.pallas import tpu as pltpu
from jax.sharding import Mesh, PartitionSpec as P

NEG_LARGE = -1e30
LOG2E = math.log2(math.e)
HEAD = 128
LONGEST = 3072
TOP, TOTAL, INNER = 0, 1, 2


def matmul(left, right):
    return jnp.dot(left, right, preferred_element_type=jnp.float32)


def fold(array):
    return array.reshape(array.shape[0] // 8, 8, array.shape[1])


def forward_kernel(
    bounds_ref, starts_ref, turned_ref, pairs_ref, turned_grad_ref,
    weights_ref, acc_ref, stats_ref, scores_ref, top_ref,
):
    rows = starts_ref.shape[2]
    groups = turned_ref.shape[1] // rows
    heads = groups // 2
    scale = LOG2E / math.sqrt(HEAD)
    chip, own, clear, last = bounds_ref[0], bounds_ref[1], bounds_ref[3], bounds_ref[4]
    top_ref[...] = jnp.full_like(top_ref, NEG_LARGE)
    acc_ref[...] = jnp.zeros_like(acc_ref)

    def measure(back, masked):
        at = pl.ds(pl.multiple_of((chip - back) * rows, rows), rows)
        to = pl.ds(pl.multiple_of(back * rows, rows), rows)
        keys = pairs_ref[at, :HEAD]
        allowed = []
        if masked:
            key_pos = (own - 2 * back) * rows + lax.broadcasted_iota(jnp.int32, (rows, rows), 0)
            across = lax.broadcasted_iota(jnp.int32, (rows, rows), 1)
            for slot in range(2):
                query_pos = bounds_ref[1 + slot] * rows + across
                allowed.append((key_pos <= query_pos) & (key_pos >= starts_ref[slot]))
        for group in range(groups):
            span = slice(group * rows, (group + 1) * rows)
            scores = matmul(keys, turned_ref[:, span])
            if masked:
                scores = jnp.where(allowed[group // heads], scores, NEG_LARGE)
            scores_ref[to, span] = scores
            top_ref[:, span] = jnp.maximum(top_ref[:, span], jnp.max(fold(scores), axis=0))

    def masked(step, unused):
        measure(jnp.where(step == 0, 0, clear + step), True)
        return unused

    def plain(back, unused):
        measure(back, False)
        return unused

    lax.fori_loop(0, last - clear + 1, masked, 0)
    lax.fori_loop(1, clear + 1, plain, 0)
    top = jnp.max(top_ref[...], axis=0, keepdims=True) * scale
    stats_ref[TOP : TOP + 1, :] = top
    top_ref[...] = jnp.broadcast_to(top, top_ref.shape)

    def weigh(back, unused):
        at = pl.ds(pl.multiple_of((chip - back) * rows, rows), rows)
        to = pl.ds(pl.multiple_of(back * rows, rows), rows)
        turned_values = jnp.concatenate(
            [pairs_ref[at, HEAD:].T, jnp.ones((16, rows), jnp.bfloat16)], axis=0
        )
        for group in range(groups):
            span = slice(group * rows, (group + 1) * rows)
            weights_ref[to, span] = jnp.exp2(
                scores_ref[to, span] * scale - top_ref[:1, span]
            ).astype(jnp.bfloat16)
        acc_ref[...] += matmul(turned_values, weights_ref[to, :])
        return unused

    lax.fori_loop(0, last + 1, weigh, 0)
    stats_ref[TOTAL : TOTAL + 1, :] = acc_ref[HEAD : HEAD + 1, :]
    for group in range(groups):
        span = slice(group * rows, (group + 1) * rows)
        stats_ref[INNER : INNER + 1, span] = jnp.sum(
            acc_ref[:HEAD, span] * turned_grad_ref[:, span].astype(jnp.float32),
            axis=0,
            keepdims=True,
        )


def backward_kernel(
    bounds_ref, stats_ref, arrived_ref, acc_ref, turned_grad_ref, query_ref,
    pairs_ref, weights_ref,
    out_ref, out_other_ref, query_grad_ref, query_grad_other_ref, pair_grad_ref,
    scaled_ref, turned_scaled_ref, delta_ref, total_ref, move_ref,
):
    rows = out_ref.shape[0]
    wide = turned_grad_ref.shape[1]
    groups = wide // rows
    heads = groups // 2
    root = 1.0 / math.sqrt(HEAD)
    chip, last = bounds_ref[0], bounds_ref[4]
    total_ref[...] = jnp.zeros_like(total_ref)

    for group in range(groups):
        span = slice(group * rows, (group + 1) * rows)
        there = (group + heads) % groups
        theirs = slice(there * rows, (there + 1) * rows)
        own_top, other_top = stats_ref[TOP : TOP + 1, span], arrived_ref[TOP : TOP + 1, theirs]
        top = jnp.maximum(own_top, other_top)
        own_part, other_part = jnp.exp2(own_top - top), jnp.exp2(other_top - top)

        def whole(row):
            return (
                stats_ref[row : row + 1, span] * own_part
                + arrived_ref[row : row + 1, theirs] * other_part
            )

        inverse = 1.0 / whole(TOTAL)
        part = own_part * inverse
        delta_ref[:, span] = whole(INNER) * inverse * part
        result = acc_ref[:HEAD, span] * part
        column = slice(group % heads * HEAD, (group % heads + 1) * HEAD)
        to_ref = out_ref if group < heads else out_other_ref
        to_ref[:, column] = result.astype(jnp.bfloat16).T
        low = (turned_grad_ref[:, span].astype(jnp.float32) * part).astype(jnp.bfloat16)
        turned_scaled_ref[:, span] = low
        scaled_ref[span, :] = low.T

    def visit(back, unused):
        at = pl.ds(pl.multiple_of((chip - back) * rows, rows), rows)
        to = pl.ds(pl.multiple_of(back * rows, rows), rows)
        values = pairs_ref[at, HEAD:]
        turned_keys = pairs_ref[at, :HEAD].T
        for group in range(groups):
            span = slice(group * rows, (group + 1) * rows)
            prob_grad = matmul(values, turned_scaled_ref[:, span])
            move_ref[:, span] = (
                weights_ref[to, span].astype(jnp.float32) * (prob_grad - delta_ref[:, span])
            ).astype(jnp.bfloat16)
        pair_grad_ref[to, HEAD:] = matmul(weights_ref[to, :], scaled_ref[...]).astype(jnp.bfloat16)
        pair_grad_ref[to, :HEAD] = (matmul(move_ref[...], query_ref[...]) * root).astype(
            jnp.bfloat16
        )
        total_ref[...] += matmul(turned_keys, move_ref[...])
        return unused

    def unseen(back, unused):
        to = pl.ds(pl.multiple_of(back * rows, rows), rows)
        pair_grad_ref[to, :] = jnp.zeros((rows, 2 * HEAD), jnp.bfloat16)
        return unused

    lax.fori_loop(0, last + 1, visit, 0)
    lax.fori_loop(last + 1, pair_grad_ref.shape[0] // rows, unseen, 0)
    for group in range(groups):
        span = slice(group * rows, (group + 1) * rows)
        column = slice(group % heads * HEAD, (group % heads + 1) * HEAD)
        to_ref = query_grad_ref if group < heads else query_grad_other_ref
        to_ref[:, column] = (total_ref[:, span] * root).astype(jnp.bfloat16).T


def smem():
    return pl.BlockSpec(memory_space=pltpu.SMEM)


def vmem():
    return pl.BlockSpec(memory_space=pltpu.VMEM)


def swap_cores(value):
    return lax.ppermute(value, "core", [(0, 1), (1, 0)])


def attend(bounds, starts, queries, grads, pairs, slots, swap=swap_cores):
    rows, columns = queries[0].shape
    heads = columns // HEAD
    wide = 2 * heads * rows
    params = pltpu.CompilerParams(vmem_limit_bytes=40 << 20)
    turned = jnp.concatenate([turn(q) for q in queries], axis=1)
    turned_grad = jnp.concatenate([turn(g) for g in grads], axis=1)
    stacked = jnp.concatenate([stack(q) for q in queries], axis=0)
    weights, acc, stats = pl.pallas_call(
        forward_kernel,
        out_shape=(
            pltpu.VMEM((slots * rows, wide), jnp.bfloat16),
            jax.ShapeDtypeStruct((HEAD + 16, wide), jnp.float32),
            jax.ShapeDtypeStruct((8, wide), jnp.float32),
        ),
        in_specs=[smem()] + [vmem()] * 4,
        out_specs=(vmem(),) * 3,
        scratch_shapes=[
            pltpu.VMEM((slots * rows, wide), jnp.float32),
            pltpu.VMEM((8, wide), jnp.float32),
        ],
        compiler_params=params,
        name="attend_forward",
    )(bounds, starts, turned, pairs, turned_grad)
    arrived = swap(stats)
    half = jax.ShapeDtypeStruct((rows, columns), jnp.bfloat16)
    return pl.pallas_call(
        backward_kernel,
        out_shape=(half,) * 4 + (jax.ShapeDtypeStruct((slots * rows, 2 * HEAD), jnp.bfloat16),),
        in_specs=[smem()] + [vmem()] * 7,
        out_specs=(vmem(),) * 5,
        scratch_shapes=[
            pltpu.VMEM((wide, HEAD), jnp.bfloat16),
            pltpu.VMEM((HEAD, wide), jnp.bfloat16),
            pltpu.VMEM((1, wide), jnp.float32),
            pltpu.VMEM((HEAD, wide), jnp.float32),
            pltpu.VMEM((rows, wide), jnp.bfloat16),
        ],
        compiler_params=params,
        name="attend_backward",
    )(bounds, stats, arrived, acc, turned_grad, stacked, pairs, weights)


def turn(array):
    rows, columns = array.shape
    heads = columns // HEAD
    return array.reshape(rows, heads, HEAD).transpose(2, 1, 0).reshape(HEAD, heads * rows)


def stack(array):
    rows, columns = array.shape
    heads = columns // HEAD
    return array.reshape(rows, heads, HEAD).transpose(1, 0, 2).reshape(heads * rows, HEAD)


def block_bounds(lengths, chip, core, rows):
    own, other = 2 * chip + core, 2 * chip + 1 - core
    ends = jnp.cumsum(lengths)
    begins = ends - lengths

    def starts_of(positions):
        here = begins[:, None] <= positions[None, :]
        return jnp.max(jnp.where(here, begins[:, None], 0), axis=0)

    span = jnp.arange(rows, dtype=jnp.int32)
    starts = jnp.stack([starts_of(own * rows + span), starts_of(other * rows + span)])
    edges = starts_of(jnp.stack([2 * chip * rows, (2 * chip + 2) * rows - 1]))
    last = (own - edges[0] // rows) // 2
    clear = jnp.maximum((own - (edges[1] + rows - 1) // rows) // 2, 0)
    bounds = jnp.stack([chip, own, other, clear, last]).astype(jnp.int32)
    return bounds, starts[:, None, :]


def per_device(query, keys_values, doc_lengths, incoming_output_grad):
    chips = lax.axis_size("chip")
    query = query[0, :, 0, :]
    pairs = keys_values[0, :, 0, :]
    rows = query.shape[0]
    every_pair = lax.all_gather(pairs, "chip", axis=0, tiled=True)
    sections = lax.axis_size("pipe")
    arrived = lax.ppermute(
        incoming_output_grad, "pipe", [(s, (s - 1) % sections) for s in range(sections)]
    )
    grad = lax.all_to_all(arrived, "tensor", split_axis=2, concat_axis=1, tiled=True)[0, :, 0, :]
    bounds, starts = block_bounds(
        doc_lengths[0], lax.axis_index("chip"), lax.axis_index("core"), rows
    )
    reach = min((LONGEST + 2 * rows - 1) // (2 * rows), chips - 1)
    slots = reach + 1
    out, out_other, query_grad, query_grad_other, partial = attend(
        bounds, starts, (query, swap_cores(query)), (grad, swap_cores(grad)), every_pair, slots
    )

    def add(mine, theirs):
        return (mine.astype(jnp.float32) + theirs.astype(jnp.float32)).astype(jnp.bfloat16)

    out = add(out, swap_cores(out_other))
    query_grad = add(query_grad, swap_cores(query_grad_other))
    partial = partial.reshape(slots, rows, 2 * HEAD)
    sums = partial[0].astype(jnp.float32)
    for back in range(1, slots):
        sums += lax.ppermute(
            partial[back], "chip", [(c, c - back) for c in range(back, chips)]
        ).astype(jnp.float32)
    pair_grad = sums.astype(jnp.bfloat16)
    return (out[None, :, None, :], query_grad[None, :, None, :], pair_grad[None, :, None, :])


def solution(mesh):
    shape = mesh.devices.shape
    split = Mesh(
        mesh.devices.reshape((shape[0] // 2, 2) + shape[1:]), ("chip", "core", "tensor", "pipe")
    )
    dp = ("chip", "core")
    by_head = P("pipe", dp, "tensor", None)
    in_specs = (by_head, by_head, P("pipe", None), P("pipe", dp + ("tensor",), None, None))
    return jax.shard_map(
        per_device, mesh=split, in_specs=in_specs, out_specs=(by_head,) * 3, check_vma=False
    )
```

time: 131 us -> 122 us (0.931)
  the two profiles are of different devices: /device:TPU:192 before, /device:TPU:71 now
where the time goes in v2:
time: 122 us; the launch traced here: 121 us
  waiting for transfers between devices  42.5 us (35%)
  starting transfers between devices  38.4 us (31%)
  between operations  17.7 us (15%)
  Pallas kernels  10.3 us (8%)
  local copies, waits for them, and re-layouts  9.08 us (7%)
  other arithmetic  3.07 us (3%)
    ppermute x6, waiting for transfers between devices, per_device(): lax.ppermute(partial[back], 'chip', [(c, c - back) for c in range(back, c...  24.8 us
    ppermute x5, starting transfers between devices, swap_cores(): return lax.ppermute(value, 'core', [(0, 1), (1, 0)])  20.7 us
    ppermute x1, waiting for transfers between devices, per_device(): lax.ppermute(incoming_output_grad, 'pipe', [(s, (s - 1) % sections) for s...  9.32 us
    ppermute x6, starting transfers between devices, per_device(): lax.ppermute(partial[back], 'chip', [(c, c - back) for c in range(back, c...  8.37 us
    pallas_call x1, Pallas kernels, attend(): pl.pallas_call(backward_kernel, out_shape=(half,) * 4 + (jax.ShapeDtypeSt...  7.14 us
    all_to_all x1, starting transfers between devices, per_device(): lax.all_to_all(arrived, 'tensor', split_axis=2, concat_axis=1, tiled=True)  6.82 us
    unnamed x12, local copies, waits for them, and re-layouts  5.96 us
    all_gather x1, waiting for transfers between devices, per_device(): every_pair = lax.all_gather(pairs, 'chip', axis=0, tiled=True)  4 us
  transfers between devices with their start and end apart: 14, of which 6 were waited for; matrix products, arithmetic and copies ran while one was open for 5% of the time, Pallas kernels for 0%

profile of v2, /device:TPU:71, one launch (start us, length us, event | category | flops | bytes accessed | tf_op | source)
XLA Modules:
  0.0 121.0 jit_solution(4894816497880149402)
XLA Ops:
  7.9 1.0 copy.45
  8.9 2.5 %collective-permute-start.1 = (bf16[1,32,8,640]{3,1,0,2:T(8,128)(2,1)S(1)}, bf16[1,32,8,640]{3,1,0,2:T(8,128)(2,1)}, u32[]{:S(2)}, u32[]{:S(2)}) collective-permute-start(bf16[1,32,8,640]{3,1,0,2:T(8,128)(2,1)S(1)} %copy.45), channel_id=1, source_target_pairs={{0,3},{1,0},{2,1},{3,2},{4,7},{5,4},{6,5},{7,6},{8,11},{9,8},{10,9... | collective-permute-start | bytes 983048 | tf_op jit(solution)/shard_map/ppermute | solution.py:259
  11.4 9.3 %collective-permute-done.1 = bf16[1,32,8,640]{3,1,0,2:T(8,128)(2,1)} collective-permute-done((bf16[1,32,8,640]{3,1,0,2:T(8,128)(2,1)S(1)}, bf16[1,32,8,640]{3,1,0,2:T(8,128)(2,1)}, u32[]{:S(2)}, u32[]{:S(2)}) %collective-permute-start.1) | collective-permute-done | bytes 327712 | tf_op jit(solution)/shard_map/ppermute | solution.py:259
  20.7 6.8 %all-to-all-start = ((bf16[1,32,8,640]{3,1,0,2:T(8,128)(2,1)}), bf16[1,32,8,640]{3,1,0,2:T(8,128)(2,1)S(1)}, u32[]{:S(2)}, u32[]{:S(2)}) async-start(bf16[1,32,8,640]{3,1,0,2:T(8,128)(2,1)} %collective-permute-done.1), calls=%async_computation | async-start | bytes 655360 | tf_op jit(solution)/shard_map/all_to_all | solution.py:262
  27.7 3.7 %collective-permute-start = (bf16[256,640]{0,1:T(8,128)(2,1)S(1)}, bf16[256,640]{0,1:T(8,128)(2,1)S(1)}, u32[]{:S(2)}, u32[]{:S(2)}) collective-permute-start(bf16[256,640]{0,1:T(8,128)(2,1)S(1)} %bitcast.55), channel_id=1, source_target_pairs={{0,32},{32,0},{1,33},{33,1},{2,34},{34,2},{3,35},{35,3},{4,36},{36... | collective-permute-start | bytes 983048 | tf_op jit(solution)/shard_map/ppermute | solution.py:176
  35.9 2.8 %all-to-all-done = bf16[1,32,8,640]{3,1,0,2:T(8,128)(2,1)S(1)} async-done(((bf16[1,32,8,640]{3,1,0,2:T(8,128)(2,1)}), bf16[1,32,8,640]{3,1,0,2:T(8,128)(2,1)S(1)}, u32[]{:S(2)}, u32[]{:S(2)}) %all-to-all-start) | async-done | bytes 327712 | tf_op jit(solution)/shard_map/all_to_all | solution.py:262
  38.6 5.1 %collective-permute-start.2 = (bf16[256,640]{1,0:T(8,128)(2,1)S(1)}, bf16[256,640]{1,0:T(8,128)(2,1)S(1)}, u32[]{:S(2)}, u32[]{:S(2)}) collective-permute-start(bf16[256,640]{1,0:T(8,128)(2,1)S(1)} %bitcast.61), channel_id=1, source_target_pairs={{0,32},{32,0},{1,33},{33,1},{2,34},{34,2},{3,35},{35,3},{4,36},{36... | collective-permute-start | bytes 983048 | tf_op jit(solution)/shard_map/ppermute | solution.py:176
  46.5 4.0 %all-gather.3.cloned.1.call-done = bf16[1,2048,1,256]{3,1,2,0:T(8,128)(2,1)} async-done(((bf16[1,256,1,256]{3,1,2,0:T(8,128)(2,1)}), bf16[1,2048,1,256]{3,1,2,0:T(8,128)(2,1)}) %all-gather.3.cloned.1.call-update) | async-done | bytes 1048592 | tf_op jit(solution)/shard_map/all_gather | solution.py:257
  50.5 1.2 %copy-done.1 = bf16[1,2048,1,256]{3,1,2,0:T(8,128)(2,1)S(1)} copy-done((bf16[1,2048,1,256]{3,1,2,0:T(8,128)(2,1)S(1)}, bf16[1,2048,1,256]{3,1,2,0:T(8,128)(2,1)}, u32[]{:S(2)}) %copy-start.1) | copy-done | bytes 1048600
  51.7 3.2 %attend_forward.1 = (bf16[1792,2560]{1,0:T(8,128)(2,1)S(1)}, f32[144,2560]{1,0:T(8,128)S(1)}, f32[8,2560]{1,0:T(8,128)S(1)}) custom-call(s32[5]{0:T(128)S(1)} %stack.44.bounds_ref, s32[2,1,256]{2,1,0:T(1,128)S(1)} %broadcast_in_dim.47.starts_ref, bf16[128,2560]{1,0:T(8,128)(2,1)S(1)} %get-tuple-element.31.turned_ref, bf16[2048,256]{1,0:T(8,128)(2,1)S(1)} %bitcast.53, ...), custom_call_target="tpu_custom_call" | custom-call | tf_op jit(solution)/shard_map/attend_forward/pallas_call | solution.py:187
  54.8 3.5 %copy-done = bf16[1792,2560]{1,0:T(8,128)(2,1)} copy-done((bf16[1792,2560]{1,0:T(8,128)(2,1)}, bf16[1792,2560]{1,0:T(8,128)(2,1)S(1)}, u32[]{:S(2)}) %copy-start) | copy-done | bytes 9175064
  58.4 7.6 %collective-permute-start.3 = (f32[8,2560]{1,0:T(8,128)S(1)}, f32[8,2560]{1,0:T(8,128)S(1)}, u32[]{:S(2)}, u32[]{:S(2)}) collective-permute-start(f32[8,2560]{1,0:T(8,128)S(1)} %get-tuple-element.11.stats_ref), channel_id=1, source_target_pairs={{0,32},{32,0},{1,33},{33,1},{2,34},{34,2},{3,35},{35,3},{4,36},{36... | collective-permute-start | bytes 245768 | tf_op jit(solution)/shard_map/ppermute | solution.py:176
  66.0 0.8 collective-permute-done.3.arrived_ref
  66.8 7.1 %attend_backward.1 = (bf16[256,640]{1,0:T(8,128)(2,1)S(1)}, bf16[256,640]{1,0:T(8,128)(2,1)S(1)}, bf16[256,640]{1,0:T(8,128)(2,1)S(1)}, bf16[256,640]{1,0:T(8,128)(2,1)S(1)}, bf16[1792,256]{1,0:T(8,128)(2,1)S(1)}) custom-call(s32[5]{0:T(128)S(1)} %stack.44.bounds_ref, f32[8,2560]{1,0:T(8,128)S(1)} %get-tuple-element.11.stats_ref, ...), custom_call_target="tpu_custom_call" | custom-call | tf_op jit(solution)/shard_map/attend_backward/pallas_call | solution.py:205
  74.1 1.9 %collective-permute-start.6 = (bf16[256,256]{1,0:T(8,128)(2,1)S(1)}, bf16[256,256]{1,0:T(8,128)(2,1)S(1)}, u32[]{:S(2)}, u32[]{:S(2)}) collective-permute-start(bf16[256,256]{1,0:T(8,128)(2,1)S(1)} %get-tuple-element.21), channel_id=1, source_target_pairs={{64,0},{128,64},{192,128},{256,192},{320,256},{384,320},{448,384},... | collective-permute-start | bytes 393224 | tf_op jit(solution)/shard_map/ppermute | solution.py:280
  76.0 1.3 %collective-permute-start.11 = (bf16[256,256]{1,0:T(8,128)(2,1)S(1)}, bf16[256,256]{1,0:T(8,128)(2,1)S(1)}, u32[]{:S(2)}, u32[]{:S(2)}) collective-permute-start(bf16[256,256]{1,0:T(8,128)(2,1)S(1)} %get-tuple-element.22), channel_id=1, source_target_pairs={{384,0},{448,64},{385,1},{449,65},{386,2},{450,66},{387,3},{451,67... | collective-permute-start | bytes 393224 | tf_op jit(solution)/shard_map/ppermute | solution.py:280
  77.3 1.3 %collective-permute-start.10 = (bf16[256,256]{1,0:T(8,128)(2,1)S(1)}, bf16[256,256]{1,0:T(8,128)(2,1)S(1)}, u32[]{:S(2)}, u32[]{:S(2)}) collective-permute-start(bf16[256,256]{1,0:T(8,128)(2,1)S(1)} %get-tuple-element.23), channel_id=1, source_target_pairs={{320,0},{384,64},{448,128},{321,1},{385,65},{449,129},{322,2},{386... | collective-permute-start | bytes 393224 | tf_op jit(solution)/shard_map/ppermute | solution.py:280
  78.6 1.3 %collective-permute-start.9 = (bf16[256,256]{1,0:T(8,128)(2,1)S(1)}, bf16[256,256]{1,0:T(8,128)(2,1)S(1)}, u32[]{:S(2)}, u32[]{:S(2)}) collective-permute-start(bf16[256,256]{1,0:T(8,128)(2,1)S(1)} %get-tuple-element.24), channel_id=1, source_target_pairs={{256,0},{320,64},{384,128},{448,192},{257,1},{321,65},{385,129},{4... | collective-permute-start | bytes 393224 | tf_op jit(solution)/shard_map/ppermute | solution.py:280
  79.9 1.3 %collective-permute-start.8 = (bf16[256,256]{1,0:T(8,128)(2,1)S(1)}, bf16[256,256]{1,0:T(8,128)(2,1)S(1)}, u32[]{:S(2)}, u32[]{:S(2)}) collective-permute-start(bf16[256,256]{1,0:T(8,128)(2,1)S(1)} %get-tuple-element.25), channel_id=1, source_target_pairs={{192,0},{256,64},{320,128},{384,192},{448,256},{193,1},{257,65},{3... | collective-permute-start | bytes 393224 | tf_op jit(solution)/shard_map/ppermute | solution.py:280
  81.2 1.3 %collective-permute-done.6 = bf16[256,256]{1,0:T(8,128)(2,1)S(1)} collective-permute-done((bf16[256,256]{1,0:T(8,128)(2,1)S(1)}, bf16[256,256]{1,0:T(8,128)(2,1)S(1)}, u32[]{:S(2)}, u32[]{:S(2)}) %collective-permute-start.6) | collective-permute-done | bytes 131104 | tf_op jit(solution)/shard_map/ppermute | solution.py:280
  82.5 1.3 %collective-permute-start.7 = (bf16[256,256]{1,0:T(8,128)(2,1)S(1)}, bf16[256,256]{1,0:T(8,128)(2,1)S(1)}, u32[]{:S(2)}, u32[]{:S(2)}) collective-permute-start(bf16[256,256]{1,0:T(8,128)(2,1)S(1)} %get-tuple-element.26), channel_id=1, source_target_pairs={{128,0},{192,64},{256,128},{320,192},{384,256},{448,320},{129,1},{... | collective-permute-start | bytes 393224 | tf_op jit(solution)/shard_map/ppermute | solution.py:280
  83.8 23.5 %collective-permute-done.11 = bf16[256,256]{1,0:T(8,128)(2,1)S(1)} collective-permute-done((bf16[256,256]{1,0:T(8,128)(2,1)S(1)}, bf16[256,256]{1,0:T(8,128)(2,1)S(1)}, u32[]{:S(2)}, u32[]{:S(2)}) %collective-permute-start.11) | collective-permute-done | bytes 131104 | tf_op jit(solution)/shard_map/ppermute | solution.py:280
  107.3 2.4 %collective-permute-start.4 = (bf16[256,640]{1,0:T(8,128)(2,1)S(1)}, bf16[256,640]{1,0:T(8,128)(2,1)S(1)}, u32[]{:S(2)}, u32[]{:S(2)}) collective-permute-start(bf16[256,640]{1,0:T(8,128)(2,1)S(1)} %get-tuple-element.15), channel_id=1, source_target_pairs={{0,32},{32,0},{1,33},{33,1},{2,34},{34,2},{3,35},{35,3},{4,36},{36... | collective-permute-start | bytes 983048 | tf_op jit(solution)/shard_map/ppermute | solution.py:176
  109.8 1.9 %collective-permute-start.5 = (bf16[256,640]{1,0:T(8,128)(2,1)S(1)}, bf16[256,640]{1,0:T(8,128)(2,1)S(1)}, u32[]{:S(2)}, u32[]{:S(2)}) collective-permute-start(bf16[256,640]{1,0:T(8,128)(2,1)S(1)} %get-tuple-element.17), channel_id=1, source_target_pairs={{0,32},{32,0},{1,33},{33,1},{2,34},{34,2},{3,35},{35,3},{4,36},{36... | collective-permute-start | bytes 983048 | tf_op jit(solution)/shard_map/ppermute | solution.py:176
  (47 shorter events, 7.1 us)
Async XLA Ops:
  7.2 20.4 %copy-start.3 = (bf16[1,256,1,640]{3,1,2,0:T(8,128)(2,1)S(1)}, bf16[1,256,1,640]{3,1,2,0:T(8,128)(2,1)}, u32[]{:S(2)}) copy-start(bf16[1,256,1,640]{3,1,2,0:T(8,128)(2,1)} %param.4) | copy-start | bytes 983044
  7.2 24.3 %copy-start.4 = (s32[1,8]{1,0:T(1,128)S(1)}, s32[1,8]{1,0:T(1,128)}, u32[]{:S(2)}) copy-start(s32[1,8]{1,0:T(1,128)} %param.6) | copy-start | bytes 100
  7.2 43.3 %all-gather.3.cloned.1.call-start = ((), (), s32[]{:S(2)}) async-start(), calls=%async_computation.1 | async-start | bytes 1179648 | tf_op jit(solution)/shard_map/all_gather | solution.py:257
  8.9 11.8 %collective-permute-start.1 = (bf16[1,32,8,640]{3,1,0,2:T(8,128)(2,1)S(1)}, bf16[1,32,8,640]{3,1,0,2:T(8,128)(2,1)}, u32[]{:S(2)}, u32[]{:S(2)}) collective-permute-start(bf16[1,32,8,640]{3,1,0,2:T(8,128)(2,1)S(1)} %copy.45), channel_id=1, source_target_pairs={{0,3},{1,0},{2,1},{3,2},{4,7},{5,4},{6,5},{7,6},{8,11},{9,8},{10,9... | collective-permute-start | bytes 983048 | tf_op jit(solution)/shard_map/ppermute | solution.py:259
  20.7 17.9 %all-to-all-start = ((bf16[1,32,8,640]{3,1,0,2:T(8,128)(2,1)}), bf16[1,32,8,640]{3,1,0,2:T(8,128)(2,1)S(1)}, u32[]{:S(2)}, u32[]{:S(2)}) async-start(bf16[1,32,8,640]{3,1,0,2:T(8,128)(2,1)} %collective-permute-done.1), calls=%async_computation | async-start | bytes 655360 | tf_op jit(solution)/shard_map/all_to_all | solution.py:262
  27.7 16.8 %collective-permute-start = (bf16[256,640]{0,1:T(8,128)(2,1)S(1)}, bf16[256,640]{0,1:T(8,128)(2,1)S(1)}, u32[]{:S(2)}, u32[]{:S(2)}) collective-permute-start(bf16[256,640]{0,1:T(8,128)(2,1)S(1)} %bitcast.55), channel_id=1, source_target_pairs={{0,32},{32,0},{1,33},{33,1},{2,34},{34,2},{3,35},{35,3},{4,36},{36... | collective-permute-start | bytes 983048 | tf_op jit(solution)/shard_map/ppermute | solution.py:176
  38.6 7.1 %collective-permute-start.2 = (bf16[256,640]{1,0:T(8,128)(2,1)S(1)}, bf16[256,640]{1,0:T(8,128)(2,1)S(1)}, u32[]{:S(2)}, u32[]{:S(2)}) collective-permute-start(bf16[256,640]{1,0:T(8,128)(2,1)S(1)} %bitcast.61), channel_id=1, source_target_pairs={{0,32},{32,0},{1,33},{33,1},{2,34},{34,2},{3,35},{35,3},{4,36},{36... | collective-permute-start | bytes 983048 | tf_op jit(solution)/shard_map/ppermute | solution.py:176
  50.5 1.2 %copy-start.1 = (bf16[1,2048,1,256]{3,1,2,0:T(8,128)(2,1)S(1)}, bf16[1,2048,1,256]{3,1,2,0:T(8,128)(2,1)}, u32[]{:S(2)}) copy-start(bf16[1,2048,1,256]{3,1,2,0:T(8,128)(2,1)} %all-gather.3.cloned.1.call-done) | copy-start | bytes 3145732
  51.7 15.2 %copy-start.2 = (bf16[1,2048,1,256]{3,1,2,0:T(8,128)(2,1)S(1)}, bf16[1,2048,1,256]{3,1,2,0:T(8,128)(2,1)}, u32[]{:S(2)}) copy-start(bf16[1,2048,1,256]{3,1,2,0:T(8,128)(2,1)} %all-gather.3.cloned.1.call-done) | copy-start | bytes 3145732
  54.8 3.5 %copy-start = (bf16[1792,2560]{1,0:T(8,128)(2,1)}, bf16[1792,2560]{1,0:T(8,128)(2,1)S(1)}, u32[]{:S(2)}) copy-start(bf16[1792,2560]{1,0:T(8,128)(2,1)S(1)} %get-tuple-element.13.weights_ref) | copy-start | bytes 27525124
  58.4 8.5 %collective-permute-start.3 = (f32[8,2560]{1,0:T(8,128)S(1)}, f32[8,2560]{1,0:T(8,128)S(1)}, u32[]{:S(2)}, u32[]{:S(2)}) collective-permute-start(f32[8,2560]{1,0:T(8,128)S(1)} %get-tuple-element.11.stats_ref), channel_id=1, source_target_pairs={{0,32},{32,0},{1,33},{33,1},{2,34},{34,2},{3,35},{35,3},{4,36},{36... | collective-permute-start | bytes 245768 | tf_op jit(solution)/shard_map/ppermute | solution.py:176
  74.1 8.4 %collective-permute-start.6 = (bf16[256,256]{1,0:T(8,128)(2,1)S(1)}, bf16[256,256]{1,0:T(8,128)(2,1)S(1)}, u32[]{:S(2)}, u32[]{:S(2)}) collective-permute-start(bf16[256,256]{1,0:T(8,128)(2,1)S(1)} %get-tuple-element.21), channel_id=1, source_target_pairs={{64,0},{128,64},{192,128},{256,192},{320,256},{384,320},{448,384},... | collective-permute-start | bytes 393224 | tf_op jit(solution)/shard_map/ppermute | solution.py:280
  76.0 31.3 %collective-permute-start.11 = (bf16[256,256]{1,0:T(8,128)(2,1)S(1)}, bf16[256,256]{1,0:T(8,128)(2,1)S(1)}, u32[]{:S(2)}, u32[]{:S(2)}) collective-permute-start(bf16[256,256]{1,0:T(8,128)(2,1)S(1)} %get-tuple-element.22), channel_id=1, source_target_pairs={{384,0},{448,64},{385,1},{449,65},{386,2},{450,66},{387,3},{451,67... | collective-permute-start | bytes 393224 | tf_op jit(solution)/shard_map/ppermute | solution.py:280
  77.3 32.5 %collective-permute-start.10 = (bf16[256,256]{1,0:T(8,128)(2,1)S(1)}, bf16[256,256]{1,0:T(8,128)(2,1)S(1)}, u32[]{:S(2)}, u32[]{:S(2)}) collective-permute-start(bf16[256,256]{1,0:T(8,128)(2,1)S(1)} %get-tuple-element.23), channel_id=1, source_target_pairs={{320,0},{384,64},{448,128},{321,1},{385,65},{449,129},{322,2},{386... | collective-permute-start | bytes 393224 | tf_op jit(solution)/shard_map/ppermute | solution.py:280
  78.6 33.1 %collective-permute-start.9 = (bf16[256,256]{1,0:T(8,128)(2,1)S(1)}, bf16[256,256]{1,0:T(8,128)(2,1)S(1)}, u32[]{:S(2)}, u32[]{:S(2)}) collective-permute-start(bf16[256,256]{1,0:T(8,128)(2,1)S(1)} %get-tuple-element.24), channel_id=1, source_target_pairs={{256,0},{320,64},{384,128},{448,192},{257,1},{321,65},{385,129},{4... | collective-permute-start | bytes 393224 | tf_op jit(solution)/shard_map/ppermute | solution.py:280
  79.9 31.8 %collective-permute-start.8 = (bf16[256,256]{1,0:T(8,128)(2,1)S(1)}, bf16[256,256]{1,0:T(8,128)(2,1)S(1)}, u32[]{:S(2)}, u32[]{:S(2)}) collective-permute-start(bf16[256,256]{1,0:T(8,128)(2,1)S(1)} %get-tuple-element.25), channel_id=1, source_target_pairs={{192,0},{256,64},{320,128},{384,192},{448,256},{193,1},{257,65},{3... | collective-permute-start | bytes 393224 | tf_op jit(solution)/shard_map/ppermute | solution.py:280
  82.5 29.2 %collective-permute-start.7 = (bf16[256,256]{1,0:T(8,128)(2,1)S(1)}, bf16[256,256]{1,0:T(8,128)(2,1)S(1)}, u32[]{:S(2)}, u32[]{:S(2)}) collective-permute-start(bf16[256,256]{1,0:T(8,128)(2,1)S(1)} %get-tuple-element.26), channel_id=1, source_target_pairs={{128,0},{192,64},{256,128},{320,192},{384,256},{448,320},{129,1},{... | collective-permute-start | bytes 393224 | tf_op jit(solution)/shard_map/ppermute | solution.py:280
  107.3 5.2 %collective-permute-start.4 = (bf16[256,640]{1,0:T(8,128)(2,1)S(1)}, bf16[256,640]{1,0:T(8,128)(2,1)S(1)}, u32[]{:S(2)}, u32[]{:S(2)}) collective-permute-start(bf16[256,640]{1,0:T(8,128)(2,1)S(1)} %get-tuple-element.15), channel_id=1, source_target_pairs={{0,32},{32,0},{1,33},{33,1},{2,34},{34,2},{3,35},{35,3},{4,36},{36... | collective-permute-start | bytes 983048 | tf_op jit(solution)/shard_map/ppermute | solution.py:176
  109.8 3.5 %collective-permute-start.5 = (bf16[256,640]{1,0:T(8,128)(2,1)S(1)}, bf16[256,640]{1,0:T(8,128)(2,1)S(1)}, u32[]{:S(2)}, u32[]{:S(2)}) collective-permute-start(bf16[256,640]{1,0:T(8,128)(2,1)S(1)} %get-tuple-element.17), channel_id=1, source_target_pairs={{0,32},{32,0},{1,33},{33,1},{2,34},{34,2},{3,35},{35,3},{4,36},{36... | collective-permute-start | bytes 983048 | tf_op jit(solution)/shard_map/ppermute | solution.py:176
Sparse Core Ops, SparseCore 0:
  10.1 40.3 all-gather.2

commit v3 on v2

--- a/solution.py
+++ b/solution.py
@@ -12,7 +12,7 @@
 LOG2E = math.log2(math.e)
 HEAD = 128
 LONGEST = 3072
-TOP, TOTAL, INNER = 0, 1, 2
+EXTRA = 16
 
 
 def matmul(left, right):
@@ -24,8 +24,8 @@
 
 
 def forward_kernel(
-    bounds_ref, starts_ref, turned_ref, pairs_ref, turned_grad_ref,
-    weights_ref, acc_ref, stats_ref, scores_ref, top_ref,
+    bounds_ref, starts_ref, turned_ref, pairs_ref,
+    kept_ref, acc_ref, stats_ref, sent_ref, scores_ref, top_ref, weights_ref, kept_sem,
 ):
     rows = starts_ref.shape[2]
     groups = turned_ref.shape[1] // rows
@@ -65,7 +65,6 @@
     lax.fori_loop(0, last - clear + 1, masked, 0)
     lax.fori_loop(1, clear + 1, plain, 0)
     top = jnp.max(top_ref[...], axis=0, keepdims=True) * scale
-    stats_ref[TOP : TOP + 1, :] = top
     top_ref[...] = jnp.broadcast_to(top, top_ref.shape)
 
     def weigh(back, unused):
@@ -79,64 +78,69 @@
             weights_ref[to, span] = jnp.exp2(
                 scores_ref[to, span] * scale - top_ref[:1, span]
             ).astype(jnp.bfloat16)
+        keep(back).start()
         acc_ref[...] += matmul(turned_values, weights_ref[to, :])
         return unused
 
+    def keep(back):
+        to = pl.ds(pl.multiple_of(back * rows, rows), rows)
+        return pltpu.make_async_copy(weights_ref.at[to], kept_ref.at[to], kept_sem.at[back])
+
+    def kept(back, unused):
+        keep(back).wait()
+        return unused
+
     lax.fori_loop(0, last + 1, weigh, 0)
-    stats_ref[TOTAL : TOTAL + 1, :] = acc_ref[HEAD : HEAD + 1, :]
+    totals = acc_ref[HEAD : HEAD + 1, :]
+    log_totals = top_ref[:1, :] + jnp.log2(totals)
+    stats_ref[...] = jnp.concatenate([top_ref[:1, :], log_totals] + [top] * 6, axis=0)
+    parts, rest = [], log_totals
+    for _ in range(3):
+        parts.append(rest.astype(jnp.bfloat16))
+        rest = rest - parts[-1].astype(jnp.float32)
+    sent_ref[HEAD:, :] = jnp.concatenate(
+        parts + [jnp.zeros((EXTRA - 3, totals.shape[1]), jnp.bfloat16)], axis=0
+    )
+    inverse = 1.0 / totals
     for group in range(groups):
         span = slice(group * rows, (group + 1) * rows)
-        stats_ref[INNER : INNER + 1, span] = jnp.sum(
-            acc_ref[:HEAD, span] * turned_grad_ref[:, span].astype(jnp.float32),
-            axis=0,
-            keepdims=True,
-        )
-
-
-def backward_kernel(
-    bounds_ref, stats_ref, arrived_ref, acc_ref, turned_grad_ref, query_ref,
-    pairs_ref, weights_ref,
-    out_ref, out_other_ref, query_grad_ref, query_grad_other_ref, pair_grad_ref,
-    scaled_ref, turned_scaled_ref, delta_ref, total_ref, move_ref,
+        result = acc_ref[:HEAD, span] * inverse[:, span]
+        acc_ref[:HEAD, span] = result
+        sent_ref[:HEAD, span] = result.astype(jnp.bfloat16)
+    lax.fori_loop(0, last + 1, kept, 0)
+
+
+def fetch(slot, kept_ref, weights_ref, kept_sem, rows):
+    def copy(back):
+        of = pl.ds(pl.multiple_of(back * rows, rows), rows)
+        to = pl.ds(pl.multiple_of((back - slot) * rows, rows), rows)
+        return pltpu.make_async_copy(kept_ref.at[of], weights_ref.at[to], kept_sem.at[back - slot])
+
+    return copy
+
+
+def fetch_all(first, stop, copy):
+    def start(back, unused):
+        copy(back).start()
+        return unused
+
+    lax.fori_loop(first, stop, start, 0)
+
+
+def accumulate(
+    first, stop, chip, pairs_ref, weights_ref, copy, query_ref,
+    scaled_ref, turned_scaled_ref, delta_ref, total_ref, move_ref, pair_grad_ref, slot,
 ):
-    rows = out_ref.shape[0]
-    wide = turned_grad_ref.shape[1]
-    groups = wide // rows
-    heads = groups // 2
+    rows = move_ref.shape[0]
+    groups = move_ref.shape[1] // rows
     root = 1.0 / math.sqrt(HEAD)
-    chip, last = bounds_ref[0], bounds_ref[4]
-    total_ref[...] = jnp.zeros_like(total_ref)
-
-    for group in range(groups):
-        span = slice(group * rows, (group + 1) * rows)
-        there = (group + heads) % groups
-        theirs = slice(there * rows, (there + 1) * rows)
-        own_top, other_top = stats_ref[TOP : TOP + 1, span], arrived_ref[TOP : TOP + 1, theirs]
-        top = jnp.maximum(own_top, other_top)
-        own_part, other_part = jnp.exp2(own_top - top), jnp.exp2(other_top - top)
-
-        def whole(row):
-            return (
-                stats_ref[row : row + 1, span] * own_part
-                + arrived_ref[row : row + 1, theirs] * other_part
-            )
-
-        inverse = 1.0 / whole(TOTAL)
-        part = own_part * inverse
-        delta_ref[:, span] = whole(INNER) * inverse * part
-        result = acc_ref[:HEAD, span] * part
-        column = slice(group % heads * HEAD, (group % heads + 1) * HEAD)
-        to_ref = out_ref if group < heads else out_other_ref
-        to_ref[:, column] = result.astype(jnp.bfloat16).T
-        low = (turned_grad_ref[:, span].astype(jnp.float32) * part).astype(jnp.bfloat16)
-        turned_scaled_ref[:, span] = low
-        scaled_ref[span, :] = low.T
 
     def visit(back, unused):
         at = pl.ds(pl.multiple_of((chip - back) * rows, rows), rows)
-        to = pl.ds(pl.multiple_of(back * rows, rows), rows)
+        to = pl.ds(pl.multiple_of((back - slot) * rows, rows), rows)
         values = pairs_ref[at, HEAD:]
         turned_keys = pairs_ref[at, :HEAD].T
+        copy(back).wait()
         for group in range(groups):
             span = slice(group * rows, (group + 1) * rows)
             prob_grad = matmul(values, turned_scaled_ref[:, span])
@@ -151,12 +155,78 @@
         return unused
 
     def unseen(back, unused):
-        to = pl.ds(pl.multiple_of(back * rows, rows), rows)
+        to = pl.ds(pl.multiple_of((back - slot) * rows, rows), rows)
         pair_grad_ref[to, :] = jnp.zeros((rows, 2 * HEAD), jnp.bfloat16)
         return unused
 
-    lax.fori_loop(0, last + 1, visit, 0)
-    lax.fori_loop(last + 1, pair_grad_ref.shape[0] // rows, unseen, 0)
+    lax.fori_loop(first, stop, visit, 0)
+    lax.fori_loop(jnp.maximum(first, stop), slot + pair_grad_ref.shape[0] // rows, unseen, 0)
+
+
+def hand_out(pair_grad_ref, block_refs):
+    rows = block_refs[0].shape[0]
+    for at, block_ref in enumerate(block_refs):
+        block_ref[...] = pair_grad_ref[at * rows : (at + 1) * rows, :]
+
+
+def backward_far_kernel(
+    bounds_ref, stats_ref, arrived_ref, acc_ref, turned_grad_ref, query_ref, pairs_ref, kept_ref,
+    out_ref, scaled_ref, turned_scaled_ref, delta_ref, total_ref, *rest, split,
+):
+    *block_refs, move_ref, pair_grad_ref, weights_ref, kept_sem = rest
+    rows = out_ref.shape[0]
+    groups = turned_grad_ref.shape[1] // rows
+    heads = groups // 2
+    copy = fetch(split, kept_ref, weights_ref, kept_sem, rows)
+    fetch_all(split, bounds_ref[4] + 1, copy)
+    total_ref[...] = jnp.zeros_like(total_ref)
+    for group in range(groups):
+        span = slice(group * rows, (group + 1) * rows)
+        there = (group + heads) % groups
+        theirs = slice(there * rows, (there + 1) * rows)
+        other_log = arrived_ref[HEAD : HEAD + 1, theirs].astype(jnp.float32)
+        for part in range(1, 3):
+            other_log += arrived_ref[HEAD + part : HEAD + part + 1, theirs].astype(jnp.float32)
+        own_top, own_log = stats_ref[0:1, span], stats_ref[1:2, span]
+        most = jnp.maximum(own_log, other_log)
+        log_totals = most + jnp.log2(jnp.exp2(own_log - most) + jnp.exp2(other_log - most))
+        result = acc_ref[:HEAD, span] * jnp.exp2(own_log - log_totals) + arrived_ref[
+            :HEAD, theirs
+        ].astype(jnp.float32) * jnp.exp2(other_log - log_totals)
+        result = result.astype(jnp.bfloat16)
+        if group < heads:
+            out_ref[:, group * HEAD : (group + 1) * HEAD] = result.T
+        scaled = turned_grad_ref[:, span].astype(jnp.float32) * jnp.exp2(own_top - log_totals)
+        delta_ref[:, span] = jnp.sum(result.astype(jnp.float32) * scaled, axis=0, keepdims=True)
+        low = scaled.astype(jnp.bfloat16)
+        turned_scaled_ref[:, span] = low
+        scaled_ref[span, :] = low.T
+    accumulate(
+        split, bounds_ref[4] + 1, bounds_ref[0], pairs_ref, weights_ref, copy, query_ref,
+        scaled_ref, turned_scaled_ref, delta_ref, total_ref, move_ref, pair_grad_ref, split,
+    )
+    hand_out(pair_grad_ref, block_refs)
+
+
+def backward_near_kernel(
+    bounds_ref, scaled_ref, turned_scaled_ref, delta_ref, begun_ref, query_ref, pairs_ref,
+    kept_ref, query_grad_ref, query_grad_other_ref, *rest,
+):
+    *block_refs, total_ref, move_ref, pair_grad_ref, weights_ref, kept_sem = rest
+    rows = query_grad_ref.shape[0]
+    groups = turned_scaled_ref.shape[1] // rows
+    heads = groups // 2
+    root = 1.0 / math.sqrt(HEAD)
+    slots = pair_grad_ref.shape[0] // rows
+    stop = jnp.minimum(bounds_ref[4] + 1, slots)
+    copy = fetch(0, kept_ref, weights_ref, kept_sem, rows)
+    fetch_all(0, stop, copy)
+    total_ref[...] = begun_ref[...]
+    accumulate(
+        0, stop, bounds_ref[0], pairs_ref, weights_ref, copy, query_ref,
+        scaled_ref, turned_scaled_ref, delta_ref, total_ref, move_ref, pair_grad_ref, 0,
+    )
+    hand_out(pair_grad_ref, block_refs)
     for group in range(groups):
         span = slice(group * rows, (group + 1) * rows)
         column = slice(group % heads * HEAD, (group % heads + 1) * HEAD)
@@ -172,51 +242,95 @@
     return pl.BlockSpec(memory_space=pltpu.VMEM)
 
 
+def hbm():
+    return pl.BlockSpec(memory_space=pltpu.HBM)
+
+
 def swap_cores(value):
     return lax.ppermute(value, "core", [(0, 1), (1, 0)])
 
 
-def attend(bounds, starts, queries, grads, pairs, slots, swap=swap_cores):
+def cost(blocks, rows, wide, matmuls):
+    return pl.CostEstimate(
+        flops=2 * matmuls * blocks * rows * wide * HEAD,
+        transcendentals=0,
+        bytes_accessed=2 * blocks * rows * wide,
+    )
+
+
+def attend(bounds, starts, queries, grads, pairs, slots, split, send, swap=swap_cores):
     rows, columns = queries[0].shape
     heads = columns // HEAD
     wide = 2 * heads * rows
-    params = pltpu.CompilerParams(vmem_limit_bytes=40 << 20)
     turned = jnp.concatenate([turn(q) for q in queries], axis=1)
     turned_grad = jnp.concatenate([turn(g) for g in grads], axis=1)
     stacked = jnp.concatenate([stack(q) for q in queries], axis=0)
-    weights, acc, stats = pl.pallas_call(
+    pairs, turned, turned_grad, stacked = lax.optimization_barrier(
+        (pairs, turned, turned_grad, stacked)
+    )
+    weights, acc, stats, sent = pl.pallas_call(
         forward_kernel,
         out_shape=(
-            pltpu.VMEM((slots * rows, wide), jnp.bfloat16),
-            jax.ShapeDtypeStruct((HEAD + 16, wide), jnp.float32),
+            pltpu.HBM((slots * rows, wide), jnp.bfloat16),
+            jax.ShapeDtypeStruct((HEAD + EXTRA, wide), jnp.float32),
             jax.ShapeDtypeStruct((8, wide), jnp.float32),
+            jax.ShapeDtypeStruct((HEAD + EXTRA, wide), jnp.bfloat16),
         ),
-        in_specs=[smem()] + [vmem()] * 4,
-        out_specs=(vmem(),) * 3,
+        in_specs=[smem()] + [vmem()] * 3,
+        out_specs=(hbm(),) + (vmem(),) * 3,
         scratch_shapes=[
             pltpu.VMEM((slots * rows, wide), jnp.float32),
             pltpu.VMEM((8, wide), jnp.float32),
+            pltpu.VMEM((slots * rows, wide), jnp.bfloat16),
+            pltpu.SemaphoreType.DMA((slots,)),
         ],
+        compiler_params=pltpu.CompilerParams(vmem_limit_bytes=36 << 20),
+        cost_estimate=cost(slots, rows, wide, 2),
+        name="attend_forward",
+    )(bounds, starts, turned, pairs)
+    weights = pltpu.with_memory_space_constraint(weights, pltpu.HBM)
+    arrived = swap(sent)
+    half = jax.ShapeDtypeStruct((rows, columns), jnp.bfloat16)
+    params = pltpu.CompilerParams(vmem_limit_bytes=20 << 20)
+    move = pltpu.VMEM((rows, wide), jnp.bfloat16)
+
+    def held(blocks):
+        return [
+            pltpu.VMEM((blocks * rows, 2 * HEAD), jnp.bfloat16),
+            pltpu.VMEM((blocks * rows, wide), jnp.bfloat16),
+            pltpu.SemaphoreType.DMA((blocks,)),
+        ]
+
+    block = jax.ShapeDtypeStruct((rows, 2 * HEAD), jnp.bfloat16)
+    out, scaled, turned_scaled, delta, total, *far = pl.pallas_call(
+        functools.partial(backward_far_kernel, split=split),
+        out_shape=(
+            half,
+            jax.ShapeDtypeStruct((wide, HEAD), jnp.bfloat16),
+            jax.ShapeDtypeStruct((HEAD, wide), jnp.bfloat16),
+            jax.ShapeDtypeStruct((1, wide), jnp.float32),
+            jax.ShapeDtypeStruct((HEAD, wide), jnp.float32),
+        )
+        + (block,) * (slots - split),
+        in_specs=[smem()] + [vmem()] * 6 + [hbm()],
+        out_specs=(vmem(),) * (5 + slots - split),
+        scratch_shapes=[move] + held(slots - split),
         compiler_params=params,
-        name="attend_forward",
-    )(bounds, starts, turned, pairs, turned_grad)
-    arrived = swap(stats)
-    half = jax.ShapeDtypeStruct((rows, columns), jnp.bfloat16)
-    return pl.pallas_call(
-        backward_kernel,
-        out_shape=(half,) * 4 + (jax.ShapeDtypeStruct((slots * rows, 2 * HEAD), jnp.bfloat16),),
-        in_specs=[smem()] + [vmem()] * 7,
-        out_specs=(vmem(),) * 5,
-        scratch_shapes=[
-            pltpu.VMEM((wide, HEAD), jnp.bfloat16),
-            pltpu.VMEM((HEAD, wide), jnp.bfloat16),
-            pltpu.VMEM((1, wide), jnp.float32),
-            pltpu.VMEM((HEAD, wide), jnp.float32),
-            pltpu.VMEM((rows, wide), jnp.bfloat16),
-        ],
+        cost_estimate=cost(slots - split, rows, wide, 4),
+        name="attend_backward_far",
+    )(bounds, stats, arrived, acc, turned_grad, stacked, pairs, weights)
+    sent_far = send(far)
+    query_grad, query_grad_other, *near = pl.pallas_call(
+        backward_near_kernel,
+        out_shape=(half, half) + (block,) * split,
+        in_specs=[smem()] + [vmem()] * 6 + [hbm()],
+        out_specs=(vmem(),) * (2 + split),
+        scratch_shapes=[pltpu.VMEM((HEAD, wide), jnp.float32), move] + held(split),
         compiler_params=params,
-        name="attend_backward",
-    )(bounds, stats, arrived, acc, turned_grad, stacked, pairs, weights)
+        cost_estimate=cost(split, rows, wide, 4),
+        name="attend_backward_near",
+    )(bounds, scaled, turned_scaled, delta, total, stacked, pairs, weights)
+    return out, query_grad, query_grad_other, near, sent_far
 
 
 def turn(array):
@@ -265,22 +379,25 @@
     )
     reach = min((LONGEST + 2 * rows - 1) // (2 * rows), chips - 1)
     slots = reach + 1
-    out, out_other, query_grad, query_grad_other, partial = attend(
-        bounds, starts, (query, swap_cores(query)), (grad, swap_cores(grad)), every_pair, slots
-    )
-
-    def add(mine, theirs):
-        return (mine.astype(jnp.float32) + theirs.astype(jnp.float32)).astype(jnp.bfloat16)
-
-    out = add(out, swap_cores(out_other))
-    query_grad = add(query_grad, swap_cores(query_grad_other))
-    partial = partial.reshape(slots, rows, 2 * HEAD)
-    sums = partial[0].astype(jnp.float32)
-    for back in range(1, slots):
-        sums += lax.ppermute(
-            partial[back], "chip", [(c, c - back) for c in range(back, chips)]
-        ).astype(jnp.float32)
+    split = (slots + 1) // 2
+
+    def send(blocks, first):
+        return [
+            lax.ppermute(block, "chip", [(c, c - first - at) for c in range(first + at, chips)])
+            for at, block in enumerate(blocks)
+        ]
+
+    out, query_grad, query_grad_other, near, far = attend(
+        bounds, starts, (query, swap_cores(query)), (grad, swap_cores(grad)), every_pair, slots,
+        split, functools.partial(send, first=split),
+    )
+    near, far = lax.optimization_barrier((near, far))
+    sums = near[0].astype(jnp.float32)
+    for sent in far + send(near[1:], 1):
+        sums += sent.astype(jnp.float32)
     pair_grad = sums.astype(jnp.bfloat16)
+    query_grad = query_grad.astype(jnp.float32) + swap_cores(query_grad_other).astype(jnp.float32)
+    query_grad = query_grad.astype(jnp.bfloat16)
     return (out[None, :, None, :], query_grad[None, :, None, :], pair_grad[None, :, None, :])
 
 

time: 122 us -> 127 us (1.041)
  the two profiles are of different devices: /device:TPU:71 before, /device:TPU:1 now
where the time goes in v3:
time: 127 us; the launch traced here: 125 us
  waiting for transfers between devices  51.3 us (40%)
  starting transfers between devices  39.1 us (31%)
  between operations  17.6 us (14%)
  Pallas kernels  8.44 us (7%)
  local copies, waits for them, and re-layouts  6.45 us (5%)
  other arithmetic  2.27 us (2%)
    ppermute x6, waiting for transfers between devices, send(): lax.ppermute(block, 'chip', [(c, c - first - at) for c in range(first + a...  34.6 us
    ppermute x4, starting transfers between devices, swap_cores(): return lax.ppermute(value, 'core', [(0, 1), (1, 0)])  19.8 us
    all_gather x1, waiting for transfers between devices, per_device(): every_pair = lax.all_gather(pairs, 'chip', axis=0, tiled=True)  8.19 us
    ppermute x6, starting transfers between devices, send(): lax.ppermute(block, 'chip', [(c, c - first - at) for c in range(first + a...  7.74 us
    all_to_all x1, starting transfers between devices, per_device(): lax.all_to_all(arrived, 'tensor', split_axis=2, concat_axis=1, tiled=True)  6.32 us
    all_to_all x1, waiting for transfers between devices, per_device(): lax.all_to_all(arrived, 'tensor', split_axis=2, concat_axis=1, tiled=True)  5.45 us
    ppermute x1, starting transfers between devices, per_device(): lax.ppermute(incoming_output_grad, 'pipe', [(s, (s - 1) % sections) for s...  5.22 us
    pallas_call x1, Pallas kernels, attend(): pl.pallas_call(backward_near_kernel, out_shape=(half, half) + (block,) *...  3.53 us
  transfers between devices with their start and end apart: 13, of which 10 were waited for; matrix products, arithmetic and copies ran while one was open for 5% of the time, Pallas kernels for 3%

profile of v3, /device:TPU:1, one launch (start us, length us, event | category | flops | bytes accessed | tf_op | source)
XLA Modules:
  0.0 125.2 jit_solution(4690428923625723861)
XLA Ops:
  8.9 5.2 %collective-permute-start.1 = (bf16[1,32,8,640]{3,1,0,2:T(8,128)(2,1)S(1)}, bf16[1,32,8,640]{3,1,0,2:T(8,128)(2,1)}, u32[]{:S(2)}, u32[]{:S(2)}) collective-permute-start(bf16[1,32,8,640]{3,1,0,2:T(8,128)(2,1)S(1)} %copy.45), channel_id=1, source_target_pairs={{0,3},{1,0},{2,1},{3,2},{4,7},{5,4},{6,5},{7,6},{8,11},{9,8},{10,9... | collective-permute-start | bytes 983048 | tf_op jit(solution)/shard_map/ppermute | solution.py:373
  15.3 5.5 %collective-permute-start = (bf16[256,640]{0,1:T(8,128)(2,1)S(1)}, bf16[256,640]{0,1:T(8,128)(2,1)S(1)}, u32[]{:S(2)}, u32[]{:S(2)}) collective-permute-start(bf16[256,640]{0,1:T(8,128)(2,1)S(1)} %bitcast.55), channel_id=1, source_target_pairs={{0,32},{32,0},{1,33},{33,1},{2,34},{34,2},{3,35},{35,3},{4,36},{36... | collective-permute-start | bytes 983048 | tf_op jit(solution)/shard_map/ppermute | solution.py:250
  21.0 6.3 %all-to-all-start = ((bf16[1,32,8,640]{3,1,0,2:T(8,128)(2,1)}), bf16[1,32,8,640]{3,1,0,2:T(8,128)(2,1)S(1)}, u32[]{:S(2)}, u32[]{:S(2)}) async-start(bf16[1,32,8,640]{3,1,0,2:T(8,128)(2,1)} %collective-permute-done.1), calls=%async_computation | async-start | bytes 655360 | tf_op jit(solution)/shard_map/all_to_all | solution.py:376
  33.0 5.5 %all-to-all-done = bf16[1,32,8,640]{3,1,0,2:T(8,128)(2,1)S(1)} async-done(((bf16[1,32,8,640]{3,1,0,2:T(8,128)(2,1)}), bf16[1,32,8,640]{3,1,0,2:T(8,128)(2,1)S(1)}, u32[]{:S(2)}, u32[]{:S(2)}) %all-to-all-start) | async-done | bytes 327712 | tf_op jit(solution)/shard_map/all_to_all | solution.py:376
  38.4 5.1 %collective-permute-start.2 = (bf16[256,640]{1,0:T(8,128)(2,1)S(1)}, bf16[256,640]{1,0:T(8,128)(2,1)S(1)}, u32[]{:S(2)}, u32[]{:S(2)}) collective-permute-start(bf16[256,640]{1,0:T(8,128)(2,1)S(1)} %bitcast.63), channel_id=1, source_target_pairs={{0,32},{32,0},{1,33},{33,1},{2,34},{34,2},{3,35},{35,3},{4,36},{36... | collective-permute-start | bytes 983048 | tf_op jit(solution)/shard_map/ppermute | solution.py:250
  45.4 8.2 %all-gather.3.cloned.1.call-done = bf16[1,2048,1,256]{3,1,2,0:T(8,128)(2,1)} async-done(((bf16[1,256,1,256]{3,1,2,0:T(8,128)(2,1)}), bf16[1,2048,1,256]{3,1,2,0:T(8,128)(2,1)}) %all-gather.3.cloned.1.call-update) | async-done | bytes 1048592 | tf_op jit(solution)/shard_map/all_gather | solution.py:371
  54.8 2.8 %attend_forward.1 = (bf16[1792,2560]{1,0:T(8,128)(2,1)}, f32[144,2560]{1,0:T(8,128)S(1)}, f32[8,2560]{1,0:T(8,128)S(1)}, bf16[144,2560]{1,0:T(8,128)(2,1)S(1)}) custom-call(s32[5]{0:T(128)S(1)} %stack.44.bounds_ref, s32[2,1,256]{2,1,0:T(1,128)S(1)} %broadcast_in_dim.47.starts_ref, bf16[128,2560]{1,0:T(8,128)(2,1)S(1)} %get-tuple-element.32.turned_ref, ...), custom_call_target="tpu_custom_call" | custom-call | flops 2348810240 | bytes 9175040 | tf_op jit(solution)/shard_map/attend_forward/pallas_call | solution.py:271
  57.6 6.8 %collective-permute-start.3 = (bf16[144,2560]{1,0:T(8,128)(2,1)S(1)}, bf16[144,2560]{1,0:T(8,128)(2,1)S(1)}, u32[]{:S(2)}, u32[]{:S(2)}) collective-permute-start(bf16[144,2560]{1,0:T(8,128)(2,1)S(1)} %get-tuple-element.35), channel_id=1, source_target_pairs={{0,32},{32,0},{1,33},{33,1},{2,34},{34,2},{3,35},{35,3},{4,36},{36... | collective-permute-start | bytes 2211848 | tf_op jit(solution)/shard_map/ppermute | solution.py:250
  64.4 1.8 %collective-permute-done.3.arrived_ref = bf16[144,2560]{1,0:T(8,128)(2,1)S(1)} collective-permute-done((bf16[144,2560]{1,0:T(8,128)(2,1)S(1)}, bf16[144,2560]{1,0:T(8,128)(2,1)S(1)}, u32[]{:S(2)}, u32[]{:S(2)}) %collective-permute-start.3) | collective-permute-done | bytes 737312 | tf_op jit(solution)/shard_map/ppermute | solution.py:250
  66.3 2.1 %attend_backward_far.1 = (bf16[256,640]{1,0:T(8,128)(2,1)}, bf16[2560,128]{1,0:T(8,128)(2,1)S(1)}, bf16[128,2560]{1,0:T(8,128)(2,1)S(1)}, f32[1,2560]{1,0:T(1,12...) custom-call(s32[5]{0:T(128)S(1)} %stack.44.bounds_ref, ...), custom_call_target="tpu_custom_call" | custom-call | flops 2013265920 | bytes 3932160 | tf_op jit(solution)/shard_map/attend_backward_far/pallas_call | solution.py:305
  68.4 1.3 %collective-permute-start.5 = (bf16[256,256]{1,0:T(8,128)(2,1)S(1)}, bf16[256,256]{1,0:T(8,128)(2,1)S(1)}, u32[]{:S(2)}, u32[]{:S(2)}) collective-permute-start(bf16[256,256]{1,0:T(8,128)(2,1)S(1)} %get-tuple-element.51), channel_id=1, source_target_pairs={{256,0},{320,64},{384,128},{448,192},{257,1},{321,65},{385,129},{4... | collective-permute-start | bytes 393224 | tf_op jit(solution)/shard_map/ppermute | solution.py:386
  69.7 1.3 %collective-permute-start.6 = (bf16[256,256]{1,0:T(8,128)(2,1)S(1)}, bf16[256,256]{1,0:T(8,128)(2,1)S(1)}, u32[]{:S(2)}, u32[]{:S(2)}) collective-permute-start(bf16[256,256]{1,0:T(8,128)(2,1)S(1)} %get-tuple-element.52), channel_id=1, source_target_pairs={{320,0},{384,64},{448,128},{321,1},{385,65},{449,129},{322,2},{386... | collective-permute-start | bytes 393224 | tf_op jit(solution)/shard_map/ppermute | solution.py:386
  71.0 1.3 %collective-permute-start.7 = (bf16[256,256]{1,0:T(8,128)(2,1)S(1)}, bf16[256,256]{1,0:T(8,128)(2,1)S(1)}, u32[]{:S(2)}, u32[]{:S(2)}) collective-permute-start(bf16[256,256]{1,0:T(8,128)(2,1)S(1)} %get-tuple-element.53), channel_id=1, source_target_pairs={{384,0},{448,64},{385,1},{449,65},{386,2},{450,66},{387,3},{451,67... | collective-permute-start | bytes 393224 | tf_op jit(solution)/shard_map/ppermute | solution.py:386
  72.3 3.5 %attend_backward_near.1 = (bf16[256,640]{1,0:T(8,128)(2,1)S(1)}, bf16[256,640]{1,0:T(8,128)(2,1)S(1)}, bf16[256,256]{1,0:T(8,128)(2,1)S(1)}, bf16[256,256]{1,0:T...) custom-call(s32[5]{0:T(128)S(1)} %stack.44.bounds_ref, ...), custom_call_target="tpu_custom_call" | custom-call | flops 2684354560 | bytes 5242880 | tf_op jit(solution)/shard_map/attend_backward_near/pallas_call | solution.py:323
  75.8 3.1 %collective-permute-done.5 = bf16[256,256]{1,0:T(8,128)(2,1)S(1)} collective-permute-done((bf16[256,256]{1,0:T(8,128)(2,1)S(1)}, bf16[256,256]{1,0:T(8,128)(2,1)S(1)}, u32[]{:S(2)}, u32[]{:S(2)}) %collective-permute-start.5) | collective-permute-done | bytes 131104 | tf_op jit(solution)/shard_map/ppermute | solution.py:386
  78.9 4.5 %collective-permute-done.6 = bf16[256,256]{1,0:T(8,128)(2,1)S(1)} collective-permute-done((bf16[256,256]{1,0:T(8,128)(2,1)S(1)}, bf16[256,256]{1,0:T(8,128)(2,1)S(1)}, u32[]{:S(2)}, u32[]{:S(2)}) %collective-permute-start.6) | collective-permute-done | bytes 131104 | tf_op jit(solution)/shard_map/ppermute | solution.py:386
  83.4 8.9 %collective-permute-done.7 = bf16[256,256]{1,0:T(8,128)(2,1)S(1)} collective-permute-done((bf16[256,256]{1,0:T(8,128)(2,1)S(1)}, bf16[256,256]{1,0:T(8,128)(2,1)S(1)}, u32[]{:S(2)}, u32[]{:S(2)}) %collective-permute-start.7) | collective-permute-done | bytes 131104 | tf_op jit(solution)/shard_map/ppermute | solution.py:386
  92.2 1.3 %collective-permute-start.8 = (bf16[256,256]{1,0:T(8,128)(2,1)S(1)}, bf16[256,256]{1,0:T(8,128)(2,1)S(1)}, u32[]{:S(2)}, u32[]{:S(2)}) collective-permute-start(bf16[256,256]{1,0:T(8,128)(2,1)S(1)} %get-tuple-element.58), channel_id=1, source_target_pairs={{64,0},{128,64},{192,128},{256,192},{320,256},{384,320},{448,384},... | collective-permute-start | bytes 393224 | tf_op jit(solution)/shard_map/ppermute | solution.py:386
  93.5 1.3 %collective-permute-start.9 = (bf16[256,256]{1,0:T(8,128)(2,1)S(1)}, bf16[256,256]{1,0:T(8,128)(2,1)S(1)}, u32[]{:S(2)}, u32[]{:S(2)}) collective-permute-start(bf16[256,256]{1,0:T(8,128)(2,1)S(1)} %get-tuple-element.59), channel_id=1, source_target_pairs={{128,0},{192,64},{256,128},{320,192},{384,256},{448,320},{129,1},{... | collective-permute-start | bytes 393224 | tf_op jit(solution)/shard_map/ppermute | solution.py:386
  94.8 1.3 %collective-permute-start.10 = (bf16[256,256]{1,0:T(8,128)(2,1)S(1)}, bf16[256,256]{1,0:T(8,128)(2,1)S(1)}, u32[]{:S(2)}, u32[]{:S(2)}) collective-permute-start(bf16[256,256]{1,0:T(8,128)(2,1)S(1)} %get-tuple-element.60), channel_id=1, source_target_pairs={{192,0},{256,64},{320,128},{384,192},{448,256},{193,1},{257,65},{3... | collective-permute-start | bytes 393224 | tf_op jit(solution)/shard_map/ppermute | solution.py:386
  96.1 2.4 %collective-permute-start.4 = (bf16[256,640]{1,0:T(8,128)(2,1)S(1)}, bf16[256,640]{1,0:T(8,128)(2,1)S(1)}, u32[]{:S(2)}, u32[]{:S(2)}) collective-permute-start(bf16[256,640]{1,0:T(8,128)(2,1)S(1)} %get-tuple-element.46), channel_id=1, source_target_pairs={{0,32},{32,0},{1,33},{33,1},{2,34},{34,2},{3,35},{35,3},{4,36},{36... | collective-permute-start | bytes 983048 | tf_op jit(solution)/shard_map/ppermute | solution.py:250
  98.5 5.8 %collective-permute-done.8 = bf16[256,256]{1,0:T(8,128)(2,1)S(1)} collective-permute-done((bf16[256,256]{1,0:T(8,128)(2,1)S(1)}, bf16[256,256]{1,0:T(8,128)(2,1)S(1)}, u32[]{:S(2)}, u32[]{:S(2)}) %collective-permute-start.8) | collective-permute-done | bytes 131104 | tf_op jit(solution)/shard_map/ppermute | solution.py:386
  104.4 7.0 %collective-permute-done.9 = bf16[256,256]{1,0:T(8,128)(2,1)S(1)} collective-permute-done((bf16[256,256]{1,0:T(8,128)(2,1)S(1)}, bf16[256,256]{1,0:T(8,128)(2,1)S(1)}, u32[]{:S(2)}, u32[]{:S(2)}) %collective-permute-start.9) | collective-permute-done | bytes 131104 | tf_op jit(solution)/shard_map/ppermute | solution.py:386
  111.4 5.4 %collective-permute-done.10 = bf16[256,256]{1,0:T(8,128)(2,1)S(1)} collective-permute-done((bf16[256,256]{1,0:T(8,128)(2,1)S(1)}, bf16[256,256]{1,0:T(8,128)(2,1)S(1)}, u32[]{:S(2)}, u32[]{:S(2)}) %collective-permute-start.10) | collective-permute-done | bytes 131104 | tf_op jit(solution)/shard_map/ppermute | solution.py:386
  (38 shorter events, 10.0 us)
Async XLA Ops:
  7.2 13.6 %copy-start.1 = (s32[1,8]{1,0:T(1,128)S(1)}, s32[1,8]{1,0:T(1,128)}, u32[]{:S(2)}) copy-start(s32[1,8]{1,0:T(1,128)} %param.6) | copy-start | bytes 100
  7.2 46.4 %all-gather.3.cloned.1.call-start = ((), (), s32[]{:S(2)}) async-start(), calls=%async_computation.1 | async-start | bytes 1179648 | tf_op jit(solution)/shard_map/all_gather | solution.py:371
  8.9 12.1 %collective-permute-start.1 = (bf16[1,32,8,640]{3,1,0,2:T(8,128)(2,1)S(1)}, bf16[1,32,8,640]{3,1,0,2:T(8,128)(2,1)}, u32[]{:S(2)}, u32[]{:S(2)}) collective-permute-start(bf16[1,32,8,640]{3,1,0,2:T(8,128)(2,1)S(1)} %copy.45), channel_id=1, source_target_pairs={{0,3},{1,0},{2,1},{3,2},{4,7},{5,4},{6,5},{7,6},{8,11},{9,8},{10,9... | collective-permute-start | bytes 983048 | tf_op jit(solution)/shard_map/ppermute | solution.py:373
  15.3 17.0 %collective-permute-start = (bf16[256,640]{0,1:T(8,128)(2,1)S(1)}, bf16[256,640]{0,1:T(8,128)(2,1)S(1)}, u32[]{:S(2)}, u32[]{:S(2)}) collective-permute-start(bf16[256,640]{0,1:T(8,128)(2,1)S(1)} %bitcast.55), channel_id=1, source_target_pairs={{0,32},{32,0},{1,33},{33,1},{2,34},{34,2},{3,35},{35,3},{4,36},{36... | collective-permute-start | bytes 983048 | tf_op jit(solution)/shard_map/ppermute | solution.py:250
  21.0 17.4 %all-to-all-start = ((bf16[1,32,8,640]{3,1,0,2:T(8,128)(2,1)}), bf16[1,32,8,640]{3,1,0,2:T(8,128)(2,1)S(1)}, u32[]{:S(2)}, u32[]{:S(2)}) async-start(bf16[1,32,8,640]{3,1,0,2:T(8,128)(2,1)} %collective-permute-done.1), calls=%async_computation | async-start | bytes 655360 | tf_op jit(solution)/shard_map/all_to_all | solution.py:376
  38.4 6.3 %collective-permute-start.2 = (bf16[256,640]{1,0:T(8,128)(2,1)S(1)}, bf16[256,640]{1,0:T(8,128)(2,1)S(1)}, u32[]{:S(2)}, u32[]{:S(2)}) collective-permute-start(bf16[256,640]{1,0:T(8,128)(2,1)S(1)} %bitcast.63), channel_id=1, source_target_pairs={{0,32},{32,0},{1,33},{33,1},{2,34},{34,2},{3,35},{35,3},{4,36},{36... | collective-permute-start | bytes 983048 | tf_op jit(solution)/shard_map/ppermute | solution.py:250
  53.6 1.2 copy-start
  57.6 8.7 %collective-permute-start.3 = (bf16[144,2560]{1,0:T(8,128)(2,1)S(1)}, bf16[144,2560]{1,0:T(8,128)(2,1)S(1)}, u32[]{:S(2)}, u32[]{:S(2)}) collective-permute-start(bf16[144,2560]{1,0:T(8,128)(2,1)S(1)} %get-tuple-element.35), channel_id=1, source_target_pairs={{0,32},{32,0},{1,33},{33,1},{2,34},{34,2},{3,35},{35,3},{4,36},{36... | collective-permute-start | bytes 2211848 | tf_op jit(solution)/shard_map/ppermute | solution.py:250
  68.4 10.5 %collective-permute-start.5 = (bf16[256,256]{1,0:T(8,128)(2,1)S(1)}, bf16[256,256]{1,0:T(8,128)(2,1)S(1)}, u32[]{:S(2)}, u32[]{:S(2)}) collective-permute-start(bf16[256,256]{1,0:T(8,128)(2,1)S(1)} %get-tuple-element.51), channel_id=1, source_target_pairs={{256,0},{320,64},{384,128},{448,192},{257,1},{321,65},{385,129},{4... | collective-permute-start | bytes 393224 | tf_op jit(solution)/shard_map/ppermute | solution.py:386
  69.7 13.7 %collective-permute-start.6 = (bf16[256,256]{1,0:T(8,128)(2,1)S(1)}, bf16[256,256]{1,0:T(8,128)(2,1)S(1)}, u32[]{:S(2)}, u32[]{:S(2)}) collective-permute-start(bf16[256,256]{1,0:T(8,128)(2,1)S(1)} %get-tuple-element.52), channel_id=1, source_target_pairs={{320,0},{384,64},{448,128},{321,1},{385,65},{449,129},{322,2},{386... | collective-permute-start | bytes 393224 | tf_op jit(solution)/shard_map/ppermute | solution.py:386
  71.0 21.2 %collective-permute-start.7 = (bf16[256,256]{1,0:T(8,128)(2,1)S(1)}, bf16[256,256]{1,0:T(8,128)(2,1)S(1)}, u32[]{:S(2)}, u32[]{:S(2)}) collective-permute-start(bf16[256,256]{1,0:T(8,128)(2,1)S(1)} %get-tuple-element.53), channel_id=1, source_target_pairs={{384,0},{448,64},{385,1},{449,65},{386,2},{450,66},{387,3},{451,67... | collective-permute-start | bytes 393224 | tf_op jit(solution)/shard_map/ppermute | solution.py:386
  92.2 12.1 %collective-permute-start.8 = (bf16[256,256]{1,0:T(8,128)(2,1)S(1)}, bf16[256,256]{1,0:T(8,128)(2,1)S(1)}, u32[]{:S(2)}, u32[]{:S(2)}) collective-permute-start(bf16[256,256]{1,0:T(8,128)(2,1)S(1)} %get-tuple-element.58), channel_id=1, source_target_pairs={{64,0},{128,64},{192,128},{256,192},{320,256},{384,320},{448,384},... | collective-permute-start | bytes 393224 | tf_op jit(solution)/shard_map/ppermute | solution.py:386
  93.5 17.9 %collective-permute-start.9 = (bf16[256,256]{1,0:T(8,128)(2,1)S(1)}, bf16[256,256]{1,0:T(8,128)(2,1)S(1)}, u32[]{:S(2)}, u32[]{:S(2)}) collective-permute-start(bf16[256,256]{1,0:T(8,128)(2,1)S(1)} %get-tuple-element.59), channel_id=1, source_target_pairs={{128,0},{192,64},{256,128},{320,192},{384,256},{448,320},{129,1},{... | collective-permute-start | bytes 393224 | tf_op jit(solution)/shard_map/ppermute | solution.py:386
  94.8 21.9 %collective-permute-start.10 = (bf16[256,256]{1,0:T(8,128)(2,1)S(1)}, bf16[256,256]{1,0:T(8,128)(2,1)S(1)}, u32[]{:S(2)}, u32[]{:S(2)}) collective-permute-start(bf16[256,256]{1,0:T(8,128)(2,1)S(1)} %get-tuple-element.60), channel_id=1, source_target_pairs={{192,0},{256,64},{320,128},{384,192},{448,256},{193,1},{257,65},{3... | collective-permute-start | bytes 393224 | tf_op jit(solution)/shard_map/ppermute | solution.py:386
  96.1 21.4 %collective-permute-start.4 = (bf16[256,640]{1,0:T(8,128)(2,1)S(1)}, bf16[256,640]{1,0:T(8,128)(2,1)S(1)}, u32[]{:S(2)}, u32[]{:S(2)}) collective-permute-start(bf16[256,640]{1,0:T(8,128)(2,1)S(1)} %get-tuple-element.46), channel_id=1, source_target_pairs={{0,32},{32,0},{1,33},{33,1},{2,34},{34,2},{3,35},{35,3},{4,36},{36... | collective-permute-start | bytes 983048 | tf_op jit(solution)/shard_map/ppermute | solution.py:250
Sparse Core Ops, SparseCore 0:
  10.1 43.4 all-gather.2

commit v4 on v3

--- a/solution.py
+++ b/solution.py
@@ -391,9 +391,11 @@
         bounds, starts, (query, swap_cores(query)), (grad, swap_cores(grad)), every_pair, slots,
         split, functools.partial(send, first=split),
     )
-    near, far = lax.optimization_barrier((near, far))
     sums = near[0].astype(jnp.float32)
-    for sent in far + send(near[1:], 1):
+    for sent in far:
+        sums += sent.astype(jnp.float32)
+    sums = lax.optimization_barrier(sums)
+    for sent in send(near[1:], 1):
         sums += sent.astype(jnp.float32)
     pair_grad = sums.astype(jnp.bfloat16)
     query_grad = query_grad.astype(jnp.float32) + swap_cores(query_grad_other).astype(jnp.float32)

time: 127 us -> 115 us (0.906)
  the two profiles are of different devices: /device:TPU:1 before, /device:TPU:198 now
where the time goes in v4:
time: 115 us; the launch traced here: 114 us
  waiting for transfers between devices  45.5 us (40%)
  starting transfers between devices  26.1 us (23%)
  between operations  17.6 us (15%)
  Pallas kernels  16.2 us (14%)
  local copies, waits for them, and re-layouts  6.45 us (6%)
  other arithmetic  2.28 us (2%)
    ppermute x6, waiting for transfers between devices, send(): lax.ppermute(block, 'chip', [(c, c - first - at) for c in range(first + a...  20.2 us
    ppermute x6, starting transfers between devices, send(): lax.ppermute(block, 'chip', [(c, c - first - at) for c in range(first + a...  8.39 us
    all_gather x1, waiting for transfers between devices, per_device(): every_pair = lax.all_gather(pairs, 'chip', axis=0, tiled=True)  8.19 us
    pallas_call x1, Pallas kernels, attend(): pl.pallas_call(backward_near_kernel, out_shape=(half, half) + (block,) *...  7.81 us
    ppermute x4, starting transfers between devices, swap_cores(): return lax.ppermute(value, 'core', [(0, 1), (1, 0)])  7.78 us
    all_to_all x1, starting transfers between devices, per_device(): lax.all_to_all(arrived, 'tensor', split_axis=2, concat_axis=1, tiled=True)  7.1 us
    all_to_all x1, waiting for transfers between devices, per_device(): lax.all_to_all(arrived, 'tensor', split_axis=2, concat_axis=1, tiled=True)  6.78 us
    ppermute x1, waiting for transfers between devices, per_device(): lax.ppermute(incoming_output_grad, 'pipe', [(s, (s - 1) % sections) for s...  6.63 us
  transfers between devices with their start and end apart: 13, of which 8 were waited for; matrix products, arithmetic and copies ran while one was open for 6% of the time, Pallas kernels for 7%

profile of v4, /device:TPU:198, one launch (start us, length us, event | category | flops | bytes accessed | tf_op | source)
XLA Modules:
  0.0 114.1 jit_solution(8274175236328423168)
XLA Ops:
  7.9 1.0 copy.45
  8.9 2.7 %collective-permute-start.1 = (bf16[1,32,8,640]{3,1,0,2:T(8,128)(2,1)S(1)}, bf16[1,32,8,640]{3,1,0,2:T(8,128)(2,1)}, u32[]{:S(2)}, u32[]{:S(2)}) collective-permute-start(bf16[1,32,8,640]{3,1,0,2:T(8,128)(2,1)S(1)} %copy.45), channel_id=1, source_target_pairs={{0,3},{1,0},{2,1},{3,2},{4,7},{5,4},{6,5},{7,6},{8,11},{9,8},{10,9... | collective-permute-start | bytes 983048 | tf_op jit(solution)/shard_map/ppermute | solution.py:373
  11.7 1.1 %copy.39 = bf16[1,256,1,640]{1,3,2,0:T(8,128)(2,1)S(1)} copy(bf16[1,256,1,640]{3,1,2,0:T(8,128)(2,1)} %param.4) | data formatting | bytes 655360 | tf_op args[0]
  12.8 1.9 %collective-permute-start = (bf16[256,640]{0,1:T(8,128)(2,1)S(1)}, bf16[256,640]{0,1:T(8,128)(2,1)S(1)}, u32[]{:S(2)}, u32[]{:S(2)}) collective-permute-start(bf16[256,640]{0,1:T(8,128)(2,1)S(1)} %bitcast.55), channel_id=1, source_target_pairs={{0,32},{32,0},{1,33},{33,1},{2,34},{34,2},{3,35},{35,3},{4,36},{36... | collective-permute-start | bytes 983048 | tf_op jit(solution)/shard_map/ppermute | solution.py:250
  15.0 6.6 %collective-permute-done.1 = bf16[1,32,8,640]{3,1,0,2:T(8,128)(2,1)} collective-permute-done((bf16[1,32,8,640]{3,1,0,2:T(8,128)(2,1)S(1)}, bf16[1,32,8,640]{3,1,0,2:T(8,128)(2,1)}, u32[]{:S(2)}, u32[]{:S(2)}) %collective-permute-start.1) | collective-permute-done | bytes 327712 | tf_op jit(solution)/shard_map/ppermute | solution.py:373
  21.6 7.1 %all-to-all-start = ((bf16[1,32,8,640]{3,1,0,2:T(8,128)(2,1)}), bf16[1,32,8,640]{3,1,0,2:T(8,128)(2,1)S(1)}, u32[]{:S(2)}, u32[]{:S(2)}) async-start(bf16[1,32,8,640]{3,1,0,2:T(8,128)(2,1)} %collective-permute-done.1), calls=%async_computation | async-start | bytes 655360 | tf_op jit(solution)/shard_map/all_to_all | solution.py:376
  34.3 6.8 %all-to-all-done = bf16[1,32,8,640]{3,1,0,2:T(8,128)(2,1)S(1)} async-done(((bf16[1,32,8,640]{3,1,0,2:T(8,128)(2,1)}), bf16[1,32,8,640]{3,1,0,2:T(8,128)(2,1)S(1)}, u32[]{:S(2)}, u32[]{:S(2)}) %all-to-all-start) | async-done | bytes 327712 | tf_op jit(solution)/shard_map/all_to_all | solution.py:376
  41.1 1.9 %collective-permute-start.2 = (bf16[256,640]{1,0:T(8,128)(2,1)S(1)}, bf16[256,640]{1,0:T(8,128)(2,1)S(1)}, u32[]{:S(2)}, u32[]{:S(2)}) collective-permute-start(bf16[256,640]{1,0:T(8,128)(2,1)S(1)} %bitcast.63), channel_id=1, source_target_pairs={{0,32},{32,0},{1,33},{33,1},{2,34},{34,2},{3,35},{35,3},{4,36},{36... | collective-permute-start | bytes 983048 | tf_op jit(solution)/shard_map/ppermute | solution.py:250
  43.7 0.9 collective-permute-done.2
  45.3 8.2 %all-gather.3.cloned.1.call-done = bf16[1,2048,1,256]{3,1,2,0:T(8,128)(2,1)} async-done(((bf16[1,256,1,256]{3,1,2,0:T(8,128)(2,1)}), bf16[1,2048,1,256]{3,1,2,0:T(8,128)(2,1)}) %all-gather.3.cloned.1.call-update) | async-done | bytes 1048592 | tf_op jit(solution)/shard_map/all_gather | solution.py:371
  53.5 1.2 %copy-done = bf16[1,2048,1,256]{3,1,2,0:T(8,128)(2,1)S(1)} copy-done((bf16[1,2048,1,256]{3,1,2,0:T(8,128)(2,1)S(1)}, bf16[1,2048,1,256]{3,1,2,0:T(8,128)(2,1)}, u32[]{:S(2)}) %copy-start) | copy-done | bytes 1048600
  54.7 6.3 %attend_forward.1 = (bf16[1792,2560]{1,0:T(8,128)(2,1)}, f32[144,2560]{1,0:T(8,128)S(1)}, f32[8,2560]{1,0:T(8,128)S(1)}, bf16[144,2560]{1,0:T(8,128)(2,1)S(1)}) custom-call(s32[5]{0:T(128)S(1)} %stack.44.bounds_ref, s32[2,1,256]{2,1,0:T(1,128)S(1)} %broadcast_in_dim.47.starts_ref, bf16[128,2560]{1,0:T(8,128)(2,1)S(1)} %get-tuple-element.25.turned_ref, ...), custom_call_target="tpu_custom_call" | custom-call | flops 2348810240 | bytes 9175040 | tf_op jit(solution)/shard_map/attend_forward/pallas_call | solution.py:271
  61.0 1.9 %collective-permute-start.3 = (bf16[144,2560]{1,0:T(8,128)(2,1)S(1)}, bf16[144,2560]{1,0:T(8,128)(2,1)S(1)}, u32[]{:S(2)}, u32[]{:S(2)}) collective-permute-start(bf16[144,2560]{1,0:T(8,128)(2,1)S(1)} %get-tuple-element.28), channel_id=1, source_target_pairs={{0,32},{32,0},{1,33},{33,1},{2,34},{34,2},{3,35},{35,3},{4,36},{36... | collective-permute-start | bytes 2211848 | tf_op jit(solution)/shard_map/ppermute | solution.py:250
  62.9 2.2 %collective-permute-done.3.arrived_ref = bf16[144,2560]{1,0:T(8,128)(2,1)S(1)} collective-permute-done((bf16[144,2560]{1,0:T(8,128)(2,1)S(1)}, bf16[144,2560]{1,0:T(8,128)(2,1)S(1)}, u32[]{:S(2)}, u32[]{:S(2)}) %collective-permute-start.3) | collective-permute-done | bytes 737312 | tf_op jit(solution)/shard_map/ppermute | solution.py:250
  65.1 2.1 %attend_backward_far.1 = (bf16[256,640]{1,0:T(8,128)(2,1)}, bf16[2560,128]{1,0:T(8,128)(2,1)S(1)}, bf16[128,2560]{1,0:T(8,128)(2,1)S(1)}, f32[1,2560]{1,0:T(1,12...) custom-call(s32[5]{0:T(128)S(1)} %stack.44.bounds_ref, ...), custom_call_target="tpu_custom_call" | custom-call | flops 2013265920 | bytes 3932160 | tf_op jit(solution)/shard_map/attend_backward_far/pallas_call | solution.py:305
  67.2 1.3 %collective-permute-start.5 = (bf16[256,256]{1,0:T(8,128)(2,1)S(1)}, bf16[256,256]{1,0:T(8,128)(2,1)S(1)}, u32[]{:S(2)}, u32[]{:S(2)}) collective-permute-start(bf16[256,256]{1,0:T(8,128)(2,1)S(1)} %get-tuple-element.41), channel_id=1, source_target_pairs={{256,0},{320,64},{384,128},{448,192},{257,1},{321,65},{385,129},{4... | collective-permute-start | bytes 393224 | tf_op jit(solution)/shard_map/ppermute | solution.py:386
  69.9 7.8 %attend_backward_near.1 = (bf16[256,640]{1,0:T(8,128)(2,1)S(1)}, bf16[256,640]{1,0:T(8,128)(2,1)S(1)}, bf16[256,256]{1,0:T(8,128)(2,1)S(1)}, bf16[256,256]{1,0:T...) custom-call(s32[5]{0:T(128)S(1)} %stack.44.bounds_ref, ...), custom_call_target="tpu_custom_call" | custom-call | flops 2684354560 | bytes 5242880 | tf_op jit(solution)/shard_map/attend_backward_near/pallas_call | solution.py:323
  77.7 1.9 %collective-permute-start.8 = (bf16[256,256]{1,0:T(8,128)(2,1)S(1)}, bf16[256,256]{1,0:T(8,128)(2,1)S(1)}, u32[]{:S(2)}, u32[]{:S(2)}) collective-permute-start(bf16[256,256]{1,0:T(8,128)(2,1)S(1)} %get-tuple-element.44), channel_id=1, source_target_pairs={{64,0},{128,64},{192,128},{256,192},{320,256},{384,320},{448,384},... | collective-permute-start | bytes 393224 | tf_op jit(solution)/shard_map/ppermute | solution.py:386
  79.6 1.9 %collective-permute-start.9 = (bf16[256,256]{1,0:T(8,128)(2,1)S(1)}, bf16[256,256]{1,0:T(8,128)(2,1)S(1)}, u32[]{:S(2)}, u32[]{:S(2)}) collective-permute-start(bf16[256,256]{1,0:T(8,128)(2,1)S(1)} %get-tuple-element.45), channel_id=1, source_target_pairs={{128,0},{192,64},{256,128},{320,192},{384,256},{448,320},{129,1},{... | collective-permute-start | bytes 393224 | tf_op jit(solution)/shard_map/ppermute | solution.py:386
  81.6 1.9 %collective-permute-start.10 = (bf16[256,256]{1,0:T(8,128)(2,1)S(1)}, bf16[256,256]{1,0:T(8,128)(2,1)S(1)}, u32[]{:S(2)}, u32[]{:S(2)}) collective-permute-start(bf16[256,256]{1,0:T(8,128)(2,1)S(1)} %get-tuple-element.46), channel_id=1, source_target_pairs={{192,0},{256,64},{320,128},{384,192},{448,256},{193,1},{257,65},{3... | collective-permute-start | bytes 393224 | tf_op jit(solution)/shard_map/ppermute | solution.py:386
  83.5 2.0 %collective-permute-start.4 = (bf16[256,640]{1,0:T(8,128)(2,1)S(1)}, bf16[256,640]{1,0:T(8,128)(2,1)S(1)}, u32[]{:S(2)}, u32[]{:S(2)}) collective-permute-start(bf16[256,640]{1,0:T(8,128)(2,1)S(1)} %get-tuple-element.39), channel_id=1, source_target_pairs={{0,32},{32,0},{1,33},{33,1},{2,34},{34,2},{3,35},{35,3},{4,36},{36... | collective-permute-start | bytes 983048 | tf_op jit(solution)/shard_map/ppermute | solution.py:250
  85.6 2.2 %collective-permute-done.8 = bf16[256,256]{1,0:T(8,128)(2,1)S(1)} collective-permute-done((bf16[256,256]{1,0:T(8,128)(2,1)S(1)}, bf16[256,256]{1,0:T(8,128)(2,1)S(1)}, u32[]{:S(2)}, u32[]{:S(2)}) %collective-permute-start.8) | collective-permute-done | bytes 131104 | tf_op jit(solution)/shard_map/ppermute | solution.py:386
  87.8 7.0 %collective-permute-done.9 = bf16[256,256]{1,0:T(8,128)(2,1)S(1)} collective-permute-done((bf16[256,256]{1,0:T(8,128)(2,1)S(1)}, bf16[256,256]{1,0:T(8,128)(2,1)S(1)}, u32[]{:S(2)}, u32[]{:S(2)}) %collective-permute-start.9) | collective-permute-done | bytes 131104 | tf_op jit(solution)/shard_map/ppermute | solution.py:386
  94.9 10.9 %collective-permute-done.10 = bf16[256,256]{1,0:T(8,128)(2,1)S(1)} collective-permute-done((bf16[256,256]{1,0:T(8,128)(2,1)S(1)}, bf16[256,256]{1,0:T(8,128)(2,1)S(1)}, u32[]{:S(2)}, u32[]{:S(2)}) %collective-permute-start.10) | collective-permute-done | bytes 131104 | tf_op jit(solution)/shard_map/ppermute | solution.py:386
  (39 shorter events, 7.4 us)
Async XLA Ops:
  7.2 7.6 %copy-start.1 = (s32[1,8]{1,0:T(1,128)S(1)}, s32[1,8]{1,0:T(1,128)}, u32[]{:S(2)}) copy-start(s32[1,8]{1,0:T(1,128)} %param.6) | copy-start | bytes 100
  7.2 46.3 %all-gather.3.cloned.1.call-start = ((), (), s32[]{:S(2)}) async-start(), calls=%async_computation.1 | async-start | bytes 1179648 | tf_op jit(solution)/shard_map/all_gather | solution.py:371
  8.9 12.7 %collective-permute-start.1 = (bf16[1,32,8,640]{3,1,0,2:T(8,128)(2,1)S(1)}, bf16[1,32,8,640]{3,1,0,2:T(8,128)(2,1)}, u32[]{:S(2)}, u32[]{:S(2)}) collective-permute-start(bf16[1,32,8,640]{3,1,0,2:T(8,128)(2,1)S(1)} %copy.45), channel_id=1, source_target_pairs={{0,3},{1,0},{2,1},{3,2},{4,7},{5,4},{6,5},{7,6},{8,11},{9,8},{10,9... | collective-permute-start | bytes 983048 | tf_op jit(solution)/shard_map/ppermute | solution.py:373
  12.8 20.9 %collective-permute-start = (bf16[256,640]{0,1:T(8,128)(2,1)S(1)}, bf16[256,640]{0,1:T(8,128)(2,1)S(1)}, u32[]{:S(2)}, u32[]{:S(2)}) collective-permute-start(bf16[256,640]{0,1:T(8,128)(2,1)S(1)} %bitcast.55), channel_id=1, source_target_pairs={{0,32},{32,0},{1,33},{33,1},{2,34},{34,2},{3,35},{35,3},{4,36},{36... | collective-permute-start | bytes 983048 | tf_op jit(solution)/shard_map/ppermute | solution.py:250
  21.6 19.5 %all-to-all-start = ((bf16[1,32,8,640]{3,1,0,2:T(8,128)(2,1)}), bf16[1,32,8,640]{3,1,0,2:T(8,128)(2,1)S(1)}, u32[]{:S(2)}, u32[]{:S(2)}) async-start(bf16[1,32,8,640]{3,1,0,2:T(8,128)(2,1)} %collective-permute-done.1), calls=%async_computation | async-start | bytes 655360 | tf_op jit(solution)/shard_map/all_to_all | solution.py:376
  41.1 3.5 %collective-permute-start.2 = (bf16[256,640]{1,0:T(8,128)(2,1)S(1)}, bf16[256,640]{1,0:T(8,128)(2,1)S(1)}, u32[]{:S(2)}, u32[]{:S(2)}) collective-permute-start(bf16[256,640]{1,0:T(8,128)(2,1)S(1)} %bitcast.63), channel_id=1, source_target_pairs={{0,32},{32,0},{1,33},{33,1},{2,34},{34,2},{3,35},{35,3},{4,36},{36... | collective-permute-start | bytes 983048 | tf_op jit(solution)/shard_map/ppermute | solution.py:250
  53.5 1.2 %copy-start = (bf16[1,2048,1,256]{3,1,2,0:T(8,128)(2,1)S(1)}, bf16[1,2048,1,256]{3,1,2,0:T(8,128)(2,1)}, u32[]{:S(2)}) copy-start(bf16[1,2048,1,256]{3,1,2,0:T(8,128)(2,1)} %all-gather.3.cloned.1.call-done) | copy-start | bytes 3145732
  61.0 4.1 %collective-permute-start.3 = (bf16[144,2560]{1,0:T(8,128)(2,1)S(1)}, bf16[144,2560]{1,0:T(8,128)(2,1)S(1)}, u32[]{:S(2)}, u32[]{:S(2)}) collective-permute-start(bf16[144,2560]{1,0:T(8,128)(2,1)S(1)} %get-tuple-element.28), channel_id=1, source_target_pairs={{0,32},{32,0},{1,33},{33,1},{2,34},{34,2},{3,35},{35,3},{4,36},{36... | collective-permute-start | bytes 2211848 | tf_op jit(solution)/shard_map/ppermute | solution.py:250
  67.2 14.3 %collective-permute-start.5 = (bf16[256,256]{1,0:T(8,128)(2,1)S(1)}, bf16[256,256]{1,0:T(8,128)(2,1)S(1)}, u32[]{:S(2)}, u32[]{:S(2)}) collective-permute-start(bf16[256,256]{1,0:T(8,128)(2,1)S(1)} %get-tuple-element.41), channel_id=1, source_target_pairs={{256,0},{320,64},{384,128},{448,192},{257,1},{321,65},{385,129},{4... | collective-permute-start | bytes 393224 | tf_op jit(solution)/shard_map/ppermute | solution.py:386
  68.5 15.0 %collective-permute-start.6 = (bf16[256,256]{1,0:T(8,128)(2,1)S(1)}, bf16[256,256]{1,0:T(8,128)(2,1)S(1)}, u32[]{:S(2)}, u32[]{:S(2)}) collective-permute-start(bf16[256,256]{1,0:T(8,128)(2,1)S(1)} %get-tuple-element.42), channel_id=1, source_target_pairs={{320,0},{384,64},{448,128},{321,1},{385,65},{449,129},{322,2},{386... | collective-permute-start | bytes 393224 | tf_op jit(solution)/shard_map/ppermute | solution.py:386
  69.2 16.3 %collective-permute-start.7 = (bf16[256,256]{1,0:T(8,128)(2,1)S(1)}, bf16[256,256]{1,0:T(8,128)(2,1)S(1)}, u32[]{:S(2)}, u32[]{:S(2)}) collective-permute-start(bf16[256,256]{1,0:T(8,128)(2,1)S(1)} %get-tuple-element.43), channel_id=1, source_target_pairs={{384,0},{448,64},{385,1},{449,65},{386,2},{450,66},{387,3},{451,67... | collective-permute-start | bytes 393224 | tf_op jit(solution)/shard_map/ppermute | solution.py:386
  77.7 10.1 %collective-permute-start.8 = (bf16[256,256]{1,0:T(8,128)(2,1)S(1)}, bf16[256,256]{1,0:T(8,128)(2,1)S(1)}, u32[]{:S(2)}, u32[]{:S(2)}) collective-permute-start(bf16[256,256]{1,0:T(8,128)(2,1)S(1)} %get-tuple-element.44), channel_id=1, source_target_pairs={{64,0},{128,64},{192,128},{256,192},{320,256},{384,320},{448,384},... | collective-permute-start | bytes 393224 | tf_op jit(solution)/shard_map/ppermute | solution.py:386
  79.6 15.3 %collective-permute-start.9 = (bf16[256,256]{1,0:T(8,128)(2,1)S(1)}, bf16[256,256]{1,0:T(8,128)(2,1)S(1)}, u32[]{:S(2)}, u32[]{:S(2)}) collective-permute-start(bf16[256,256]{1,0:T(8,128)(2,1)S(1)} %get-tuple-element.45), channel_id=1, source_target_pairs={{128,0},{192,64},{256,128},{320,192},{384,256},{448,320},{129,1},{... | collective-permute-start | bytes 393224 | tf_op jit(solution)/shard_map/ppermute | solution.py:386
  81.6 24.2 %collective-permute-start.10 = (bf16[256,256]{1,0:T(8,128)(2,1)S(1)}, bf16[256,256]{1,0:T(8,128)(2,1)S(1)}, u32[]{:S(2)}, u32[]{:S(2)}) collective-permute-start(bf16[256,256]{1,0:T(8,128)(2,1)S(1)} %get-tuple-element.46), channel_id=1, source_target_pairs={{192,0},{256,64},{320,128},{384,192},{448,256},{193,1},{257,65},{3... | collective-permute-start | bytes 393224 | tf_op jit(solution)/shard_map/ppermute | solution.py:386
  83.5 23.0 %collective-permute-start.4 = (bf16[256,640]{1,0:T(8,128)(2,1)S(1)}, bf16[256,640]{1,0:T(8,128)(2,1)S(1)}, u32[]{:S(2)}, u32[]{:S(2)}) collective-permute-start(bf16[256,640]{1,0:T(8,128)(2,1)S(1)} %get-tuple-element.39), channel_id=1, source_target_pairs={{0,32},{32,0},{1,33},{33,1},{2,34},{34,2},{3,35},{35,3},{4,36},{36... | collective-permute-start | bytes 983048 | tf_op jit(solution)/shard_map/ppermute | solution.py:250
Sparse Core Ops, SparseCore 0:
  10.1 43.3 all-gather.2

commit v5 on v4

--- a/solution.py
+++ b/solution.py
@@ -24,27 +24,29 @@
 
 
 def forward_kernel(
-    bounds_ref, starts_ref, turned_ref, pairs_ref,
-    kept_ref, acc_ref, stats_ref, sent_ref, scores_ref, top_ref, weights_ref, kept_sem,
+    bounds_ref, starts_ref, turned_ref, *rest,
 ):
+    *block_refs, kept_ref, pairs_ref, acc_ref, stats_ref, sent_ref = rest[:-4]
+    scores_ref, top_ref, weights_ref, kept_sem = rest[-4:]
     rows = starts_ref.shape[2]
     groups = turned_ref.shape[1] // rows
     heads = groups // 2
     scale = LOG2E / math.sqrt(HEAD)
-    chip, own, clear, last = bounds_ref[0], bounds_ref[1], bounds_ref[3], bounds_ref[4]
+    own, clear, last = bounds_ref[0], bounds_ref[2], bounds_ref[3]
+    for back, block_ref in enumerate(block_refs):
+        pairs_ref[back * rows : (back + 1) * rows, :] = block_ref[...]
     top_ref[...] = jnp.full_like(top_ref, NEG_LARGE)
     acc_ref[...] = jnp.zeros_like(acc_ref)
 
     def measure(back, masked):
-        at = pl.ds(pl.multiple_of((chip - back) * rows, rows), rows)
         to = pl.ds(pl.multiple_of(back * rows, rows), rows)
-        keys = pairs_ref[at, :HEAD]
+        keys = pairs_ref[to, :HEAD]
         allowed = []
         if masked:
             key_pos = (own - 2 * back) * rows + lax.broadcasted_iota(jnp.int32, (rows, rows), 0)
             across = lax.broadcasted_iota(jnp.int32, (rows, rows), 1)
             for slot in range(2):
-                query_pos = bounds_ref[1 + slot] * rows + across
+                query_pos = bounds_ref[slot] * rows + across
                 allowed.append((key_pos <= query_pos) & (key_pos >= starts_ref[slot]))
         for group in range(groups):
             span = slice(group * rows, (group + 1) * rows)
@@ -68,10 +70,9 @@
     top_ref[...] = jnp.broadcast_to(top, top_ref.shape)
 
     def weigh(back, unused):
-        at = pl.ds(pl.multiple_of((chip - back) * rows, rows), rows)
         to = pl.ds(pl.multiple_of(back * rows, rows), rows)
         turned_values = jnp.concatenate(
-            [pairs_ref[at, HEAD:].T, jnp.ones((16, rows), jnp.bfloat16)], axis=0
+            [pairs_ref[to, HEAD:].T, jnp.ones((16, rows), jnp.bfloat16)], axis=0
         )
         for group in range(groups):
             span = slice(group * rows, (group + 1) * rows)
@@ -128,7 +129,7 @@
 
 
 def accumulate(
-    first, stop, chip, pairs_ref, weights_ref, copy, query_ref,
+    first, stop, pairs_ref, weights_ref, copy, query_ref,
     scaled_ref, turned_scaled_ref, delta_ref, total_ref, move_ref, pair_grad_ref, slot,
 ):
     rows = move_ref.shape[0]
@@ -136,7 +137,7 @@
     root = 1.0 / math.sqrt(HEAD)
 
     def visit(back, unused):
-        at = pl.ds(pl.multiple_of((chip - back) * rows, rows), rows)
+        at = pl.ds(pl.multiple_of(back * rows, rows), rows)
         to = pl.ds(pl.multiple_of((back - slot) * rows, rows), rows)
         values = pairs_ref[at, HEAD:]
         turned_keys = pairs_ref[at, :HEAD].T
@@ -178,7 +179,7 @@
     groups = turned_grad_ref.shape[1] // rows
     heads = groups // 2
     copy = fetch(split, kept_ref, weights_ref, kept_sem, rows)
-    fetch_all(split, bounds_ref[4] + 1, copy)
+    fetch_all(split, bounds_ref[3] + 1, copy)
     total_ref[...] = jnp.zeros_like(total_ref)
     for group in range(groups):
         span = slice(group * rows, (group + 1) * rows)
@@ -202,7 +203,7 @@
         turned_scaled_ref[:, span] = low
         scaled_ref[span, :] = low.T
     accumulate(
-        split, bounds_ref[4] + 1, bounds_ref[0], pairs_ref, weights_ref, copy, query_ref,
+        split, bounds_ref[3] + 1, pairs_ref, weights_ref, copy, query_ref,
         scaled_ref, turned_scaled_ref, delta_ref, total_ref, move_ref, pair_grad_ref, split,
     )
     hand_out(pair_grad_ref, block_refs)
@@ -218,12 +219,12 @@
     heads = groups // 2
     root = 1.0 / math.sqrt(HEAD)
     slots = pair_grad_ref.shape[0] // rows
-    stop = jnp.minimum(bounds_ref[4] + 1, slots)
+    stop = jnp.minimum(bounds_ref[3] + 1, slots)
     copy = fetch(0, kept_ref, weights_ref, kept_sem, rows)
     fetch_all(0, stop, copy)
     total_ref[...] = begun_ref[...]
     accumulate(
-        0, stop, bounds_ref[0], pairs_ref, weights_ref, copy, query_ref,
+        0, stop, pairs_ref, weights_ref, copy, query_ref,
         scaled_ref, turned_scaled_ref, delta_ref, total_ref, move_ref, pair_grad_ref, 0,
     )
     hand_out(pair_grad_ref, block_refs)
@@ -258,26 +259,28 @@
     )
 
 
-def attend(bounds, starts, queries, grads, pairs, slots, split, send, swap=swap_cores):
+def attend(bounds, starts, queries, grads, blocks, split, send, swap=swap_cores):
+    slots = len(blocks)
     rows, columns = queries[0].shape
     heads = columns // HEAD
     wide = 2 * heads * rows
     turned = jnp.concatenate([turn(q) for q in queries], axis=1)
     turned_grad = jnp.concatenate([turn(g) for g in grads], axis=1)
     stacked = jnp.concatenate([stack(q) for q in queries], axis=0)
-    pairs, turned, turned_grad, stacked = lax.optimization_barrier(
-        (pairs, turned, turned_grad, stacked)
-    )
-    weights, acc, stats, sent = pl.pallas_call(
+    blocks, turned, turned_grad, stacked = lax.optimization_barrier(
+        (blocks, turned, turned_grad, stacked)
+    )
+    weights, pairs, acc, stats, sent = pl.pallas_call(
         forward_kernel,
         out_shape=(
             pltpu.HBM((slots * rows, wide), jnp.bfloat16),
+            jax.ShapeDtypeStruct((slots * rows, 2 * HEAD), jnp.bfloat16),
             jax.ShapeDtypeStruct((HEAD + EXTRA, wide), jnp.float32),
             jax.ShapeDtypeStruct((8, wide), jnp.float32),
             jax.ShapeDtypeStruct((HEAD + EXTRA, wide), jnp.bfloat16),
         ),
-        in_specs=[smem()] + [vmem()] * 3,
-        out_specs=(hbm(),) + (vmem(),) * 3,
+        in_specs=[smem()] + [vmem()] * (2 + slots),
+        out_specs=(hbm(),) + (vmem(),) * 4,
         scratch_shapes=[
             pltpu.VMEM((slots * rows, wide), jnp.float32),
             pltpu.VMEM((8, wide), jnp.float32),
@@ -287,7 +290,7 @@
         compiler_params=pltpu.CompilerParams(vmem_limit_bytes=36 << 20),
         cost_estimate=cost(slots, rows, wide, 2),
         name="attend_forward",
-    )(bounds, starts, turned, pairs)
+    )(bounds, starts, turned, *blocks)
     weights = pltpu.with_memory_space_constraint(weights, pltpu.HBM)
     arrived = swap(sent)
     half = jax.ShapeDtypeStruct((rows, columns), jnp.bfloat16)
@@ -359,7 +362,7 @@
     edges = starts_of(jnp.stack([2 * chip * rows, (2 * chip + 2) * rows - 1]))
     last = (own - edges[0] // rows) // 2
     clear = jnp.maximum((own - (edges[1] + rows - 1) // rows) // 2, 0)
-    bounds = jnp.stack([chip, own, other, clear, last]).astype(jnp.int32)
+    bounds = jnp.stack([own, other, clear, last]).astype(jnp.int32)
     return bounds, starts[:, None, :]
 
 
@@ -368,17 +371,21 @@
     query = query[0, :, 0, :]
     pairs = keys_values[0, :, 0, :]
     rows = query.shape[0]
-    every_pair = lax.all_gather(pairs, "chip", axis=0, tiled=True)
+    reach = min((LONGEST + 2 * rows - 1) // (2 * rows), chips - 1)
+    slots = reach + 1
+    blocks = [pairs] + [
+        lax.ppermute(pairs, "chip", [(c, c + back) for c in range(chips - back)])
+        for back in range(1, slots)
+    ]
     sections = lax.axis_size("pipe")
     arrived = lax.ppermute(
         incoming_output_grad, "pipe", [(s, (s - 1) % sections) for s in range(sections)]
     )
+    arrived, *blocks[1:3] = lax.optimization_barrier((arrived, *blocks[1:3]))
     grad = lax.all_to_all(arrived, "tensor", split_axis=2, concat_axis=1, tiled=True)[0, :, 0, :]
     bounds, starts = block_bounds(
         doc_lengths[0], lax.axis_index("chip"), lax.axis_index("core"), rows
     )
-    reach = min((LONGEST + 2 * rows - 1) // (2 * rows), chips - 1)
-    slots = reach + 1
     split = (slots + 1) // 2
 
     def send(blocks, first):
@@ -388,7 +395,7 @@
         ]
 
     out, query_grad, query_grad_other, near, far = attend(
-        bounds, starts, (query, swap_cores(query)), (grad, swap_cores(grad)), every_pair, slots,
+        bounds, starts, (query, swap_cores(query)), (grad, swap_cores(grad)), blocks,
         split, functools.partial(send, first=split),
     )
     sums = near[0].astype(jnp.float32)

time: 115 us -> 109 us (0.948)
  the two profiles are of different devices: /device:TPU:198 before, /device:TPU:134 now
where the time goes in v5:
time: 109 us; the launch traced here: 108 us
  starting transfers between devices  44.5 us (41%)
  waiting for transfers between devices  35.9 us (33%)
  Pallas kernels  13.6 us (12%)
  local copies, waits for them, and re-layouts  6.1 us (6%)
  between operations  4.31 us (4%)
  other arithmetic  3.66 us (3%)
    ppermute x6, waiting for transfers between devices, send(): lax.ppermute(block, 'chip', [(c, c - first - at) for c in range(first + a...  21.6 us
    ppermute x6, starting transfers between devices, per_device(): lax.ppermute(pairs, 'chip', [(c, c + back) for c in range(chips - back)])  18.4 us
    all_to_all x1, waiting for transfers between devices, per_device(): lax.all_to_all(arrived, 'tensor', split_axis=2, concat_axis=1, tiled=True)  8.4 us
    ppermute x6, starting transfers between devices, send(): lax.ppermute(block, 'chip', [(c, c - first - at) for c in range(first + a...  8.37 us
    ppermute x4, starting transfers between devices, swap_cores(): return lax.ppermute(value, 'core', [(0, 1), (1, 0)])  7.81 us
    all_to_all x1, starting transfers between devices, per_device(): lax.all_to_all(arrived, 'tensor', split_axis=2, concat_axis=1, tiled=True)  7.11 us
    pallas_call x1, Pallas kernels, attend(): pl.pallas_call(backward_near_kernel, out_shape=(half, half) + (block,) *...  6.31 us
    pallas_call x1, Pallas kernels, attend(): pl.pallas_call(forward_kernel, out_shape=(pltpu.HBM((slots * rows, wide),...  5.16 us
  transfers between devices with their start and end apart: 18, of which 7 were waited for; matrix products, arithmetic and copies ran while one was open for 8% of the time, Pallas kernels for 6%

profile of v5, /device:TPU:134, one launch (start us, length us, event | category | flops | bytes accessed | tf_op | source)
XLA Modules:
  0.0 108.0 jit_solution(18150918018228842584)
XLA Ops:
  1.4 9.8 %collective-permute-start.5 = (bf16[256,256]{1,0:T(8,128)(2,1)}, bf16[256,256]{1,0:T(8,128)(2,1)S(1)}, u32[]{:S(2)}, u32[]{:S(2)}) collective-permute-start(bf16[256,256]{1,0:T(8,128)(2,1)} %bitcast.52), channel_id=1, source_target_pairs={{0,320},{64,384},{128,448},{1,321},{65,385},{129,449},{2,322},{66,... | collective-permute-start | bytes 393224 | tf_op jit(solution)/shard_map/ppermute | solution.py:377
  11.2 1.9 %collective-permute-start.2 = (bf16[256,256]{1,0:T(8,128)(2,1)}, bf16[256,256]{1,0:T(8,128)(2,1)S(1)}, u32[]{:S(2)}, u32[]{:S(2)}) collective-permute-start(bf16[256,256]{1,0:T(8,128)(2,1)} %bitcast.53), channel_id=1, source_target_pairs={{0,128},{64,192},{128,256},{192,320},{256,384},{320,448},{1,129},{... | collective-permute-start | bytes 393224 | tf_op jit(solution)/shard_map/ppermute | solution.py:377
  13.1 1.9 %collective-permute-start.1 = (bf16[256,256]{1,0:T(8,128)(2,1)}, bf16[256,256]{1,0:T(8,128)(2,1)S(1)}, u32[]{:S(2)}, u32[]{:S(2)}) collective-permute-start(bf16[256,256]{1,0:T(8,128)(2,1)} %bitcast.54), channel_id=1, source_target_pairs={{0,64},{64,128},{128,192},{192,256},{256,320},{320,384},{384,448},... | collective-permute-start | bytes 393224 | tf_op jit(solution)/shard_map/ppermute | solution.py:377
  16.1 2.7 %collective-permute-start = (bf16[1,32,8,640]{3,1,0,2:T(8,128)(2,1)S(1)}, bf16[1,32,8,640]{3,1,0,2:T(8,128)(2,1)}, u32[]{:S(2)}, u32[]{:S(2)}) collective-permute-start(bf16[1,32,8,640]{3,1,0,2:T(8,128)(2,1)S(1)} %copy.39), channel_id=1, source_target_pairs={{0,3},{1,0},{2,1},{3,2},{4,7},{5,4},{6,5},{7,6},{8,11},{9,8},{10,9... | collective-permute-start | bytes 983048 | tf_op jit(solution)/shard_map/ppermute | solution.py:381
  21.5 2.7 %collective-permute-start.4 = (bf16[256,256]{1,0:T(8,128)(2,1)S(1)}, bf16[256,256]{1,0:T(8,128)(2,1)S(1)}, u32[]{:S(2)}, u32[]{:S(2)}) collective-permute-start(bf16[256,256]{1,0:T(8,128)(2,1)S(1)} %bitcast.55), channel_id=1, source_target_pairs={{0,256},{64,320},{128,384},{192,448},{1,257},{65,321},{129,385},{1... | collective-permute-start | bytes 393224 | tf_op jit(solution)/shard_map/ppermute | solution.py:377
  24.3 1.3 %collective-permute-start.3 = (bf16[256,256]{1,0:T(8,128)(2,1)S(1)}, bf16[256,256]{1,0:T(8,128)(2,1)S(1)}, u32[]{:S(2)}, u32[]{:S(2)}) collective-permute-start(bf16[256,256]{1,0:T(8,128)(2,1)S(1)} %bitcast.56), channel_id=1, source_target_pairs={{0,192},{64,256},{128,320},{192,384},{256,448},{1,193},{65,257},{1... | collective-permute-start | bytes 393224 | tf_op jit(solution)/shard_map/ppermute | solution.py:377
  25.6 2.9 %collective-permute-done = bf16[1,32,8,640]{3,1,0,2:T(8,128)(2,1)} collective-permute-done((bf16[1,32,8,640]{3,1,0,2:T(8,128)(2,1)S(1)}, bf16[1,32,8,640]{3,1,0,2:T(8,128)(2,1)}, u32[]{:S(2)}, u32[]{:S(2)}) %collective-permute-start) | collective-permute-done | bytes 327712 | tf_op jit(solution)/shard_map/ppermute | solution.py:381
  28.5 1.9 %collective-permute-start.7 = (bf16[256,640]{0,1:T(8,128)(2,1)S(1)}, bf16[256,640]{0,1:T(8,128)(2,1)S(1)}, u32[]{:S(2)}, u32[]{:S(2)}) collective-permute-start(bf16[256,640]{0,1:T(8,128)(2,1)S(1)} %bitcast.58), channel_id=1, source_target_pairs={{0,32},{32,0},{1,33},{33,1},{2,34},{34,2},{3,35},{35,3},{4,36},{36... | collective-permute-start | bytes 983048 | tf_op jit(solution)/shard_map/ppermute | solution.py:251
  30.4 7.1 %all-to-all-start = ((bf16[1,32,8,640]{3,1,0,2:T(8,128)(2,1)}), bf16[1,32,8,640]{3,1,0,2:T(8,128)(2,1)S(1)}, u32[]{:S(2)}, u32[]{:S(2)}) async-start(bf16[1,32,8,640]{3,1,0,2:T(8,128)(2,1)} %collective-permute-done), calls=%async_computation | async-start | bytes 655360 | tf_op jit(solution)/shard_map/all_to_all | solution.py:385
  43.0 8.4 %all-to-all-done = bf16[1,32,8,640]{3,1,0,2:T(8,128)(2,1)S(1)} async-done(((bf16[1,32,8,640]{3,1,0,2:T(8,128)(2,1)}), bf16[1,32,8,640]{3,1,0,2:T(8,128)(2,1)S(1)}, u32[]{:S(2)}, u32[]{:S(2)}) %all-to-all-start) | async-done | bytes 327712 | tf_op jit(solution)/shard_map/all_to_all | solution.py:385
  51.4 1.9 %collective-permute-start.8 = (bf16[256,640]{1,0:T(8,128)(2,1)S(1)}, bf16[256,640]{1,0:T(8,128)(2,1)}, u32[]{:S(2)}, u32[]{:S(2)}) collective-permute-start(bf16[256,640]{1,0:T(8,128)(2,1)S(1)} %bitcast.64), channel_id=1, source_target_pairs={{0,32},{32,0},{1,33},{33,1},{2,34},{34,2},{3,35},{35,3},{4,36},{36... | collective-permute-start | bytes 983048 | tf_op jit(solution)/shard_map/ppermute | solution.py:251
  56.8 5.2 %attend_forward.1 = (bf16[1792,2560]{1,0:T(8,128)(2,1)}, bf16[1792,256]{1,0:T(8,128)(2,1)S(1)}, f32[144,2560]{1,0:T(8,128)S(1)}, f32[8,2560]{1,0:T(8,128)S(1)}, bf16[144,2560]{1,0:T(8,128)(2,1)S(1)}) custom-call(s32[4]{0:T(128)S(1)} %pad_add_fusion.2.bounds_ref, s32[2,1,256]{2,1,0:T(1,128)S(1)} %broadcast_in_dim.47.starts_ref, ...), custom_call_target="tpu_custom_call" | custom-call | flops 2348810240 | bytes 9175040 | tf_op jit(solution)/shard_map/attend_forward/pallas_call | solution.py:273
  61.9 2.0 %collective-permute-start.9 = (bf16[144,2560]{1,0:T(8,128)(2,1)S(1)}, bf16[144,2560]{1,0:T(8,128)(2,1)S(1)}, u32[]{:S(2)}, u32[]{:S(2)}) collective-permute-start(bf16[144,2560]{1,0:T(8,128)(2,1)S(1)} %get-tuple-element.47), channel_id=1, source_target_pairs={{0,32},{32,0},{1,33},{33,1},{2,34},{34,2},{3,35},{35,3},{4,36},{36... | collective-permute-start | bytes 2211848 | tf_op jit(solution)/shard_map/ppermute | solution.py:251
  64.0 2.1 %collective-permute-done.9.arrived_ref = bf16[144,2560]{1,0:T(8,128)(2,1)S(1)} collective-permute-done((bf16[144,2560]{1,0:T(8,128)(2,1)S(1)}, bf16[144,2560]{1,0:T(8,128)(2,1)S(1)}, u32[]{:S(2)}, u32[]{:S(2)}) %collective-permute-start.9) | collective-permute-done | bytes 737312 | tf_op jit(solution)/shard_map/ppermute | solution.py:251
  66.0 2.1 %attend_backward_far.1 = (bf16[256,640]{1,0:T(8,128)(2,1)}, bf16[2560,128]{1,0:T(8,128)(2,1)S(1)}, bf16[128,2560]{1,0:T(8,128)(2,1)S(1)}, f32[1,2560]{1,0:T(1,12...) custom-call(s32[4]{0:T(128)S(1)} %pad_add_fusion.2.bounds_ref, ...), custom_call_target="tpu_custom_call" | custom-call | flops 2013265920 | bytes 3932160 | tf_op jit(solution)/shard_map/attend_backward_far/pallas_call | solution.py:308
  68.2 1.3 %collective-permute-start.11 = (bf16[256,256]{1,0:T(8,128)(2,1)S(1)}, bf16[256,256]{1,0:T(8,128)(2,1)S(1)}, u32[]{:S(2)}, u32[]{:S(2)}) collective-permute-start(bf16[256,256]{1,0:T(8,128)(2,1)S(1)} %get-tuple-element.61), channel_id=1, source_target_pairs={{256,0},{320,64},{384,128},{448,192},{257,1},{321,65},{385,129},{4... | collective-permute-start | bytes 393224 | tf_op jit(solution)/shard_map/ppermute | solution.py:393
  69.5 1.3 %collective-permute-start.12 = (bf16[256,256]{1,0:T(8,128)(2,1)S(1)}, bf16[256,256]{1,0:T(8,128)(2,1)S(1)}, u32[]{:S(2)}, u32[]{:S(2)}) collective-permute-start(bf16[256,256]{1,0:T(8,128)(2,1)S(1)} %get-tuple-element.62), channel_id=1, source_target_pairs={{320,0},{384,64},{448,128},{321,1},{385,65},{449,129},{322,2},{386... | collective-permute-start | bytes 393224 | tf_op jit(solution)/shard_map/ppermute | solution.py:393
  71.4 6.3 %attend_backward_near.1 = (bf16[256,640]{1,0:T(8,128)(2,1)S(1)}, bf16[256,640]{1,0:T(8,128)(2,1)S(1)}, bf16[256,256]{1,0:T(8,128)(2,1)S(1)}, bf16[256,256]{1,0:T...) custom-call(s32[4]{0:T(128)S(1)} %pad_add_fusion.2.bounds_ref, ...), custom_call_target="tpu_custom_call" | custom-call | flops 2684354560 | bytes 5242880 | tf_op jit(solution)/shard_map/attend_backward_near/pallas_call | solution.py:326
  77.8 1.9 %collective-permute-start.14 = (bf16[256,256]{1,0:T(8,128)(2,1)S(1)}, bf16[256,256]{1,0:T(8,128)(2,1)S(1)}, u32[]{:S(2)}, u32[]{:S(2)}) collective-permute-start(bf16[256,256]{1,0:T(8,128)(2,1)S(1)} %get-tuple-element.64), channel_id=1, source_target_pairs={{64,0},{128,64},{192,128},{256,192},{320,256},{384,320},{448,384},... | collective-permute-start | bytes 393224 | tf_op jit(solution)/shard_map/ppermute | solution.py:393
  79.7 1.9 %collective-permute-start.15 = (bf16[256,256]{1,0:T(8,128)(2,1)S(1)}, bf16[256,256]{1,0:T(8,128)(2,1)S(1)}, u32[]{:S(2)}, u32[]{:S(2)}) collective-permute-start(bf16[256,256]{1,0:T(8,128)(2,1)S(1)} %get-tuple-element.65), channel_id=1, source_target_pairs={{128,0},{192,64},{256,128},{320,192},{384,256},{448,320},{129,1},{... | collective-permute-start | bytes 393224 | tf_op jit(solution)/shard_map/ppermute | solution.py:393
  81.6 4.4 %collective-permute-done.11 = bf16[256,256]{1,0:T(8,128)(2,1)S(1)} collective-permute-done((bf16[256,256]{1,0:T(8,128)(2,1)S(1)}, bf16[256,256]{1,0:T(8,128)(2,1)S(1)}, u32[]{:S(2)}, u32[]{:S(2)}) %collective-permute-start.11) | collective-permute-done | bytes 131104 | tf_op jit(solution)/shard_map/ppermute | solution.py:393
  87.3 6.3 %collective-permute-done.12 = bf16[256,256]{1,0:T(8,128)(2,1)S(1)} collective-permute-done((bf16[256,256]{1,0:T(8,128)(2,1)S(1)}, bf16[256,256]{1,0:T(8,128)(2,1)S(1)}, u32[]{:S(2)}, u32[]{:S(2)}) %collective-permute-start.12) | collective-permute-done | bytes 131104 | tf_op jit(solution)/shard_map/ppermute | solution.py:393
  93.6 1.9 %collective-permute-start.10 = (bf16[256,640]{1,0:T(8,128)(2,1)S(1)}, bf16[256,640]{1,0:T(8,128)(2,1)S(1)}, u32[]{:S(2)}, u32[]{:S(2)}) collective-permute-start(bf16[256,640]{1,0:T(8,128)(2,1)S(1)} %get-tuple-element.59), channel_id=1, source_target_pairs={{0,32},{32,0},{1,33},{33,1},{2,34},{34,2},{3,35},{35,3},{4,36},{36... | collective-permute-start | bytes 983048 | tf_op jit(solution)/shard_map/ppermute | solution.py:251
  95.6 10.9 %collective-permute-done.16 = bf16[256,256]{1,0:T(8,128)(2,1)S(1)} collective-permute-done((bf16[256,256]{1,0:T(8,128)(2,1)S(1)}, bf16[256,256]{1,0:T(8,128)(2,1)S(1)}, u32[]{:S(2)}, u32[]{:S(2)}) %collective-permute-start.16) | collective-permute-done | bytes 131104 | tf_op jit(solution)/shard_map/ppermute | solution.py:393
  (46 shorter events, 13.6 us)
Async XLA Ops:
  0.6 20.9 %copy-start = (bf16[1,256,1,256]{3,1,2,0:T(8,128)(2,1)S(1)}, bf16[1,256,1,256]{3,1,2,0:T(8,128)(2,1)}, u32[]{:S(2)}) copy-start(bf16[1,256,1,256]{3,1,2,0:T(8,128)(2,1)} %param.5) | copy-start | bytes 393220
  0.6 56.1 %collective-permute-start.6 = (bf16[256,256]{1,0:T(8,128)(2,1)}, bf16[256,256]{1,0:T(8,128)(2,1)S(1)}, u32[]{:S(2)}, u32[]{:S(2)}) collective-permute-start(bf16[256,256]{1,0:T(8,128)(2,1)} %bitcast.51), channel_id=1, source_target_pairs={{0,384},{64,448},{1,385},{65,449},{2,386},{66,450},{3,387},{67,451... | collective-permute-start | bytes 393224 | tf_op jit(solution)/shard_map/ppermute | solution.py:377
  1.4 55.3 %collective-permute-start.5 = (bf16[256,256]{1,0:T(8,128)(2,1)}, bf16[256,256]{1,0:T(8,128)(2,1)S(1)}, u32[]{:S(2)}, u32[]{:S(2)}) collective-permute-start(bf16[256,256]{1,0:T(8,128)(2,1)} %bitcast.52), channel_id=1, source_target_pairs={{0,320},{64,384},{128,448},{1,321},{65,385},{129,449},{2,322},{66,... | collective-permute-start | bytes 393224 | tf_op jit(solution)/shard_map/ppermute | solution.py:377
  11.2 10.3 %collective-permute-start.2 = (bf16[256,256]{1,0:T(8,128)(2,1)}, bf16[256,256]{1,0:T(8,128)(2,1)S(1)}, u32[]{:S(2)}, u32[]{:S(2)}) collective-permute-start(bf16[256,256]{1,0:T(8,128)(2,1)} %bitcast.53), channel_id=1, source_target_pairs={{0,128},{64,192},{128,256},{192,320},{256,384},{320,448},{1,129},{... | collective-permute-start | bytes 393224 | tf_op jit(solution)/shard_map/ppermute | solution.py:377
  13.1 11.1 %collective-permute-start.1 = (bf16[256,256]{1,0:T(8,128)(2,1)}, bf16[256,256]{1,0:T(8,128)(2,1)S(1)}, u32[]{:S(2)}, u32[]{:S(2)}) collective-permute-start(bf16[256,256]{1,0:T(8,128)(2,1)} %bitcast.54), channel_id=1, source_target_pairs={{0,64},{64,128},{128,192},{192,256},{256,320},{320,384},{384,448},... | collective-permute-start | bytes 393224 | tf_op jit(solution)/shard_map/ppermute | solution.py:377
  16.1 12.4 %collective-permute-start = (bf16[1,32,8,640]{3,1,0,2:T(8,128)(2,1)S(1)}, bf16[1,32,8,640]{3,1,0,2:T(8,128)(2,1)}, u32[]{:S(2)}, u32[]{:S(2)}) collective-permute-start(bf16[1,32,8,640]{3,1,0,2:T(8,128)(2,1)S(1)} %copy.39), channel_id=1, source_target_pairs={{0,3},{1,0},{2,1},{3,2},{4,7},{5,4},{6,5},{7,6},{8,11},{9,8},{10,9... | collective-permute-start | bytes 983048 | tf_op jit(solution)/shard_map/ppermute | solution.py:381
  21.5 35.2 %collective-permute-start.4 = (bf16[256,256]{1,0:T(8,128)(2,1)S(1)}, bf16[256,256]{1,0:T(8,128)(2,1)S(1)}, u32[]{:S(2)}, u32[]{:S(2)}) collective-permute-start(bf16[256,256]{1,0:T(8,128)(2,1)S(1)} %bitcast.55), channel_id=1, source_target_pairs={{0,256},{64,320},{128,384},{192,448},{1,257},{65,321},{129,385},{1... | collective-permute-start | bytes 393224 | tf_op jit(solution)/shard_map/ppermute | solution.py:377
  24.3 32.5 %collective-permute-start.3 = (bf16[256,256]{1,0:T(8,128)(2,1)S(1)}, bf16[256,256]{1,0:T(8,128)(2,1)S(1)}, u32[]{:S(2)}, u32[]{:S(2)}) collective-permute-start(bf16[256,256]{1,0:T(8,128)(2,1)S(1)} %bitcast.56), channel_id=1, source_target_pairs={{0,192},{64,256},{128,320},{192,384},{256,448},{1,193},{65,257},{1... | collective-permute-start | bytes 393224 | tf_op jit(solution)/shard_map/ppermute | solution.py:377
  28.5 14.0 %collective-permute-start.7 = (bf16[256,640]{0,1:T(8,128)(2,1)S(1)}, bf16[256,640]{0,1:T(8,128)(2,1)S(1)}, u32[]{:S(2)}, u32[]{:S(2)}) collective-permute-start(bf16[256,640]{0,1:T(8,128)(2,1)S(1)} %bitcast.58), channel_id=1, source_target_pairs={{0,32},{32,0},{1,33},{33,1},{2,34},{34,2},{3,35},{35,3},{4,36},{36... | collective-permute-start | bytes 983048 | tf_op jit(solution)/shard_map/ppermute | solution.py:251
  30.4 21.1 %all-to-all-start = ((bf16[1,32,8,640]{3,1,0,2:T(8,128)(2,1)}), bf16[1,32,8,640]{3,1,0,2:T(8,128)(2,1)S(1)}, u32[]{:S(2)}, u32[]{:S(2)}) async-start(bf16[1,32,8,640]{3,1,0,2:T(8,128)(2,1)} %collective-permute-done), calls=%async_computation | async-start | bytes 655360 | tf_op jit(solution)/shard_map/all_to_all | solution.py:385
  51.4 3.6 %collective-permute-start.8 = (bf16[256,640]{1,0:T(8,128)(2,1)S(1)}, bf16[256,640]{1,0:T(8,128)(2,1)}, u32[]{:S(2)}, u32[]{:S(2)}) collective-permute-start(bf16[256,640]{1,0:T(8,128)(2,1)S(1)} %bitcast.64), channel_id=1, source_target_pairs={{0,32},{32,0},{1,33},{33,1},{2,34},{34,2},{3,35},{35,3},{4,36},{36... | collective-permute-start | bytes 983048 | tf_op jit(solution)/shard_map/ppermute | solution.py:251
  61.9 4.1 %collective-permute-start.9 = (bf16[144,2560]{1,0:T(8,128)(2,1)S(1)}, bf16[144,2560]{1,0:T(8,128)(2,1)S(1)}, u32[]{:S(2)}, u32[]{:S(2)}) collective-permute-start(bf16[144,2560]{1,0:T(8,128)(2,1)S(1)} %get-tuple-element.47), channel_id=1, source_target_pairs={{0,32},{32,0},{1,33},{33,1},{2,34},{34,2},{3,35},{35,3},{4,36},{36... | collective-permute-start | bytes 2211848 | tf_op jit(solution)/shard_map/ppermute | solution.py:251
  68.2 17.9 %collective-permute-start.11 = (bf16[256,256]{1,0:T(8,128)(2,1)S(1)}, bf16[256,256]{1,0:T(8,128)(2,1)S(1)}, u32[]{:S(2)}, u32[]{:S(2)}) collective-permute-start(bf16[256,256]{1,0:T(8,128)(2,1)S(1)} %get-tuple-element.61), channel_id=1, source_target_pairs={{256,0},{320,64},{384,128},{448,192},{257,1},{321,65},{385,129},{4... | collective-permute-start | bytes 393224 | tf_op jit(solution)/shard_map/ppermute | solution.py:393
  69.5 24.2 %collective-permute-start.12 = (bf16[256,256]{1,0:T(8,128)(2,1)S(1)}, bf16[256,256]{1,0:T(8,128)(2,1)S(1)}, u32[]{:S(2)}, u32[]{:S(2)}) collective-permute-start(bf16[256,256]{1,0:T(8,128)(2,1)S(1)} %get-tuple-element.62), channel_id=1, source_target_pairs={{320,0},{384,64},{448,128},{321,1},{385,65},{449,129},{322,2},{386... | collective-permute-start | bytes 393224 | tf_op jit(solution)/shard_map/ppermute | solution.py:393
  70.8 24.8 %collective-permute-start.13 = (bf16[256,256]{1,0:T(8,128)(2,1)S(1)}, bf16[256,256]{1,0:T(8,128)(2,1)S(1)}, u32[]{:S(2)}, u32[]{:S(2)}) collective-permute-start(bf16[256,256]{1,0:T(8,128)(2,1)S(1)} %get-tuple-element.63), channel_id=1, source_target_pairs={{384,0},{448,64},{385,1},{449,65},{386,2},{450,66},{387,3},{451,67... | collective-permute-start | bytes 393224 | tf_op jit(solution)/shard_map/ppermute | solution.py:393
  77.8 17.9 %collective-permute-start.14 = (bf16[256,256]{1,0:T(8,128)(2,1)S(1)}, bf16[256,256]{1,0:T(8,128)(2,1)S(1)}, u32[]{:S(2)}, u32[]{:S(2)}) collective-permute-start(bf16[256,256]{1,0:T(8,128)(2,1)S(1)} %get-tuple-element.64), channel_id=1, source_target_pairs={{64,0},{128,64},{192,128},{256,192},{320,256},{384,320},{448,384},... | collective-permute-start | bytes 393224 | tf_op jit(solution)/shard_map/ppermute | solution.py:393
  79.7 16.0 %collective-permute-start.15 = (bf16[256,256]{1,0:T(8,128)(2,1)S(1)}, bf16[256,256]{1,0:T(8,128)(2,1)S(1)}, u32[]{:S(2)}, u32[]{:S(2)}) collective-permute-start(bf16[256,256]{1,0:T(8,128)(2,1)S(1)} %get-tuple-element.65), channel_id=1, source_target_pairs={{128,0},{192,64},{256,128},{320,192},{384,256},{448,320},{129,1},{... | collective-permute-start | bytes 393224 | tf_op jit(solution)/shard_map/ppermute | solution.py:393
  86.0 20.5 %collective-permute-start.16 = (bf16[256,256]{1,0:T(8,128)(2,1)S(1)}, bf16[256,256]{1,0:T(8,128)(2,1)S(1)}, u32[]{:S(2)}, u32[]{:S(2)}) collective-permute-start(bf16[256,256]{1,0:T(8,128)(2,1)S(1)} %get-tuple-element.66), channel_id=1, source_target_pairs={{192,0},{256,64},{320,128},{384,192},{448,256},{193,1},{257,65},{3... | collective-permute-start | bytes 393224 | tf_op jit(solution)/shard_map/ppermute | solution.py:393
  93.6 13.6 %collective-permute-start.10 = (bf16[256,640]{1,0:T(8,128)(2,1)S(1)}, bf16[256,640]{1,0:T(8,128)(2,1)S(1)}, u32[]{:S(2)}, u32[]{:S(2)}) collective-permute-start(bf16[256,640]{1,0:T(8,128)(2,1)S(1)} %get-tuple-element.59), channel_id=1, source_target_pairs={{0,32},{32,0},{1,33},{33,1},{2,34},{34,2},{3,35},{35,3},{4,36},{36... | collective-permute-start | bytes 983048 | tf_op jit(solution)/shard_map/ppermute | solution.py:251

commit v6 on v5

--- a/solution.py
+++ b/solution.py
@@ -26,20 +26,29 @@
 def forward_kernel(
     bounds_ref, starts_ref, turned_ref, *rest,
 ):
-    *block_refs, kept_ref, pairs_ref, acc_ref, stats_ref, sent_ref = rest[:-4]
-    scores_ref, top_ref, weights_ref, kept_sem = rest[-4:]
+    *block_refs, kept_ref, pairs_ref, acc_ref, stats_ref, sent_ref = rest[:-5]
+    scores_ref, top_ref, weights_ref, kept_sem, block_sem = rest[-5:]
     rows = starts_ref.shape[2]
     groups = turned_ref.shape[1] // rows
     heads = groups // 2
     scale = LOG2E / math.sqrt(HEAD)
     own, clear, last = bounds_ref[0], bounds_ref[2], bounds_ref[3]
+
+    def bring(block_ref, back):
+        to = pl.ds(pl.multiple_of(back * rows, rows), rows)
+        return pltpu.make_async_copy(block_ref, pairs_ref.at[to], block_sem.at[back])
+
     for back, block_ref in enumerate(block_refs):
-        pairs_ref[back * rows : (back + 1) * rows, :] = block_ref[...]
+        @pl.when(back <= last)
+        def start():
+            bring(block_ref, back).start()
+
     top_ref[...] = jnp.full_like(top_ref, NEG_LARGE)
     acc_ref[...] = jnp.zeros_like(acc_ref)
 
     def measure(back, masked):
         to = pl.ds(pl.multiple_of(back * rows, rows), rows)
+        bring(block_refs[0], back).wait()
         keys = pairs_ref[to, :HEAD]
         allowed = []
         if masked:
@@ -171,13 +180,14 @@
 
 
 def backward_far_kernel(
-    bounds_ref, stats_ref, arrived_ref, acc_ref, turned_grad_ref, query_ref, pairs_ref, kept_ref,
+    bounds_ref, stats_ref, arrived_ref, acc_ref, grad_ref, grad_other_ref, query_ref, pairs_ref,
+    kept_ref,
     out_ref, scaled_ref, turned_scaled_ref, delta_ref, total_ref, *rest, split,
 ):
     *block_refs, move_ref, pair_grad_ref, weights_ref, kept_sem = rest
     rows = out_ref.shape[0]
-    groups = turned_grad_ref.shape[1] // rows
-    heads = groups // 2
+    heads = grad_ref.shape[1] // HEAD
+    groups = 2 * heads
     copy = fetch(split, kept_ref, weights_ref, kept_sem, rows)
     fetch_all(split, bounds_ref[3] + 1, copy)
     total_ref[...] = jnp.zeros_like(total_ref)
@@ -195,9 +205,11 @@
             :HEAD, theirs
         ].astype(jnp.float32) * jnp.exp2(other_log - log_totals)
         result = result.astype(jnp.bfloat16)
+        column = slice(group % heads * HEAD, (group % heads + 1) * HEAD)
         if group < heads:
-            out_ref[:, group * HEAD : (group + 1) * HEAD] = result.T
-        scaled = turned_grad_ref[:, span].astype(jnp.float32) * jnp.exp2(own_top - log_totals)
+            out_ref[:, column] = result.T
+        grads = (grad_ref if group < heads else grad_other_ref)[:, column].T
+        scaled = grads.astype(jnp.float32) * jnp.exp2(own_top - log_totals)
         delta_ref[:, span] = jnp.sum(result.astype(jnp.float32) * scaled, axis=0, keepdims=True)
         low = scaled.astype(jnp.bfloat16)
         turned_scaled_ref[:, span] = low
@@ -259,17 +271,15 @@
     )
 
 
-def attend(bounds, starts, queries, grads, blocks, split, send, swap=swap_cores):
+def attend(bounds, starts, queries, grad, blocks, split, send, swap=swap_cores):
     slots = len(blocks)
     rows, columns = queries[0].shape
     heads = columns // HEAD
     wide = 2 * heads * rows
     turned = jnp.concatenate([turn(q) for q in queries], axis=1)
-    turned_grad = jnp.concatenate([turn(g) for g in grads], axis=1)
     stacked = jnp.concatenate([stack(q) for q in queries], axis=0)
-    blocks, turned, turned_grad, stacked = lax.optimization_barrier(
-        (blocks, turned, turned_grad, stacked)
-    )
+    blocks, turned, stacked = lax.optimization_barrier((blocks, turned, stacked))
+    blocks = [pltpu.with_memory_space_constraint(block, pltpu.HBM) for block in blocks]
     weights, pairs, acc, stats, sent = pl.pallas_call(
         forward_kernel,
         out_shape=(
@@ -279,12 +289,13 @@
             jax.ShapeDtypeStruct((8, wide), jnp.float32),
             jax.ShapeDtypeStruct((HEAD + EXTRA, wide), jnp.bfloat16),
         ),
-        in_specs=[smem()] + [vmem()] * (2 + slots),
+        in_specs=[smem()] + [vmem()] * 2 + [hbm()] * slots,
         out_specs=(hbm(),) + (vmem(),) * 4,
         scratch_shapes=[
             pltpu.VMEM((slots * rows, wide), jnp.float32),
             pltpu.VMEM((8, wide), jnp.float32),
             pltpu.VMEM((slots * rows, wide), jnp.bfloat16),
+            pltpu.SemaphoreType.DMA((slots,)),
             pltpu.SemaphoreType.DMA((slots,)),
         ],
         compiler_params=pltpu.CompilerParams(vmem_limit_bytes=36 << 20),
@@ -293,6 +304,8 @@
     )(bounds, starts, turned, *blocks)
     weights = pltpu.with_memory_space_constraint(weights, pltpu.HBM)
     arrived = swap(sent)
+    grad, stats = lax.optimization_barrier((grad, stats))
+    grad_other = swap(grad)
     half = jax.ShapeDtypeStruct((rows, columns), jnp.bfloat16)
     params = pltpu.CompilerParams(vmem_limit_bytes=20 << 20)
     move = pltpu.VMEM((rows, wide), jnp.bfloat16)
@@ -315,13 +328,13 @@
             jax.ShapeDtypeStruct((HEAD, wide), jnp.float32),
         )
         + (block,) * (slots - split),
-        in_specs=[smem()] + [vmem()] * 6 + [hbm()],
+        in_specs=[smem()] + [vmem()] * 7 + [hbm()],
         out_specs=(vmem(),) * (5 + slots - split),
         scratch_shapes=[move] + held(slots - split),
         compiler_params=params,
         cost_estimate=cost(slots - split, rows, wide, 4),
         name="attend_backward_far",
-    )(bounds, stats, arrived, acc, turned_grad, stacked, pairs, weights)
+    )(bounds, stats, arrived, acc, grad, grad_other, stacked, pairs, weights)
     sent_far = send(far)
     query_grad, query_grad_other, *near = pl.pallas_call(
         backward_near_kernel,
@@ -395,7 +408,7 @@
         ]
 
     out, query_grad, query_grad_other, near, far = attend(
-        bounds, starts, (query, swap_cores(query)), (grad, swap_cores(grad)), blocks,
+        bounds, starts, (query, swap_cores(query)), grad, blocks,
         split, functools.partial(send, first=split),
     )
     sums = near[0].astype(jnp.float32)

time: 109 us -> 105 us (0.963)
  the two profiles are of different devices: /device:TPU:134 before, /device:TPU:129 now
where the time goes in v6:
time: 105 us; the launch traced here: 104 us
  starting transfers between devices  52.8 us (50%)
  waiting for transfers between devices  23.6 us (22%)
  Pallas kernels  16 us (15%)
  local copies, waits for them, and re-layouts  5.29 us (5%)
  between operations  4.35 us (4%)
  other arithmetic  2.31 us (2%)
    ppermute x6, waiting for transfers between devices, send(): lax.ppermute(block, 'chip', [(c, c - first - at) for c in range(first + a...  19.6 us
    ppermute x6, starting transfers between devices, per_device(): lax.ppermute(pairs, 'chip', [(c, c + back) for c in range(chips - back)])  18.1 us
    ppermute x4, starting transfers between devices, swap_cores(): return lax.ppermute(value, 'core', [(0, 1), (1, 0)])  14.5 us
    ppermute x6, starting transfers between devices, send(): lax.ppermute(block, 'chip', [(c, c - first - at) for c in range(first + a...  8.75 us
    all_to_all x1, starting transfers between devices, per_device(): lax.all_to_all(arrived, 'tensor', split_axis=2, concat_axis=1, tiled=True)  6.82 us
    pallas_call x1, Pallas kernels, attend(): pl.pallas_call(forward_kernel, out_shape=(pltpu.HBM((slots * rows, wide),...  6.81 us
    pallas_call x1, Pallas kernels, attend(): pl.pallas_call(backward_near_kernel, out_shape=(half, half) + (block,) *...  6.37 us
    ppermute x1, starting transfers between devices, per_device(): lax.ppermute(incoming_output_grad, 'pipe', [(s, (s - 1) % sections) for s...  4.52 us
  transfers between devices with their start and end apart: 18, of which 5 were waited for; matrix products, arithmetic and copies ran while one was open for 5% of the time, Pallas kernels for 13%

profile of v6, /device:TPU:129, one launch (start us, length us, event | category | flops | bytes accessed | tf_op | source)
XLA Modules:
  0.0 104.4 jit_solution(12835366251833528592)
XLA Ops:
  1.3 7.0 %collective-permute-start.2 = (bf16[256,256]{1,0:T(8,128)(2,1)}, bf16[256,256]{1,0:T(8,128)(2,1)S(1)}, u32[]{:S(2)}, u32[]{:S(2)}) collective-permute-start(bf16[256,256]{1,0:T(8,128)(2,1)} %bitcast.56), channel_id=1, source_target_pairs={{0,128},{64,192},{128,256},{192,320},{256,384},{320,448},{1,129},{... | collective-permute-start | bytes 393224 | tf_op jit(solution)/shard_map/ppermute | solution.py:390
  8.3 3.1 %collective-permute-start.1 = (bf16[256,256]{1,0:T(8,128)(2,1)}, bf16[256,256]{1,0:T(8,128)(2,1)S(1)}, u32[]{:S(2)}, u32[]{:S(2)}) collective-permute-start(bf16[256,256]{1,0:T(8,128)(2,1)} %bitcast.57), channel_id=1, source_target_pairs={{0,64},{64,128},{128,192},{192,256},{256,320},{320,384},{384,448},... | collective-permute-start | bytes 393224 | tf_op jit(solution)/shard_map/ppermute | solution.py:390
  12.5 4.5 %collective-permute-start = (bf16[1,32,8,640]{3,1,0,2:T(8,128)(2,1)S(1)}, bf16[1,32,8,640]{3,1,0,2:T(8,128)(2,1)}, u32[]{:S(2)}, u32[]{:S(2)}) collective-permute-start(bf16[1,32,8,640]{3,1,0,2:T(8,128)(2,1)S(1)} %copy.30), channel_id=1, source_target_pairs={{0,3},{1,0},{2,1},{3,2},{4,7},{5,4},{6,5},{7,6},{8,11},{9,8},{10,9... | collective-permute-start | bytes 983048 | tf_op jit(solution)/shard_map/ppermute | solution.py:394
  17.0 1.1 %copy.31 = bf16[1,256,1,640]{1,3,2,0:T(8,128)(2,1)S(1)} copy(bf16[1,256,1,640]{3,1,2,0:T(8,128)(2,1)} %param.4) | data formatting | bytes 655360 | tf_op args[0]
  18.2 3.4 %collective-permute-start.7 = (bf16[256,640]{0,1:T(8,128)(2,1)S(1)}, bf16[256,640]{0,1:T(8,128)(2,1)S(1)}, u32[]{:S(2)}, u32[]{:S(2)}) collective-permute-start(bf16[256,640]{0,1:T(8,128)(2,1)S(1)} %bitcast.43), channel_id=1, source_target_pairs={{0,32},{32,0},{1,33},{33,1},{2,34},{34,2},{3,35},{35,3},{4,36},{36... | collective-permute-start | bytes 983048 | tf_op jit(solution)/shard_map/ppermute | solution.py:263
  26.8 1.4 %collective-permute-start.5 = (bf16[256,256]{1,0:T(8,128)(2,1)S(1)}, bf16[256,256]{1,0:T(8,128)(2,1)S(1)}, u32[]{:S(2)}, u32[]{:S(2)}) collective-permute-start(bf16[256,256]{1,0:T(8,128)(2,1)S(1)} %bitcast.59), channel_id=1, source_target_pairs={{0,320},{64,384},{128,448},{1,321},{65,385},{129,449},{2,322},{66,... | collective-permute-start | bytes 393224 | tf_op jit(solution)/shard_map/ppermute | solution.py:390
  28.2 3.4 %collective-permute-start.4 = (bf16[256,256]{1,0:T(8,128)(2,1)S(1)}, bf16[256,256]{1,0:T(8,128)(2,1)S(1)}, u32[]{:S(2)}, u32[]{:S(2)}) collective-permute-start(bf16[256,256]{1,0:T(8,128)(2,1)S(1)} %bitcast.60), channel_id=1, source_target_pairs={{0,256},{64,320},{128,384},{192,448},{1,257},{65,321},{129,385},{1... | collective-permute-start | bytes 393224 | tf_op jit(solution)/shard_map/ppermute | solution.py:390
  31.6 2.6 %collective-permute-start.3 = (bf16[256,256]{1,0:T(8,128)(2,1)S(1)}, bf16[256,256]{1,0:T(8,128)(2,1)}, u32[]{:S(2)}, u32[]{:S(2)}) collective-permute-start(bf16[256,256]{1,0:T(8,128)(2,1)S(1)} %bitcast.61), channel_id=1, source_target_pairs={{0,192},{64,256},{128,320},{192,384},{256,448},{1,193},{65,257},{1... | collective-permute-start | bytes 393224 | tf_op jit(solution)/shard_map/ppermute | solution.py:390
  34.2 6.8 %all-to-all-start = ((bf16[1,32,8,640]{3,1,0,2:T(8,128)(2,1)}), bf16[1,32,8,640]{3,1,0,2:T(8,128)(2,1)S(1)}, u32[]{:S(2)}, u32[]{:S(2)}) async-start(bf16[1,32,8,640]{3,1,0,2:T(8,128)(2,1)} %collective-permute-done), calls=%async_computation | async-start | bytes 655360 | tf_op jit(solution)/shard_map/all_to_all | solution.py:398
  43.1 2.6 %collective-permute-done.3.rest_3_ = bf16[256,256]{1,0:T(8,128)(2,1)} collective-permute-done((bf16[256,256]{1,0:T(8,128)(2,1)S(1)}, bf16[256,256]{1,0:T(8,128)(2,1)}, u32[]{:S(2)}, u32[]{:S(2)}) %collective-permute-start.3) | collective-permute-done | bytes 131104 | tf_op jit(solution)/shard_map/ppermute | solution.py:390
  45.8 6.8 %attend_forward.1 = (bf16[1792,2560]{1,0:T(8,128)(2,1)}, bf16[1792,256]{1,0:T(8,128)(2,1)S(1)}, f32[144,2560]{1,0:T(8,128)S(1)}, f32[8,2560]{1,0:T(8,128)S(1)}, bf16[144,2560]{1,0:T(8,128)(2,1)}) custom-call(s32[4]{0:T(128)S(1)} %pad_add_fusion.2.bounds_ref, s32[2,1,256]{2,1,0:T(1,128)S(1)} %broadcast_in_dim.47.starts_ref, ...), custom_call_target="tpu_custom_call" | custom-call | flops 2348810240 | bytes 9175040 | tf_op jit(solution)/shard_map/attend_forward/pallas_call | solution.py:283
  52.6 1.9 %collective-permute-start.8 = (bf16[144,2560]{1,0:T(8,128)(2,1)}, bf16[144,2560]{1,0:T(8,128)(2,1)}, u32[]{:S(2)}, u32[]{:S(2)}) collective-permute-start(bf16[144,2560]{1,0:T(8,128)(2,1)} %get-tuple-element.49), channel_id=1, source_target_pairs={{0,32},{32,0},{1,33},{33,1},{2,34},{34,2},{3,35},{35,3},{4,36},{36... | collective-permute-start | bytes 2211848 | tf_op jit(solution)/shard_map/ppermute | solution.py:263
  54.7 2.4 %collective-permute-start.9 = (bf16[256,640]{1,0:T(8,128)(2,1)S(1)}, bf16[256,640]{1,0:T(8,128)(2,1)S(1)}, u32[]{:S(2)}, u32[]{:S(2)}) collective-permute-start(bf16[256,640]{1,0:T(8,128)(2,1)S(1)} %bitcast.41), channel_id=1, source_target_pairs={{0,32},{32,0},{1,33},{33,1},{2,34},{34,2},{3,35},{35,3},{4,36},{36... | collective-permute-start | bytes 983048 | tf_op jit(solution)/shard_map/ppermute | solution.py:263
  57.2 1.2 %collective-permute-done.9.grad_other_ref = bf16[256,640]{1,0:T(8,128)(2,1)S(1)} collective-permute-done((bf16[256,640]{1,0:T(8,128)(2,1)S(1)}, bf16[256,640]{1,0:T(8,128)(2,1)S(1)}, u32[]{:S(2)}, u32[]{:S(2)}) %collective-permute-start.9) | collective-permute-done | bytes 327712 | tf_op jit(solution)/shard_map/ppermute | solution.py:263
  58.4 2.9 %attend_backward_far.1 = (bf16[256,640]{1,0:T(8,128)(2,1)}, bf16[2560,128]{1,0:T(8,128)(2,1)S(1)}, bf16[128,2560]{1,0:T(8,128)(2,1)S(1)}, f32[1,2560]{1,0:T(1,12...) custom-call(s32[4]{0:T(128)S(1)} %pad_add_fusion.2.bounds_ref, ...), custom_call_target="tpu_custom_call" | custom-call | flops 2013265920 | bytes 3932160 | tf_op jit(solution)/shard_map/attend_backward_far/pallas_call | solution.py:321
  61.3 1.3 %collective-permute-start.11 = (bf16[256,256]{1,0:T(8,128)(2,1)S(1)}, bf16[256,256]{1,0:T(8,128)(2,1)S(1)}, u32[]{:S(2)}, u32[]{:S(2)}) collective-permute-start(bf16[256,256]{1,0:T(8,128)(2,1)S(1)} %get-tuple-element.63), channel_id=1, source_target_pairs={{256,0},{320,64},{384,128},{448,192},{257,1},{321,65},{385,129},{4... | collective-permute-start | bytes 393224 | tf_op jit(solution)/shard_map/ppermute | solution.py:406
  62.6 1.3 %collective-permute-start.12 = (bf16[256,256]{1,0:T(8,128)(2,1)S(1)}, bf16[256,256]{1,0:T(8,128)(2,1)S(1)}, u32[]{:S(2)}, u32[]{:S(2)}) collective-permute-start(bf16[256,256]{1,0:T(8,128)(2,1)S(1)} %get-tuple-element.64), channel_id=1, source_target_pairs={{320,0},{384,64},{448,128},{321,1},{385,65},{449,129},{322,2},{386... | collective-permute-start | bytes 393224 | tf_op jit(solution)/shard_map/ppermute | solution.py:406
  64.5 6.4 %attend_backward_near.1 = (bf16[256,640]{1,0:T(8,128)(2,1)S(1)}, bf16[256,640]{1,0:T(8,128)(2,1)S(1)}, bf16[256,256]{1,0:T(8,128)(2,1)S(1)}, bf16[256,256]{1,0:T...) custom-call(s32[4]{0:T(128)S(1)} %pad_add_fusion.2.bounds_ref, ...), custom_call_target="tpu_custom_call" | custom-call | flops 2684354560 | bytes 5242880 | tf_op jit(solution)/shard_map/attend_backward_near/pallas_call | solution.py:339
  70.9 2.3 %collective-permute-start.14 = (bf16[256,256]{1,0:T(8,128)(2,1)S(1)}, bf16[256,256]{1,0:T(8,128)(2,1)S(1)}, u32[]{:S(2)}, u32[]{:S(2)}) collective-permute-start(bf16[256,256]{1,0:T(8,128)(2,1)S(1)} %get-tuple-element.66), channel_id=1, source_target_pairs={{64,0},{128,64},{192,128},{256,192},{320,256},{384,320},{448,384},... | collective-permute-start | bytes 393224 | tf_op jit(solution)/shard_map/ppermute | solution.py:406
  73.2 1.9 %collective-permute-start.15 = (bf16[256,256]{1,0:T(8,128)(2,1)S(1)}, bf16[256,256]{1,0:T(8,128)(2,1)S(1)}, u32[]{:S(2)}, u32[]{:S(2)}) collective-permute-start(bf16[256,256]{1,0:T(8,128)(2,1)S(1)} %get-tuple-element.67), channel_id=1, source_target_pairs={{128,0},{192,64},{256,128},{320,192},{384,256},{448,320},{129,1},{... | collective-permute-start | bytes 393224 | tf_op jit(solution)/shard_map/ppermute | solution.py:406
  75.1 6.9 %collective-permute-done.11 = bf16[256,256]{1,0:T(8,128)(2,1)S(1)} collective-permute-done((bf16[256,256]{1,0:T(8,128)(2,1)S(1)}, bf16[256,256]{1,0:T(8,128)(2,1)S(1)}, u32[]{:S(2)}, u32[]{:S(2)}) %collective-permute-start.11) | collective-permute-done | bytes 131104 | tf_op jit(solution)/shard_map/ppermute | solution.py:406
  82.0 1.3 %collective-permute-start.16 = (bf16[256,256]{1,0:T(8,128)(2,1)S(1)}, bf16[256,256]{1,0:T(8,128)(2,1)S(1)}, u32[]{:S(2)}, u32[]{:S(2)}) collective-permute-start(bf16[256,256]{1,0:T(8,128)(2,1)S(1)} %get-tuple-element.68), channel_id=1, source_target_pairs={{192,0},{256,64},{320,128},{384,192},{448,256},{193,1},{257,65},{3... | collective-permute-start | bytes 393224 | tf_op jit(solution)/shard_map/ppermute | solution.py:406
  83.3 6.8 %collective-permute-start.10 = (bf16[256,640]{1,0:T(8,128)(2,1)S(1)}, bf16[256,640]{1,0:T(8,128)(2,1)S(1)}, u32[]{:S(2)}, u32[]{:S(2)}) collective-permute-start(bf16[256,640]{1,0:T(8,128)(2,1)S(1)} %get-tuple-element.61), channel_id=1, source_target_pairs={{0,32},{32,0},{1,33},{33,1},{2,34},{34,2},{3,35},{35,3},{4,36},{36... | collective-permute-start | bytes 983048 | tf_op jit(solution)/shard_map/ppermute | solution.py:263
  90.2 12.6 %collective-permute-done.16 = bf16[256,256]{1,0:T(8,128)(2,1)S(1)} collective-permute-done((bf16[256,256]{1,0:T(8,128)(2,1)S(1)}, bf16[256,256]{1,0:T(8,128)(2,1)S(1)}, u32[]{:S(2)}, u32[]{:S(2)}) %collective-permute-start.16) | collective-permute-done | bytes 131104 | tf_op jit(solution)/shard_map/ppermute | solution.py:406
  (52 shorter events, 8.0 us)
Async XLA Ops:
  0.6 21.0 %copy-start.6 = (s32[1,8]{1,0:T(1,128)S(1)}, s32[1,8]{1,0:T(1,128)}, u32[]{:S(2)}) copy-start(s32[1,8]{1,0:T(1,128)} %param.6) | copy-start | bytes 100
  0.6 41.1 %collective-permute-start.6 = (bf16[256,256]{1,0:T(8,128)(2,1)}, bf16[256,256]{1,0:T(8,128)(2,1)S(1)}, u32[]{:S(2)}, u32[]{:S(2)}) collective-permute-start(bf16[256,256]{1,0:T(8,128)(2,1)} %bitcast.55), channel_id=1, source_target_pairs={{0,384},{64,448},{1,385},{65,449},{2,386},{66,450},{3,387},{67,451... | collective-permute-start | bytes 393224 | tf_op jit(solution)/shard_map/ppermute | solution.py:390
  1.3 25.5 %collective-permute-start.2 = (bf16[256,256]{1,0:T(8,128)(2,1)}, bf16[256,256]{1,0:T(8,128)(2,1)S(1)}, u32[]{:S(2)}, u32[]{:S(2)}) collective-permute-start(bf16[256,256]{1,0:T(8,128)(2,1)} %bitcast.56), channel_id=1, source_target_pairs={{0,128},{64,192},{128,256},{192,320},{256,384},{320,448},{1,129},{... | collective-permute-start | bytes 393224 | tf_op jit(solution)/shard_map/ppermute | solution.py:390
  8.3 19.8 %collective-permute-start.1 = (bf16[256,256]{1,0:T(8,128)(2,1)}, bf16[256,256]{1,0:T(8,128)(2,1)S(1)}, u32[]{:S(2)}, u32[]{:S(2)}) collective-permute-start(bf16[256,256]{1,0:T(8,128)(2,1)} %bitcast.57), channel_id=1, source_target_pairs={{0,64},{64,128},{128,192},{192,256},{256,320},{320,384},{384,448},... | collective-permute-start | bytes 393224 | tf_op jit(solution)/shard_map/ppermute | solution.py:390
  12.5 14.3 %copy-start = (bf16[1,256,1,256]{3,1,2,0:T(8,128)(2,1)S(1)}, bf16[1,256,1,256]{3,1,2,0:T(8,128)(2,1)}, u32[]{:S(2)}) copy-start(bf16[1,256,1,256]{3,1,2,0:T(8,128)(2,1)} %param.5) | copy-start | bytes 393220
  12.5 19.1 %collective-permute-start = (bf16[1,32,8,640]{3,1,0,2:T(8,128)(2,1)S(1)}, bf16[1,32,8,640]{3,1,0,2:T(8,128)(2,1)}, u32[]{:S(2)}, u32[]{:S(2)}) collective-permute-start(bf16[1,32,8,640]{3,1,0,2:T(8,128)(2,1)S(1)} %copy.30), channel_id=1, source_target_pairs={{0,3},{1,0},{2,1},{3,2},{4,7},{5,4},{6,5},{7,6},{8,11},{9,8},{10,9... | collective-permute-start | bytes 983048 | tf_op jit(solution)/shard_map/ppermute | solution.py:394
  18.2 22.8 %collective-permute-start.7 = (bf16[256,640]{0,1:T(8,128)(2,1)S(1)}, bf16[256,640]{0,1:T(8,128)(2,1)S(1)}, u32[]{:S(2)}, u32[]{:S(2)}) collective-permute-start(bf16[256,640]{0,1:T(8,128)(2,1)S(1)} %bitcast.43), channel_id=1, source_target_pairs={{0,32},{32,0},{1,33},{33,1},{2,34},{34,2},{3,35},{35,3},{4,36},{36... | collective-permute-start | bytes 983048 | tf_op jit(solution)/shard_map/ppermute | solution.py:263
  26.8 14.8 %copy-start.2 = (bf16[256,256]{1,0:T(8,128)(2,1)}, bf16[256,256]{1,0:T(8,128)(2,1)S(1)}, u32[]{:S(2)}) copy-start(bf16[256,256]{1,0:T(8,128)(2,1)S(1)} %collective-permute-done.2.rest_2_) | copy-start | bytes 393220
  26.8 15.0 %collective-permute-start.5 = (bf16[256,256]{1,0:T(8,128)(2,1)S(1)}, bf16[256,256]{1,0:T(8,128)(2,1)S(1)}, u32[]{:S(2)}, u32[]{:S(2)}) collective-permute-start(bf16[256,256]{1,0:T(8,128)(2,1)S(1)} %bitcast.59), channel_id=1, source_target_pairs={{0,320},{64,384},{128,448},{1,321},{65,385},{129,449},{2,322},{66,... | collective-permute-start | bytes 393224 | tf_op jit(solution)/shard_map/ppermute | solution.py:390
  28.2 13.4 %copy-start.3 = (bf16[256,256]{1,0:T(8,128)(2,1)}, bf16[256,256]{1,0:T(8,128)(2,1)S(1)}, u32[]{:S(2)}) copy-start(bf16[256,256]{1,0:T(8,128)(2,1)S(1)} %collective-permute-done.1.rest_1_) | copy-start | bytes 393220
  28.2 13.6 %collective-permute-start.4 = (bf16[256,256]{1,0:T(8,128)(2,1)S(1)}, bf16[256,256]{1,0:T(8,128)(2,1)S(1)}, u32[]{:S(2)}, u32[]{:S(2)}) collective-permute-start(bf16[256,256]{1,0:T(8,128)(2,1)S(1)} %bitcast.60), channel_id=1, source_target_pairs={{0,256},{64,320},{128,384},{192,448},{1,257},{65,321},{129,385},{1... | collective-permute-start | bytes 393224 | tf_op jit(solution)/shard_map/ppermute | solution.py:390
  31.6 14.2 %collective-permute-start.3 = (bf16[256,256]{1,0:T(8,128)(2,1)S(1)}, bf16[256,256]{1,0:T(8,128)(2,1)}, u32[]{:S(2)}, u32[]{:S(2)}) collective-permute-start(bf16[256,256]{1,0:T(8,128)(2,1)S(1)} %bitcast.61), channel_id=1, source_target_pairs={{0,192},{64,256},{128,320},{192,384},{256,448},{1,193},{65,257},{1... | collective-permute-start | bytes 393224 | tf_op jit(solution)/shard_map/ppermute | solution.py:390
  34.2 20.5 %all-to-all-start = ((bf16[1,32,8,640]{3,1,0,2:T(8,128)(2,1)}), bf16[1,32,8,640]{3,1,0,2:T(8,128)(2,1)S(1)}, u32[]{:S(2)}, u32[]{:S(2)}) async-start(bf16[1,32,8,640]{3,1,0,2:T(8,128)(2,1)} %collective-permute-done), calls=%async_computation | async-start | bytes 655360 | tf_op jit(solution)/shard_map/all_to_all | solution.py:398
  41.8 0.7 copy-start.4
  42.5 0.7 copy-start.5
  52.6 4.6 %collective-permute-start.8 = (bf16[144,2560]{1,0:T(8,128)(2,1)}, bf16[144,2560]{1,0:T(8,128)(2,1)}, u32[]{:S(2)}, u32[]{:S(2)}) collective-permute-start(bf16[144,2560]{1,0:T(8,128)(2,1)} %get-tuple-element.49), channel_id=1, source_target_pairs={{0,32},{32,0},{1,33},{33,1},{2,34},{34,2},{3,35},{35,3},{4,36},{36... | collective-permute-start | bytes 2211848 | tf_op jit(solution)/shard_map/ppermute | solution.py:263
  54.7 3.7 %collective-permute-start.9 = (bf16[256,640]{1,0:T(8,128)(2,1)S(1)}, bf16[256,640]{1,0:T(8,128)(2,1)S(1)}, u32[]{:S(2)}, u32[]{:S(2)}) collective-permute-start(bf16[256,640]{1,0:T(8,128)(2,1)S(1)} %bitcast.41), channel_id=1, source_target_pairs={{0,32},{32,0},{1,33},{33,1},{2,34},{34,2},{3,35},{35,3},{4,36},{36... | collective-permute-start | bytes 983048 | tf_op jit(solution)/shard_map/ppermute | solution.py:263
  61.3 20.8 %collective-permute-start.11 = (bf16[256,256]{1,0:T(8,128)(2,1)S(1)}, bf16[256,256]{1,0:T(8,128)(2,1)S(1)}, u32[]{:S(2)}, u32[]{:S(2)}) collective-permute-start(bf16[256,256]{1,0:T(8,128)(2,1)S(1)} %get-tuple-element.63), channel_id=1, source_target_pairs={{256,0},{320,64},{384,128},{448,192},{257,1},{321,65},{385,129},{4... | collective-permute-start | bytes 393224 | tf_op jit(solution)/shard_map/ppermute | solution.py:406
  62.6 20.8 %collective-permute-start.12 = (bf16[256,256]{1,0:T(8,128)(2,1)S(1)}, bf16[256,256]{1,0:T(8,128)(2,1)S(1)}, u32[]{:S(2)}, u32[]{:S(2)}) collective-permute-start(bf16[256,256]{1,0:T(8,128)(2,1)S(1)} %get-tuple-element.64), channel_id=1, source_target_pairs={{320,0},{384,64},{448,128},{321,1},{385,65},{449,129},{322,2},{386... | collective-permute-start | bytes 393224 | tf_op jit(solution)/shard_map/ppermute | solution.py:406
  63.9 26.3 %collective-permute-start.13 = (bf16[256,256]{1,0:T(8,128)(2,1)S(1)}, bf16[256,256]{1,0:T(8,128)(2,1)S(1)}, u32[]{:S(2)}, u32[]{:S(2)}) collective-permute-start(bf16[256,256]{1,0:T(8,128)(2,1)S(1)} %get-tuple-element.65), channel_id=1, source_target_pairs={{384,0},{448,64},{385,1},{449,65},{386,2},{450,66},{387,3},{451,67... | collective-permute-start | bytes 393224 | tf_op jit(solution)/shard_map/ppermute | solution.py:406
  70.9 19.3 %collective-permute-start.14 = (bf16[256,256]{1,0:T(8,128)(2,1)S(1)}, bf16[256,256]{1,0:T(8,128)(2,1)S(1)}, u32[]{:S(2)}, u32[]{:S(2)}) collective-permute-start(bf16[256,256]{1,0:T(8,128)(2,1)S(1)} %get-tuple-element.66), channel_id=1, source_target_pairs={{64,0},{128,64},{192,128},{256,192},{320,256},{384,320},{448,384},... | collective-permute-start | bytes 393224 | tf_op jit(solution)/shard_map/ppermute | solution.py:406
  73.2 17.0 %collective-permute-start.15 = (bf16[256,256]{1,0:T(8,128)(2,1)S(1)}, bf16[256,256]{1,0:T(8,128)(2,1)S(1)}, u32[]{:S(2)}, u32[]{:S(2)}) collective-permute-start(bf16[256,256]{1,0:T(8,128)(2,1)S(1)} %get-tuple-element.67), channel_id=1, source_target_pairs={{128,0},{192,64},{256,128},{320,192},{384,256},{448,320},{129,1},{... | collective-permute-start | bytes 393224 | tf_op jit(solution)/shard_map/ppermute | solution.py:406
  82.0 20.8 %collective-permute-start.16 = (bf16[256,256]{1,0:T(8,128)(2,1)S(1)}, bf16[256,256]{1,0:T(8,128)(2,1)S(1)}, u32[]{:S(2)}, u32[]{:S(2)}) collective-permute-start(bf16[256,256]{1,0:T(8,128)(2,1)S(1)} %get-tuple-element.68), channel_id=1, source_target_pairs={{192,0},{256,64},{320,128},{384,192},{448,256},{193,1},{257,65},{3... | collective-permute-start | bytes 393224 | tf_op jit(solution)/shard_map/ppermute | solution.py:406
  83.3 20.2 %collective-permute-start.10 = (bf16[256,640]{1,0:T(8,128)(2,1)S(1)}, bf16[256,640]{1,0:T(8,128)(2,1)S(1)}, u32[]{:S(2)}, u32[]{:S(2)}) collective-permute-start(bf16[256,640]{1,0:T(8,128)(2,1)S(1)} %get-tuple-element.61), channel_id=1, source_target_pairs={{0,32},{32,0},{1,33},{33,1},{2,34},{34,2},{3,35},{35,3},{4,36},{36... | collective-permute-start | bytes 983048 | tf_op jit(solution)/shard_map/ppermute | solution.py:263
  (1 other events, 0.7 us)

commit v7 on v6

--- a/solution.py
+++ b/solution.py
@@ -23,16 +23,54 @@
     return array.reshape(array.shape[0] // 8, 8, array.shape[1])
 
 
+def begins_of(lengths_ref):
+    begins = [jnp.int32(0)]
+    for doc in range(lengths_ref.shape[0] - 1):
+        begins.append(begins[-1] + lengths_ref[doc])
+    return begins
+
+
+def start_of(position, begins):
+    start = jnp.zeros_like(position)
+    for begin in begins:
+        start = jnp.where(begin <= position, begin, start)
+    return start
+
+
+def last_of(begins, place_ref, rows):
+    chip, core = place_ref[0], place_ref[1]
+    first = start_of(2 * chip * rows, begins)
+    return lax.div(2 * chip + core - lax.div(first, jnp.int32(rows)), jnp.int32(2))
+
+
+def clear_of(begins, place_ref, rows):
+    chip, core = place_ref[0], place_ref[1]
+    start = start_of((2 * chip + 2) * rows - 1, begins)
+    blocks = 2 * chip + core - lax.div(start + rows - 1, jnp.int32(rows))
+    return jnp.maximum(lax.div(blocks, jnp.int32(2)), 0)
+
+
+def stack(to_ref, query_refs):
+    rows = query_refs[0].shape[0]
+    heads = query_refs[0].shape[1] // HEAD
+    for group in range(2 * heads):
+        column = slice(group % heads * HEAD, (group % heads + 1) * HEAD)
+        to_ref[group * rows : (group + 1) * rows, :] = query_refs[group // heads][:, column]
+
+
 def forward_kernel(
-    bounds_ref, starts_ref, turned_ref, *rest,
+    lengths_ref, place_ref, query_ref, query_other_ref, *rest,
 ):
-    *block_refs, kept_ref, pairs_ref, acc_ref, stats_ref, sent_ref = rest[:-5]
-    scores_ref, top_ref, weights_ref, kept_sem, block_sem = rest[-5:]
-    rows = starts_ref.shape[2]
-    groups = turned_ref.shape[1] // rows
-    heads = groups // 2
+    *block_refs, kept_ref, pairs_ref, acc_ref, stats_ref, sent_ref = rest[:-7]
+    scores_ref, top_ref, weights_ref, turned_ref, starts_ref, kept_sem, block_sem = rest[-7:]
+    rows = query_ref.shape[0]
+    heads = query_ref.shape[1] // HEAD
+    groups = 2 * heads
     scale = LOG2E / math.sqrt(HEAD)
-    own, clear, last = bounds_ref[0], bounds_ref[2], bounds_ref[3]
+    begins = begins_of(lengths_ref)
+    last, clear = last_of(begins, place_ref, rows), clear_of(begins, place_ref, rows)
+    own = 2 * place_ref[0] + place_ref[1]
+    shards = (own, 2 * place_ref[0] + 1 - place_ref[1])
 
     def bring(block_ref, back):
         to = pl.ds(pl.multiple_of(back * rows, rows), rows)
@@ -43,6 +81,12 @@
         def start():
             bring(block_ref, back).start()
 
+    along = lax.broadcasted_iota(jnp.int32, (1, rows), 1)
+    for slot, rows_ref in enumerate((query_ref, query_other_ref)):
+        starts_ref[slot] = start_of(shards[slot] * rows + along, begins)
+        for head in range(heads):
+            span = slice((slot * heads + head) * rows, (slot * heads + head + 1) * rows)
+            turned_ref[:, span] = rows_ref[:, head * HEAD : (head + 1) * HEAD].T
     top_ref[...] = jnp.full_like(top_ref, NEG_LARGE)
     acc_ref[...] = jnp.zeros_like(acc_ref)
 
@@ -55,7 +99,7 @@
             key_pos = (own - 2 * back) * rows + lax.broadcasted_iota(jnp.int32, (rows, rows), 0)
             across = lax.broadcasted_iota(jnp.int32, (rows, rows), 1)
             for slot in range(2):
-                query_pos = bounds_ref[slot] * rows + across
+                query_pos = shards[slot] * rows + across
                 allowed.append((key_pos <= query_pos) & (key_pos >= starts_ref[slot]))
         for group in range(groups):
             span = slice(group * rows, (group + 1) * rows)
@@ -180,16 +224,18 @@
 
 
 def backward_far_kernel(
-    bounds_ref, stats_ref, arrived_ref, acc_ref, grad_ref, grad_other_ref, query_ref, pairs_ref,
-    kept_ref,
+    lengths_ref, place_ref, stats_ref, arrived_ref, acc_ref, grad_ref, grad_other_ref,
+    query_ref, query_other_ref, pairs_ref, kept_ref,
     out_ref, scaled_ref, turned_scaled_ref, delta_ref, total_ref, *rest, split,
 ):
-    *block_refs, move_ref, pair_grad_ref, weights_ref, kept_sem = rest
+    *block_refs, move_ref, stacked_ref, pair_grad_ref, weights_ref, kept_sem = rest
     rows = out_ref.shape[0]
     heads = grad_ref.shape[1] // HEAD
     groups = 2 * heads
     copy = fetch(split, kept_ref, weights_ref, kept_sem, rows)
-    fetch_all(split, bounds_ref[3] + 1, copy)
+    last = last_of(begins_of(lengths_ref), place_ref, rows)
+    fetch_all(split, last + 1, copy)
+    stack(stacked_ref, (query_ref, query_other_ref))
     total_ref[...] = jnp.zeros_like(total_ref)
     for group in range(groups):
         span = slice(group * rows, (group + 1) * rows)
@@ -215,28 +261,29 @@
         turned_scaled_ref[:, span] = low
         scaled_ref[span, :] = low.T
     accumulate(
-        split, bounds_ref[3] + 1, pairs_ref, weights_ref, copy, query_ref,
+        split, last + 1, pairs_ref, weights_ref, copy, stacked_ref,
         scaled_ref, turned_scaled_ref, delta_ref, total_ref, move_ref, pair_grad_ref, split,
     )
     hand_out(pair_grad_ref, block_refs)
 
 
 def backward_near_kernel(
-    bounds_ref, scaled_ref, turned_scaled_ref, delta_ref, begun_ref, query_ref, pairs_ref,
-    kept_ref, query_grad_ref, query_grad_other_ref, *rest,
+    lengths_ref, place_ref, scaled_ref, turned_scaled_ref, delta_ref, begun_ref,
+    query_ref, query_other_ref, pairs_ref, kept_ref, query_grad_ref, query_grad_other_ref, *rest,
 ):
-    *block_refs, total_ref, move_ref, pair_grad_ref, weights_ref, kept_sem = rest
+    *block_refs, total_ref, move_ref, stacked_ref, pair_grad_ref, weights_ref, kept_sem = rest
     rows = query_grad_ref.shape[0]
     groups = turned_scaled_ref.shape[1] // rows
     heads = groups // 2
     root = 1.0 / math.sqrt(HEAD)
-    slots = pair_grad_ref.shape[0] // rows
-    stop = jnp.minimum(bounds_ref[3] + 1, slots)
+    slots = len(block_refs)
+    stop = jnp.minimum(last_of(begins_of(lengths_ref), place_ref, rows) + 1, slots)
     copy = fetch(0, kept_ref, weights_ref, kept_sem, rows)
     fetch_all(0, stop, copy)
+    stack(stacked_ref, (query_ref, query_other_ref))
     total_ref[...] = begun_ref[...]
     accumulate(
-        0, stop, pairs_ref, weights_ref, copy, query_ref,
+        0, stop, pairs_ref, weights_ref, copy, stacked_ref,
         scaled_ref, turned_scaled_ref, delta_ref, total_ref, move_ref, pair_grad_ref, 0,
     )
     hand_out(pair_grad_ref, block_refs)
@@ -271,14 +318,12 @@
     )
 
 
-def attend(bounds, starts, queries, grad, blocks, split, send, swap=swap_cores):
+def attend(lengths, place, queries, grad, blocks, split, send, swap=swap_cores):
     slots = len(blocks)
     rows, columns = queries[0].shape
     heads = columns // HEAD
     wide = 2 * heads * rows
-    turned = jnp.concatenate([turn(q) for q in queries], axis=1)
-    stacked = jnp.concatenate([stack(q) for q in queries], axis=0)
-    blocks, turned, stacked = lax.optimization_barrier((blocks, turned, stacked))
+    blocks, queries = lax.optimization_barrier((blocks, queries))
     blocks = [pltpu.with_memory_space_constraint(block, pltpu.HBM) for block in blocks]
     weights, pairs, acc, stats, sent = pl.pallas_call(
         forward_kernel,
@@ -289,19 +334,21 @@
             jax.ShapeDtypeStruct((8, wide), jnp.float32),
             jax.ShapeDtypeStruct((HEAD + EXTRA, wide), jnp.bfloat16),
         ),
-        in_specs=[smem()] + [vmem()] * 2 + [hbm()] * slots,
+        in_specs=[smem()] * 2 + [vmem()] * 2 + [hbm()] * slots,
         out_specs=(hbm(),) + (vmem(),) * 4,
         scratch_shapes=[
             pltpu.VMEM((slots * rows, wide), jnp.float32),
             pltpu.VMEM((8, wide), jnp.float32),
             pltpu.VMEM((slots * rows, wide), jnp.bfloat16),
+            pltpu.VMEM((HEAD, wide), jnp.bfloat16),
+            pltpu.VMEM((2, 1, rows), jnp.int32),
             pltpu.SemaphoreType.DMA((slots,)),
             pltpu.SemaphoreType.DMA((slots,)),
         ],
         compiler_params=pltpu.CompilerParams(vmem_limit_bytes=36 << 20),
         cost_estimate=cost(slots, rows, wide, 2),
         name="attend_forward",
-    )(bounds, starts, turned, *blocks)
+    )(lengths, place, *queries, *blocks)
     weights = pltpu.with_memory_space_constraint(weights, pltpu.HBM)
     arrived = swap(sent)
     grad, stats = lax.optimization_barrier((grad, stats))
@@ -312,6 +359,7 @@
 
     def held(blocks):
         return [
+            pltpu.VMEM((wide, HEAD), jnp.bfloat16),
             pltpu.VMEM((blocks * rows, 2 * HEAD), jnp.bfloat16),
             pltpu.VMEM((blocks * rows, wide), jnp.bfloat16),
             pltpu.SemaphoreType.DMA((blocks,)),
@@ -328,55 +376,25 @@
             jax.ShapeDtypeStruct((HEAD, wide), jnp.float32),
         )
         + (block,) * (slots - split),
-        in_specs=[smem()] + [vmem()] * 7 + [hbm()],
+        in_specs=[smem()] * 2 + [vmem()] * 8 + [hbm()],
         out_specs=(vmem(),) * (5 + slots - split),
         scratch_shapes=[move] + held(slots - split),
         compiler_params=params,
         cost_estimate=cost(slots - split, rows, wide, 4),
         name="attend_backward_far",
-    )(bounds, stats, arrived, acc, grad, grad_other, stacked, pairs, weights)
+    )(lengths, place, stats, arrived, acc, grad, grad_other, *queries, pairs, weights)
     sent_far = send(far)
     query_grad, query_grad_other, *near = pl.pallas_call(
         backward_near_kernel,
         out_shape=(half, half) + (block,) * split,
-        in_specs=[smem()] + [vmem()] * 6 + [hbm()],
+        in_specs=[smem()] * 2 + [vmem()] * 7 + [hbm()],
         out_specs=(vmem(),) * (2 + split),
         scratch_shapes=[pltpu.VMEM((HEAD, wide), jnp.float32), move] + held(split),
         compiler_params=params,
         cost_estimate=cost(split, rows, wide, 4),
         name="attend_backward_near",
-    )(bounds, scaled, turned_scaled, delta, total, stacked, pairs, weights)
+    )(lengths, place, scaled, turned_scaled, delta, total, *queries, pairs, weights)
     return out, query_grad, query_grad_other, near, sent_far
-
-
-def turn(array):
-    rows, columns = array.shape
-    heads = columns // HEAD
-    return array.reshape(rows, heads, HEAD).transpose(2, 1, 0).reshape(HEAD, heads * rows)
-
-
-def stack(array):
-    rows, columns = array.shape
-    heads = columns // HEAD
-    return array.reshape(rows, heads, HEAD).transpose(1, 0, 2).reshape(heads * rows, HEAD)
-
-
-def block_bounds(lengths, chip, core, rows):
-    own, other = 2 * chip + core, 2 * chip + 1 - core
-    ends = jnp.cumsum(lengths)
-    begins = ends - lengths
-
-    def starts_of(positions):
-        here = begins[:, None] <= positions[None, :]
-        return jnp.max(jnp.where(here, begins[:, None], 0), axis=0)
-
-    span = jnp.arange(rows, dtype=jnp.int32)
-    starts = jnp.stack([starts_of(own * rows + span), starts_of(other * rows + span)])
-    edges = starts_of(jnp.stack([2 * chip * rows, (2 * chip + 2) * rows - 1]))
-    last = (own - edges[0] // rows) // 2
-    clear = jnp.maximum((own - (edges[1] + rows - 1) // rows) // 2, 0)
-    bounds = jnp.stack([own, other, clear, last]).astype(jnp.int32)
-    return bounds, starts[:, None, :]
 
 
 def per_device(query, keys_values, doc_lengths, incoming_output_grad):
@@ -396,19 +414,17 @@
     )
     arrived, *blocks[1:3] = lax.optimization_barrier((arrived, *blocks[1:3]))
     grad = lax.all_to_all(arrived, "tensor", split_axis=2, concat_axis=1, tiled=True)[0, :, 0, :]
-    bounds, starts = block_bounds(
-        doc_lengths[0], lax.axis_index("chip"), lax.axis_index("core"), rows
-    )
+    place = jnp.stack([lax.axis_index("chip"), lax.axis_index("core")]).astype(jnp.int32)
     split = (slots + 1) // 2
 
     def send(blocks, first):
         return [
             lax.ppermute(block, "chip", [(c, c - first - at) for c in range(first + at, chips)])
-            for at, block in enumerate(blocks)
+            for at, block in reversed(list(enumerate(blocks)))
         ]
 
     out, query_grad, query_grad_other, near, far = attend(
-        bounds, starts, (query, swap_cores(query)), grad, blocks,
+        doc_lengths[0], place, (query, swap_cores(query)), grad, blocks,
         split, functools.partial(send, first=split),
     )
     sums = near[0].astype(jnp.float32)

time: 105 us -> 100 us (0.952)
  the two profiles are of different devices: /device:TPU:129 before, /device:TPU:249 now
where the time goes in v7:
time: 100 us; the launch traced here: 99.5 us
  starting transfers between devices  50.3 us (50%)
  waiting for transfers between devices  24.6 us (25%)
  Pallas kernels  18.8 us (19%)
  local copies, waits for them, and re-layouts  3.29 us (3%)
  other arithmetic  1.67 us (2%)
    ppermute x6, starting transfers between devices, per_device(): lax.ppermute(pairs, 'chip', [(c, c + back) for c in range(chips - back)])  17 us
    ppermute x6, waiting for transfers between devices, send(): lax.ppermute(block, 'chip', [(c, c - first - at) for c in range(first + a...  16.6 us
    ppermute x6, starting transfers between devices, send(): lax.ppermute(block, 'chip', [(c, c - first - at) for c in range(first + a...  12.3 us
    ppermute x4, starting transfers between devices, swap_cores(): return lax.ppermute(value, 'core', [(0, 1), (1, 0)])  10.4 us
    pallas_call x1, Pallas kernels, attend(): pl.pallas_call(forward_kernel, out_shape=(pltpu.HBM((slots * rows, wide),...  8.04 us
    pallas_call x1, Pallas kernels, attend(): pl.pallas_call(backward_near_kernel, out_shape=(half, half) + (block,) *...  7.77 us
    ppermute x6, waiting for transfers between devices, per_device(): lax.ppermute(pairs, 'chip', [(c, c + back) for c in range(chips - back)])  6.36 us
    all_to_all x1, starting transfers between devices, per_device(): lax.all_to_all(arrived, 'tensor', split_axis=2, concat_axis=1, tiled=True)  6.31 us
  transfers between devices with their start and end apart: 18, of which 7 were waited for; matrix products, arithmetic and copies ran while one was open for 1% of the time, Pallas kernels for 16%

profile of v7, /device:TPU:249, one launch (start us, length us, event | category | flops | bytes accessed | tf_op | source)
XLA Modules:
  0.0 99.5 jit_solution(5992155505247393815)
XLA Ops:
  0.6 1.0 %copy.8 = bf16[1,32,8,640]{3,1,0,2:T(8,128)(2,1)S(1)} copy(bf16[1,32,8,640]{3,2,1,0:T(8,128)(2,1)} %param.7) | data formatting | bytes 655360 | tf_op args[3]
  1.6 4.4 %collective-permute-start = (bf16[1,32,8,640]{3,1,0,2:T(8,128)(2,1)S(1)}, bf16[1,32,8,640]{3,1,0,2:T(8,128)(2,1)}, u32[]{:S(2)}, u32[]{:S(2)}) collective-permute-start(bf16[1,32,8,640]{3,1,0,2:T(8,128)(2,1)S(1)} %copy.8), channel_id=1, source_target_pairs={{0,3},{1,0},{2,1},{3,2},{4,7},{5,4},{6,5},{7,6},{8,11},{9,8},{10,9... | collective-permute-start | bytes 983048 | tf_op jit(solution)/shard_map/ppermute | solution.py:412
  6.0 2.9 %collective-permute-start.7 = (bf16[256,640]{1,0:T(8,128)(2,1)}, bf16[256,640]{1,0:T(8,128)(2,1)S(1)}, u32[]{:S(2)}, u32[]{:S(2)}) collective-permute-start(bf16[256,640]{1,0:T(8,128)(2,1)} %bitcast.15), channel_id=1, source_target_pairs={{0,32},{32,0},{1,33},{33,1},{2,34},{34,2},{3,35},{35,3},{4,36},{36... | collective-permute-start | bytes 983048 | tf_op jit(solution)/shard_map/ppermute | solution.py:310
  8.9 6.1 %collective-permute-start.2 = (bf16[256,256]{1,0:T(8,128)(2,1)}, bf16[256,256]{1,0:T(8,128)(2,1)S(1)}, u32[]{:S(2)}, u32[]{:S(2)}) collective-permute-start(bf16[256,256]{1,0:T(8,128)(2,1)} %bitcast.25), channel_id=1, source_target_pairs={{0,128},{64,192},{128,256},{192,320},{256,384},{320,448},{1,129},{... | collective-permute-start | bytes 393224 | tf_op jit(solution)/shard_map/ppermute | solution.py:408
  15.0 3.1 %collective-permute-start.1 = (bf16[256,256]{1,0:T(8,128)(2,1)}, bf16[256,256]{1,0:T(8,128)(2,1)S(1)}, u32[]{:S(2)}, u32[]{:S(2)}) collective-permute-start(bf16[256,256]{1,0:T(8,128)(2,1)} %bitcast.26), channel_id=1, source_target_pairs={{0,64},{64,128},{128,192},{192,256},{256,320},{320,384},{384,448},... | collective-permute-start | bytes 393224 | tf_op jit(solution)/shard_map/ppermute | solution.py:408
  20.0 5.0 %collective-permute-done.1.rest_1_ = bf16[256,256]{1,0:T(8,128)(2,1)S(1)} collective-permute-done((bf16[256,256]{1,0:T(8,128)(2,1)}, bf16[256,256]{1,0:T(8,128)(2,1)S(1)}, u32[]{:S(2)}, u32[]{:S(2)}) %collective-permute-start.1) | collective-permute-done | bytes 131104 | tf_op jit(solution)/shard_map/ppermute | solution.py:408
  25.0 4.3 %collective-permute-start.4 = (bf16[256,256]{1,0:T(8,128)(2,1)}, bf16[256,256]{1,0:T(8,128)(2,1)S(1)}, u32[]{:S(2)}, u32[]{:S(2)}) collective-permute-start(bf16[256,256]{1,0:T(8,128)(2,1)} %bitcast.29), channel_id=1, source_target_pairs={{0,256},{64,320},{128,384},{192,448},{1,257},{65,321},{129,385},{1... | collective-permute-start | bytes 393224 | tf_op jit(solution)/shard_map/ppermute | solution.py:408
  29.2 2.2 %collective-permute-start.3 = (bf16[256,256]{1,0:T(8,128)(2,1)}, bf16[256,256]{1,0:T(8,128)(2,1)S(1)}, u32[]{:S(2)}, u32[]{:S(2)}) collective-permute-start(bf16[256,256]{1,0:T(8,128)(2,1)} %bitcast.30), channel_id=1, source_target_pairs={{0,192},{64,256},{128,320},{192,384},{256,448},{1,193},{65,257},{1... | collective-permute-start | bytes 393224 | tf_op jit(solution)/shard_map/ppermute | solution.py:408
  31.5 6.3 %all-to-all-start = ((bf16[1,32,8,640]{3,1,0,2:T(8,128)(2,1)}), bf16[1,32,8,640]{3,1,0,2:T(8,128)(2,1)S(1)}, u32[]{:S(2)}, u32[]{:S(2)}) async-start(bf16[1,32,8,640]{3,1,0,2:T(8,128)(2,1)} %collective-permute-done), calls=%async_computation | async-start | bytes 655360 | tf_op jit(solution)/shard_map/all_to_all | solution.py:416
  37.9 0.9 collective-permute-done.3.rest_3_
  39.4 1.0 copy-done
  41.0 8.0 %attend_forward.1 = (bf16[1792,2560]{1,0:T(8,128)(2,1)}, bf16[1792,256]{1,0:T(8,128)(2,1)S(1)}, f32[144,2560]{1,0:T(8,128)S(1)}, f32[8,2560]{1,0:T(8,128)S(1)}, bf16[144,2560]{1,0:T(8,128)(2,1)}) custom-call(s32[8]{0:T(128)S(1)} %bitcast.21, s32[2]{0:T(128)S(1)} %pad_add_fusion.place_ref, bf16[256,640]{1,0:T(8,128)(2,1)S(1)} %bitcast.16, ...), custom_call_target="tpu_custom_call" | custom-call | flops 2348810240 | bytes 9175040 | tf_op jit(solution)/shard_map/attend_forward/pallas_call | solution.py:328
  49.1 3.2 %collective-permute-start.8 = (bf16[144,2560]{1,0:T(8,128)(2,1)}, bf16[144,2560]{1,0:T(8,128)(2,1)}, u32[]{:S(2)}, u32[]{:S(2)}) collective-permute-start(bf16[144,2560]{1,0:T(8,128)(2,1)} %get-tuple-element.50), channel_id=1, source_target_pairs={{0,32},{32,0},{1,33},{33,1},{2,34},{34,2},{3,35},{35,3},{4,36},{36... | collective-permute-start | bytes 2211848 | tf_op jit(solution)/shard_map/ppermute | solution.py:310
  52.4 1.9 %collective-permute-start.9 = (bf16[256,640]{1,0:T(8,128)(2,1)S(1)}, bf16[256,640]{1,0:T(8,128)(2,1)S(1)}, u32[]{:S(2)}, u32[]{:S(2)}) collective-permute-start(bf16[256,640]{1,0:T(8,128)(2,1)S(1)} %bitcast.19), channel_id=1, source_target_pairs={{0,32},{32,0},{1,33},{33,1},{2,34},{34,2},{3,35},{35,3},{4,36},{36... | collective-permute-start | bytes 983048 | tf_op jit(solution)/shard_map/ppermute | solution.py:310
  54.5 1.4 %collective-permute-done.9.grad_other_ref = bf16[256,640]{1,0:T(8,128)(2,1)S(1)} collective-permute-done((bf16[256,640]{1,0:T(8,128)(2,1)S(1)}, bf16[256,640]{1,0:T(8,128)(2,1)S(1)}, u32[]{:S(2)}, u32[]{:S(2)}) %collective-permute-start.9) | collective-permute-done | bytes 327712 | tf_op jit(solution)/shard_map/ppermute | solution.py:310
  55.9 3.0 %attend_backward_far.1 = (bf16[256,640]{1,0:T(8,128)(2,1)}, bf16[2560,128]{1,0:T(8,128)(2,1)S(1)}, bf16[128,2560]{1,0:T(8,128)(2,1)S(1)}, f32[1,2560]{1,0:T(1,12...) custom-call(s32[8]{0:T(128)S(1)} %bitcast.22, ...), custom_call_target="tpu_custom_call" | custom-call | flops 2013265920 | bytes 3932160 | tf_op jit(solution)/shard_map/attend_backward_far/pallas_call | solution.py:369
  60.2 1.3 %collective-permute-start.13 = (bf16[256,256]{1,0:T(8,128)(2,1)S(1)}, bf16[256,256]{1,0:T(8,128)(2,1)S(1)}, u32[]{:S(2)}, u32[]{:S(2)}) collective-permute-start(bf16[256,256]{1,0:T(8,128)(2,1)S(1)} %get-tuple-element.65), channel_id=1, source_target_pairs={{256,0},{320,64},{384,128},{448,192},{257,1},{321,65},{385,129},{4... | collective-permute-start | bytes 393224 | tf_op jit(solution)/shard_map/ppermute | solution.py:422
  61.5 7.8 %attend_backward_near.1 = (bf16[256,640]{1,0:T(8,128)(2,1)S(1)}, bf16[256,640]{1,0:T(8,128)(2,1)S(1)}, bf16[256,256]{1,0:T(8,128)(2,1)S(1)}, bf16[256,256]{1,0:T...) custom-call(s32[8]{0:T(128)S(1)} %bitcast.23, s32[2]{0:T(128)S(1)} %pad_add_fusion.place_ref, ...), custom_call_target="tpu_custom_call" | custom-call | flops 2684354560 | bytes 5242880 | tf_op jit(solution)/shard_map/attend_backward_near/pallas_call | solution.py:387
  69.3 1.9 %collective-permute-start.14 = (bf16[256,256]{1,0:T(8,128)(2,1)S(1)}, bf16[256,256]{1,0:T(8,128)(2,1)S(1)}, u32[]{:S(2)}, u32[]{:S(2)}) collective-permute-start(bf16[256,256]{1,0:T(8,128)(2,1)S(1)} %get-tuple-element.66), channel_id=1, source_target_pairs={{192,0},{256,64},{320,128},{384,192},{448,256},{193,1},{257,65},{3... | collective-permute-start | bytes 393224 | tf_op jit(solution)/shard_map/ppermute | solution.py:422
  71.2 1.9 %collective-permute-start.15 = (bf16[256,256]{1,0:T(8,128)(2,1)S(1)}, bf16[256,256]{1,0:T(8,128)(2,1)S(1)}, u32[]{:S(2)}, u32[]{:S(2)}) collective-permute-start(bf16[256,256]{1,0:T(8,128)(2,1)S(1)} %get-tuple-element.67), channel_id=1, source_target_pairs={{128,0},{192,64},{256,128},{320,192},{384,256},{448,320},{129,1},{... | collective-permute-start | bytes 393224 | tf_op jit(solution)/shard_map/ppermute | solution.py:422
  73.2 5.8 %collective-permute-start.16 = (bf16[256,256]{1,0:T(8,128)(2,1)S(1)}, bf16[256,256]{1,0:T(8,128)(2,1)S(1)}, u32[]{:S(2)}, u32[]{:S(2)}) collective-permute-start(bf16[256,256]{1,0:T(8,128)(2,1)S(1)} %get-tuple-element.68), channel_id=1, source_target_pairs={{64,0},{128,64},{192,128},{256,192},{320,256},{384,320},{448,384},... | collective-permute-start | bytes 393224 | tf_op jit(solution)/shard_map/ppermute | solution.py:422
  79.0 2.3 %collective-permute-start.10 = (bf16[256,640]{1,0:T(8,128)(2,1)S(1)}, bf16[256,640]{1,0:T(8,128)(2,1)S(1)}, u32[]{:S(2)}, u32[]{:S(2)}) collective-permute-start(bf16[256,640]{1,0:T(8,128)(2,1)S(1)} %get-tuple-element.61), channel_id=1, source_target_pairs={{0,32},{32,0},{1,33},{33,1},{2,34},{34,2},{3,35},{35,3},{4,36},{36... | collective-permute-start | bytes 983048 | tf_op jit(solution)/shard_map/ppermute | solution.py:310
  81.4 13.8 %collective-permute-done.15 = bf16[256,256]{1,0:T(8,128)(2,1)S(1)} collective-permute-done((bf16[256,256]{1,0:T(8,128)(2,1)S(1)}, bf16[256,256]{1,0:T(8,128)(2,1)S(1)}, u32[]{:S(2)}, u32[]{:S(2)}) %collective-permute-start.15) | collective-permute-done | bytes 131104 | tf_op jit(solution)/shard_map/ppermute | solution.py:422
  95.2 2.8 %collective-permute-done.16 = bf16[256,256]{1,0:T(8,128)(2,1)S(1)} collective-permute-done((bf16[256,256]{1,0:T(8,128)(2,1)S(1)}, bf16[256,256]{1,0:T(8,128)(2,1)S(1)}, u32[]{:S(2)}, u32[]{:S(2)}) %collective-permute-start.16) | collective-permute-done | bytes 131104 | tf_op jit(solution)/shard_map/ppermute | solution.py:422
  (40 shorter events, 6.4 us)
Async XLA Ops:
  1.6 27.6 %collective-permute-start = (bf16[1,32,8,640]{3,1,0,2:T(8,128)(2,1)S(1)}, bf16[1,32,8,640]{3,1,0,2:T(8,128)(2,1)}, u32[]{:S(2)}, u32[]{:S(2)}) collective-permute-start(bf16[1,32,8,640]{3,1,0,2:T(8,128)(2,1)S(1)} %copy.8), channel_id=1, source_target_pairs={{0,3},{1,0},{2,1},{3,2},{4,7},{5,4},{6,5},{7,6},{8,11},{9,8},{10,9... | collective-permute-start | bytes 983048 | tf_op jit(solution)/shard_map/ppermute | solution.py:412
  6.0 32.7 %collective-permute-start.7 = (bf16[256,640]{1,0:T(8,128)(2,1)}, bf16[256,640]{1,0:T(8,128)(2,1)S(1)}, u32[]{:S(2)}, u32[]{:S(2)}) collective-permute-start(bf16[256,640]{1,0:T(8,128)(2,1)} %bitcast.15), channel_id=1, source_target_pairs={{0,32},{32,0},{1,33},{33,1},{2,34},{34,2},{3,35},{35,3},{4,36},{36... | collective-permute-start | bytes 983048 | tf_op jit(solution)/shard_map/ppermute | solution.py:310
  8.9 10.4 %collective-permute-start.2 = (bf16[256,256]{1,0:T(8,128)(2,1)}, bf16[256,256]{1,0:T(8,128)(2,1)S(1)}, u32[]{:S(2)}, u32[]{:S(2)}) collective-permute-start(bf16[256,256]{1,0:T(8,128)(2,1)} %bitcast.25), channel_id=1, source_target_pairs={{0,128},{64,192},{128,256},{192,320},{256,384},{320,448},{1,129},{... | collective-permute-start | bytes 393224 | tf_op jit(solution)/shard_map/ppermute | solution.py:408
  15.0 9.9 %collective-permute-start.1 = (bf16[256,256]{1,0:T(8,128)(2,1)}, bf16[256,256]{1,0:T(8,128)(2,1)S(1)}, u32[]{:S(2)}, u32[]{:S(2)}) collective-permute-start(bf16[256,256]{1,0:T(8,128)(2,1)} %bitcast.26), channel_id=1, source_target_pairs={{0,64},{64,128},{128,192},{192,256},{256,320},{320,384},{384,448},... | collective-permute-start | bytes 393224 | tf_op jit(solution)/shard_map/ppermute | solution.py:408
  18.2 19.7 %collective-permute-start.6 = (bf16[256,256]{1,0:T(8,128)(2,1)}, bf16[256,256]{1,0:T(8,128)(2,1)S(1)}, u32[]{:S(2)}, u32[]{:S(2)}) collective-permute-start(bf16[256,256]{1,0:T(8,128)(2,1)} %bitcast.27), channel_id=1, source_target_pairs={{0,384},{64,448},{1,385},{65,449},{2,386},{66,450},{3,387},{67,451... | collective-permute-start | bytes 393224 | tf_op jit(solution)/shard_map/ppermute | solution.py:408
  19.3 9.9 %copy-start.4 = (bf16[256,256]{1,0:T(8,128)(2,1)}, bf16[256,256]{1,0:T(8,128)(2,1)S(1)}, u32[]{:S(2)}) copy-start(bf16[256,256]{1,0:T(8,128)(2,1)S(1)} %collective-permute-done.2.rest_2_) | copy-start | bytes 393220
  19.3 18.5 %collective-permute-start.5 = (bf16[256,256]{1,0:T(8,128)(2,1)}, bf16[256,256]{1,0:T(8,128)(2,1)S(1)}, u32[]{:S(2)}, u32[]{:S(2)}) collective-permute-start(bf16[256,256]{1,0:T(8,128)(2,1)} %bitcast.28), channel_id=1, source_target_pairs={{0,320},{64,384},{128,448},{1,321},{65,385},{129,449},{2,322},{66,... | collective-permute-start | bytes 393224 | tf_op jit(solution)/shard_map/ppermute | solution.py:408
  25.0 6.5 %copy-start.5 = (bf16[256,256]{1,0:T(8,128)(2,1)}, bf16[256,256]{1,0:T(8,128)(2,1)S(1)}, u32[]{:S(2)}) copy-start(bf16[256,256]{1,0:T(8,128)(2,1)S(1)} %collective-permute-done.1.rest_1_) | copy-start | bytes 393220
  25.0 12.9 %collective-permute-start.4 = (bf16[256,256]{1,0:T(8,128)(2,1)}, bf16[256,256]{1,0:T(8,128)(2,1)S(1)}, u32[]{:S(2)}, u32[]{:S(2)}) collective-permute-start(bf16[256,256]{1,0:T(8,128)(2,1)} %bitcast.29), channel_id=1, source_target_pairs={{0,256},{64,320},{128,384},{192,448},{1,257},{65,321},{129,385},{1... | collective-permute-start | bytes 393224 | tf_op jit(solution)/shard_map/ppermute | solution.py:408
  29.2 9.5 %collective-permute-start.3 = (bf16[256,256]{1,0:T(8,128)(2,1)}, bf16[256,256]{1,0:T(8,128)(2,1)S(1)}, u32[]{:S(2)}, u32[]{:S(2)}) collective-permute-start(bf16[256,256]{1,0:T(8,128)(2,1)} %bitcast.30), channel_id=1, source_target_pairs={{0,192},{64,256},{128,320},{192,384},{256,448},{1,193},{65,257},{1... | collective-permute-start | bytes 393224 | tf_op jit(solution)/shard_map/ppermute | solution.py:408
  31.5 20.9 %all-to-all-start = ((bf16[1,32,8,640]{3,1,0,2:T(8,128)(2,1)}), bf16[1,32,8,640]{3,1,0,2:T(8,128)(2,1)S(1)}, u32[]{:S(2)}, u32[]{:S(2)}) async-start(bf16[1,32,8,640]{3,1,0,2:T(8,128)(2,1)} %collective-permute-done), calls=%async_computation | async-start | bytes 655360 | tf_op jit(solution)/shard_map/all_to_all | solution.py:416
  37.8 1.0 copy-start.6
  39.4 1.0 copy-start
  41.0 14.8 %copy-start.1 = (bf16[1,256,1,640]{3,1,2,0:T(8,128)(2,1)S(1)}, bf16[1,256,1,640]{3,1,2,0:T(8,128)(2,1)}, u32[]{:S(2)}) copy-start(bf16[1,256,1,640]{3,1,2,0:T(8,128)(2,1)} %param.4) | copy-start | bytes 983044
  41.0 14.8 %copy-start.3 = (s32[1,8]{1,0:T(1,128)S(1)}, s32[1,8]{1,0:T(1,128)}, u32[]{:S(2)}) copy-start(s32[1,8]{1,0:T(1,128)} %param.6) | copy-start | bytes 100
  49.1 5.4 %collective-permute-start.8 = (bf16[144,2560]{1,0:T(8,128)(2,1)}, bf16[144,2560]{1,0:T(8,128)(2,1)}, u32[]{:S(2)}, u32[]{:S(2)}) collective-permute-start(bf16[144,2560]{1,0:T(8,128)(2,1)} %get-tuple-element.50), channel_id=1, source_target_pairs={{0,32},{32,0},{1,33},{33,1},{2,34},{34,2},{3,35},{35,3},{4,36},{36... | collective-permute-start | bytes 2211848 | tf_op jit(solution)/shard_map/ppermute | solution.py:310
  52.4 3.5 %collective-permute-start.9 = (bf16[256,640]{1,0:T(8,128)(2,1)S(1)}, bf16[256,640]{1,0:T(8,128)(2,1)S(1)}, u32[]{:S(2)}, u32[]{:S(2)}) collective-permute-start(bf16[256,640]{1,0:T(8,128)(2,1)S(1)} %bitcast.19), channel_id=1, source_target_pairs={{0,32},{32,0},{1,33},{33,1},{2,34},{34,2},{3,35},{35,3},{4,36},{36... | collective-permute-start | bytes 983048 | tf_op jit(solution)/shard_map/ppermute | solution.py:310
  58.9 14.3 %collective-permute-start.11 = (bf16[256,256]{1,0:T(8,128)(2,1)S(1)}, bf16[256,256]{1,0:T(8,128)(2,1)S(1)}, u32[]{:S(2)}, u32[]{:S(2)}) collective-permute-start(bf16[256,256]{1,0:T(8,128)(2,1)S(1)} %get-tuple-element.63), channel_id=1, source_target_pairs={{384,0},{448,64},{385,1},{449,65},{386,2},{450,66},{387,3},{451,67... | collective-permute-start | bytes 393224 | tf_op jit(solution)/shard_map/ppermute | solution.py:422
  59.5 19.4 %collective-permute-start.12 = (bf16[256,256]{1,0:T(8,128)(2,1)S(1)}, bf16[256,256]{1,0:T(8,128)(2,1)S(1)}, u32[]{:S(2)}, u32[]{:S(2)}) collective-permute-start(bf16[256,256]{1,0:T(8,128)(2,1)S(1)} %get-tuple-element.64), channel_id=1, source_target_pairs={{320,0},{384,64},{448,128},{321,1},{385,65},{449,129},{322,2},{386... | collective-permute-start | bytes 393224 | tf_op jit(solution)/shard_map/ppermute | solution.py:422
  60.2 21.1 %collective-permute-start.13 = (bf16[256,256]{1,0:T(8,128)(2,1)S(1)}, bf16[256,256]{1,0:T(8,128)(2,1)S(1)}, u32[]{:S(2)}, u32[]{:S(2)}) collective-permute-start(bf16[256,256]{1,0:T(8,128)(2,1)S(1)} %get-tuple-element.65), channel_id=1, source_target_pairs={{256,0},{320,64},{384,128},{448,192},{257,1},{321,65},{385,129},{4... | collective-permute-start | bytes 393224 | tf_op jit(solution)/shard_map/ppermute | solution.py:422
  69.3 12.1 %collective-permute-start.14 = (bf16[256,256]{1,0:T(8,128)(2,1)S(1)}, bf16[256,256]{1,0:T(8,128)(2,1)S(1)}, u32[]{:S(2)}, u32[]{:S(2)}) collective-permute-start(bf16[256,256]{1,0:T(8,128)(2,1)S(1)} %get-tuple-element.66), channel_id=1, source_target_pairs={{192,0},{256,64},{320,128},{384,192},{448,256},{193,1},{257,65},{3... | collective-permute-start | bytes 393224 | tf_op jit(solution)/shard_map/ppermute | solution.py:422
  71.2 24.0 %collective-permute-start.15 = (bf16[256,256]{1,0:T(8,128)(2,1)S(1)}, bf16[256,256]{1,0:T(8,128)(2,1)S(1)}, u32[]{:S(2)}, u32[]{:S(2)}) collective-permute-start(bf16[256,256]{1,0:T(8,128)(2,1)S(1)} %get-tuple-element.67), channel_id=1, source_target_pairs={{128,0},{192,64},{256,128},{320,192},{384,256},{448,320},{129,1},{... | collective-permute-start | bytes 393224 | tf_op jit(solution)/shard_map/ppermute | solution.py:422
  73.2 24.8 %collective-permute-start.16 = (bf16[256,256]{1,0:T(8,128)(2,1)S(1)}, bf16[256,256]{1,0:T(8,128)(2,1)S(1)}, u32[]{:S(2)}, u32[]{:S(2)}) collective-permute-start(bf16[256,256]{1,0:T(8,128)(2,1)S(1)} %get-tuple-element.68), channel_id=1, source_target_pairs={{64,0},{128,64},{192,128},{256,192},{320,256},{384,320},{448,384},... | collective-permute-start | bytes 393224 | tf_op jit(solution)/shard_map/ppermute | solution.py:422
  79.0 19.7 %collective-permute-start.10 = (bf16[256,640]{1,0:T(8,128)(2,1)S(1)}, bf16[256,640]{1,0:T(8,128)(2,1)S(1)}, u32[]{:S(2)}, u32[]{:S(2)}) collective-permute-start(bf16[256,640]{1,0:T(8,128)(2,1)S(1)} %get-tuple-element.61), channel_id=1, source_target_pairs={{0,32},{32,0},{1,33},{33,1},{2,34},{34,2},{3,35},{35,3},{4,36},{36... | collective-permute-start | bytes 983048 | tf_op jit(solution)/shard_map/ppermute | solution.py:310
  (4 other events, 3.2 us)

commit v8 on v7

--- a/solution.py
+++ b/solution.py
@@ -23,10 +23,10 @@
     return array.reshape(array.shape[0] // 8, 8, array.shape[1])
 
 
-def begins_of(lengths_ref):
+def begins_of(place_ref):
     begins = [jnp.int32(0)]
-    for doc in range(lengths_ref.shape[0] - 1):
-        begins.append(begins[-1] + lengths_ref[doc])
+    for at in range(2, place_ref.shape[0] - 1):
+        begins.append(begins[-1] + place_ref[at])
     return begins
 
 
@@ -59,15 +59,18 @@
 
 
 def forward_kernel(
-    lengths_ref, place_ref, query_ref, query_other_ref, *rest,
+    place_ref, query_hbm_ref, query_other_ref, *rest,
 ):
-    *block_refs, kept_ref, pairs_ref, acc_ref, stats_ref, sent_ref = rest[:-7]
-    scores_ref, top_ref, weights_ref, turned_ref, starts_ref, kept_sem, block_sem = rest[-7:]
+    *block_refs, kept_ref, pairs_ref, acc_ref, stats_ref, sent_ref = rest[:-9]
+    scores_ref, top_ref, weights_ref, turned_ref, starts_ref, query_ref = rest[-9:-3]
+    kept_sem, block_sem, query_sem = rest[-3:]
     rows = query_ref.shape[0]
     heads = query_ref.shape[1] // HEAD
     groups = 2 * heads
     scale = LOG2E / math.sqrt(HEAD)
-    begins = begins_of(lengths_ref)
+    own_rows = pltpu.make_async_copy(query_hbm_ref, query_ref, query_sem)
+    own_rows.start()
+    begins = begins_of(place_ref)
     last, clear = last_of(begins, place_ref, rows), clear_of(begins, place_ref, rows)
     own = 2 * place_ref[0] + place_ref[1]
     shards = (own, 2 * place_ref[0] + 1 - place_ref[1])
@@ -82,7 +85,9 @@
             bring(block_ref, back).start()
 
     along = lax.broadcasted_iota(jnp.int32, (1, rows), 1)
-    for slot, rows_ref in enumerate((query_ref, query_other_ref)):
+    for slot, rows_ref in ((1, query_other_ref), (0, query_ref)):
+        if slot == 0:
+            own_rows.wait()
         starts_ref[slot] = start_of(shards[slot] * rows + along, begins)
         for head in range(heads):
             span = slice((slot * heads + head) * rows, (slot * heads + head + 1) * rows)
@@ -90,9 +95,10 @@
     top_ref[...] = jnp.full_like(top_ref, NEG_LARGE)
     acc_ref[...] = jnp.zeros_like(acc_ref)
 
-    def measure(back, masked):
-        to = pl.ds(pl.multiple_of(back * rows, rows), rows)
-        bring(block_refs[0], back).wait()
+    def measure(back, masked, count=1):
+        to = pl.ds(pl.multiple_of(back * rows, rows), count * rows)
+        for more in range(count):
+            bring(block_refs[0], back + more).wait()
         keys = pairs_ref[to, :HEAD]
         allowed = []
         if masked:
@@ -117,23 +123,37 @@
         measure(back, False)
         return unused
 
+    def two_plain(pair, unused):
+        measure(1 + 2 * pair, False, 2)
+        return unused
+
     lax.fori_loop(0, last - clear + 1, masked, 0)
-    lax.fori_loop(1, clear + 1, plain, 0)
+    twos = lax.div(clear, jnp.int32(2))
+    lax.fori_loop(0, twos, two_plain, 0)
+    lax.fori_loop(1 + 2 * twos, clear + 1, plain, 0)
     top = jnp.max(top_ref[...], axis=0, keepdims=True) * scale
     top_ref[...] = jnp.broadcast_to(top, top_ref.shape)
 
-    def weigh(back, unused):
-        to = pl.ds(pl.multiple_of(back * rows, rows), rows)
+    def weigh(back, count):
+        to = pl.ds(pl.multiple_of(back * rows, rows), count * rows)
         turned_values = jnp.concatenate(
-            [pairs_ref[to, HEAD:].T, jnp.ones((16, rows), jnp.bfloat16)], axis=0
+            [pairs_ref[to, HEAD:].T, jnp.ones((16, count * rows), jnp.bfloat16)], axis=0
         )
         for group in range(groups):
             span = slice(group * rows, (group + 1) * rows)
             weights_ref[to, span] = jnp.exp2(
                 scores_ref[to, span] * scale - top_ref[:1, span]
             ).astype(jnp.bfloat16)
-        keep(back).start()
+        for more in range(count):
+            keep(back + more).start()
         acc_ref[...] += matmul(turned_values, weights_ref[to, :])
+
+    def weigh_two(pair, unused):
+        weigh(2 * pair, 2)
+        return unused
+
+    def weigh_one(back, unused):
+        weigh(back, 1)
         return unused
 
     def keep(back):
@@ -144,7 +164,9 @@
         keep(back).wait()
         return unused
 
-    lax.fori_loop(0, last + 1, weigh, 0)
+    twos = lax.div(last + 1, jnp.int32(2))
+    lax.fori_loop(0, twos, weigh_two, 0)
+    lax.fori_loop(2 * twos, last + 1, weigh_one, 0)
     totals = acc_ref[HEAD : HEAD + 1, :]
     log_totals = top_ref[:1, :] + jnp.log2(totals)
     stats_ref[...] = jnp.concatenate([top_ref[:1, :], log_totals] + [top] * 6, axis=0)
@@ -224,7 +246,7 @@
 
 
 def backward_far_kernel(
-    lengths_ref, place_ref, stats_ref, arrived_ref, acc_ref, grad_ref, grad_other_ref,
+    place_ref, stats_ref, arrived_ref, acc_ref, grad_ref, grad_other_ref,
     query_ref, query_other_ref, pairs_ref, kept_ref,
     out_ref, scaled_ref, turned_scaled_ref, delta_ref, total_ref, *rest, split,
 ):
@@ -233,7 +255,7 @@
     heads = grad_ref.shape[1] // HEAD
     groups = 2 * heads
     copy = fetch(split, kept_ref, weights_ref, kept_sem, rows)
-    last = last_of(begins_of(lengths_ref), place_ref, rows)
+    last = last_of(begins_of(place_ref), place_ref, rows)
     fetch_all(split, last + 1, copy)
     stack(stacked_ref, (query_ref, query_other_ref))
     total_ref[...] = jnp.zeros_like(total_ref)
@@ -268,30 +290,34 @@
 
 
 def backward_near_kernel(
-    lengths_ref, place_ref, scaled_ref, turned_scaled_ref, delta_ref, begun_ref,
-    query_ref, query_other_ref, pairs_ref, kept_ref, query_grad_ref, query_grad_other_ref, *rest,
+    place_ref, scaled_ref, turned_scaled_ref, delta_ref, begun_ref,
+    query_ref, query_other_ref, pairs_ref, kept_ref, *rest, first, ends,
 ):
-    *block_refs, total_ref, move_ref, stacked_ref, pair_grad_ref, weights_ref, kept_sem = rest
-    rows = query_grad_ref.shape[0]
+    *out_refs, move_ref, stacked_ref, pair_grad_ref, weights_ref, kept_sem = rest
+    rows = query_ref.shape[0]
     groups = turned_scaled_ref.shape[1] // rows
     heads = groups // 2
     root = 1.0 / math.sqrt(HEAD)
-    slots = len(block_refs)
-    stop = jnp.minimum(last_of(begins_of(lengths_ref), place_ref, rows) + 1, slots)
-    copy = fetch(0, kept_ref, weights_ref, kept_sem, rows)
-    fetch_all(0, stop, copy)
+    if ends:
+        query_grad_ref, query_grad_other_ref, *block_refs, total_ref = out_refs
+    else:
+        total_ref, *block_refs = out_refs
+    stop = jnp.minimum(last_of(begins_of(place_ref), place_ref, rows) + 1, first + len(block_refs))
+    copy = fetch(first, kept_ref, weights_ref, kept_sem, rows)
+    fetch_all(first, stop, copy)
     stack(stacked_ref, (query_ref, query_other_ref))
     total_ref[...] = begun_ref[...]
     accumulate(
-        0, stop, pairs_ref, weights_ref, copy, stacked_ref,
-        scaled_ref, turned_scaled_ref, delta_ref, total_ref, move_ref, pair_grad_ref, 0,
+        first, stop, pairs_ref, weights_ref, copy, stacked_ref,
+        scaled_ref, turned_scaled_ref, delta_ref, total_ref, move_ref, pair_grad_ref, first,
     )
     hand_out(pair_grad_ref, block_refs)
-    for group in range(groups):
-        span = slice(group * rows, (group + 1) * rows)
-        column = slice(group % heads * HEAD, (group % heads + 1) * HEAD)
-        to_ref = query_grad_ref if group < heads else query_grad_other_ref
-        to_ref[:, column] = (total_ref[:, span] * root).astype(jnp.bfloat16).T
+    if ends:
+        for group in range(groups):
+            span = slice(group * rows, (group + 1) * rows)
+            column = slice(group % heads * HEAD, (group % heads + 1) * HEAD)
+            to_ref = query_grad_ref if group < heads else query_grad_other_ref
+            to_ref[:, column] = (total_ref[:, span] * root).astype(jnp.bfloat16).T
 
 
 def smem():
@@ -318,7 +344,7 @@
     )
 
 
-def attend(lengths, place, queries, grad, blocks, split, send, swap=swap_cores):
+def attend(place, queries, grad, blocks, split, send, swap=swap_cores):
     slots = len(blocks)
     rows, columns = queries[0].shape
     heads = columns // HEAD
@@ -334,7 +360,7 @@
             jax.ShapeDtypeStruct((8, wide), jnp.float32),
             jax.ShapeDtypeStruct((HEAD + EXTRA, wide), jnp.bfloat16),
         ),
-        in_specs=[smem()] * 2 + [vmem()] * 2 + [hbm()] * slots,
+        in_specs=[smem()] + [hbm(), vmem()] + [hbm()] * slots,
         out_specs=(hbm(),) + (vmem(),) * 4,
         scratch_shapes=[
             pltpu.VMEM((slots * rows, wide), jnp.float32),
@@ -342,13 +368,15 @@
             pltpu.VMEM((slots * rows, wide), jnp.bfloat16),
             pltpu.VMEM((HEAD, wide), jnp.bfloat16),
             pltpu.VMEM((2, 1, rows), jnp.int32),
+            pltpu.VMEM((rows, columns), jnp.bfloat16),
             pltpu.SemaphoreType.DMA((slots,)),
             pltpu.SemaphoreType.DMA((slots,)),
+            pltpu.SemaphoreType.DMA,
         ],
         compiler_params=pltpu.CompilerParams(vmem_limit_bytes=36 << 20),
         cost_estimate=cost(slots, rows, wide, 2),
         name="attend_forward",
-    )(lengths, place, *queries, *blocks)
+    )(place, pltpu.with_memory_space_constraint(queries[0], pltpu.HBM), queries[1], *blocks)
     weights = pltpu.with_memory_space_constraint(weights, pltpu.HBM)
     arrived = swap(sent)
     grad, stats = lax.optimization_barrier((grad, stats))
@@ -376,25 +404,35 @@
             jax.ShapeDtypeStruct((HEAD, wide), jnp.float32),
         )
         + (block,) * (slots - split),
-        in_specs=[smem()] * 2 + [vmem()] * 8 + [hbm()],
+        in_specs=[smem()] + [vmem()] * 8 + [hbm()],
         out_specs=(vmem(),) * (5 + slots - split),
         scratch_shapes=[move] + held(slots - split),
         compiler_params=params,
         cost_estimate=cost(slots - split, rows, wide, 4),
         name="attend_backward_far",
-    )(lengths, place, stats, arrived, acc, grad, grad_other, *queries, pairs, weights)
-    sent_far = send(far)
-    query_grad, query_grad_other, *near = pl.pallas_call(
-        backward_near_kernel,
-        out_shape=(half, half) + (block,) * split,
-        in_specs=[smem()] * 2 + [vmem()] * 7 + [hbm()],
-        out_specs=(vmem(),) * (2 + split),
-        scratch_shapes=[pltpu.VMEM((HEAD, wide), jnp.float32), move] + held(split),
-        compiler_params=params,
-        cost_estimate=cost(split, rows, wide, 4),
-        name="attend_backward_near",
-    )(lengths, place, scaled, turned_scaled, delta, total, *queries, pairs, weights)
-    return out, query_grad, query_grad_other, near, sent_far
+    )(place, stats, arrived, acc, grad, grad_other, *queries, pairs, weights)
+    sent_far = send(far, split)
+    whole = jax.ShapeDtypeStruct((HEAD, wide), jnp.float32)
+
+    def near_call(total, first, count, outs, scratch, ends, name):
+        return pl.pallas_call(
+            functools.partial(backward_near_kernel, first=first, ends=ends),
+            out_shape=outs + (block,) * count,
+            in_specs=[smem()] + [vmem()] * 7 + [hbm()],
+            out_specs=(vmem(),) * (len(outs) + count),
+            scratch_shapes=scratch + [move] + held(count),
+            compiler_params=params,
+            cost_estimate=cost(count, rows, wide, 4),
+            name=name,
+        )(place, scaled, turned_scaled, delta, total, *queries, pairs, weights)
+
+    total, *near = near_call(total, 1, split - 1, (whole,), [], False, "attend_backward_near")
+    sent_near = send(near, 1)
+    query_grad, query_grad_other, own = near_call(
+        total, 0, 1, (half, half), [pltpu.VMEM((HEAD, wide), jnp.float32)], True,
+        "attend_backward_own",
+    )
+    return out, query_grad, query_grad_other, own, sent_near, sent_far
 
 
 def per_device(query, keys_values, doc_lengths, incoming_output_grad):
@@ -414,7 +452,8 @@
     )
     arrived, *blocks[1:3] = lax.optimization_barrier((arrived, *blocks[1:3]))
     grad = lax.all_to_all(arrived, "tensor", split_axis=2, concat_axis=1, tiled=True)[0, :, 0, :]
-    place = jnp.stack([lax.axis_index("chip"), lax.axis_index("core")]).astype(jnp.int32)
+    position = jnp.stack([lax.axis_index("chip"), lax.axis_index("core")]).astype(jnp.int32)
+    place = jnp.concatenate([position, doc_lengths[0]])
     split = (slots + 1) // 2
 
     def send(blocks, first):
@@ -423,19 +462,18 @@
             for at, block in reversed(list(enumerate(blocks)))
         ]
 
-    out, query_grad, query_grad_other, near, far = attend(
-        doc_lengths[0], place, (query, swap_cores(query)), grad, blocks,
-        split, functools.partial(send, first=split),
-    )
-    sums = near[0].astype(jnp.float32)
+    out, query_grad, query_grad_other, own, near, far = attend(
+        place, (query, swap_cores(query)), grad, blocks, split, send
+    )
+    query_grad = query_grad.astype(jnp.float32) + swap_cores(query_grad_other).astype(jnp.float32)
+    query_grad = query_grad.astype(jnp.bfloat16)
+    sums = own.astype(jnp.float32)
     for sent in far:
         sums += sent.astype(jnp.float32)
     sums = lax.optimization_barrier(sums)
-    for sent in send(near[1:], 1):
+    for sent in near:
         sums += sent.astype(jnp.float32)
     pair_grad = sums.astype(jnp.bfloat16)
-    query_grad = query_grad.astype(jnp.float32) + swap_cores(query_grad_other).astype(jnp.float32)
-    query_grad = query_grad.astype(jnp.bfloat16)
     return (out[None, :, None, :], query_grad[None, :, None, :], pair_grad[None, :, None, :])
 
 

time: 100 us -> 97.5 us (0.975)
  the two profiles are of different devices: /device:TPU:249 before, /device:TPU:193 now
where the time goes in v8:
time: 97.5 us; the launch traced here: 96.7 us
  starting transfers between devices  48.7 us (50%)
  waiting for transfers between devices  23.9 us (25%)
  Pallas kernels  18.5 us (19%)
  local copies, waits for them, and re-layouts  2.4 us (2%)
  other arithmetic  2.33 us (2%)
    ppermute x6, starting transfers between devices, per_device(): lax.ppermute(pairs, 'chip', [(c, c + back) for c in range(chips - back)])  17 us
    ppermute x6, waiting for transfers between devices, send(): lax.ppermute(block, 'chip', [(c, c - first - at) for c in range(first + a...  16.1 us
    ppermute x4, starting transfers between devices, swap_cores(): return lax.ppermute(value, 'core', [(0, 1), (1, 0)])  11.5 us
    ppermute x6, starting transfers between devices, send(): lax.ppermute(block, 'chip', [(c, c - first - at) for c in range(first + a...  8.99 us
    pallas_call x2, Pallas kernels, near_call(): pl.pallas_call(functools.partial(backward_near_kernel, first=first, ends=...  8.22 us
    pallas_call x1, Pallas kernels, attend(): pl.pallas_call(forward_kernel, out_shape=(pltpu.HBM((slots * rows, wide),...  7.29 us
    all_to_all x1, starting transfers between devices, per_device(): lax.all_to_all(arrived, 'tensor', split_axis=2, concat_axis=1, tiled=True)  6.82 us
    ppermute x6, waiting for transfers between devices, per_device(): lax.ppermute(pairs, 'chip', [(c, c + back) for c in range(chips - back)])  5.46 us
  transfers between devices with their start and end apart: 18, of which 6 were waited for; matrix products, arithmetic and copies ran while one was open for 2% of the time, Pallas kernels for 16%

profile of v8, /device:TPU:193, one launch (start us, length us, event | category | flops | bytes accessed | tf_op | source)
XLA Modules:
  0.0 96.7 jit_solution(10378313173718809896)
XLA Ops:
  0.6 1.0 %copy.8 = bf16[1,32,8,640]{3,1,0,2:T(8,128)(2,1)S(1)} copy(bf16[1,32,8,640]{3,2,1,0:T(8,128)(2,1)} %param.7) | data formatting | bytes 655360 | tf_op args[3]
  1.6 4.4 %collective-permute-start = (bf16[1,32,8,640]{3,1,0,2:T(8,128)(2,1)S(1)}, bf16[1,32,8,640]{3,1,0,2:T(8,128)(2,1)}, u32[]{:S(2)}, u32[]{:S(2)}) collective-permute-start(bf16[1,32,8,640]{3,1,0,2:T(8,128)(2,1)S(1)} %copy.8), channel_id=1, source_target_pairs={{0,3},{1,0},{2,1},{3,2},{4,7},{5,4},{6,5},{7,6},{8,11},{9,8},{10,9... | collective-permute-start | bytes 983048 | tf_op jit(solution)/shard_map/ppermute | solution.py:450
  6.0 2.9 %collective-permute-start.7 = (bf16[256,640]{1,0:T(8,128)(2,1)}, bf16[256,640]{1,0:T(8,128)(2,1)S(1)}, u32[]{:S(2)}, u32[]{:S(2)}) collective-permute-start(bf16[256,640]{1,0:T(8,128)(2,1)} %bitcast.15), channel_id=1, source_target_pairs={{0,32},{32,0},{1,33},{33,1},{2,34},{34,2},{3,35},{35,3},{4,36},{36... | collective-permute-start | bytes 983048 | tf_op jit(solution)/shard_map/ppermute | solution.py:336
  8.9 6.1 %collective-permute-start.2 = (bf16[256,256]{1,0:T(8,128)(2,1)}, bf16[256,256]{1,0:T(8,128)(2,1)S(1)}, u32[]{:S(2)}, u32[]{:S(2)}) collective-permute-start(bf16[256,256]{1,0:T(8,128)(2,1)} %bitcast.24), channel_id=1, source_target_pairs={{0,128},{64,192},{128,256},{192,320},{256,384},{320,448},{1,129},{... | collective-permute-start | bytes 393224 | tf_op jit(solution)/shard_map/ppermute | solution.py:446
  15.0 3.1 %collective-permute-start.1 = (bf16[256,256]{1,0:T(8,128)(2,1)}, bf16[256,256]{1,0:T(8,128)(2,1)S(1)}, u32[]{:S(2)}, u32[]{:S(2)}) collective-permute-start(bf16[256,256]{1,0:T(8,128)(2,1)} %bitcast.25), channel_id=1, source_target_pairs={{0,64},{64,128},{128,192},{192,256},{256,320},{320,384},{384,448},... | collective-permute-start | bytes 393224 | tf_op jit(solution)/shard_map/ppermute | solution.py:446
  20.0 5.0 %collective-permute-done.1.rest_1_ = bf16[256,256]{1,0:T(8,128)(2,1)S(1)} collective-permute-done((bf16[256,256]{1,0:T(8,128)(2,1)}, bf16[256,256]{1,0:T(8,128)(2,1)S(1)}, u32[]{:S(2)}, u32[]{:S(2)}) %collective-permute-start.1) | collective-permute-done | bytes 131104 | tf_op jit(solution)/shard_map/ppermute | solution.py:446
  25.0 4.3 %collective-permute-start.4 = (bf16[256,256]{1,0:T(8,128)(2,1)}, bf16[256,256]{1,0:T(8,128)(2,1)S(1)}, u32[]{:S(2)}, u32[]{:S(2)}) collective-permute-start(bf16[256,256]{1,0:T(8,128)(2,1)} %bitcast.28), channel_id=1, source_target_pairs={{0,256},{64,320},{128,384},{192,448},{1,257},{65,321},{129,385},{1... | collective-permute-start | bytes 393224 | tf_op jit(solution)/shard_map/ppermute | solution.py:446
  29.2 2.2 %collective-permute-start.3 = (bf16[256,256]{1,0:T(8,128)(2,1)}, bf16[256,256]{1,0:T(8,128)(2,1)S(1)}, u32[]{:S(2)}, u32[]{:S(2)}) collective-permute-start(bf16[256,256]{1,0:T(8,128)(2,1)} %bitcast.29), channel_id=1, source_target_pairs={{0,192},{64,256},{128,320},{192,384},{256,448},{1,193},{65,257},{1... | collective-permute-start | bytes 393224 | tf_op jit(solution)/shard_map/ppermute | solution.py:446
  32.2 6.8 %all-to-all-start = ((bf16[1,32,8,640]{3,1,0,2:T(8,128)(2,1)}), bf16[1,32,8,640]{3,1,0,2:T(8,128)(2,1)S(1)}, u32[]{:S(2)}, u32[]{:S(2)}) async-start(bf16[1,32,8,640]{3,1,0,2:T(8,128)(2,1)} %collective-permute-done), calls=%async_computation | async-start | bytes 655360 | tf_op jit(solution)/shard_map/all_to_all | solution.py:454
  40.4 7.3 %attend_forward.1 = (bf16[1792,2560]{1,0:T(8,128)(2,1)}, bf16[1792,256]{1,0:T(8,128)(2,1)S(1)}, f32[144,2560]{1,0:T(8,128)S(1)}, f32[8,2560]{1,0:T(8,128)S(1)}, bf16[144,2560]{1,0:T(8,128)(2,1)}) custom-call(s32[10]{0:T(128)S(1)} %pad_add_fusion.place_ref, bf16[256,640]{1,0:T(8,128)(2,1)} %bitcast.16, ...), custom_call_target="tpu_custom_call" | custom-call | flops 2348810240 | bytes 9175040 | tf_op jit(solution)/shard_map/attend_forward/pallas_call | solution.py:354
  47.7 2.0 %collective-permute-start.8 = (bf16[144,2560]{1,0:T(8,128)(2,1)}, bf16[144,2560]{1,0:T(8,128)(2,1)}, u32[]{:S(2)}, u32[]{:S(2)}) collective-permute-start(bf16[144,2560]{1,0:T(8,128)(2,1)} %get-tuple-element.51), channel_id=1, source_target_pairs={{0,32},{32,0},{1,33},{33,1},{2,34},{34,2},{3,35},{35,3},{4,36},{36... | collective-permute-start | bytes 2211848 | tf_op jit(solution)/shard_map/ppermute | solution.py:336
  49.7 1.1 %all-to-all-done = bf16[1,32,8,640]{3,1,0,2:T(8,128)(2,1)S(1)} async-done(((bf16[1,32,8,640]{3,1,0,2:T(8,128)(2,1)}), bf16[1,32,8,640]{3,1,0,2:T(8,128)(2,1)S(1)}, u32[]{:S(2)}, u32[]{:S(2)}) %all-to-all-start) | async-done | bytes 327712 | tf_op jit(solution)/shard_map/all_to_all | solution.py:454
  50.8 4.3 %collective-permute-start.9 = (bf16[256,640]{1,0:T(8,128)(2,1)S(1)}, bf16[256,640]{1,0:T(8,128)(2,1)S(1)}, u32[]{:S(2)}, u32[]{:S(2)}) collective-permute-start(bf16[256,640]{1,0:T(8,128)(2,1)S(1)} %bitcast.20), channel_id=1, source_target_pairs={{0,32},{32,0},{1,33},{33,1},{2,34},{34,2},{3,35},{35,3},{4,36},{36... | collective-permute-start | bytes 983048 | tf_op jit(solution)/shard_map/ppermute | solution.py:336
  55.1 1.2 %collective-permute-done.9.grad_other_ref = bf16[256,640]{1,0:T(8,128)(2,1)S(1)} collective-permute-done((bf16[256,640]{1,0:T(8,128)(2,1)S(1)}, bf16[256,640]{1,0:T(8,128)(2,1)S(1)}, u32[]{:S(2)}, u32[]{:S(2)}) %collective-permute-start.9) | collective-permute-done | bytes 327712 | tf_op jit(solution)/shard_map/ppermute | solution.py:336
  56.4 3.0 %attend_backward_far.1 = (bf16[256,640]{1,0:T(8,128)(2,1)}, bf16[2560,128]{1,0:T(8,128)(2,1)S(1)}, bf16[128,2560]{1,0:T(8,128)(2,1)S(1)}, f32[1,2560]{1,0:T(1,12...) custom-call(s32[10]{0:T(128)S(1)} %pad_add_fusion.place_ref, ...), custom_call_target="tpu_custom_call" | custom-call | flops 2013265920 | bytes 3932160 | tf_op jit(solution)/shard_map/attend_backward_far/pallas_call | solution.py:397
  60.7 1.3 %collective-permute-start.13 = (bf16[256,256]{1,0:T(8,128)(2,1)S(1)}, bf16[256,256]{1,0:T(8,128)(2,1)S(1)}, u32[]{:S(2)}, u32[]{:S(2)}) collective-permute-start(bf16[256,256]{1,0:T(8,128)(2,1)S(1)} %get-tuple-element.67), channel_id=1, source_target_pairs={{256,0},{320,64},{384,128},{448,192},{257,1},{321,65},{385,129},{4... | collective-permute-start | bytes 393224 | tf_op jit(solution)/shard_map/ppermute | solution.py:461
  62.0 4.7 %attend_backward_near.1 = (f32[128,2560]{1,0:T(8,128)S(1)}, bf16[256,256]{1,0:T(8,128)(2,1)S(1)}, bf16[256,256]{1,0:T(8,128)(2,1)S(1)}, bf16[256,256]{1,0:T(8,128)(2,1)S(1)}) custom-call(s32[10]{0:T(128)S(1)} %pad_add_fusion.place_ref, bf16[2560,128]{1,0:T(8,128)(2,1)S(1)} %get-tuple-element.57.scaled_ref, ...), custom_call_target="tpu_custom_call" | custom-call | flops 2013265920 | bytes 3932160 | tf_op jit(solution)/shard_map/attend_backward_near/pallas_call | solution.py:418
  66.7 2.3 %collective-permute-start.14 = (bf16[256,256]{1,0:T(8,128)(2,1)S(1)}, bf16[256,256]{1,0:T(8,128)(2,1)S(1)}, u32[]{:S(2)}, u32[]{:S(2)}) collective-permute-start(bf16[256,256]{1,0:T(8,128)(2,1)S(1)} %get-tuple-element.68), channel_id=1, source_target_pairs={{192,0},{256,64},{320,128},{384,192},{448,256},{193,1},{257,65},{3... | collective-permute-start | bytes 393224 | tf_op jit(solution)/shard_map/ppermute | solution.py:461
  69.0 2.1 %collective-permute-start.15 = (bf16[256,256]{1,0:T(8,128)(2,1)S(1)}, bf16[256,256]{1,0:T(8,128)(2,1)S(1)}, u32[]{:S(2)}, u32[]{:S(2)}) collective-permute-start(bf16[256,256]{1,0:T(8,128)(2,1)S(1)} %get-tuple-element.69), channel_id=1, source_target_pairs={{128,0},{192,64},{256,128},{320,192},{384,256},{448,320},{129,1},{... | collective-permute-start | bytes 393224 | tf_op jit(solution)/shard_map/ppermute | solution.py:461
  71.2 3.5 %attend_backward_own.1 = (bf16[256,640]{1,0:T(8,128)(2,1)S(1)}, bf16[256,640]{1,0:T(8,128)(2,1)S(1)}, bf16[256,256]{1,0:T(8,128)(2,1)S(1)}) custom-call(s32[10]{0:T(128)S(1)} %pad_add_fusion.place_ref, bf16[2560,128]{1,0:T(8,128)(2,1)S(1)} %get-tuple-element.57.scaled_ref, bf16[128,2560]{1,0:T(8,128)(2,1)S(1)} %get-tuple-element.58.turned_scaled_ref, ...), custom_call_target="tpu_custom_call" | custom-call | flops 671088640 | bytes 1310720 | tf_op jit(solution)/shard_map/attend_backward_own/pallas_call | solution.py:418
  74.7 1.9 %collective-permute-start.16 = (bf16[256,256]{1,0:T(8,128)(2,1)S(1)}, bf16[256,256]{1,0:T(8,128)(2,1)S(1)}, u32[]{:S(2)}, u32[]{:S(2)}) collective-permute-start(bf16[256,256]{1,0:T(8,128)(2,1)S(1)} %get-tuple-element.70), channel_id=1, source_target_pairs={{64,0},{128,64},{192,128},{256,192},{320,256},{384,320},{448,384},... | collective-permute-start | bytes 393224 | tf_op jit(solution)/shard_map/ppermute | solution.py:461
  76.6 2.3 %collective-permute-start.10 = (bf16[256,640]{1,0:T(8,128)(2,1)S(1)}, bf16[256,640]{1,0:T(8,128)(2,1)S(1)}, u32[]{:S(2)}, u32[]{:S(2)}) collective-permute-start(bf16[256,640]{1,0:T(8,128)(2,1)S(1)} %get-tuple-element.63), channel_id=1, source_target_pairs={{0,32},{32,0},{1,33},{33,1},{2,34},{34,2},{3,35},{35,3},{4,36},{36... | collective-permute-start | bytes 983048 | tf_op jit(solution)/shard_map/ppermute | solution.py:336
  79.1 10.6 %collective-permute-done.14 = bf16[256,256]{1,0:T(8,128)(2,1)S(1)} collective-permute-done((bf16[256,256]{1,0:T(8,128)(2,1)S(1)}, bf16[256,256]{1,0:T(8,128)(2,1)S(1)}, u32[]{:S(2)}, u32[]{:S(2)}) %collective-permute-start.14) | collective-permute-done | bytes 131104 | tf_op jit(solution)/shard_map/ppermute | solution.py:461
  89.7 5.5 %collective-permute-done.15 = bf16[256,256]{1,0:T(8,128)(2,1)S(1)} collective-permute-done((bf16[256,256]{1,0:T(8,128)(2,1)S(1)}, bf16[256,256]{1,0:T(8,128)(2,1)S(1)}, u32[]{:S(2)}, u32[]{:S(2)}) %collective-permute-start.15) | collective-permute-done | bytes 131104 | tf_op jit(solution)/shard_map/ppermute | solution.py:461
  (35 shorter events, 6.9 us)
Async XLA Ops:
  1.6 27.6 %collective-permute-start = (bf16[1,32,8,640]{3,1,0,2:T(8,128)(2,1)S(1)}, bf16[1,32,8,640]{3,1,0,2:T(8,128)(2,1)}, u32[]{:S(2)}, u32[]{:S(2)}) collective-permute-start(bf16[1,32,8,640]{3,1,0,2:T(8,128)(2,1)S(1)} %copy.8), channel_id=1, source_target_pairs={{0,3},{1,0},{2,1},{3,2},{4,7},{5,4},{6,5},{7,6},{8,11},{9,8},{10,9... | collective-permute-start | bytes 983048 | tf_op jit(solution)/shard_map/ppermute | solution.py:450
  6.0 34.4 %collective-permute-start.7 = (bf16[256,640]{1,0:T(8,128)(2,1)}, bf16[256,640]{1,0:T(8,128)(2,1)S(1)}, u32[]{:S(2)}, u32[]{:S(2)}) collective-permute-start(bf16[256,640]{1,0:T(8,128)(2,1)} %bitcast.15), channel_id=1, source_target_pairs={{0,32},{32,0},{1,33},{33,1},{2,34},{34,2},{3,35},{35,3},{4,36},{36... | collective-permute-start | bytes 983048 | tf_op jit(solution)/shard_map/ppermute | solution.py:336
  8.9 10.4 %collective-permute-start.2 = (bf16[256,256]{1,0:T(8,128)(2,1)}, bf16[256,256]{1,0:T(8,128)(2,1)S(1)}, u32[]{:S(2)}, u32[]{:S(2)}) collective-permute-start(bf16[256,256]{1,0:T(8,128)(2,1)} %bitcast.24), channel_id=1, source_target_pairs={{0,128},{64,192},{128,256},{192,320},{256,384},{320,448},{1,129},{... | collective-permute-start | bytes 393224 | tf_op jit(solution)/shard_map/ppermute | solution.py:446
  15.0 9.9 %collective-permute-start.1 = (bf16[256,256]{1,0:T(8,128)(2,1)}, bf16[256,256]{1,0:T(8,128)(2,1)S(1)}, u32[]{:S(2)}, u32[]{:S(2)}) collective-permute-start(bf16[256,256]{1,0:T(8,128)(2,1)} %bitcast.25), channel_id=1, source_target_pairs={{0,64},{64,128},{128,192},{192,256},{256,320},{320,384},{384,448},... | collective-permute-start | bytes 393224 | tf_op jit(solution)/shard_map/ppermute | solution.py:446
  18.2 20.8 %collective-permute-start.6 = (bf16[256,256]{1,0:T(8,128)(2,1)}, bf16[256,256]{1,0:T(8,128)(2,1)S(1)}, u32[]{:S(2)}, u32[]{:S(2)}) collective-permute-start(bf16[256,256]{1,0:T(8,128)(2,1)} %bitcast.26), channel_id=1, source_target_pairs={{0,384},{64,448},{1,385},{65,449},{2,386},{66,450},{3,387},{67,451... | collective-permute-start | bytes 393224 | tf_op jit(solution)/shard_map/ppermute | solution.py:446
  19.3 9.9 %copy-start.1 = (bf16[256,256]{1,0:T(8,128)(2,1)}, bf16[256,256]{1,0:T(8,128)(2,1)S(1)}, u32[]{:S(2)}) copy-start(bf16[256,256]{1,0:T(8,128)(2,1)S(1)} %collective-permute-done.2.rest_2_) | copy-start | bytes 393220
  19.3 19.7 %collective-permute-start.5 = (bf16[256,256]{1,0:T(8,128)(2,1)}, bf16[256,256]{1,0:T(8,128)(2,1)S(1)}, u32[]{:S(2)}, u32[]{:S(2)}) collective-permute-start(bf16[256,256]{1,0:T(8,128)(2,1)} %bitcast.27), channel_id=1, source_target_pairs={{0,320},{64,384},{128,448},{1,321},{65,385},{129,449},{2,322},{66,... | collective-permute-start | bytes 393224 | tf_op jit(solution)/shard_map/ppermute | solution.py:446
  25.0 6.5 %copy-start.2 = (bf16[256,256]{1,0:T(8,128)(2,1)}, bf16[256,256]{1,0:T(8,128)(2,1)S(1)}, u32[]{:S(2)}) copy-start(bf16[256,256]{1,0:T(8,128)(2,1)S(1)} %collective-permute-done.1.rest_1_) | copy-start | bytes 393220
  25.0 14.1 %collective-permute-start.4 = (bf16[256,256]{1,0:T(8,128)(2,1)}, bf16[256,256]{1,0:T(8,128)(2,1)S(1)}, u32[]{:S(2)}, u32[]{:S(2)}) collective-permute-start(bf16[256,256]{1,0:T(8,128)(2,1)} %bitcast.28), channel_id=1, source_target_pairs={{0,256},{64,320},{128,384},{192,448},{1,257},{65,321},{129,385},{1... | collective-permute-start | bytes 393224 | tf_op jit(solution)/shard_map/ppermute | solution.py:446
  29.2 9.8 %collective-permute-start.3 = (bf16[256,256]{1,0:T(8,128)(2,1)}, bf16[256,256]{1,0:T(8,128)(2,1)S(1)}, u32[]{:S(2)}, u32[]{:S(2)}) collective-permute-start(bf16[256,256]{1,0:T(8,128)(2,1)} %bitcast.29), channel_id=1, source_target_pairs={{0,192},{64,256},{128,320},{192,384},{256,448},{1,193},{65,257},{1... | collective-permute-start | bytes 393224 | tf_op jit(solution)/shard_map/ppermute | solution.py:446
  32.2 18.6 %all-to-all-start = ((bf16[1,32,8,640]{3,1,0,2:T(8,128)(2,1)}), bf16[1,32,8,640]{3,1,0,2:T(8,128)(2,1)S(1)}, u32[]{:S(2)}, u32[]{:S(2)}) async-start(bf16[1,32,8,640]{3,1,0,2:T(8,128)(2,1)} %collective-permute-done), calls=%async_computation | async-start | bytes 655360 | tf_op jit(solution)/shard_map/all_to_all | solution.py:454
  39.0 17.4 %copy-start = (bf16[1,256,1,640]{3,1,2,0:T(8,128)(2,1)S(1)}, bf16[1,256,1,640]{3,1,2,0:T(8,128)(2,1)}, u32[]{:S(2)}) copy-start(bf16[1,256,1,640]{3,1,2,0:T(8,128)(2,1)} %param.4) | copy-start | bytes 983044
  39.0 0.7 copy-start.3
  39.0 0.7 copy-start.4
  39.0 0.7 copy-start.5
  47.7 7.4 %collective-permute-start.8 = (bf16[144,2560]{1,0:T(8,128)(2,1)}, bf16[144,2560]{1,0:T(8,128)(2,1)}, u32[]{:S(2)}, u32[]{:S(2)}) collective-permute-start(bf16[144,2560]{1,0:T(8,128)(2,1)} %get-tuple-element.51), channel_id=1, source_target_pairs={{0,32},{32,0},{1,33},{33,1},{2,34},{34,2},{3,35},{35,3},{4,36},{36... | collective-permute-start | bytes 2211848 | tf_op jit(solution)/shard_map/ppermute | solution.py:336
  50.8 5.6 %collective-permute-start.9 = (bf16[256,640]{1,0:T(8,128)(2,1)S(1)}, bf16[256,640]{1,0:T(8,128)(2,1)S(1)}, u32[]{:S(2)}, u32[]{:S(2)}) collective-permute-start(bf16[256,640]{1,0:T(8,128)(2,1)S(1)} %bitcast.20), channel_id=1, source_target_pairs={{0,32},{32,0},{1,33},{33,1},{2,34},{34,2},{3,35},{35,3},{4,36},{36... | collective-permute-start | bytes 983048 | tf_op jit(solution)/shard_map/ppermute | solution.py:336
  59.3 15.3 %collective-permute-start.11 = (bf16[256,256]{1,0:T(8,128)(2,1)S(1)}, bf16[256,256]{1,0:T(8,128)(2,1)S(1)}, u32[]{:S(2)}, u32[]{:S(2)}) collective-permute-start(bf16[256,256]{1,0:T(8,128)(2,1)S(1)} %get-tuple-element.65), channel_id=1, source_target_pairs={{384,0},{448,64},{385,1},{449,65},{386,2},{450,66},{387,3},{451,67... | collective-permute-start | bytes 393224 | tf_op jit(solution)/shard_map/ppermute | solution.py:461
  60.0 16.6 %collective-permute-start.12 = (bf16[256,256]{1,0:T(8,128)(2,1)S(1)}, bf16[256,256]{1,0:T(8,128)(2,1)S(1)}, u32[]{:S(2)}, u32[]{:S(2)}) collective-permute-start(bf16[256,256]{1,0:T(8,128)(2,1)S(1)} %get-tuple-element.66), channel_id=1, source_target_pairs={{320,0},{384,64},{448,128},{321,1},{385,65},{449,129},{322,2},{386... | collective-permute-start | bytes 393224 | tf_op jit(solution)/shard_map/ppermute | solution.py:461
  60.7 18.3 %collective-permute-start.13 = (bf16[256,256]{1,0:T(8,128)(2,1)S(1)}, bf16[256,256]{1,0:T(8,128)(2,1)S(1)}, u32[]{:S(2)}, u32[]{:S(2)}) collective-permute-start(bf16[256,256]{1,0:T(8,128)(2,1)S(1)} %get-tuple-element.67), channel_id=1, source_target_pairs={{256,0},{320,64},{384,128},{448,192},{257,1},{321,65},{385,129},{4... | collective-permute-start | bytes 393224 | tf_op jit(solution)/shard_map/ppermute | solution.py:461
  66.7 22.9 %collective-permute-start.14 = (bf16[256,256]{1,0:T(8,128)(2,1)S(1)}, bf16[256,256]{1,0:T(8,128)(2,1)S(1)}, u32[]{:S(2)}, u32[]{:S(2)}) collective-permute-start(bf16[256,256]{1,0:T(8,128)(2,1)S(1)} %get-tuple-element.68), channel_id=1, source_target_pairs={{192,0},{256,64},{320,128},{384,192},{448,256},{193,1},{257,65},{3... | collective-permute-start | bytes 393224 | tf_op jit(solution)/shard_map/ppermute | solution.py:461
  69.0 26.1 %collective-permute-start.15 = (bf16[256,256]{1,0:T(8,128)(2,1)S(1)}, bf16[256,256]{1,0:T(8,128)(2,1)S(1)}, u32[]{:S(2)}, u32[]{:S(2)}) collective-permute-start(bf16[256,256]{1,0:T(8,128)(2,1)S(1)} %get-tuple-element.69), channel_id=1, source_target_pairs={{128,0},{192,64},{256,128},{320,192},{384,256},{448,320},{129,1},{... | collective-permute-start | bytes 393224 | tf_op jit(solution)/shard_map/ppermute | solution.py:461
  74.7 20.5 %collective-permute-start.16 = (bf16[256,256]{1,0:T(8,128)(2,1)S(1)}, bf16[256,256]{1,0:T(8,128)(2,1)S(1)}, u32[]{:S(2)}, u32[]{:S(2)}) collective-permute-start(bf16[256,256]{1,0:T(8,128)(2,1)S(1)} %get-tuple-element.70), channel_id=1, source_target_pairs={{64,0},{128,64},{192,128},{256,192},{320,256},{384,320},{448,384},... | collective-permute-start | bytes 393224 | tf_op jit(solution)/shard_map/ppermute | solution.py:461
  76.6 19.3 %collective-permute-start.10 = (bf16[256,640]{1,0:T(8,128)(2,1)S(1)}, bf16[256,640]{1,0:T(8,128)(2,1)S(1)}, u32[]{:S(2)}, u32[]{:S(2)}) collective-permute-start(bf16[256,640]{1,0:T(8,128)(2,1)S(1)} %get-tuple-element.63), channel_id=1, source_target_pairs={{0,32},{32,0},{1,33},{33,1},{2,34},{34,2},{3,35},{35,3},{4,36},{36... | collective-permute-start | bytes 983048 | tf_op jit(solution)/shard_map/ppermute | solution.py:336
  (1 other events, 0.7 us)

commit v9 on v8

--- a/solution.py
+++ b/solution.py
@@ -450,7 +450,7 @@
     arrived = lax.ppermute(
         incoming_output_grad, "pipe", [(s, (s - 1) % sections) for s in range(sections)]
     )
-    arrived, *blocks[1:3] = lax.optimization_barrier((arrived, *blocks[1:3]))
+    arrived, *blocks[-2:] = lax.optimization_barrier((arrived, *blocks[-2:]))
     grad = lax.all_to_all(arrived, "tensor", split_axis=2, concat_axis=1, tiled=True)[0, :, 0, :]
     position = jnp.stack([lax.axis_index("chip"), lax.axis_index("core")]).astype(jnp.int32)
     place = jnp.concatenate([position, doc_lengths[0]])

time: 97.5 us -> 110 us (1.13)
  the two profiles are of different devices: /device:TPU:193 before, /device:TPU:1 now
where the time goes in v9:
time: 110 us; the launch traced here: 109 us
  starting transfers between devices  59.3 us (54%)
  waiting for transfers between devices  32.1 us (29%)
  Pallas kernels  12.2 us (11%)
  local copies, waits for them, and re-layouts  2.36 us (2%)
  other arithmetic  2.33 us (2%)
    ppermute x6, starting transfers between devices, per_device(): lax.ppermute(pairs, 'chip', [(c, c + back) for c in range(chips - back)])  21.4 us
    ppermute x4, starting transfers between devices, swap_cores(): return lax.ppermute(value, 'core', [(0, 1), (1, 0)])  18.1 us
    ppermute x6, waiting for transfers between devices, per_device(): lax.ppermute(pairs, 'chip', [(c, c + back) for c in range(chips - back)])  16.2 us
    ppermute x6, waiting for transfers between devices, send(): lax.ppermute(block, 'chip', [(c, c - first - at) for c in range(first + a...  14.7 us
    ppermute x6, starting transfers between devices, send(): lax.ppermute(block, 'chip', [(c, c - first - at) for c in range(first + a...  7.74 us
    all_to_all x1, starting transfers between devices, per_device(): lax.all_to_all(arrived, 'tensor', split_axis=2, concat_axis=1, tiled=True)  6.82 us
    ppermute x1, starting transfers between devices, per_device(): lax.ppermute(incoming_output_grad, 'pipe', [(s, (s - 1) % sections) for s...  5.22 us
    pallas_call x1, Pallas kernels, attend(): pl.pallas_call(forward_kernel, out_shape=(pltpu.HBM((slots * rows, wide),...  4.9 us
  transfers between devices with their start and end apart: 18, of which 6 were waited for; matrix products, arithmetic and copies ran while one was open for 1% of the time, Pallas kernels for 8%

profile of v9, /device:TPU:1, one launch (start us, length us, event | category | flops | bytes accessed | tf_op | source)
XLA Modules:
  0.0 109.3 jit_solution(3459370836718063782)
XLA Ops:
  1.6 5.2 %collective-permute-start = (bf16[1,32,8,640]{3,1,0,2:T(8,128)(2,1)S(1)}, bf16[1,32,8,640]{3,1,0,2:T(8,128)(2,1)}, u32[]{:S(2)}, u32[]{:S(2)}) collective-permute-start(bf16[1,32,8,640]{3,1,0,2:T(8,128)(2,1)S(1)} %copy.8), channel_id=1, source_target_pairs={{0,3},{1,0},{2,1},{3,2},{4,7},{5,4},{6,5},{7,6},{8,11},{9,8},{10,9... | collective-permute-start | bytes 983048 | tf_op jit(solution)/shard_map/ppermute | solution.py:450
  6.9 5.5 %collective-permute-start.7 = (bf16[256,640]{1,0:T(8,128)(2,1)}, bf16[256,640]{1,0:T(8,128)(2,1)S(1)}, u32[]{:S(2)}, u32[]{:S(2)}) collective-permute-start(bf16[256,640]{1,0:T(8,128)(2,1)} %bitcast.15), channel_id=1, source_target_pairs={{0,32},{32,0},{1,33},{33,1},{2,34},{34,2},{3,35},{35,3},{4,36},{36... | collective-permute-start | bytes 983048 | tf_op jit(solution)/shard_map/ppermute | solution.py:336
  12.4 8.0 %collective-permute-start.2 = (bf16[256,256]{1,0:T(8,128)(2,1)}, bf16[256,256]{1,0:T(8,128)(2,1)S(1)}, u32[]{:S(2)}, u32[]{:S(2)}) collective-permute-start(bf16[256,256]{1,0:T(8,128)(2,1)} %bitcast.24), channel_id=1, source_target_pairs={{0,384},{64,448},{1,385},{65,449},{2,386},{66,450},{3,387},{67,451... | collective-permute-start | bytes 393224 | tf_op jit(solution)/shard_map/ppermute | solution.py:446
  20.4 1.3 %collective-permute-start.1 = (bf16[256,256]{1,0:T(8,128)(2,1)}, bf16[256,256]{1,0:T(8,128)(2,1)S(1)}, u32[]{:S(2)}, u32[]{:S(2)}) collective-permute-start(bf16[256,256]{1,0:T(8,128)(2,1)} %bitcast.25), channel_id=1, source_target_pairs={{0,320},{64,384},{128,448},{1,321},{65,385},{129,449},{2,322},{66,... | collective-permute-start | bytes 393224 | tf_op jit(solution)/shard_map/ppermute | solution.py:446
  21.7 1.3 %collective-permute-start.6 = (bf16[256,256]{1,0:T(8,128)(2,1)}, bf16[256,256]{1,0:T(8,128)(2,1)S(1)}, u32[]{:S(2)}, u32[]{:S(2)}) collective-permute-start(bf16[256,256]{1,0:T(8,128)(2,1)} %bitcast.26), channel_id=1, source_target_pairs={{0,256},{64,320},{128,384},{192,448},{1,257},{65,321},{129,385},{1... | collective-permute-start | bytes 393224 | tf_op jit(solution)/shard_map/ppermute | solution.py:446
  23.0 14.5 %collective-permute-done.2.rest_6_ = bf16[256,256]{1,0:T(8,128)(2,1)S(1)} collective-permute-done((bf16[256,256]{1,0:T(8,128)(2,1)}, bf16[256,256]{1,0:T(8,128)(2,1)S(1)}, u32[]{:S(2)}, u32[]{:S(2)}) %collective-permute-start.2) | collective-permute-done | bytes 131104 | tf_op jit(solution)/shard_map/ppermute | solution.py:446
  37.5 1.3 %collective-permute-start.5 = (bf16[256,256]{1,0:T(8,128)(2,1)}, bf16[256,256]{1,0:T(8,128)(2,1)S(1)}, u32[]{:S(2)}, u32[]{:S(2)}) collective-permute-start(bf16[256,256]{1,0:T(8,128)(2,1)} %bitcast.27), channel_id=1, source_target_pairs={{0,192},{64,256},{128,320},{192,384},{256,448},{1,193},{65,257},{1... | collective-permute-start | bytes 393224 | tf_op jit(solution)/shard_map/ppermute | solution.py:446
  38.8 1.7 %collective-permute-done.1.rest_5_ = bf16[256,256]{1,0:T(8,128)(2,1)S(1)} collective-permute-done((bf16[256,256]{1,0:T(8,128)(2,1)}, bf16[256,256]{1,0:T(8,128)(2,1)S(1)}, u32[]{:S(2)}, u32[]{:S(2)}) %collective-permute-start.1) | collective-permute-done | bytes 131104 | tf_op jit(solution)/shard_map/ppermute | solution.py:446
  41.8 8.2 %collective-permute-start.3 = (bf16[256,256]{1,0:T(8,128)(2,1)}, bf16[256,256]{1,0:T(8,128)(2,1)S(1)}, u32[]{:S(2)}, u32[]{:S(2)}) collective-permute-start(bf16[256,256]{1,0:T(8,128)(2,1)} %bitcast.29), channel_id=1, source_target_pairs={{0,64},{64,128},{128,192},{192,256},{256,320},{320,384},{384,448},... | collective-permute-start | bytes 393224 | tf_op jit(solution)/shard_map/ppermute | solution.py:446
  50.8 6.8 %all-to-all-start = ((bf16[1,32,8,640]{3,1,0,2:T(8,128)(2,1)}), bf16[1,32,8,640]{3,1,0,2:T(8,128)(2,1)S(1)}, u32[]{:S(2)}, u32[]{:S(2)}) async-start(bf16[1,32,8,640]{3,1,0,2:T(8,128)(2,1)} %collective-permute-done), calls=%async_computation | async-start | bytes 655360 | tf_op jit(solution)/shard_map/all_to_all | solution.py:454
  59.0 4.9 %attend_forward.1 = (bf16[1792,2560]{1,0:T(8,128)(2,1)}, bf16[1792,256]{1,0:T(8,128)(2,1)S(1)}, f32[144,2560]{1,0:T(8,128)S(1)}, f32[8,2560]{1,0:T(8,128)S(1)}, bf16[144,2560]{1,0:T(8,128)(2,1)}) custom-call(s32[10]{0:T(128)S(1)} %pad_add_fusion.place_ref, bf16[256,640]{1,0:T(8,128)(2,1)} %bitcast.16, ...), custom_call_target="tpu_custom_call" | custom-call | flops 2348810240 | bytes 9175040 | tf_op jit(solution)/shard_map/attend_forward/pallas_call | solution.py:354
  63.9 4.2 %collective-permute-start.8 = (bf16[144,2560]{1,0:T(8,128)(2,1)}, bf16[144,2560]{1,0:T(8,128)(2,1)}, u32[]{:S(2)}, u32[]{:S(2)}) collective-permute-start(bf16[144,2560]{1,0:T(8,128)(2,1)} %get-tuple-element.51), channel_id=1, source_target_pairs={{0,32},{32,0},{1,33},{33,1},{2,34},{34,2},{3,35},{35,3},{4,36},{36... | collective-permute-start | bytes 2211848 | tf_op jit(solution)/shard_map/ppermute | solution.py:336
  68.2 5.6 %collective-permute-start.9 = (bf16[256,640]{1,0:T(8,128)(2,1)S(1)}, bf16[256,640]{1,0:T(8,128)(2,1)S(1)}, u32[]{:S(2)}, u32[]{:S(2)}) collective-permute-start(bf16[256,640]{1,0:T(8,128)(2,1)S(1)} %bitcast.20), channel_id=1, source_target_pairs={{0,32},{32,0},{1,33},{33,1},{2,34},{34,2},{3,35},{35,3},{4,36},{36... | collective-permute-start | bytes 983048 | tf_op jit(solution)/shard_map/ppermute | solution.py:336
  75.0 3.0 %attend_backward_far.1 = (bf16[256,640]{1,0:T(8,128)(2,1)}, bf16[2560,128]{1,0:T(8,128)(2,1)S(1)}, bf16[128,2560]{1,0:T(8,128)(2,1)S(1)}, f32[1,2560]{1,0:T(1,12...) custom-call(s32[10]{0:T(128)S(1)} %pad_add_fusion.place_ref, ...), custom_call_target="tpu_custom_call" | custom-call | flops 2013265920 | bytes 3932160 | tf_op jit(solution)/shard_map/attend_backward_far/pallas_call | solution.py:397
  78.0 1.3 %collective-permute-start.11 = (bf16[256,256]{1,0:T(8,128)(2,1)S(1)}, bf16[256,256]{1,0:T(8,128)(2,1)S(1)}, u32[]{:S(2)}, u32[]{:S(2)}) collective-permute-start(bf16[256,256]{1,0:T(8,128)(2,1)S(1)} %get-tuple-element.65), channel_id=1, source_target_pairs={{384,0},{448,64},{385,1},{449,65},{386,2},{450,66},{387,3},{451,67... | collective-permute-start | bytes 393224 | tf_op jit(solution)/shard_map/ppermute | solution.py:461
  79.3 1.3 %collective-permute-start.12 = (bf16[256,256]{1,0:T(8,128)(2,1)S(1)}, bf16[256,256]{1,0:T(8,128)(2,1)S(1)}, u32[]{:S(2)}, u32[]{:S(2)}) collective-permute-start(bf16[256,256]{1,0:T(8,128)(2,1)S(1)} %get-tuple-element.66), channel_id=1, source_target_pairs={{320,0},{384,64},{448,128},{321,1},{385,65},{449,129},{322,2},{386... | collective-permute-start | bytes 393224 | tf_op jit(solution)/shard_map/ppermute | solution.py:461
  80.6 1.3 %collective-permute-start.13 = (bf16[256,256]{1,0:T(8,128)(2,1)S(1)}, bf16[256,256]{1,0:T(8,128)(2,1)S(1)}, u32[]{:S(2)}, u32[]{:S(2)}) collective-permute-start(bf16[256,256]{1,0:T(8,128)(2,1)S(1)} %get-tuple-element.67), channel_id=1, source_target_pairs={{256,0},{320,64},{384,128},{448,192},{257,1},{321,65},{385,129},{4... | collective-permute-start | bytes 393224 | tf_op jit(solution)/shard_map/ppermute | solution.py:461
  82.7 1.3 %collective-permute-start.14 = (bf16[256,256]{1,0:T(8,128)(2,1)S(1)}, bf16[256,256]{1,0:T(8,128)(2,1)S(1)}, u32[]{:S(2)}, u32[]{:S(2)}) collective-permute-start(bf16[256,256]{1,0:T(8,128)(2,1)S(1)} %get-tuple-element.68), channel_id=1, source_target_pairs={{192,0},{256,64},{320,128},{384,192},{448,256},{193,1},{257,65},{3... | collective-permute-start | bytes 393224 | tf_op jit(solution)/shard_map/ppermute | solution.py:461
  84.0 1.3 %collective-permute-start.15 = (bf16[256,256]{1,0:T(8,128)(2,1)S(1)}, bf16[256,256]{1,0:T(8,128)(2,1)S(1)}, u32[]{:S(2)}, u32[]{:S(2)}) collective-permute-start(bf16[256,256]{1,0:T(8,128)(2,1)S(1)} %get-tuple-element.69), channel_id=1, source_target_pairs={{128,0},{192,64},{256,128},{320,192},{384,256},{448,320},{129,1},{... | collective-permute-start | bytes 393224 | tf_op jit(solution)/shard_map/ppermute | solution.py:461
  85.3 3.5 %attend_backward_own.1 = (bf16[256,640]{1,0:T(8,128)(2,1)S(1)}, bf16[256,640]{1,0:T(8,128)(2,1)S(1)}, bf16[256,256]{1,0:T(8,128)(2,1)S(1)}) custom-call(s32[10]{0:T(128)S(1)} %pad_add_fusion.place_ref, bf16[2560,128]{1,0:T(8,128)(2,1)S(1)} %get-tuple-element.57.scaled_ref, bf16[128,2560]{1,0:T(8,128)(2,1)S(1)} %get-tuple-element.58.turned_scaled_ref, ...), custom_call_target="tpu_custom_call" | custom-call | flops 671088640 | bytes 1310720 | tf_op jit(solution)/shard_map/attend_backward_own/pallas_call | solution.py:418
  88.8 4.7 %collective-permute-done.11 = bf16[256,256]{1,0:T(8,128)(2,1)S(1)} collective-permute-done((bf16[256,256]{1,0:T(8,128)(2,1)S(1)}, bf16[256,256]{1,0:T(8,128)(2,1)S(1)}, u32[]{:S(2)}, u32[]{:S(2)}) %collective-permute-start.11) | collective-permute-done | bytes 131104 | tf_op jit(solution)/shard_map/ppermute | solution.py:461
  94.8 2.8 %collective-permute-start.10 = (bf16[256,640]{1,0:T(8,128)(2,1)S(1)}, bf16[256,640]{1,0:T(8,128)(2,1)S(1)}, u32[]{:S(2)}, u32[]{:S(2)}) collective-permute-start(bf16[256,640]{1,0:T(8,128)(2,1)S(1)} %get-tuple-element.63), channel_id=1, source_target_pairs={{0,32},{32,0},{1,33},{33,1},{2,34},{34,2},{3,35},{35,3},{4,36},{36... | collective-permute-start | bytes 983048 | tf_op jit(solution)/shard_map/ppermute | solution.py:336
  97.7 5.1 %collective-permute-done.15 = bf16[256,256]{1,0:T(8,128)(2,1)S(1)} collective-permute-done((bf16[256,256]{1,0:T(8,128)(2,1)S(1)}, bf16[256,256]{1,0:T(8,128)(2,1)S(1)}, u32[]{:S(2)}, u32[]{:S(2)}) %collective-permute-start.15) | collective-permute-done | bytes 131104 | tf_op jit(solution)/shard_map/ppermute | solution.py:461
  102.9 4.9 %collective-permute-done.16 = bf16[256,256]{1,0:T(8,128)(2,1)S(1)} collective-permute-done((bf16[256,256]{1,0:T(8,128)(2,1)S(1)}, bf16[256,256]{1,0:T(8,128)(2,1)S(1)}, u32[]{:S(2)}, u32[]{:S(2)}) %collective-permute-start.16) | collective-permute-done | bytes 131104 | tf_op jit(solution)/shard_map/ppermute | solution.py:461
  (35 shorter events, 9.4 us)
Async XLA Ops:
  1.6 40.1 %collective-permute-start = (bf16[1,32,8,640]{3,1,0,2:T(8,128)(2,1)S(1)}, bf16[1,32,8,640]{3,1,0,2:T(8,128)(2,1)}, u32[]{:S(2)}, u32[]{:S(2)}) collective-permute-start(bf16[1,32,8,640]{3,1,0,2:T(8,128)(2,1)S(1)} %copy.8), channel_id=1, source_target_pairs={{0,3},{1,0},{2,1},{3,2},{4,7},{5,4},{6,5},{7,6},{8,11},{9,8},{10,9... | collective-permute-start | bytes 983048 | tf_op jit(solution)/shard_map/ppermute | solution.py:450
  6.9 52.1 %collective-permute-start.7 = (bf16[256,640]{1,0:T(8,128)(2,1)}, bf16[256,640]{1,0:T(8,128)(2,1)S(1)}, u32[]{:S(2)}, u32[]{:S(2)}) collective-permute-start(bf16[256,640]{1,0:T(8,128)(2,1)} %bitcast.15), channel_id=1, source_target_pairs={{0,32},{32,0},{1,33},{33,1},{2,34},{34,2},{3,35},{35,3},{4,36},{36... | collective-permute-start | bytes 983048 | tf_op jit(solution)/shard_map/ppermute | solution.py:336
  12.4 25.2 %collective-permute-start.2 = (bf16[256,256]{1,0:T(8,128)(2,1)}, bf16[256,256]{1,0:T(8,128)(2,1)S(1)}, u32[]{:S(2)}, u32[]{:S(2)}) collective-permute-start(bf16[256,256]{1,0:T(8,128)(2,1)} %bitcast.24), channel_id=1, source_target_pairs={{0,384},{64,448},{1,385},{65,449},{2,386},{66,450},{3,387},{67,451... | collective-permute-start | bytes 393224 | tf_op jit(solution)/shard_map/ppermute | solution.py:446
  20.4 20.1 %collective-permute-start.1 = (bf16[256,256]{1,0:T(8,128)(2,1)}, bf16[256,256]{1,0:T(8,128)(2,1)S(1)}, u32[]{:S(2)}, u32[]{:S(2)}) collective-permute-start(bf16[256,256]{1,0:T(8,128)(2,1)} %bitcast.25), channel_id=1, source_target_pairs={{0,320},{64,384},{128,448},{1,321},{65,385},{129,449},{2,322},{66,... | collective-permute-start | bytes 393224 | tf_op jit(solution)/shard_map/ppermute | solution.py:446
  21.7 35.9 %collective-permute-start.6 = (bf16[256,256]{1,0:T(8,128)(2,1)}, bf16[256,256]{1,0:T(8,128)(2,1)S(1)}, u32[]{:S(2)}, u32[]{:S(2)}) collective-permute-start(bf16[256,256]{1,0:T(8,128)(2,1)} %bitcast.26), channel_id=1, source_target_pairs={{0,256},{64,320},{128,384},{192,448},{1,257},{65,321},{129,385},{1... | collective-permute-start | bytes 393224 | tf_op jit(solution)/shard_map/ppermute | solution.py:446
  37.5 4.3 %copy-start.1 = (bf16[256,256]{1,0:T(8,128)(2,1)}, bf16[256,256]{1,0:T(8,128)(2,1)S(1)}, u32[]{:S(2)}) copy-start(bf16[256,256]{1,0:T(8,128)(2,1)S(1)} %collective-permute-done.2.rest_6_) | copy-start | bytes 393220
  37.5 20.1 %collective-permute-start.5 = (bf16[256,256]{1,0:T(8,128)(2,1)}, bf16[256,256]{1,0:T(8,128)(2,1)S(1)}, u32[]{:S(2)}, u32[]{:S(2)}) collective-permute-start(bf16[256,256]{1,0:T(8,128)(2,1)} %bitcast.27), channel_id=1, source_target_pairs={{0,192},{64,256},{128,320},{192,384},{256,448},{1,193},{65,257},{1... | collective-permute-start | bytes 393224 | tf_op jit(solution)/shard_map/ppermute | solution.py:446
  40.5 9.6 %copy-start.2 = (bf16[256,256]{1,0:T(8,128)(2,1)}, bf16[256,256]{1,0:T(8,128)(2,1)S(1)}, u32[]{:S(2)}) copy-start(bf16[256,256]{1,0:T(8,128)(2,1)S(1)} %collective-permute-done.1.rest_5_) | copy-start | bytes 393220
  40.5 17.2 %collective-permute-start.4 = (bf16[256,256]{1,0:T(8,128)(2,1)}, bf16[256,256]{1,0:T(8,128)(2,1)S(1)}, u32[]{:S(2)}, u32[]{:S(2)}) collective-permute-start(bf16[256,256]{1,0:T(8,128)(2,1)} %bitcast.28), channel_id=1, source_target_pairs={{0,128},{64,192},{128,256},{192,320},{256,384},{320,448},{1,129},{... | collective-permute-start | bytes 393224 | tf_op jit(solution)/shard_map/ppermute | solution.py:446
  41.8 15.9 %collective-permute-start.3 = (bf16[256,256]{1,0:T(8,128)(2,1)}, bf16[256,256]{1,0:T(8,128)(2,1)S(1)}, u32[]{:S(2)}, u32[]{:S(2)}) collective-permute-start(bf16[256,256]{1,0:T(8,128)(2,1)} %bitcast.29), channel_id=1, source_target_pairs={{0,64},{64,128},{128,192},{192,256},{256,320},{320,384},{384,448},... | collective-permute-start | bytes 393224 | tf_op jit(solution)/shard_map/ppermute | solution.py:446
  50.8 17.4 %all-to-all-start = ((bf16[1,32,8,640]{3,1,0,2:T(8,128)(2,1)}), bf16[1,32,8,640]{3,1,0,2:T(8,128)(2,1)S(1)}, u32[]{:S(2)}, u32[]{:S(2)}) async-start(bf16[1,32,8,640]{3,1,0,2:T(8,128)(2,1)} %collective-permute-done), calls=%async_computation | async-start | bytes 655360 | tf_op jit(solution)/shard_map/all_to_all | solution.py:454
  57.6 17.4 %copy-start = (bf16[1,256,1,640]{3,1,2,0:T(8,128)(2,1)S(1)}, bf16[1,256,1,640]{3,1,2,0:T(8,128)(2,1)}, u32[]{:S(2)}) copy-start(bf16[1,256,1,640]{3,1,2,0:T(8,128)(2,1)} %param.4) | copy-start | bytes 983044
  57.6 0.7 copy-start.4
  57.7 0.7 copy-start.5
  58.4 0.7 copy-start.6
  63.9 9.8 %collective-permute-start.8 = (bf16[144,2560]{1,0:T(8,128)(2,1)}, bf16[144,2560]{1,0:T(8,128)(2,1)}, u32[]{:S(2)}, u32[]{:S(2)}) collective-permute-start(bf16[144,2560]{1,0:T(8,128)(2,1)} %get-tuple-element.51), channel_id=1, source_target_pairs={{0,32},{32,0},{1,33},{33,1},{2,34},{34,2},{3,35},{35,3},{4,36},{36... | collective-permute-start | bytes 2211848 | tf_op jit(solution)/shard_map/ppermute | solution.py:336
  68.2 6.8 %collective-permute-start.9 = (bf16[256,640]{1,0:T(8,128)(2,1)S(1)}, bf16[256,640]{1,0:T(8,128)(2,1)S(1)}, u32[]{:S(2)}, u32[]{:S(2)}) collective-permute-start(bf16[256,640]{1,0:T(8,128)(2,1)S(1)} %bitcast.20), channel_id=1, source_target_pairs={{0,32},{32,0},{1,33},{33,1},{2,34},{34,2},{3,35},{35,3},{4,36},{36... | collective-permute-start | bytes 983048 | tf_op jit(solution)/shard_map/ppermute | solution.py:336
  78.0 15.5 %collective-permute-start.11 = (bf16[256,256]{1,0:T(8,128)(2,1)S(1)}, bf16[256,256]{1,0:T(8,128)(2,1)S(1)}, u32[]{:S(2)}, u32[]{:S(2)}) collective-permute-start(bf16[256,256]{1,0:T(8,128)(2,1)S(1)} %get-tuple-element.65), channel_id=1, source_target_pairs={{384,0},{448,64},{385,1},{449,65},{386,2},{450,66},{387,3},{451,67... | collective-permute-start | bytes 393224 | tf_op jit(solution)/shard_map/ppermute | solution.py:461
  79.3 15.5 %collective-permute-start.12 = (bf16[256,256]{1,0:T(8,128)(2,1)S(1)}, bf16[256,256]{1,0:T(8,128)(2,1)S(1)}, u32[]{:S(2)}, u32[]{:S(2)}) collective-permute-start(bf16[256,256]{1,0:T(8,128)(2,1)S(1)} %get-tuple-element.66), channel_id=1, source_target_pairs={{320,0},{384,64},{448,128},{321,1},{385,65},{449,129},{322,2},{386... | collective-permute-start | bytes 393224 | tf_op jit(solution)/shard_map/ppermute | solution.py:461
  80.6 17.1 %collective-permute-start.13 = (bf16[256,256]{1,0:T(8,128)(2,1)S(1)}, bf16[256,256]{1,0:T(8,128)(2,1)S(1)}, u32[]{:S(2)}, u32[]{:S(2)}) collective-permute-start(bf16[256,256]{1,0:T(8,128)(2,1)S(1)} %get-tuple-element.67), channel_id=1, source_target_pairs={{256,0},{320,64},{384,128},{448,192},{257,1},{321,65},{385,129},{4... | collective-permute-start | bytes 393224 | tf_op jit(solution)/shard_map/ppermute | solution.py:461
  82.7 15.0 %collective-permute-start.14 = (bf16[256,256]{1,0:T(8,128)(2,1)S(1)}, bf16[256,256]{1,0:T(8,128)(2,1)S(1)}, u32[]{:S(2)}, u32[]{:S(2)}) collective-permute-start(bf16[256,256]{1,0:T(8,128)(2,1)S(1)} %get-tuple-element.68), channel_id=1, source_target_pairs={{192,0},{256,64},{320,128},{384,192},{448,256},{193,1},{257,65},{3... | collective-permute-start | bytes 393224 | tf_op jit(solution)/shard_map/ppermute | solution.py:461
  84.0 18.9 %collective-permute-start.15 = (bf16[256,256]{1,0:T(8,128)(2,1)S(1)}, bf16[256,256]{1,0:T(8,128)(2,1)S(1)}, u32[]{:S(2)}, u32[]{:S(2)}) collective-permute-start(bf16[256,256]{1,0:T(8,128)(2,1)S(1)} %get-tuple-element.69), channel_id=1, source_target_pairs={{128,0},{192,64},{256,128},{320,192},{384,256},{448,320},{129,1},{... | collective-permute-start | bytes 393224 | tf_op jit(solution)/shard_map/ppermute | solution.py:461
  93.5 14.3 %collective-permute-start.16 = (bf16[256,256]{1,0:T(8,128)(2,1)S(1)}, bf16[256,256]{1,0:T(8,128)(2,1)S(1)}, u32[]{:S(2)}, u32[]{:S(2)}) collective-permute-start(bf16[256,256]{1,0:T(8,128)(2,1)S(1)} %get-tuple-element.70), channel_id=1, source_target_pairs={{64,0},{128,64},{192,128},{256,192},{320,256},{384,320},{448,384},... | collective-permute-start | bytes 393224 | tf_op jit(solution)/shard_map/ppermute | solution.py:461
  94.8 13.7 %collective-permute-start.10 = (bf16[256,640]{1,0:T(8,128)(2,1)S(1)}, bf16[256,640]{1,0:T(8,128)(2,1)S(1)}, u32[]{:S(2)}, u32[]{:S(2)}) collective-permute-start(bf16[256,640]{1,0:T(8,128)(2,1)S(1)} %get-tuple-element.63), channel_id=1, source_target_pairs={{0,32},{32,0},{1,33},{33,1},{2,34},{34,2},{3,35},{35,3},{4,36},{36... | collective-permute-start | bytes 983048 | tf_op jit(solution)/shard_map/ppermute | solution.py:336
  (1 other events, 0.6 us)

commit v10 on v8

--- a/solution.py
+++ b/solution.py
@@ -426,12 +426,11 @@
             name=name,
         )(place, scaled, turned_scaled, delta, total, *queries, pairs, weights)
 
-    total, *near = near_call(total, 1, split - 1, (whole,), [], False, "attend_backward_near")
+    query_grad, query_grad_other, own, *near = near_call(
+        total, 0, split, (half, half), [pltpu.VMEM((HEAD, wide), jnp.float32)], True,
+        "attend_backward_near",
+    )
     sent_near = send(near, 1)
-    query_grad, query_grad_other, own = near_call(
-        total, 0, 1, (half, half), [pltpu.VMEM((HEAD, wide), jnp.float32)], True,
-        "attend_backward_own",
-    )
     return out, query_grad, query_grad_other, own, sent_near, sent_far
 
 

time: 97.5 us -> 98 us (level)
  the two profiles are of different devices: /device:TPU:193 before, /device:TPU:206 now
where the time goes in v10:
time: 98 us; the launch traced here: 97.3 us
  starting transfers between devices  47.8 us (49%)
  waiting for transfers between devices  24.7 us (25%)
  Pallas kernels  19.2 us (20%)
  local copies, waits for them, and re-layouts  2.4 us (2%)
  other arithmetic  2.33 us (2%)
    ppermute x6, waiting for transfers between devices, send(): lax.ppermute(block, 'chip', [(c, c - first - at) for c in range(first + a...  18.1 us
    ppermute x6, starting transfers between devices, per_device(): lax.ppermute(pairs, 'chip', [(c, c + back) for c in range(chips - back)])  17.8 us
    ppermute x6, starting transfers between devices, send(): lax.ppermute(block, 'chip', [(c, c - first - at) for c in range(first + a...  11.4 us
    pallas_call x1, Pallas kernels, attend(): pl.pallas_call(forward_kernel, out_shape=(pltpu.HBM((slots * rows, wide),...  8.43 us
    ppermute x4, starting transfers between devices, swap_cores(): return lax.ppermute(value, 'core', [(0, 1), (1, 0)])  8.24 us
    pallas_call x1, Pallas kernels, near_call(): pl.pallas_call(functools.partial(backward_near_kernel, first=first, ends=...  7.81 us
    all_to_all x1, starting transfers between devices, per_device(): lax.all_to_all(arrived, 'tensor', split_axis=2, concat_axis=1, tiled=True)  7.55 us
    ppermute x6, waiting for transfers between devices, per_device(): lax.ppermute(pairs, 'chip', [(c, c + back) for c in range(chips - back)])  5.33 us
  transfers between devices with their start and end apart: 18, of which 6 were waited for; matrix products, arithmetic and copies ran while one was open for 2% of the time, Pallas kernels for 17%

profile of v10, /device:TPU:206, one launch (start us, length us, event | category | flops | bytes accessed | tf_op | source)
XLA Modules:
  0.0 97.3 jit_solution(14776006231724733191)
XLA Ops:
  0.6 1.0 %copy.8 = bf16[1,32,8,640]{3,1,0,2:T(8,128)(2,1)S(1)} copy(bf16[1,32,8,640]{3,2,1,0:T(8,128)(2,1)} %param.7) | data formatting | bytes 655360 | tf_op args[3]
  1.6 2.7 %collective-permute-start = (bf16[1,32,8,640]{3,1,0,2:T(8,128)(2,1)S(1)}, bf16[1,32,8,640]{3,1,0,2:T(8,128)(2,1)}, u32[]{:S(2)}, u32[]{:S(2)}) collective-permute-start(bf16[1,32,8,640]{3,1,0,2:T(8,128)(2,1)S(1)} %copy.8), channel_id=1, source_target_pairs={{0,3},{1,0},{2,1},{3,2},{4,7},{5,4},{6,5},{7,6},{8,11},{9,8},{10,9... | collective-permute-start | bytes 983048 | tf_op jit(solution)/shard_map/ppermute | solution.py:449
  4.4 1.9 %collective-permute-start.7 = (bf16[256,640]{1,0:T(8,128)(2,1)}, bf16[256,640]{1,0:T(8,128)(2,1)S(1)}, u32[]{:S(2)}, u32[]{:S(2)}) collective-permute-start(bf16[256,640]{1,0:T(8,128)(2,1)} %bitcast.15), channel_id=1, source_target_pairs={{0,32},{32,0},{1,33},{33,1},{2,34},{34,2},{3,35},{35,3},{4,36},{36... | collective-permute-start | bytes 983048 | tf_op jit(solution)/shard_map/ppermute | solution.py:336
  6.3 6.4 %collective-permute-start.2 = (bf16[256,256]{1,0:T(8,128)(2,1)}, bf16[256,256]{1,0:T(8,128)(2,1)S(1)}, u32[]{:S(2)}, u32[]{:S(2)}) collective-permute-start(bf16[256,256]{1,0:T(8,128)(2,1)} %bitcast.23), channel_id=1, source_target_pairs={{0,128},{64,192},{128,256},{192,320},{256,384},{320,448},{1,129},{... | collective-permute-start | bytes 393224 | tf_op jit(solution)/shard_map/ppermute | solution.py:445
  12.7 3.4 %collective-permute-start.1 = (bf16[256,256]{1,0:T(8,128)(2,1)}, bf16[256,256]{1,0:T(8,128)(2,1)S(1)}, u32[]{:S(2)}, u32[]{:S(2)}) collective-permute-start(bf16[256,256]{1,0:T(8,128)(2,1)} %bitcast.24), channel_id=1, source_target_pairs={{0,64},{64,128},{128,192},{192,256},{256,320},{320,384},{384,448},... | collective-permute-start | bytes 393224 | tf_op jit(solution)/shard_map/ppermute | solution.py:445
  17.9 4.9 %collective-permute-done.1.rest_1_ = bf16[256,256]{1,0:T(8,128)(2,1)S(1)} collective-permute-done((bf16[256,256]{1,0:T(8,128)(2,1)}, bf16[256,256]{1,0:T(8,128)(2,1)S(1)}, u32[]{:S(2)}, u32[]{:S(2)}) %collective-permute-start.1) | collective-permute-done | bytes 131104 | tf_op jit(solution)/shard_map/ppermute | solution.py:445
  22.8 4.7 %collective-permute-start.4 = (bf16[256,256]{1,0:T(8,128)(2,1)}, bf16[256,256]{1,0:T(8,128)(2,1)S(1)}, u32[]{:S(2)}, u32[]{:S(2)}) collective-permute-start(bf16[256,256]{1,0:T(8,128)(2,1)} %bitcast.27), channel_id=1, source_target_pairs={{0,256},{64,320},{128,384},{192,448},{1,257},{65,321},{129,385},{1... | collective-permute-start | bytes 393224 | tf_op jit(solution)/shard_map/ppermute | solution.py:445
  27.5 2.0 %collective-permute-start.3 = (bf16[256,256]{1,0:T(8,128)(2,1)}, bf16[256,256]{1,0:T(8,128)(2,1)S(1)}, u32[]{:S(2)}, u32[]{:S(2)}) collective-permute-start(bf16[256,256]{1,0:T(8,128)(2,1)} %bitcast.28), channel_id=1, source_target_pairs={{0,192},{64,256},{128,320},{192,384},{256,448},{1,193},{65,257},{1... | collective-permute-start | bytes 393224 | tf_op jit(solution)/shard_map/ppermute | solution.py:445
  29.5 0.7 pad_add_fusion.place_ref
  30.3 7.5 %all-to-all-start = ((bf16[1,32,8,640]{3,1,0,2:T(8,128)(2,1)}), bf16[1,32,8,640]{3,1,0,2:T(8,128)(2,1)S(1)}, u32[]{:S(2)}, u32[]{:S(2)}) async-start(bf16[1,32,8,640]{3,1,0,2:T(8,128)(2,1)} %collective-permute-done), calls=%async_computation | async-start | bytes 655360 | tf_op jit(solution)/shard_map/all_to_all | solution.py:453
  39.3 8.4 %attend_forward.1 = (bf16[1792,2560]{1,0:T(8,128)(2,1)}, bf16[1792,256]{1,0:T(8,128)(2,1)S(1)}, f32[144,2560]{1,0:T(8,128)S(1)}, f32[8,2560]{1,0:T(8,128)S(1)}, bf16[144,2560]{1,0:T(8,128)(2,1)}) custom-call(s32[10]{0:T(128)S(1)} %pad_add_fusion.place_ref, bf16[256,640]{1,0:T(8,128)(2,1)} %bitcast.16, ...), custom_call_target="tpu_custom_call" | custom-call | flops 2348810240 | bytes 9175040 | tf_op jit(solution)/shard_map/attend_forward/pallas_call | solution.py:354
  47.7 1.9 %collective-permute-start.8 = (bf16[144,2560]{1,0:T(8,128)(2,1)}, bf16[144,2560]{1,0:T(8,128)(2,1)}, u32[]{:S(2)}, u32[]{:S(2)}) collective-permute-start(bf16[144,2560]{1,0:T(8,128)(2,1)} %get-tuple-element.50), channel_id=1, source_target_pairs={{0,32},{32,0},{1,33},{33,1},{2,34},{34,2},{3,35},{35,3},{4,36},{36... | collective-permute-start | bytes 2211848 | tf_op jit(solution)/shard_map/ppermute | solution.py:336
  49.6 2.4 %collective-permute-start.9 = (bf16[256,640]{1,0:T(8,128)(2,1)S(1)}, bf16[256,640]{1,0:T(8,128)(2,1)S(1)}, u32[]{:S(2)}, u32[]{:S(2)}) collective-permute-start(bf16[256,640]{1,0:T(8,128)(2,1)S(1)} %bitcast.19), channel_id=1, source_target_pairs={{0,32},{32,0},{1,33},{33,1},{2,34},{34,2},{3,35},{35,3},{4,36},{36... | collective-permute-start | bytes 983048 | tf_op jit(solution)/shard_map/ppermute | solution.py:336
  52.2 1.1 %collective-permute-done.9.grad_other_ref = bf16[256,640]{1,0:T(8,128)(2,1)S(1)} collective-permute-done((bf16[256,640]{1,0:T(8,128)(2,1)S(1)}, bf16[256,640]{1,0:T(8,128)(2,1)S(1)}, u32[]{:S(2)}, u32[]{:S(2)}) %collective-permute-start.9) | collective-permute-done | bytes 327712 | tf_op jit(solution)/shard_map/ppermute | solution.py:336
  53.3 3.0 %attend_backward_far.1 = (bf16[256,640]{1,0:T(8,128)(2,1)}, bf16[2560,128]{1,0:T(8,128)(2,1)S(1)}, bf16[128,2560]{1,0:T(8,128)(2,1)S(1)}, f32[1,2560]{1,0:T(1,12...) custom-call(s32[10]{0:T(128)S(1)} %pad_add_fusion.place_ref, ...), custom_call_target="tpu_custom_call" | custom-call | flops 2013265920 | bytes 3932160 | tf_op jit(solution)/shard_map/attend_backward_far/pallas_call | solution.py:397
  57.6 1.3 %collective-permute-start.13 = (bf16[256,256]{1,0:T(8,128)(2,1)S(1)}, bf16[256,256]{1,0:T(8,128)(2,1)S(1)}, u32[]{:S(2)}, u32[]{:S(2)}) collective-permute-start(bf16[256,256]{1,0:T(8,128)(2,1)S(1)} %get-tuple-element.65), channel_id=1, source_target_pairs={{256,0},{320,64},{384,128},{448,192},{257,1},{321,65},{385,129},{4... | collective-permute-start | bytes 393224 | tf_op jit(solution)/shard_map/ppermute | solution.py:460
  58.9 7.8 %attend_backward_near.1 = (bf16[256,640]{1,0:T(8,128)(2,1)S(1)}, bf16[256,640]{1,0:T(8,128)(2,1)S(1)}, bf16[256,256]{1,0:T(8,128)(2,1)S(1)}, bf16[256,256]{1,0:T...) custom-call(s32[10]{0:T(128)S(1)} %pad_add_fusion.place_ref, ...), custom_call_target="tpu_custom_call" | custom-call | flops 2684354560 | bytes 5242880 | tf_op jit(solution)/shard_map/attend_backward_near/pallas_call | solution.py:418
  66.7 2.0 %collective-permute-start.14 = (bf16[256,256]{1,0:T(8,128)(2,1)S(1)}, bf16[256,256]{1,0:T(8,128)(2,1)S(1)}, u32[]{:S(2)}, u32[]{:S(2)}) collective-permute-start(bf16[256,256]{1,0:T(8,128)(2,1)S(1)} %get-tuple-element.66), channel_id=1, source_target_pairs={{192,0},{256,64},{320,128},{384,192},{448,256},{193,1},{257,65},{3... | collective-permute-start | bytes 393224 | tf_op jit(solution)/shard_map/ppermute | solution.py:460
  68.8 1.9 %collective-permute-start.15 = (bf16[256,256]{1,0:T(8,128)(2,1)S(1)}, bf16[256,256]{1,0:T(8,128)(2,1)S(1)}, u32[]{:S(2)}, u32[]{:S(2)}) collective-permute-start(bf16[256,256]{1,0:T(8,128)(2,1)S(1)} %get-tuple-element.67), channel_id=1, source_target_pairs={{128,0},{192,64},{256,128},{320,192},{384,256},{448,320},{129,1},{... | collective-permute-start | bytes 393224 | tf_op jit(solution)/shard_map/ppermute | solution.py:460
  70.7 4.9 %collective-permute-start.16 = (bf16[256,256]{1,0:T(8,128)(2,1)S(1)}, bf16[256,256]{1,0:T(8,128)(2,1)S(1)}, u32[]{:S(2)}, u32[]{:S(2)}) collective-permute-start(bf16[256,256]{1,0:T(8,128)(2,1)S(1)} %get-tuple-element.68), channel_id=1, source_target_pairs={{64,0},{128,64},{192,128},{256,192},{320,256},{384,320},{448,384},... | collective-permute-start | bytes 393224 | tf_op jit(solution)/shard_map/ppermute | solution.py:460
  75.6 2.0 %collective-permute-start.10 = (bf16[256,640]{1,0:T(8,128)(2,1)S(1)}, bf16[256,640]{1,0:T(8,128)(2,1)S(1)}, u32[]{:S(2)}, u32[]{:S(2)}) collective-permute-start(bf16[256,640]{1,0:T(8,128)(2,1)S(1)} %get-tuple-element.61), channel_id=1, source_target_pairs={{0,32},{32,0},{1,33},{33,1},{2,34},{34,2},{3,35},{35,3},{4,36},{36... | collective-permute-start | bytes 983048 | tf_op jit(solution)/shard_map/ppermute | solution.py:336
  77.7 15.8 %collective-permute-done.14 = bf16[256,256]{1,0:T(8,128)(2,1)S(1)} collective-permute-done((bf16[256,256]{1,0:T(8,128)(2,1)S(1)}, bf16[256,256]{1,0:T(8,128)(2,1)S(1)}, u32[]{:S(2)}, u32[]{:S(2)}) %collective-permute-start.14) | collective-permute-done | bytes 131104 | tf_op jit(solution)/shard_map/ppermute | solution.py:460
  93.5 2.3 %collective-permute-done.15 = bf16[256,256]{1,0:T(8,128)(2,1)S(1)} collective-permute-done((bf16[256,256]{1,0:T(8,128)(2,1)S(1)}, bf16[256,256]{1,0:T(8,128)(2,1)S(1)}, u32[]{:S(2)}, u32[]{:S(2)}) %collective-permute-start.15) | collective-permute-done | bytes 131104 | tf_op jit(solution)/shard_map/ppermute | solution.py:460
  96.5 0.8 fusion
  (34 shorter events, 5.4 us)
Async XLA Ops:
  1.6 25.8 %collective-permute-start = (bf16[1,32,8,640]{3,1,0,2:T(8,128)(2,1)S(1)}, bf16[1,32,8,640]{3,1,0,2:T(8,128)(2,1)}, u32[]{:S(2)}, u32[]{:S(2)}) collective-permute-start(bf16[1,32,8,640]{3,1,0,2:T(8,128)(2,1)S(1)} %copy.8), channel_id=1, source_target_pairs={{0,3},{1,0},{2,1},{3,2},{4,7},{5,4},{6,5},{7,6},{8,11},{9,8},{10,9... | collective-permute-start | bytes 983048 | tf_op jit(solution)/shard_map/ppermute | solution.py:449
  4.4 34.9 %collective-permute-start.7 = (bf16[256,640]{1,0:T(8,128)(2,1)}, bf16[256,640]{1,0:T(8,128)(2,1)S(1)}, u32[]{:S(2)}, u32[]{:S(2)}) collective-permute-start(bf16[256,640]{1,0:T(8,128)(2,1)} %bitcast.15), channel_id=1, source_target_pairs={{0,32},{32,0},{1,33},{33,1},{2,34},{34,2},{3,35},{35,3},{4,36},{36... | collective-permute-start | bytes 983048 | tf_op jit(solution)/shard_map/ppermute | solution.py:336
  6.3 10.9 %collective-permute-start.2 = (bf16[256,256]{1,0:T(8,128)(2,1)}, bf16[256,256]{1,0:T(8,128)(2,1)S(1)}, u32[]{:S(2)}, u32[]{:S(2)}) collective-permute-start(bf16[256,256]{1,0:T(8,128)(2,1)} %bitcast.23), channel_id=1, source_target_pairs={{0,128},{64,192},{128,256},{192,320},{256,384},{320,448},{1,129},{... | collective-permute-start | bytes 393224 | tf_op jit(solution)/shard_map/ppermute | solution.py:445
  12.7 10.1 %collective-permute-start.1 = (bf16[256,256]{1,0:T(8,128)(2,1)}, bf16[256,256]{1,0:T(8,128)(2,1)S(1)}, u32[]{:S(2)}, u32[]{:S(2)}) collective-permute-start(bf16[256,256]{1,0:T(8,128)(2,1)} %bitcast.24), channel_id=1, source_target_pairs={{0,64},{64,128},{128,192},{192,256},{256,320},{320,384},{384,448},... | collective-permute-start | bytes 393224 | tf_op jit(solution)/shard_map/ppermute | solution.py:445
  16.1 21.7 %collective-permute-start.6 = (bf16[256,256]{1,0:T(8,128)(2,1)}, bf16[256,256]{1,0:T(8,128)(2,1)S(1)}, u32[]{:S(2)}, u32[]{:S(2)}) collective-permute-start(bf16[256,256]{1,0:T(8,128)(2,1)} %bitcast.25), channel_id=1, source_target_pairs={{0,384},{64,448},{1,385},{65,449},{2,386},{66,450},{3,387},{67,451... | collective-permute-start | bytes 393224 | tf_op jit(solution)/shard_map/ppermute | solution.py:445
  17.2 10.2 %copy-start.1 = (bf16[256,256]{1,0:T(8,128)(2,1)}, bf16[256,256]{1,0:T(8,128)(2,1)S(1)}, u32[]{:S(2)}) copy-start(bf16[256,256]{1,0:T(8,128)(2,1)S(1)} %collective-permute-done.2.rest_2_) | copy-start | bytes 393220
  17.2 20.6 %collective-permute-start.5 = (bf16[256,256]{1,0:T(8,128)(2,1)}, bf16[256,256]{1,0:T(8,128)(2,1)S(1)}, u32[]{:S(2)}, u32[]{:S(2)}) collective-permute-start(bf16[256,256]{1,0:T(8,128)(2,1)} %bitcast.26), channel_id=1, source_target_pairs={{0,320},{64,384},{128,448},{1,321},{65,385},{129,449},{2,322},{66,... | collective-permute-start | bytes 393224 | tf_op jit(solution)/shard_map/ppermute | solution.py:445
  22.8 6.7 %copy-start.2 = (bf16[256,256]{1,0:T(8,128)(2,1)}, bf16[256,256]{1,0:T(8,128)(2,1)S(1)}, u32[]{:S(2)}) copy-start(bf16[256,256]{1,0:T(8,128)(2,1)S(1)} %collective-permute-done.1.rest_1_) | copy-start | bytes 393220
  22.8 15.1 %collective-permute-start.4 = (bf16[256,256]{1,0:T(8,128)(2,1)}, bf16[256,256]{1,0:T(8,128)(2,1)S(1)}, u32[]{:S(2)}, u32[]{:S(2)}) collective-permute-start(bf16[256,256]{1,0:T(8,128)(2,1)} %bitcast.27), channel_id=1, source_target_pairs={{0,256},{64,320},{128,384},{192,448},{1,257},{65,321},{129,385},{1... | collective-permute-start | bytes 393224 | tf_op jit(solution)/shard_map/ppermute | solution.py:445
  27.5 10.4 %collective-permute-start.3 = (bf16[256,256]{1,0:T(8,128)(2,1)}, bf16[256,256]{1,0:T(8,128)(2,1)S(1)}, u32[]{:S(2)}, u32[]{:S(2)}) collective-permute-start(bf16[256,256]{1,0:T(8,128)(2,1)} %bitcast.28), channel_id=1, source_target_pairs={{0,192},{64,256},{128,320},{192,384},{256,448},{1,193},{65,257},{1... | collective-permute-start | bytes 393224 | tf_op jit(solution)/shard_map/ppermute | solution.py:445
  30.3 19.4 %all-to-all-start = ((bf16[1,32,8,640]{3,1,0,2:T(8,128)(2,1)}), bf16[1,32,8,640]{3,1,0,2:T(8,128)(2,1)S(1)}, u32[]{:S(2)}, u32[]{:S(2)}) async-start(bf16[1,32,8,640]{3,1,0,2:T(8,128)(2,1)} %collective-permute-done), calls=%async_computation | async-start | bytes 655360 | tf_op jit(solution)/shard_map/all_to_all | solution.py:453
  37.8 15.5 %copy-start = (bf16[1,256,1,640]{3,1,2,0:T(8,128)(2,1)S(1)}, bf16[1,256,1,640]{3,1,2,0:T(8,128)(2,1)}, u32[]{:S(2)}) copy-start(bf16[1,256,1,640]{3,1,2,0:T(8,128)(2,1)} %param.4) | copy-start | bytes 983044
  37.8 0.7 copy-start.4
  37.9 0.7 copy-start.5
  38.6 0.7 copy-start.6
  47.7 4.5 %collective-permute-start.8 = (bf16[144,2560]{1,0:T(8,128)(2,1)}, bf16[144,2560]{1,0:T(8,128)(2,1)}, u32[]{:S(2)}, u32[]{:S(2)}) collective-permute-start(bf16[144,2560]{1,0:T(8,128)(2,1)} %get-tuple-element.50), channel_id=1, source_target_pairs={{0,32},{32,0},{1,33},{33,1},{2,34},{34,2},{3,35},{35,3},{4,36},{36... | collective-permute-start | bytes 2211848 | tf_op jit(solution)/shard_map/ppermute | solution.py:336
  49.6 3.6 %collective-permute-start.9 = (bf16[256,640]{1,0:T(8,128)(2,1)S(1)}, bf16[256,640]{1,0:T(8,128)(2,1)S(1)}, u32[]{:S(2)}, u32[]{:S(2)}) collective-permute-start(bf16[256,640]{1,0:T(8,128)(2,1)S(1)} %bitcast.19), channel_id=1, source_target_pairs={{0,32},{32,0},{1,33},{33,1},{2,34},{34,2},{3,35},{35,3},{4,36},{36... | collective-permute-start | bytes 983048 | tf_op jit(solution)/shard_map/ppermute | solution.py:336
  56.3 14.4 %collective-permute-start.11 = (bf16[256,256]{1,0:T(8,128)(2,1)S(1)}, bf16[256,256]{1,0:T(8,128)(2,1)S(1)}, u32[]{:S(2)}, u32[]{:S(2)}) collective-permute-start(bf16[256,256]{1,0:T(8,128)(2,1)S(1)} %get-tuple-element.63), channel_id=1, source_target_pairs={{384,0},{448,64},{385,1},{449,65},{386,2},{450,66},{387,3},{451,67... | collective-permute-start | bytes 393224 | tf_op jit(solution)/shard_map/ppermute | solution.py:460
  56.9 18.6 %collective-permute-start.12 = (bf16[256,256]{1,0:T(8,128)(2,1)S(1)}, bf16[256,256]{1,0:T(8,128)(2,1)S(1)}, u32[]{:S(2)}, u32[]{:S(2)}) collective-permute-start(bf16[256,256]{1,0:T(8,128)(2,1)S(1)} %get-tuple-element.64), channel_id=1, source_target_pairs={{320,0},{384,64},{448,128},{321,1},{385,65},{449,129},{322,2},{386... | collective-permute-start | bytes 393224 | tf_op jit(solution)/shard_map/ppermute | solution.py:460
  57.6 20.0 %collective-permute-start.13 = (bf16[256,256]{1,0:T(8,128)(2,1)S(1)}, bf16[256,256]{1,0:T(8,128)(2,1)S(1)}, u32[]{:S(2)}, u32[]{:S(2)}) collective-permute-start(bf16[256,256]{1,0:T(8,128)(2,1)S(1)} %get-tuple-element.65), channel_id=1, source_target_pairs={{256,0},{320,64},{384,128},{448,192},{257,1},{321,65},{385,129},{4... | collective-permute-start | bytes 393224 | tf_op jit(solution)/shard_map/ppermute | solution.py:460
  66.7 26.8 %collective-permute-start.14 = (bf16[256,256]{1,0:T(8,128)(2,1)S(1)}, bf16[256,256]{1,0:T(8,128)(2,1)S(1)}, u32[]{:S(2)}, u32[]{:S(2)}) collective-permute-start(bf16[256,256]{1,0:T(8,128)(2,1)S(1)} %get-tuple-element.66), channel_id=1, source_target_pairs={{192,0},{256,64},{320,128},{384,192},{448,256},{193,1},{257,65},{3... | collective-permute-start | bytes 393224 | tf_op jit(solution)/shard_map/ppermute | solution.py:460
  68.8 27.0 %collective-permute-start.15 = (bf16[256,256]{1,0:T(8,128)(2,1)S(1)}, bf16[256,256]{1,0:T(8,128)(2,1)S(1)}, u32[]{:S(2)}, u32[]{:S(2)}) collective-permute-start(bf16[256,256]{1,0:T(8,128)(2,1)S(1)} %get-tuple-element.67), channel_id=1, source_target_pairs={{128,0},{192,64},{256,128},{320,192},{384,256},{448,320},{129,1},{... | collective-permute-start | bytes 393224 | tf_op jit(solution)/shard_map/ppermute | solution.py:460
  70.7 25.1 %collective-permute-start.16 = (bf16[256,256]{1,0:T(8,128)(2,1)S(1)}, bf16[256,256]{1,0:T(8,128)(2,1)S(1)}, u32[]{:S(2)}, u32[]{:S(2)}) collective-permute-start(bf16[256,256]{1,0:T(8,128)(2,1)S(1)} %get-tuple-element.68), channel_id=1, source_target_pairs={{64,0},{128,64},{192,128},{256,192},{320,256},{384,320},{448,384},... | collective-permute-start | bytes 393224 | tf_op jit(solution)/shard_map/ppermute | solution.py:460
  75.6 20.9 %collective-permute-start.10 = (bf16[256,640]{1,0:T(8,128)(2,1)S(1)}, bf16[256,640]{1,0:T(8,128)(2,1)S(1)}, u32[]{:S(2)}, u32[]{:S(2)}) collective-permute-start(bf16[256,640]{1,0:T(8,128)(2,1)S(1)} %get-tuple-element.61), channel_id=1, source_target_pairs={{0,32},{32,0},{1,33},{33,1},{2,34},{34,2},{3,35},{35,3},{4,36},{36... | collective-permute-start | bytes 983048 | tf_op jit(solution)/shard_map/ppermute | solution.py:336
  (1 other events, 0.7 us)

commit v11 on v10

--- a/solution.py
+++ b/solution.py
@@ -382,7 +382,7 @@
     grad, stats = lax.optimization_barrier((grad, stats))
     grad_other = swap(grad)
     half = jax.ShapeDtypeStruct((rows, columns), jnp.bfloat16)
-    params = pltpu.CompilerParams(vmem_limit_bytes=20 << 20)
+    params = pltpu.CompilerParams(vmem_limit_bytes=22 << 20)
     move = pltpu.VMEM((rows, wide), jnp.bfloat16)
 
     def held(blocks):
@@ -453,7 +453,7 @@
     grad = lax.all_to_all(arrived, "tensor", split_axis=2, concat_axis=1, tiled=True)[0, :, 0, :]
     position = jnp.stack([lax.axis_index("chip"), lax.axis_index("core")]).astype(jnp.int32)
     place = jnp.concatenate([position, doc_lengths[0]])
-    split = (slots + 1) // 2
+    split = slots // 2
 
     def send(blocks, first):
         return [

time: 98 us -> 97.1 us (level)
  the two profiles are of different devices: /device:TPU:206 before, /device:TPU:225 now
where the time goes in v11:
time: 97.1 us; the launch traced here: 96.6 us
  starting transfers between devices  50.2 us (52%)
  waiting for transfers between devices  24.3 us (25%)
  Pallas kernels  16.5 us (17%)
  local copies, waits for them, and re-layouts  2.4 us (2%)
  other arithmetic  2.32 us (2%)
    ppermute x6, waiting for transfers between devices, send(): lax.ppermute(block, 'chip', [(c, c - first - at) for c in range(first + a...  17.3 us
    ppermute x6, starting transfers between devices, per_device(): lax.ppermute(pairs, 'chip', [(c, c + back) for c in range(chips - back)])  17 us
    ppermute x6, starting transfers between devices, send(): lax.ppermute(block, 'chip', [(c, c - first - at) for c in range(first + a...  11.7 us
    ppermute x4, starting transfers between devices, swap_cores(): return lax.ppermute(value, 'core', [(0, 1), (1, 0)])  10.5 us
    pallas_call x1, Pallas kernels, attend(): pl.pallas_call(forward_kernel, out_shape=(pltpu.HBM((slots * rows, wide),...  7.1 us
    all_to_all x1, starting transfers between devices, per_device(): lax.all_to_all(arrived, 'tensor', split_axis=2, concat_axis=1, tiled=True)  6.65 us
    pallas_call x1, Pallas kernels, near_call(): pl.pallas_call(functools.partial(backward_near_kernel, first=first, ends=...  6.37 us
    ppermute x6, waiting for transfers between devices, per_device(): lax.ppermute(pairs, 'chip', [(c, c + back) for c in range(chips - back)])  5.46 us
  transfers between devices with their start and end apart: 18, of which 7 were waited for; matrix products, arithmetic and copies ran while one was open for 2% of the time, Pallas kernels for 14%

profile of v11, /device:TPU:225, one launch (start us, length us, event | category | flops | bytes accessed | tf_op | source)
XLA Modules:
  0.0 96.6 jit_solution(7947624649798251829)
XLA Ops:
  0.6 1.0 %copy.8 = bf16[1,32,8,640]{3,1,0,2:T(8,128)(2,1)S(1)} copy(bf16[1,32,8,640]{3,2,1,0:T(8,128)(2,1)} %param.7) | data formatting | bytes 655360 | tf_op args[3]
  1.6 4.4 %collective-permute-start = (bf16[1,32,8,640]{3,1,0,2:T(8,128)(2,1)S(1)}, bf16[1,32,8,640]{3,1,0,2:T(8,128)(2,1)}, u32[]{:S(2)}, u32[]{:S(2)}) collective-permute-start(bf16[1,32,8,640]{3,1,0,2:T(8,128)(2,1)S(1)} %copy.8), channel_id=1, source_target_pairs={{0,3},{1,0},{2,1},{3,2},{4,7},{5,4},{6,5},{7,6},{8,11},{9,8},{10,9... | collective-permute-start | bytes 983048 | tf_op jit(solution)/shard_map/ppermute | solution.py:449
  6.0 2.9 %collective-permute-start.7 = (bf16[256,640]{1,0:T(8,128)(2,1)}, bf16[256,640]{1,0:T(8,128)(2,1)S(1)}, u32[]{:S(2)}, u32[]{:S(2)}) collective-permute-start(bf16[256,640]{1,0:T(8,128)(2,1)} %bitcast.15), channel_id=1, source_target_pairs={{0,32},{32,0},{1,33},{33,1},{2,34},{34,2},{3,35},{35,3},{4,36},{36... | collective-permute-start | bytes 983048 | tf_op jit(solution)/shard_map/ppermute | solution.py:336
  8.9 6.1 %collective-permute-start.2 = (bf16[256,256]{1,0:T(8,128)(2,1)}, bf16[256,256]{1,0:T(8,128)(2,1)S(1)}, u32[]{:S(2)}, u32[]{:S(2)}) collective-permute-start(bf16[256,256]{1,0:T(8,128)(2,1)} %bitcast.23), channel_id=1, source_target_pairs={{0,128},{64,192},{128,256},{192,320},{256,384},{320,448},{1,129},{... | collective-permute-start | bytes 393224 | tf_op jit(solution)/shard_map/ppermute | solution.py:445
  15.0 3.1 %collective-permute-start.1 = (bf16[256,256]{1,0:T(8,128)(2,1)}, bf16[256,256]{1,0:T(8,128)(2,1)S(1)}, u32[]{:S(2)}, u32[]{:S(2)}) collective-permute-start(bf16[256,256]{1,0:T(8,128)(2,1)} %bitcast.24), channel_id=1, source_target_pairs={{0,64},{64,128},{128,192},{192,256},{256,320},{320,384},{384,448},... | collective-permute-start | bytes 393224 | tf_op jit(solution)/shard_map/ppermute | solution.py:445
  20.0 5.0 %collective-permute-done.1.rest_1_ = bf16[256,256]{1,0:T(8,128)(2,1)S(1)} collective-permute-done((bf16[256,256]{1,0:T(8,128)(2,1)}, bf16[256,256]{1,0:T(8,128)(2,1)S(1)}, u32[]{:S(2)}, u32[]{:S(2)}) %collective-permute-start.1) | collective-permute-done | bytes 131104 | tf_op jit(solution)/shard_map/ppermute | solution.py:445
  25.0 4.3 %collective-permute-start.4 = (bf16[256,256]{1,0:T(8,128)(2,1)}, bf16[256,256]{1,0:T(8,128)(2,1)S(1)}, u32[]{:S(2)}, u32[]{:S(2)}) collective-permute-start(bf16[256,256]{1,0:T(8,128)(2,1)} %bitcast.27), channel_id=1, source_target_pairs={{0,256},{64,320},{128,384},{192,448},{1,257},{65,321},{129,385},{1... | collective-permute-start | bytes 393224 | tf_op jit(solution)/shard_map/ppermute | solution.py:445
  29.2 2.2 %collective-permute-start.3 = (bf16[256,256]{1,0:T(8,128)(2,1)}, bf16[256,256]{1,0:T(8,128)(2,1)S(1)}, u32[]{:S(2)}, u32[]{:S(2)}) collective-permute-start(bf16[256,256]{1,0:T(8,128)(2,1)} %bitcast.28), channel_id=1, source_target_pairs={{0,192},{64,256},{128,320},{192,384},{256,448},{1,193},{65,257},{1... | collective-permute-start | bytes 393224 | tf_op jit(solution)/shard_map/ppermute | solution.py:445
  32.2 6.6 %all-to-all-start = ((bf16[1,32,8,640]{3,1,0,2:T(8,128)(2,1)}), bf16[1,32,8,640]{3,1,0,2:T(8,128)(2,1)S(1)}, u32[]{:S(2)}, u32[]{:S(2)}) async-start(bf16[1,32,8,640]{3,1,0,2:T(8,128)(2,1)} %collective-permute-done), calls=%async_computation | async-start | bytes 655360 | tf_op jit(solution)/shard_map/all_to_all | solution.py:453
  40.2 7.1 %attend_forward.1 = (bf16[1792,2560]{1,0:T(8,128)(2,1)}, bf16[1792,256]{1,0:T(8,128)(2,1)S(1)}, f32[144,2560]{1,0:T(8,128)S(1)}, f32[8,2560]{1,0:T(8,128)S(1)}, bf16[144,2560]{1,0:T(8,128)(2,1)}) custom-call(s32[10]{0:T(128)S(1)} %pad_add_fusion.place_ref, bf16[256,640]{1,0:T(8,128)(2,1)} %bitcast.16, ...), custom_call_target="tpu_custom_call" | custom-call | flops 2348810240 | bytes 9175040 | tf_op jit(solution)/shard_map/attend_forward/pallas_call | solution.py:354
  47.4 3.4 %collective-permute-start.8 = (bf16[144,2560]{1,0:T(8,128)(2,1)}, bf16[144,2560]{1,0:T(8,128)(2,1)}, u32[]{:S(2)}, u32[]{:S(2)}) collective-permute-start(bf16[144,2560]{1,0:T(8,128)(2,1)} %get-tuple-element.50), channel_id=1, source_target_pairs={{0,32},{32,0},{1,33},{33,1},{2,34},{34,2},{3,35},{35,3},{4,36},{36... | collective-permute-start | bytes 2211848 | tf_op jit(solution)/shard_map/ppermute | solution.py:336
  50.7 1.9 %collective-permute-start.9 = (bf16[256,640]{1,0:T(8,128)(2,1)S(1)}, bf16[256,640]{1,0:T(8,128)(2,1)S(1)}, u32[]{:S(2)}, u32[]{:S(2)}) collective-permute-start(bf16[256,640]{1,0:T(8,128)(2,1)S(1)} %bitcast.19), channel_id=1, source_target_pairs={{0,32},{32,0},{1,33},{33,1},{2,34},{34,2},{3,35},{35,3},{4,36},{36... | collective-permute-start | bytes 983048 | tf_op jit(solution)/shard_map/ppermute | solution.py:336
  52.9 1.4 %collective-permute-done.9.grad_other_ref = bf16[256,640]{1,0:T(8,128)(2,1)S(1)} collective-permute-done((bf16[256,640]{1,0:T(8,128)(2,1)S(1)}, bf16[256,640]{1,0:T(8,128)(2,1)S(1)}, u32[]{:S(2)}, u32[]{:S(2)}) %collective-permute-start.9) | collective-permute-done | bytes 327712 | tf_op jit(solution)/shard_map/ppermute | solution.py:336
  54.3 3.0 %attend_backward_far.1 = (bf16[256,640]{1,0:T(8,128)(2,1)}, bf16[2560,128]{1,0:T(8,128)(2,1)S(1)}, bf16[128,2560]{1,0:T(8,128)(2,1)S(1)}, f32[1,2560]{1,0:T(1,12...) custom-call(s32[10]{0:T(128)S(1)} %pad_add_fusion.place_ref, ...), custom_call_target="tpu_custom_call" | custom-call | flops 2684354560 | bytes 5242880 | tf_op jit(solution)/shard_map/attend_backward_far/pallas_call | solution.py:397
  58.6 1.3 %collective-permute-start.13 = (bf16[256,256]{1,0:T(8,128)(2,1)S(1)}, bf16[256,256]{1,0:T(8,128)(2,1)S(1)}, u32[]{:S(2)}, u32[]{:S(2)}) collective-permute-start(bf16[256,256]{1,0:T(8,128)(2,1)S(1)} %get-tuple-element.65), channel_id=1, source_target_pairs={{256,0},{320,64},{384,128},{448,192},{257,1},{321,65},{385,129},{4... | collective-permute-start | bytes 393224 | tf_op jit(solution)/shard_map/ppermute | solution.py:460
  59.9 4.2 %collective-permute-start.14 = (bf16[256,256]{1,0:T(8,128)(2,1)S(1)}, bf16[256,256]{1,0:T(8,128)(2,1)S(1)}, u32[]{:S(2)}, u32[]{:S(2)}) collective-permute-start(bf16[256,256]{1,0:T(8,128)(2,1)S(1)} %get-tuple-element.66), channel_id=1, source_target_pairs={{192,0},{256,64},{320,128},{384,192},{448,256},{193,1},{257,65},{3... | collective-permute-start | bytes 393224 | tf_op jit(solution)/shard_map/ppermute | solution.py:460
  64.1 6.4 %attend_backward_near.1 = (bf16[256,640]{1,0:T(8,128)(2,1)S(1)}, bf16[256,640]{1,0:T(8,128)(2,1)S(1)}, bf16[256,256]{1,0:T(8,128)(2,1)S(1)}, bf16[256,256]{1,0:T(8,128)(2,1)S(1)}, bf16[256,256]{1,0:T(8,128)(2,1)S(1)}) custom-call(s32[10]{0:T(128)S(1)} %pad_add_fusion.place_ref, bf16[2560,128]{1,0:T(8,128)(2,1)S(1)} %get-tuple-element.56.scaled_ref, ...), custom_call_target="tpu_custom_call" | custom-call | flops 2013265920 | bytes 3932160 | tf_op jit(solution)/shard_map/attend_backward_near/pallas_call | solution.py:418
  70.5 1.9 %collective-permute-start.15 = (bf16[256,256]{1,0:T(8,128)(2,1)S(1)}, bf16[256,256]{1,0:T(8,128)(2,1)S(1)}, u32[]{:S(2)}, u32[]{:S(2)}) collective-permute-start(bf16[256,256]{1,0:T(8,128)(2,1)S(1)} %get-tuple-element.67), channel_id=1, source_target_pairs={{128,0},{192,64},{256,128},{320,192},{384,256},{448,320},{129,1},{... | collective-permute-start | bytes 393224 | tf_op jit(solution)/shard_map/ppermute | solution.py:460
  72.4 3.0 %collective-permute-start.16 = (bf16[256,256]{1,0:T(8,128)(2,1)S(1)}, bf16[256,256]{1,0:T(8,128)(2,1)S(1)}, u32[]{:S(2)}, u32[]{:S(2)}) collective-permute-start(bf16[256,256]{1,0:T(8,128)(2,1)S(1)} %get-tuple-element.68), channel_id=1, source_target_pairs={{64,0},{128,64},{192,128},{256,192},{320,256},{384,320},{448,384},... | collective-permute-start | bytes 393224 | tf_op jit(solution)/shard_map/ppermute | solution.py:460
  75.4 2.3 %collective-permute-start.10 = (bf16[256,640]{1,0:T(8,128)(2,1)S(1)}, bf16[256,640]{1,0:T(8,128)(2,1)S(1)}, u32[]{:S(2)}, u32[]{:S(2)}) collective-permute-start(bf16[256,640]{1,0:T(8,128)(2,1)S(1)} %get-tuple-element.61), channel_id=1, source_target_pairs={{0,32},{32,0},{1,33},{33,1},{2,34},{34,2},{3,35},{35,3},{4,36},{36... | collective-permute-start | bytes 983048 | tf_op jit(solution)/shard_map/ppermute | solution.py:336
  77.8 5.2 %collective-permute-done.14 = bf16[256,256]{1,0:T(8,128)(2,1)S(1)} collective-permute-done((bf16[256,256]{1,0:T(8,128)(2,1)S(1)}, bf16[256,256]{1,0:T(8,128)(2,1)S(1)}, u32[]{:S(2)}, u32[]{:S(2)}) %collective-permute-start.14) | collective-permute-done | bytes 131104 | tf_op jit(solution)/shard_map/ppermute | solution.py:460
  83.1 6.5 %collective-permute-done.15 = bf16[256,256]{1,0:T(8,128)(2,1)S(1)} collective-permute-done((bf16[256,256]{1,0:T(8,128)(2,1)S(1)}, bf16[256,256]{1,0:T(8,128)(2,1)S(1)}, u32[]{:S(2)}, u32[]{:S(2)}) %collective-permute-start.15) | collective-permute-done | bytes 131104 | tf_op jit(solution)/shard_map/ppermute | solution.py:460
  89.6 5.5 %collective-permute-done.16 = bf16[256,256]{1,0:T(8,128)(2,1)S(1)} collective-permute-done((bf16[256,256]{1,0:T(8,128)(2,1)S(1)}, bf16[256,256]{1,0:T(8,128)(2,1)S(1)}, u32[]{:S(2)}, u32[]{:S(2)}) %collective-permute-start.16) | collective-permute-done | bytes 131104 | tf_op jit(solution)/shard_map/ppermute | solution.py:460
  95.8 0.8 fusion
  (34 shorter events, 6.3 us)
Async XLA Ops:
  1.6 27.6 %collective-permute-start = (bf16[1,32,8,640]{3,1,0,2:T(8,128)(2,1)S(1)}, bf16[1,32,8,640]{3,1,0,2:T(8,128)(2,1)}, u32[]{:S(2)}, u32[]{:S(2)}) collective-permute-start(bf16[1,32,8,640]{3,1,0,2:T(8,128)(2,1)S(1)} %copy.8), channel_id=1, source_target_pairs={{0,3},{1,0},{2,1},{3,2},{4,7},{5,4},{6,5},{7,6},{8,11},{9,8},{10,9... | collective-permute-start | bytes 983048 | tf_op jit(solution)/shard_map/ppermute | solution.py:449
  6.0 34.2 %collective-permute-start.7 = (bf16[256,640]{1,0:T(8,128)(2,1)}, bf16[256,640]{1,0:T(8,128)(2,1)S(1)}, u32[]{:S(2)}, u32[]{:S(2)}) collective-permute-start(bf16[256,640]{1,0:T(8,128)(2,1)} %bitcast.15), channel_id=1, source_target_pairs={{0,32},{32,0},{1,33},{33,1},{2,34},{34,2},{3,35},{35,3},{4,36},{36... | collective-permute-start | bytes 983048 | tf_op jit(solution)/shard_map/ppermute | solution.py:336
  8.9 10.4 %collective-permute-start.2 = (bf16[256,256]{1,0:T(8,128)(2,1)}, bf16[256,256]{1,0:T(8,128)(2,1)S(1)}, u32[]{:S(2)}, u32[]{:S(2)}) collective-permute-start(bf16[256,256]{1,0:T(8,128)(2,1)} %bitcast.23), channel_id=1, source_target_pairs={{0,128},{64,192},{128,256},{192,320},{256,384},{320,448},{1,129},{... | collective-permute-start | bytes 393224 | tf_op jit(solution)/shard_map/ppermute | solution.py:445
  15.0 9.9 %collective-permute-start.1 = (bf16[256,256]{1,0:T(8,128)(2,1)}, bf16[256,256]{1,0:T(8,128)(2,1)S(1)}, u32[]{:S(2)}, u32[]{:S(2)}) collective-permute-start(bf16[256,256]{1,0:T(8,128)(2,1)} %bitcast.24), channel_id=1, source_target_pairs={{0,64},{64,128},{128,192},{192,256},{256,320},{320,384},{384,448},... | collective-permute-start | bytes 393224 | tf_op jit(solution)/shard_map/ppermute | solution.py:445
  18.2 20.7 %collective-permute-start.6 = (bf16[256,256]{1,0:T(8,128)(2,1)}, bf16[256,256]{1,0:T(8,128)(2,1)S(1)}, u32[]{:S(2)}, u32[]{:S(2)}) collective-permute-start(bf16[256,256]{1,0:T(8,128)(2,1)} %bitcast.25), channel_id=1, source_target_pairs={{0,384},{64,448},{1,385},{65,449},{2,386},{66,450},{3,387},{67,451... | collective-permute-start | bytes 393224 | tf_op jit(solution)/shard_map/ppermute | solution.py:445
  19.3 9.9 %copy-start.1 = (bf16[256,256]{1,0:T(8,128)(2,1)}, bf16[256,256]{1,0:T(8,128)(2,1)S(1)}, u32[]{:S(2)}) copy-start(bf16[256,256]{1,0:T(8,128)(2,1)S(1)} %collective-permute-done.2.rest_2_) | copy-start | bytes 393220
  19.3 19.5 %collective-permute-start.5 = (bf16[256,256]{1,0:T(8,128)(2,1)}, bf16[256,256]{1,0:T(8,128)(2,1)S(1)}, u32[]{:S(2)}, u32[]{:S(2)}) collective-permute-start(bf16[256,256]{1,0:T(8,128)(2,1)} %bitcast.26), channel_id=1, source_target_pairs={{0,320},{64,384},{128,448},{1,321},{65,385},{129,449},{2,322},{66,... | collective-permute-start | bytes 393224 | tf_op jit(solution)/shard_map/ppermute | solution.py:445
  25.0 6.5 %copy-start.2 = (bf16[256,256]{1,0:T(8,128)(2,1)}, bf16[256,256]{1,0:T(8,128)(2,1)S(1)}, u32[]{:S(2)}) copy-start(bf16[256,256]{1,0:T(8,128)(2,1)S(1)} %collective-permute-done.1.rest_1_) | copy-start | bytes 393220
  25.0 13.9 %collective-permute-start.4 = (bf16[256,256]{1,0:T(8,128)(2,1)}, bf16[256,256]{1,0:T(8,128)(2,1)S(1)}, u32[]{:S(2)}, u32[]{:S(2)}) collective-permute-start(bf16[256,256]{1,0:T(8,128)(2,1)} %bitcast.27), channel_id=1, source_target_pairs={{0,256},{64,320},{128,384},{192,448},{1,257},{65,321},{129,385},{1... | collective-permute-start | bytes 393224 | tf_op jit(solution)/shard_map/ppermute | solution.py:445
  29.2 9.6 %collective-permute-start.3 = (bf16[256,256]{1,0:T(8,128)(2,1)}, bf16[256,256]{1,0:T(8,128)(2,1)S(1)}, u32[]{:S(2)}, u32[]{:S(2)}) collective-permute-start(bf16[256,256]{1,0:T(8,128)(2,1)} %bitcast.28), channel_id=1, source_target_pairs={{0,192},{64,256},{128,320},{192,384},{256,448},{1,193},{65,257},{1... | collective-permute-start | bytes 393224 | tf_op jit(solution)/shard_map/ppermute | solution.py:445
  32.2 18.6 %all-to-all-start = ((bf16[1,32,8,640]{3,1,0,2:T(8,128)(2,1)}), bf16[1,32,8,640]{3,1,0,2:T(8,128)(2,1)S(1)}, u32[]{:S(2)}, u32[]{:S(2)}) async-start(bf16[1,32,8,640]{3,1,0,2:T(8,128)(2,1)} %collective-permute-done), calls=%async_computation | async-start | bytes 655360 | tf_op jit(solution)/shard_map/all_to_all | solution.py:453
  38.8 15.5 %copy-start = (bf16[1,256,1,640]{3,1,2,0:T(8,128)(2,1)S(1)}, bf16[1,256,1,640]{3,1,2,0:T(8,128)(2,1)}, u32[]{:S(2)}) copy-start(bf16[1,256,1,640]{3,1,2,0:T(8,128)(2,1)} %param.4) | copy-start | bytes 983044
  38.8 0.7 copy-start.4
  38.9 0.7 copy-start.5
  39.6 0.7 copy-start.6
  47.4 5.5 %collective-permute-start.8 = (bf16[144,2560]{1,0:T(8,128)(2,1)}, bf16[144,2560]{1,0:T(8,128)(2,1)}, u32[]{:S(2)}, u32[]{:S(2)}) collective-permute-start(bf16[144,2560]{1,0:T(8,128)(2,1)} %get-tuple-element.50), channel_id=1, source_target_pairs={{0,32},{32,0},{1,33},{33,1},{2,34},{34,2},{3,35},{35,3},{4,36},{36... | collective-permute-start | bytes 2211848 | tf_op jit(solution)/shard_map/ppermute | solution.py:336
  50.7 3.5 %collective-permute-start.9 = (bf16[256,640]{1,0:T(8,128)(2,1)S(1)}, bf16[256,640]{1,0:T(8,128)(2,1)S(1)}, u32[]{:S(2)}, u32[]{:S(2)}) collective-permute-start(bf16[256,640]{1,0:T(8,128)(2,1)S(1)} %bitcast.19), channel_id=1, source_target_pairs={{0,32},{32,0},{1,33},{33,1},{2,34},{34,2},{3,35},{35,3},{4,36},{36... | collective-permute-start | bytes 983048 | tf_op jit(solution)/shard_map/ppermute | solution.py:336
  57.3 15.2 %collective-permute-start.11 = (bf16[256,256]{1,0:T(8,128)(2,1)S(1)}, bf16[256,256]{1,0:T(8,128)(2,1)S(1)}, u32[]{:S(2)}, u32[]{:S(2)}) collective-permute-start(bf16[256,256]{1,0:T(8,128)(2,1)S(1)} %get-tuple-element.63), channel_id=1, source_target_pairs={{384,0},{448,64},{385,1},{449,65},{386,2},{450,66},{387,3},{451,67... | collective-permute-start | bytes 393224 | tf_op jit(solution)/shard_map/ppermute | solution.py:460
  57.9 17.5 %collective-permute-start.12 = (bf16[256,256]{1,0:T(8,128)(2,1)S(1)}, bf16[256,256]{1,0:T(8,128)(2,1)S(1)}, u32[]{:S(2)}, u32[]{:S(2)}) collective-permute-start(bf16[256,256]{1,0:T(8,128)(2,1)S(1)} %get-tuple-element.64), channel_id=1, source_target_pairs={{320,0},{384,64},{448,128},{321,1},{385,65},{449,129},{322,2},{386... | collective-permute-start | bytes 393224 | tf_op jit(solution)/shard_map/ppermute | solution.py:460
  58.6 19.2 %collective-permute-start.13 = (bf16[256,256]{1,0:T(8,128)(2,1)S(1)}, bf16[256,256]{1,0:T(8,128)(2,1)S(1)}, u32[]{:S(2)}, u32[]{:S(2)}) collective-permute-start(bf16[256,256]{1,0:T(8,128)(2,1)S(1)} %get-tuple-element.65), channel_id=1, source_target_pairs={{256,0},{320,64},{384,128},{448,192},{257,1},{321,65},{385,129},{4... | collective-permute-start | bytes 393224 | tf_op jit(solution)/shard_map/ppermute | solution.py:460
  59.9 23.1 %collective-permute-start.14 = (bf16[256,256]{1,0:T(8,128)(2,1)S(1)}, bf16[256,256]{1,0:T(8,128)(2,1)S(1)}, u32[]{:S(2)}, u32[]{:S(2)}) collective-permute-start(bf16[256,256]{1,0:T(8,128)(2,1)S(1)} %get-tuple-element.66), channel_id=1, source_target_pairs={{192,0},{256,64},{320,128},{384,192},{448,256},{193,1},{257,65},{3... | collective-permute-start | bytes 393224 | tf_op jit(solution)/shard_map/ppermute | solution.py:460
  70.5 19.1 %collective-permute-start.15 = (bf16[256,256]{1,0:T(8,128)(2,1)S(1)}, bf16[256,256]{1,0:T(8,128)(2,1)S(1)}, u32[]{:S(2)}, u32[]{:S(2)}) collective-permute-start(bf16[256,256]{1,0:T(8,128)(2,1)S(1)} %get-tuple-element.67), channel_id=1, source_target_pairs={{128,0},{192,64},{256,128},{320,192},{384,256},{448,320},{129,1},{... | collective-permute-start | bytes 393224 | tf_op jit(solution)/shard_map/ppermute | solution.py:460
  72.4 22.7 %collective-permute-start.16 = (bf16[256,256]{1,0:T(8,128)(2,1)S(1)}, bf16[256,256]{1,0:T(8,128)(2,1)S(1)}, u32[]{:S(2)}, u32[]{:S(2)}) collective-permute-start(bf16[256,256]{1,0:T(8,128)(2,1)S(1)} %get-tuple-element.68), channel_id=1, source_target_pairs={{64,0},{128,64},{192,128},{256,192},{320,256},{384,320},{448,384},... | collective-permute-start | bytes 393224 | tf_op jit(solution)/shard_map/ppermute | solution.py:460
  75.4 20.4 %collective-permute-start.10 = (bf16[256,640]{1,0:T(8,128)(2,1)S(1)}, bf16[256,640]{1,0:T(8,128)(2,1)S(1)}, u32[]{:S(2)}, u32[]{:S(2)}) collective-permute-start(bf16[256,640]{1,0:T(8,128)(2,1)S(1)} %get-tuple-element.61), channel_id=1, source_target_pairs={{0,32},{32,0},{1,33},{33,1},{2,34},{34,2},{3,35},{35,3},{4,36},{36... | collective-permute-start | bytes 983048 | tf_op jit(solution)/shard_map/ppermute | solution.py:336
  (1 other events, 0.7 us)

commit v12 on v11

--- a/solution.py
+++ b/solution.py
@@ -382,7 +382,7 @@
     grad, stats = lax.optimization_barrier((grad, stats))
     grad_other = swap(grad)
     half = jax.ShapeDtypeStruct((rows, columns), jnp.bfloat16)
-    params = pltpu.CompilerParams(vmem_limit_bytes=22 << 20)
+    params = pltpu.CompilerParams(vmem_limit_bytes=24 << 20)
     move = pltpu.VMEM((rows, wide), jnp.bfloat16)
 
     def held(blocks):
@@ -453,7 +453,7 @@
     grad = lax.all_to_all(arrived, "tensor", split_axis=2, concat_axis=1, tiled=True)[0, :, 0, :]
     position = jnp.stack([lax.axis_index("chip"), lax.axis_index("core")]).astype(jnp.int32)
     place = jnp.concatenate([position, doc_lengths[0]])
-    split = slots // 2
+    split = max(slots // 3, 1)
 
     def send(blocks, first):
         return [

time: 97.1 us -> 97.7 us (level)
  the two profiles are of different devices: /device:TPU:225 before, /device:TPU:1 now
where the time goes in v12:
time: 97.7 us; the launch traced here: 96 us
  starting transfers between devices  61.1 us (63%)
  waiting for transfers between devices  17.8 us (18%)
  Pallas kernels  11.4 us (12%)
  local copies, waits for them, and re-layouts  2.4 us (2%)
  other arithmetic  2.33 us (2%)
    ppermute x6, starting transfers between devices, per_device(): lax.ppermute(pairs, 'chip', [(c, c + back) for c in range(chips - back)])  25.2 us
    ppermute x4, starting transfers between devices, swap_cores(): return lax.ppermute(value, 'core', [(0, 1), (1, 0)])  16.1 us
    ppermute x6, waiting for transfers between devices, send(): lax.ppermute(block, 'chip', [(c, c - first - at) for c in range(first + a...  15.1 us
    ppermute x6, starting transfers between devices, send(): lax.ppermute(block, 'chip', [(c, c - first - at) for c in range(first + a...  7.74 us
    all_to_all x1, starting transfers between devices, per_device(): lax.all_to_all(arrived, 'tensor', split_axis=2, concat_axis=1, tiled=True)  6.82 us
    ppermute x1, starting transfers between devices, per_device(): lax.ppermute(incoming_output_grad, 'pipe', [(s, (s - 1) % sections) for s...  5.22 us
    pallas_call x1, Pallas kernels, attend(): pl.pallas_call(forward_kernel, out_shape=(pltpu.HBM((slots * rows, wide),...  4.89 us
    pallas_call x1, Pallas kernels, near_call(): pl.pallas_call(functools.partial(backward_near_kernel, first=first, ends=...  3.49 us
  transfers between devices with their start and end apart: 18, of which 4 were waited for; matrix products, arithmetic and copies ran while one was open for 2% of the time, Pallas kernels for 9%

profile of v12, /device:TPU:1, one launch (start us, length us, event | category | flops | bytes accessed | tf_op | source)
XLA Modules:
  0.0 96.0 jit_solution(10487902662381324475)
XLA Ops:
  1.6 5.2 %collective-permute-start = (bf16[1,32,8,640]{3,1,0,2:T(8,128)(2,1)S(1)}, bf16[1,32,8,640]{3,1,0,2:T(8,128)(2,1)}, u32[]{:S(2)}, u32[]{:S(2)}) collective-permute-start(bf16[1,32,8,640]{3,1,0,2:T(8,128)(2,1)S(1)} %copy.8), channel_id=1, source_target_pairs={{0,3},{1,0},{2,1},{3,2},{4,7},{5,4},{6,5},{7,6},{8,11},{9,8},{10,9... | collective-permute-start | bytes 983048 | tf_op jit(solution)/shard_map/ppermute | solution.py:449
  6.9 5.5 %collective-permute-start.7 = (bf16[256,640]{1,0:T(8,128)(2,1)}, bf16[256,640]{1,0:T(8,128)(2,1)S(1)}, u32[]{:S(2)}, u32[]{:S(2)}) collective-permute-start(bf16[256,640]{1,0:T(8,128)(2,1)} %bitcast.15), channel_id=1, source_target_pairs={{0,32},{32,0},{1,33},{33,1},{2,34},{34,2},{3,35},{35,3},{4,36},{36... | collective-permute-start | bytes 983048 | tf_op jit(solution)/shard_map/ppermute | solution.py:336
  12.4 3.2 %collective-permute-start.2 = (bf16[256,256]{1,0:T(8,128)(2,1)}, bf16[256,256]{1,0:T(8,128)(2,1)S(1)}, u32[]{:S(2)}, u32[]{:S(2)}) collective-permute-start(bf16[256,256]{1,0:T(8,128)(2,1)} %bitcast.23), channel_id=1, source_target_pairs={{0,128},{64,192},{128,256},{192,320},{256,384},{320,448},{1,129},{... | collective-permute-start | bytes 393224 | tf_op jit(solution)/shard_map/ppermute | solution.py:445
  15.6 4.0 %collective-permute-start.1 = (bf16[256,256]{1,0:T(8,128)(2,1)}, bf16[256,256]{1,0:T(8,128)(2,1)S(1)}, u32[]{:S(2)}, u32[]{:S(2)}) collective-permute-start(bf16[256,256]{1,0:T(8,128)(2,1)} %bitcast.24), channel_id=1, source_target_pairs={{0,64},{64,128},{128,192},{192,256},{256,320},{320,384},{384,448},... | collective-permute-start | bytes 393224 | tf_op jit(solution)/shard_map/ppermute | solution.py:445
  19.6 5.2 %collective-permute-start.6 = (bf16[256,256]{1,0:T(8,128)(2,1)}, bf16[256,256]{1,0:T(8,128)(2,1)S(1)}, u32[]{:S(2)}, u32[]{:S(2)}) collective-permute-start(bf16[256,256]{1,0:T(8,128)(2,1)} %bitcast.25), channel_id=1, source_target_pairs={{0,384},{64,448},{1,385},{65,449},{2,386},{66,450},{3,387},{67,451... | collective-permute-start | bytes 393224 | tf_op jit(solution)/shard_map/ppermute | solution.py:445
  24.8 5.0 %collective-permute-start.5 = (bf16[256,256]{1,0:T(8,128)(2,1)}, bf16[256,256]{1,0:T(8,128)(2,1)S(1)}, u32[]{:S(2)}, u32[]{:S(2)}) collective-permute-start(bf16[256,256]{1,0:T(8,128)(2,1)} %bitcast.26), channel_id=1, source_target_pairs={{0,320},{64,384},{128,448},{1,321},{65,385},{129,449},{2,322},{66,... | collective-permute-start | bytes 393224 | tf_op jit(solution)/shard_map/ppermute | solution.py:445
  29.9 5.8 %collective-permute-start.4 = (bf16[256,256]{1,0:T(8,128)(2,1)}, bf16[256,256]{1,0:T(8,128)(2,1)S(1)}, u32[]{:S(2)}, u32[]{:S(2)}) collective-permute-start(bf16[256,256]{1,0:T(8,128)(2,1)} %bitcast.27), channel_id=1, source_target_pairs={{0,256},{64,320},{128,384},{192,448},{1,257},{65,321},{129,385},{1... | collective-permute-start | bytes 393224 | tf_op jit(solution)/shard_map/ppermute | solution.py:445
  35.7 2.0 %collective-permute-start.3 = (bf16[256,256]{1,0:T(8,128)(2,1)}, bf16[256,256]{1,0:T(8,128)(2,1)S(1)}, u32[]{:S(2)}, u32[]{:S(2)}) collective-permute-start(bf16[256,256]{1,0:T(8,128)(2,1)} %bitcast.28), channel_id=1, source_target_pairs={{0,192},{64,256},{128,320},{192,384},{256,448},{1,193},{65,257},{1... | collective-permute-start | bytes 393224 | tf_op jit(solution)/shard_map/ppermute | solution.py:445
  38.5 6.8 %all-to-all-start = ((bf16[1,32,8,640]{3,1,0,2:T(8,128)(2,1)}), bf16[1,32,8,640]{3,1,0,2:T(8,128)(2,1)S(1)}, u32[]{:S(2)}, u32[]{:S(2)}) async-start(bf16[1,32,8,640]{3,1,0,2:T(8,128)(2,1)} %collective-permute-done), calls=%async_computation | async-start | bytes 655360 | tf_op jit(solution)/shard_map/all_to_all | solution.py:453
  46.7 4.9 %attend_forward.1 = (bf16[1792,2560]{1,0:T(8,128)(2,1)}, bf16[1792,256]{1,0:T(8,128)(2,1)S(1)}, f32[144,2560]{1,0:T(8,128)S(1)}, f32[8,2560]{1,0:T(8,128)S(1)}, bf16[144,2560]{1,0:T(8,128)(2,1)}) custom-call(s32[10]{0:T(128)S(1)} %pad_add_fusion.place_ref, bf16[256,640]{1,0:T(8,128)(2,1)} %bitcast.16, ...), custom_call_target="tpu_custom_call" | custom-call | flops 2348810240 | bytes 9175040 | tf_op jit(solution)/shard_map/attend_forward/pallas_call | solution.py:354
  51.6 3.3 %collective-permute-start.8 = (bf16[144,2560]{1,0:T(8,128)(2,1)}, bf16[144,2560]{1,0:T(8,128)(2,1)}, u32[]{:S(2)}, u32[]{:S(2)}) collective-permute-start(bf16[144,2560]{1,0:T(8,128)(2,1)} %get-tuple-element.50), channel_id=1, source_target_pairs={{0,32},{32,0},{1,33},{33,1},{2,34},{34,2},{3,35},{35,3},{4,36},{36... | collective-permute-start | bytes 2211848 | tf_op jit(solution)/shard_map/ppermute | solution.py:336
  55.0 1.5 %all-to-all-done = bf16[1,32,8,640]{3,1,0,2:T(8,128)(2,1)S(1)} async-done(((bf16[1,32,8,640]{3,1,0,2:T(8,128)(2,1)}), bf16[1,32,8,640]{3,1,0,2:T(8,128)(2,1)S(1)}, u32[]{:S(2)}, u32[]{:S(2)}) %all-to-all-start) | async-done | bytes 327712 | tf_op jit(solution)/shard_map/all_to_all | solution.py:453
  56.4 5.0 %collective-permute-start.9 = (bf16[256,640]{1,0:T(8,128)(2,1)S(1)}, bf16[256,640]{1,0:T(8,128)(2,1)S(1)}, u32[]{:S(2)}, u32[]{:S(2)}) collective-permute-start(bf16[256,640]{1,0:T(8,128)(2,1)S(1)} %bitcast.19), channel_id=1, source_target_pairs={{0,32},{32,0},{1,33},{33,1},{2,34},{34,2},{3,35},{35,3},{4,36},{36... | collective-permute-start | bytes 983048 | tf_op jit(solution)/shard_map/ppermute | solution.py:336
  62.7 3.0 %attend_backward_far.1 = (bf16[256,640]{1,0:T(8,128)(2,1)}, bf16[2560,128]{1,0:T(8,128)(2,1)S(1)}, bf16[128,2560]{1,0:T(8,128)(2,1)S(1)}, f32[1,2560]{1,0:T(1,12...) custom-call(s32[10]{0:T(128)S(1)} %pad_add_fusion.place_ref, ...), custom_call_target="tpu_custom_call" | custom-call | flops 3355443200 | bytes 6553600 | tf_op jit(solution)/shard_map/attend_backward_far/pallas_call | solution.py:397
  65.7 1.3 %collective-permute-start.11 = (bf16[256,256]{1,0:T(8,128)(2,1)S(1)}, bf16[256,256]{1,0:T(8,128)(2,1)S(1)}, u32[]{:S(2)}, u32[]{:S(2)}) collective-permute-start(bf16[256,256]{1,0:T(8,128)(2,1)S(1)} %get-tuple-element.63), channel_id=1, source_target_pairs={{384,0},{448,64},{385,1},{449,65},{386,2},{450,66},{387,3},{451,67... | collective-permute-start | bytes 393224 | tf_op jit(solution)/shard_map/ppermute | solution.py:460
  67.0 1.3 %collective-permute-start.12 = (bf16[256,256]{1,0:T(8,128)(2,1)S(1)}, bf16[256,256]{1,0:T(8,128)(2,1)S(1)}, u32[]{:S(2)}, u32[]{:S(2)}) collective-permute-start(bf16[256,256]{1,0:T(8,128)(2,1)S(1)} %get-tuple-element.64), channel_id=1, source_target_pairs={{320,0},{384,64},{448,128},{321,1},{385,65},{449,129},{322,2},{386... | collective-permute-start | bytes 393224 | tf_op jit(solution)/shard_map/ppermute | solution.py:460
  68.3 1.3 %collective-permute-start.13 = (bf16[256,256]{1,0:T(8,128)(2,1)S(1)}, bf16[256,256]{1,0:T(8,128)(2,1)S(1)}, u32[]{:S(2)}, u32[]{:S(2)}) collective-permute-start(bf16[256,256]{1,0:T(8,128)(2,1)S(1)} %get-tuple-element.65), channel_id=1, source_target_pairs={{256,0},{320,64},{384,128},{448,192},{257,1},{321,65},{385,129},{4... | collective-permute-start | bytes 393224 | tf_op jit(solution)/shard_map/ppermute | solution.py:460
  69.6 1.3 %collective-permute-start.14 = (bf16[256,256]{1,0:T(8,128)(2,1)S(1)}, bf16[256,256]{1,0:T(8,128)(2,1)S(1)}, u32[]{:S(2)}, u32[]{:S(2)}) collective-permute-start(bf16[256,256]{1,0:T(8,128)(2,1)S(1)} %get-tuple-element.66), channel_id=1, source_target_pairs={{192,0},{256,64},{320,128},{384,192},{448,256},{193,1},{257,65},{3... | collective-permute-start | bytes 393224 | tf_op jit(solution)/shard_map/ppermute | solution.py:460
  70.9 1.3 %collective-permute-start.15 = (bf16[256,256]{1,0:T(8,128)(2,1)S(1)}, bf16[256,256]{1,0:T(8,128)(2,1)S(1)}, u32[]{:S(2)}, u32[]{:S(2)}) collective-permute-start(bf16[256,256]{1,0:T(8,128)(2,1)S(1)} %get-tuple-element.67), channel_id=1, source_target_pairs={{128,0},{192,64},{256,128},{320,192},{384,256},{448,320},{129,1},{... | collective-permute-start | bytes 393224 | tf_op jit(solution)/shard_map/ppermute | solution.py:460
  72.2 3.5 %attend_backward_near.1 = (bf16[256,640]{1,0:T(8,128)(2,1)S(1)}, bf16[256,640]{1,0:T(8,128)(2,1)S(1)}, bf16[256,256]{1,0:T(8,128)(2,1)S(1)}, bf16[256,256]{1,0:T(8,128)(2,1)S(1)}) custom-call(s32[10]{0:T(128)S(1)} %pad_add_fusion.place_ref, bf16[2560,128]{1,0:T(8,128)(2,1)S(1)} %get-tuple-element.56.scaled_ref, ...), custom_call_target="tpu_custom_call" | custom-call | flops 1342177280 | bytes 2621440 | tf_op jit(solution)/shard_map/attend_backward_near/pallas_call | solution.py:418
  75.7 12.3 %collective-permute-done.11 = bf16[256,256]{1,0:T(8,128)(2,1)S(1)} collective-permute-done((bf16[256,256]{1,0:T(8,128)(2,1)S(1)}, bf16[256,256]{1,0:T(8,128)(2,1)S(1)}, u32[]{:S(2)}, u32[]{:S(2)}) %collective-permute-start.11) | collective-permute-done | bytes 131104 | tf_op jit(solution)/shard_map/ppermute | solution.py:460
  87.9 1.3 %collective-permute-start.16 = (bf16[256,256]{1,0:T(8,128)(2,1)S(1)}, bf16[256,256]{1,0:T(8,128)(2,1)S(1)}, u32[]{:S(2)}, u32[]{:S(2)}) collective-permute-start(bf16[256,256]{1,0:T(8,128)(2,1)S(1)} %get-tuple-element.68), channel_id=1, source_target_pairs={{64,0},{128,64},{192,128},{256,192},{320,256},{384,320},{448,384},... | collective-permute-start | bytes 393224 | tf_op jit(solution)/shard_map/ppermute | solution.py:460
  89.2 2.3 %collective-permute-start.10 = (bf16[256,640]{1,0:T(8,128)(2,1)S(1)}, bf16[256,640]{1,0:T(8,128)(2,1)S(1)}, u32[]{:S(2)}, u32[]{:S(2)}) collective-permute-start(bf16[256,640]{1,0:T(8,128)(2,1)S(1)} %get-tuple-element.61), channel_id=1, source_target_pairs={{0,32},{32,0},{1,33},{33,1},{2,34},{34,2},{3,35},{35,3},{4,36},{36... | collective-permute-start | bytes 983048 | tf_op jit(solution)/shard_map/ppermute | solution.py:336
  91.7 2.8 %collective-permute-done.16 = bf16[256,256]{1,0:T(8,128)(2,1)S(1)} collective-permute-done((bf16[256,256]{1,0:T(8,128)(2,1)S(1)}, bf16[256,256]{1,0:T(8,128)(2,1)S(1)}, u32[]{:S(2)}, u32[]{:S(2)}) %collective-permute-start.16) | collective-permute-done | bytes 131104 | tf_op jit(solution)/shard_map/ppermute | solution.py:460
  (34 shorter events, 6.0 us)
Async XLA Ops:
  1.6 34.0 %collective-permute-start = (bf16[1,32,8,640]{3,1,0,2:T(8,128)(2,1)S(1)}, bf16[1,32,8,640]{3,1,0,2:T(8,128)(2,1)}, u32[]{:S(2)}, u32[]{:S(2)}) collective-permute-start(bf16[1,32,8,640]{3,1,0,2:T(8,128)(2,1)S(1)} %copy.8), channel_id=1, source_target_pairs={{0,3},{1,0},{2,1},{3,2},{4,7},{5,4},{6,5},{7,6},{8,11},{9,8},{10,9... | collective-permute-start | bytes 983048 | tf_op jit(solution)/shard_map/ppermute | solution.py:449
  6.9 39.9 %collective-permute-start.7 = (bf16[256,640]{1,0:T(8,128)(2,1)}, bf16[256,640]{1,0:T(8,128)(2,1)S(1)}, u32[]{:S(2)}, u32[]{:S(2)}) collective-permute-start(bf16[256,640]{1,0:T(8,128)(2,1)} %bitcast.15), channel_id=1, source_target_pairs={{0,32},{32,0},{1,33},{33,1},{2,34},{34,2},{3,35},{35,3},{4,36},{36... | collective-permute-start | bytes 983048 | tf_op jit(solution)/shard_map/ppermute | solution.py:336
  12.4 12.5 %collective-permute-start.2 = (bf16[256,256]{1,0:T(8,128)(2,1)}, bf16[256,256]{1,0:T(8,128)(2,1)S(1)}, u32[]{:S(2)}, u32[]{:S(2)}) collective-permute-start(bf16[256,256]{1,0:T(8,128)(2,1)} %bitcast.23), channel_id=1, source_target_pairs={{0,128},{64,192},{128,256},{192,320},{256,384},{320,448},{1,129},{... | collective-permute-start | bytes 393224 | tf_op jit(solution)/shard_map/ppermute | solution.py:445
  15.6 14.3 %collective-permute-start.1 = (bf16[256,256]{1,0:T(8,128)(2,1)}, bf16[256,256]{1,0:T(8,128)(2,1)S(1)}, u32[]{:S(2)}, u32[]{:S(2)}) collective-permute-start(bf16[256,256]{1,0:T(8,128)(2,1)} %bitcast.24), channel_id=1, source_target_pairs={{0,64},{64,128},{128,192},{192,256},{256,320},{320,384},{384,448},... | collective-permute-start | bytes 393224 | tf_op jit(solution)/shard_map/ppermute | solution.py:445
  19.6 25.7 %collective-permute-start.6 = (bf16[256,256]{1,0:T(8,128)(2,1)}, bf16[256,256]{1,0:T(8,128)(2,1)S(1)}, u32[]{:S(2)}, u32[]{:S(2)}) collective-permute-start(bf16[256,256]{1,0:T(8,128)(2,1)} %bitcast.25), channel_id=1, source_target_pairs={{0,384},{64,448},{1,385},{65,449},{2,386},{66,450},{3,387},{67,451... | collective-permute-start | bytes 393224 | tf_op jit(solution)/shard_map/ppermute | solution.py:445
  24.8 10.9 %copy-start.1 = (bf16[256,256]{1,0:T(8,128)(2,1)}, bf16[256,256]{1,0:T(8,128)(2,1)S(1)}, u32[]{:S(2)}) copy-start(bf16[256,256]{1,0:T(8,128)(2,1)S(1)} %collective-permute-done.2.rest_2_) | copy-start | bytes 393220
  24.8 20.5 %collective-permute-start.5 = (bf16[256,256]{1,0:T(8,128)(2,1)}, bf16[256,256]{1,0:T(8,128)(2,1)S(1)}, u32[]{:S(2)}, u32[]{:S(2)}) collective-permute-start(bf16[256,256]{1,0:T(8,128)(2,1)} %bitcast.26), channel_id=1, source_target_pairs={{0,320},{64,384},{128,448},{1,321},{65,385},{129,449},{2,322},{66,... | collective-permute-start | bytes 393224 | tf_op jit(solution)/shard_map/ppermute | solution.py:445
  29.9 7.8 %copy-start.2 = (bf16[256,256]{1,0:T(8,128)(2,1)}, bf16[256,256]{1,0:T(8,128)(2,1)S(1)}, u32[]{:S(2)}) copy-start(bf16[256,256]{1,0:T(8,128)(2,1)S(1)} %collective-permute-done.1.rest_1_) | copy-start | bytes 393220
  29.9 15.4 %collective-permute-start.4 = (bf16[256,256]{1,0:T(8,128)(2,1)}, bf16[256,256]{1,0:T(8,128)(2,1)S(1)}, u32[]{:S(2)}, u32[]{:S(2)}) collective-permute-start(bf16[256,256]{1,0:T(8,128)(2,1)} %bitcast.27), channel_id=1, source_target_pairs={{0,256},{64,320},{128,384},{192,448},{1,257},{65,321},{129,385},{1... | collective-permute-start | bytes 393224 | tf_op jit(solution)/shard_map/ppermute | solution.py:445
  35.7 9.7 %collective-permute-start.3 = (bf16[256,256]{1,0:T(8,128)(2,1)}, bf16[256,256]{1,0:T(8,128)(2,1)S(1)}, u32[]{:S(2)}, u32[]{:S(2)}) collective-permute-start(bf16[256,256]{1,0:T(8,128)(2,1)} %bitcast.28), channel_id=1, source_target_pairs={{0,192},{64,256},{128,320},{192,384},{256,448},{1,193},{65,257},{1... | collective-permute-start | bytes 393224 | tf_op jit(solution)/shard_map/ppermute | solution.py:445
  38.5 18.0 %all-to-all-start = ((bf16[1,32,8,640]{3,1,0,2:T(8,128)(2,1)}), bf16[1,32,8,640]{3,1,0,2:T(8,128)(2,1)S(1)}, u32[]{:S(2)}, u32[]{:S(2)}) async-start(bf16[1,32,8,640]{3,1,0,2:T(8,128)(2,1)} %collective-permute-done), calls=%async_computation | async-start | bytes 655360 | tf_op jit(solution)/shard_map/all_to_all | solution.py:453
  45.3 17.4 %copy-start = (bf16[1,256,1,640]{3,1,2,0:T(8,128)(2,1)S(1)}, bf16[1,256,1,640]{3,1,2,0:T(8,128)(2,1)}, u32[]{:S(2)}) copy-start(bf16[1,256,1,640]{3,1,2,0:T(8,128)(2,1)} %param.4) | copy-start | bytes 983044
  45.3 0.7 copy-start.4
  45.3 0.7 copy-start.5
  46.1 0.7 copy-start.6
  51.6 9.8 %collective-permute-start.8 = (bf16[144,2560]{1,0:T(8,128)(2,1)}, bf16[144,2560]{1,0:T(8,128)(2,1)}, u32[]{:S(2)}, u32[]{:S(2)}) collective-permute-start(bf16[144,2560]{1,0:T(8,128)(2,1)} %get-tuple-element.50), channel_id=1, source_target_pairs={{0,32},{32,0},{1,33},{33,1},{2,34},{34,2},{3,35},{35,3},{4,36},{36... | collective-permute-start | bytes 2211848 | tf_op jit(solution)/shard_map/ppermute | solution.py:336
  56.4 6.2 %collective-permute-start.9 = (bf16[256,640]{1,0:T(8,128)(2,1)S(1)}, bf16[256,640]{1,0:T(8,128)(2,1)S(1)}, u32[]{:S(2)}, u32[]{:S(2)}) collective-permute-start(bf16[256,640]{1,0:T(8,128)(2,1)S(1)} %bitcast.19), channel_id=1, source_target_pairs={{0,32},{32,0},{1,33},{33,1},{2,34},{34,2},{3,35},{35,3},{4,36},{36... | collective-permute-start | bytes 983048 | tf_op jit(solution)/shard_map/ppermute | solution.py:336
  65.7 22.3 %collective-permute-start.11 = (bf16[256,256]{1,0:T(8,128)(2,1)S(1)}, bf16[256,256]{1,0:T(8,128)(2,1)S(1)}, u32[]{:S(2)}, u32[]{:S(2)}) collective-permute-start(bf16[256,256]{1,0:T(8,128)(2,1)S(1)} %get-tuple-element.63), channel_id=1, source_target_pairs={{384,0},{448,64},{385,1},{449,65},{386,2},{450,66},{387,3},{451,67... | collective-permute-start | bytes 393224 | tf_op jit(solution)/shard_map/ppermute | solution.py:460
  67.0 22.3 %collective-permute-start.12 = (bf16[256,256]{1,0:T(8,128)(2,1)S(1)}, bf16[256,256]{1,0:T(8,128)(2,1)S(1)}, u32[]{:S(2)}, u32[]{:S(2)}) collective-permute-start(bf16[256,256]{1,0:T(8,128)(2,1)S(1)} %get-tuple-element.64), channel_id=1, source_target_pairs={{320,0},{384,64},{448,128},{321,1},{385,65},{449,129},{322,2},{386... | collective-permute-start | bytes 393224 | tf_op jit(solution)/shard_map/ppermute | solution.py:460
  68.3 23.3 %collective-permute-start.13 = (bf16[256,256]{1,0:T(8,128)(2,1)S(1)}, bf16[256,256]{1,0:T(8,128)(2,1)S(1)}, u32[]{:S(2)}, u32[]{:S(2)}) collective-permute-start(bf16[256,256]{1,0:T(8,128)(2,1)S(1)} %get-tuple-element.65), channel_id=1, source_target_pairs={{256,0},{320,64},{384,128},{448,192},{257,1},{321,65},{385,129},{4... | collective-permute-start | bytes 393224 | tf_op jit(solution)/shard_map/ppermute | solution.py:460
  69.6 22.0 %collective-permute-start.14 = (bf16[256,256]{1,0:T(8,128)(2,1)S(1)}, bf16[256,256]{1,0:T(8,128)(2,1)S(1)}, u32[]{:S(2)}, u32[]{:S(2)}) collective-permute-start(bf16[256,256]{1,0:T(8,128)(2,1)S(1)} %get-tuple-element.66), channel_id=1, source_target_pairs={{192,0},{256,64},{320,128},{384,192},{448,256},{193,1},{257,65},{3... | collective-permute-start | bytes 393224 | tf_op jit(solution)/shard_map/ppermute | solution.py:460
  70.9 20.7 %collective-permute-start.15 = (bf16[256,256]{1,0:T(8,128)(2,1)S(1)}, bf16[256,256]{1,0:T(8,128)(2,1)S(1)}, u32[]{:S(2)}, u32[]{:S(2)}) collective-permute-start(bf16[256,256]{1,0:T(8,128)(2,1)S(1)} %get-tuple-element.67), channel_id=1, source_target_pairs={{128,0},{192,64},{256,128},{320,192},{384,256},{448,320},{129,1},{... | collective-permute-start | bytes 393224 | tf_op jit(solution)/shard_map/ppermute | solution.py:460
  87.9 6.6 %collective-permute-start.16 = (bf16[256,256]{1,0:T(8,128)(2,1)S(1)}, bf16[256,256]{1,0:T(8,128)(2,1)S(1)}, u32[]{:S(2)}, u32[]{:S(2)}) collective-permute-start(bf16[256,256]{1,0:T(8,128)(2,1)S(1)} %get-tuple-element.68), channel_id=1, source_target_pairs={{64,0},{128,64},{192,128},{256,192},{320,256},{384,320},{448,384},... | collective-permute-start | bytes 393224 | tf_op jit(solution)/shard_map/ppermute | solution.py:460
  89.2 6.0 %collective-permute-start.10 = (bf16[256,640]{1,0:T(8,128)(2,1)S(1)}, bf16[256,640]{1,0:T(8,128)(2,1)S(1)}, u32[]{:S(2)}, u32[]{:S(2)}) collective-permute-start(bf16[256,640]{1,0:T(8,128)(2,1)S(1)} %get-tuple-element.61), channel_id=1, source_target_pairs={{0,32},{32,0},{1,33},{33,1},{2,34},{34,2},{3,35},{35,3},{4,36},{36... | collective-permute-start | bytes 983048 | tf_op jit(solution)/shard_map/ppermute | solution.py:336
  (1 other events, 0.7 us)
